TPU v7x, 128 devices: a whole 4x4x4 slice. The times are simulated.
128 devices in a mesh: gx: 16 (over x, y), gy: 8 (over z, core).
Axes of the slice: x: 4, y: 4, z: 4, core: 2. Of those that a mesh axis runs over, the one named last changes fastest.
Arguments:
- volts: float32 [32, 4, 128, 1024], P(None, None, 'gx', 'gy'), may hold values from -6 to 6
- cap: float32 [4, 128, 1024], P(None, 'gx', 'gy'), may hold values from 0.05 to 1
- cond_x: float32 [4, 128, 1024], P(None, 'gx', 'gy'), may hold values from 0.5 to 2
- cond_y: float32 [4, 128, 1024], P(None, 'gx', 'gy'), may hold values from 0.5 to 2
- via: float32 [4, 128, 1024], P(None, 'gx', 'gy'), may hold values from 0.2 to 2
- waveforms: float32 [64, 64], replicated, may hold values from -6 to 6
- placement: int32 [1048576, 1], P(('gx', 'gy')), may hold values from 0 to 127; in each aligned block of 8192 rows (0 to 8191, 8192 to 16383, ...) at most 128 rows name the same one
- cells: int32 [1048576], P(('gx', 'gy')), may hold values from 0 to 1023
- wave_ids: int32 [1048576], P(('gx', 'gy')), may hold values from 0 to 63
- amps: float32 [1048576], P(('gx', 'gy')), may hold values from 0.5 to 4
Outputs:
- volts_out: float32 [32, 4, 128, 1024], P(None, None, 'gx', 'gy')
- residual: float32 [32, 4, 128, 1024], P(None, None, 'gx', 'gy')
Inputs may be any that keep to these rules, and one draw needn't show every extreme that they name: `placement`: in each device's block of 8192 rows no tile is named more than 128 times, a bound that some block reaches.
All inputs are finite; a program needn't handle non-finite values.
Results may differ from a plain program's by a relative error of at most 0.0029.
Values may be sent and summed in bfloat16 or wider, within the bound.
No kernel may reach another device: no remote copies, remote signals or barrier semaphores. Data moves between devices by JAX's collectives and lax.ppermute only.
A program may use at most 64 MiB of HBM per device.

v0:
```python
import functools

import jax
import jax.numpy as jnp
from jax import lax
from jax.sharding import Mesh
from jax.sharding import PartitionSpec as P

ITERS = 3
GX_GY = ("gx_0", "gx_1", "gy_0", "gy_1")
GX = ("gx_0", "gx_1")
GY = ("gy_0", "gy_1")


def with_halo(x, sides, width):
    edges = {}
    for axis, dim in sides:
        size, length = (lax.axis_size(axis), x.shape[dim])
        up = [(i, (i + 1) % size) for i in range(size - 1)]
        last = lax.slice_in_dim(x, length - width, length, axis=dim)
        initial = lax.slice_in_dim(x, 0, width, axis=dim)
        edges[dim] = (
            lax.ppermute(last, axis, up),
            lax.ppermute(initial, axis, [(b, a) for a, b in up]),
        )
    done = []
    for _, dim in sides:
        low, high = edges[dim]
        around = [(width, width) if d in done else (0, 0) for d in range(x.ndim)]
        x = jnp.concatenate([jnp.pad(low, around), x, jnp.pad(high, around)], axis=dim)
        done.append(dim)
    return x


def shifted(x, axis, by):
    length = lax.axis_size(axis)
    pairs = [(i, i + by) for i in range(length) if 0 <= i + by < length]
    return lax.ppermute(x, axis, pairs)


def by_axis(x, axes):
    return functools.reduce(lax.psum, axes, x)


def gram(left, right):
    left_rows = left.reshape(left.shape[0], -1)
    right_rows = right.reshape(right.shape[0], -1)
    return lax.dot_general(
        left_rows, right_rows, (((1,), (1,)), ((), ())), precision=lax.Precision.HIGHEST
    )


def combine(coef, field):
    return jnp.einsum("st,slxy->tlxy", coef, field, precision=lax.Precision.HIGHEST)


def spd_solve(matrix, right):
    factor = jnp.linalg.cholesky(matrix)
    return jax.scipy.linalg.cho_solve((factor, True), right)


def make_currents(waveforms, kinds, scales):
    table_hits = (
        jnp.arange(waveforms.shape[1], dtype=jnp.int32)[:, None] == kinds[None, :]
    ).astype(jnp.float32)
    picked = jnp.dot(waveforms, table_hits, precision=lax.Precision.HIGHEST)
    return (picked * scales[None, :]).astype(jnp.bfloat16)


def operate(field, cap, cond_x, cond_x_low, cond_y, cond_y_low, via, via_low):
    padded = with_halo(field, ((GX, 2), (GY, 3)), 1)
    zero_layer = jnp.zeros_like(field[:, :1])
    upper = jnp.concatenate([field[:, 1:], zero_layer], axis=1)
    lower = jnp.concatenate([zero_layer, field[:, :-1]], axis=1)
    result = cap * field
    result = result + cond_x * (field - padded[:, :, 2:, 1:-1])
    result = result + cond_x_low * (field - padded[:, :, :-2, 1:-1])
    result = result + cond_y * (field - padded[:, :, 1:-1, 2:])
    result = result + cond_y_low * (field - padded[:, :, 1:-1, :-2])
    result = result + via * (field - upper) + via_low * (field - lower)
    return result


def body(volts, cap, cond_x, cond_y, via, waveforms, placement, cells, wave_ids, amps):
    devices = lax.axis_size(GX_GY)
    scenarios = volts.shape[0]
    steps = waveforms.shape[0] // scenarios
    tile_x = volts.shape[2]
    tile_y = volts.shape[3]
    die_cells = tile_x * tile_y
    slots_all = 2 * cells.shape[0]
    capacity = slots_all // devices
    target = placement[:, 0]
    target_hits = (jnp.arange(devices, dtype=jnp.int32)[:, None] == target[None, :]).astype(
        jnp.int32
    )
    running = jnp.cumsum(target_hits, axis=1) - 1
    position = jnp.sum(target_hits * running, axis=0)
    slot_index = target * capacity + position
    currents = make_currents(waveforms, wave_ids, amps)
    packed = jnp.zeros((currents.shape[0], slots_all), jnp.bfloat16).at[:, slot_index].set(currents)
    cell_slots = jnp.zeros((1, slots_all), jnp.int32).at[0, slot_index].set(cells)
    arrived, cell_slots = (
        lax.all_to_all(packed, GX_GY, split_axis=1, concat_axis=1, tiled=True),
        lax.all_to_all(cell_slots, GX_GY, split_axis=1, concat_axis=1, tiled=True),
    )
    block_rows = min(1024, slots_all)
    block_count = slots_all // block_rows
    cell_line = jnp.arange(die_cells, dtype=jnp.int32)

    def add_block(turn, total):
        piece_values = lax.dynamic_slice_in_dim(arrived, turn * block_rows, block_rows, 1)
        piece_cells = lax.dynamic_slice_in_dim(cell_slots[0], turn * block_rows, block_rows, 0)
        one_hot = (piece_cells[:, None] == cell_line[None, :]).astype(jnp.bfloat16)
        return total + jnp.dot(piece_values, one_hot, preferred_element_type=jnp.float32)

    injected = lax.fori_loop(
        0, block_count, add_block, jnp.zeros((arrived.shape[0], die_cells), jnp.float32)
    )
    injected = injected.reshape(steps, scenarios, tile_x, tile_y)
    rim_x = shifted(cond_x[:, -1:, :], GX, 1)
    rim_y = shifted(cond_y[:, :, -1:], GY, 1)
    cond_x_low = jnp.concatenate([rim_x, cond_x[:, :-1, :]], axis=1)
    cond_y_low = jnp.concatenate([rim_y, cond_y[:, :, :-1]], axis=2)
    via_low = jnp.concatenate([jnp.zeros_like(via[:1]), via[:-1]], axis=0)

    def apply_grid(field):
        return operate(field, cap, cond_x, cond_x_low, cond_y, cond_y_low, via, via_low)

    voltage = volts
    residual = volts
    for step in range(steps):
        rhs = cap * voltage
        rhs = rhs.at[:, 0].add(-injected[step])
        iterate = voltage
        residual = rhs - apply_grid(iterate)
        direction = residual
        norm_gram = by_axis(gram(residual, residual), GX_GY)
        for sweep in range(ITERS):
            image = apply_grid(direction)
            curve_gram, cross_gram, image_gram = (
                by_axis(gram(direction, image), GX_GY),
                by_axis(gram(residual, image), GX_GY),
                by_axis(gram(image, image), GX_GY),
            )
            step_coef = spd_solve(curve_gram, norm_gram)
            iterate = iterate + combine(step_coef, direction)
            residual = residual - combine(step_coef, image)
            if sweep + 1 < ITERS:
                cross_term = jnp.dot(cross_gram, step_coef, precision=lax.Precision.HIGHEST)
                square_term = jnp.dot(
                    step_coef.T,
                    jnp.dot(image_gram, step_coef, precision=lax.Precision.HIGHEST),
                    precision=lax.Precision.HIGHEST,
                )
                new_gram = norm_gram - cross_term - cross_term.T + square_term
                turn_coef = spd_solve(norm_gram, new_gram)
                direction = residual + combine(turn_coef, direction)
                norm_gram = new_gram
        voltage = iterate
    return (voltage, residual)


def solution(mesh):
    finer = Mesh(mesh.devices.reshape(4, 4, 4, 2), ("gx_0", "gx_1", "gy_0", "gy_1"))
    in_specs = (
        P(None, None, GX, GY),
        P(None, GX, GY),
        P(None, GX, GY),
        P(None, GX, GY),
        P(None, GX, GY),
        P(),
        P(GX_GY, None),
        P(GX_GY),
        P(GX_GY),
        P(GX_GY),
    )
    out_specs = (P(None, None, GX, GY), P(None, None, GX, GY))
    return jax.shard_map(body, mesh=finer, in_specs=in_specs, out_specs=out_specs, check_vma=False)
```

profile of v0, /device:TPU:0, one launch (start us, length us, event | category | flops | bytes accessed | tf_op | source)
XLA Modules:
  0.0 690.2 jit_solution(8659340981578746071)
XLA Ops:
  4.7 5.3 select_reduce_fusion
  12.3 23.6 %scatter_custom_fusion = bf16[64,16384]{0,1:T(8,128)(2,1)} fusion(s32[8192]{0:T(1024)S(1)} %bitcast.343, bf16[8192,64]{1,0:T(8,128)(2,1)S(1)} %copy.198, bf16[]{:T(256)} %constant.131.clone.1), kind=kCustom, calls=%fused_computation.19 | custom fusion | bytes 2097154 | tf_op jit(solution)/shard_map/scatter | solution.py:101
  36.0 4.8 copy.199
  40.8 11.2 %all-to-all-start = ((bf16[64,128,128]{2,0,1:T(8,128)(2,1)}), bf16[64,128,128]{2,0,1:T(8,128)(2,1)S(1)}, u32[]{:S(2)}, u32[]{:S(2)}) async-start(bf16[64,128,128]{2,0,1:T(8,128)(2,1)} %copy.199), calls=%async_computation | async-start | bytes 4194304 | tf_op jit(solution)/shard_map/all_to_all | solution.py:104
  67.2 31.2 %scatter_custom_fusion.1 = s32[16384]{0:T(1024)} fusion(s32[8192]{0:T(1024)S(1)} %broadcast_select_fusion, s32[8192]{0:T(1024)} %param.26, s32[]{:T(128)} %constant.129.clone.1), kind=kCustom, calls=%fused_computation.288 | custom fusion | bytes 66048
  99.5 4.7 collective-permute-start.5
  107.6 12.2 %all-to-all-start.1 = ((s32[1,128,128]{2,0,1:T(1,128)}), s32[1,128,128]{2,0,1:T(1,128)S(1)}, u32[]{:S(2)}, u32[]{:S(2)}) async-start(s32[1,128,128]{2,0,1:T(1,128)} %bitcast.5), calls=%async_computation.1 | async-start | bytes 131072 | tf_op jit(solution)/shard_map/all_to_all | solution.py:105
  121.4 8.0 %all-to-all-done.1 = s32[1,128,128]{2,0,1:T(1,128)S(1)} async-done(((s32[1,128,128]{2,0,1:T(1,128)}), s32[1,128,128]{2,0,1:T(1,128)S(1)}, u32[]{:S(2)}, u32[]{:S(2)}) %all-to-all-start.1) | async-done | bytes 65568 | tf_op jit(solution)/shard_map/all_to_all | solution.py:105
  129.4 43.1 %while.16 = (s32[]{:T(128)}, f32[64,1024]{1,0:T(8,128)}, bf16[64,16384]{1,0:T(8,128)(2,1)}, s32[1,16384]{1,0:T(1,128)S(1)}, s32[]{:T(128)}, /*index=5*/s32[]{:T(128)}, s32[]{:T(128)}, s32[]{:T(128)}) while((s32[]{:T(128)}, f32[64,1024]{1,0:T(8,128)}, bf16[64,16384]{1,0:T(8,128)(2,1)}, s32[1,16384]{1,0:T(1,128)S(1)}, s32[]{:T(128)}, ...), condition=%wide.region_6.7_spmd.clone, body=%wide.region_5.6_spmd.clone.sunk | while | flops 135397376 | bytes 667797 | solution.py:117
  181.8 4.5 collective-permute-start.7
  190.0 19.9 %all-reduce.45 = (f32[32,32]{0,1:T(8,128)S(1)}, f32[32,32]{0,1:T(8,128)S(1)}, f32[32,32]{1,0:T(8,128)S(1)}) all-reduce(f32[32,32]{0,1:T(8,128)S(1)} %convolution_bitcast_fusion.18, f32[32,32]{0,1:T(8,128)S(1)} %convolution_bitcast_fusion.19, ...), channel_id=1, replica_groups=mesh['gx_0'=4,'gx_1'=4,'gy_0'=4,'gy_1'=2] {'gx_0'}, use_global_device_ids=true, to_apply=%region_13.15 | all-reduce | flops 3072 | bytes 24576 | tf_op jit(solution)/shard_map/psum | solution.py:42
  210.0 14.7 %all-reduce.41 = (f32[32,32]{0,1:T(8,128)S(1)}, f32[32,32]{0,1:T(8,128)S(1)}, f32[32,32]{1,0:T(8,128)S(1)}) all-reduce(f32[32,32]{0,1:T(8,128)S(1)} %get-tuple-element.189, f32[32,32]{0,1:T(8,128)S(1)} %get-tuple-element.190, f32[32,32]{1,0:T(8,128)S(1)} %get-tuple-element.191), channel_id=1, replica_groups=mesh['gx_0'=4,'gx_1'=4,'gy_0'=4,'gy_1'=2] {'gx_1'}, use_global_device_ids=true, to_apply=%region_14.16 | all-reduce | flops 3072 | bytes 24576 | tf_op jit(solution)/shard_map/psum | solution.py:42
  224.7 15.5 %all-reduce.37 = (f32[32,32]{0,1:T(8,128)S(1)}, f32[32,32]{0,1:T(8,128)S(1)}, f32[32,32]{1,0:T(8,128)S(1)}) all-reduce(f32[32,32]{0,1:T(8,128)S(1)} %get-tuple-element.177, f32[32,32]{0,1:T(8,128)S(1)} %get-tuple-element.178, f32[32,32]{1,0:T(8,128)S(1)} %get-tuple-element.179), channel_id=1, replica_groups=mesh['gx_0'=4,'gx_1'=4,'gy_0'=4,'gy_1'=2] {'gy_0'}, use_global_device_ids=true, to_apply=%region_15.17 | all-reduce | flops 3072 | bytes 24576 | tf_op jit(solution)/shard_map/psum | solution.py:42
  275.0 4.8 collective-permute-start.11
  287.1 18.8 %all-reduce.44 = (f32[32,32]{0,1:T(8,128)S(1)}, f32[32,32]{1,0:T(8,128)S(1)}, f32[32,32]{1,0:T(8,128)S(1)}) all-reduce(f32[32,32]{0,1:T(8,128)S(1)} %convolution_bitcast_fusion.15, f32[32,32]{1,0:T(8,128)S(1)} %convolution_bitcast_fusion.13, ...), channel_id=1, replica_groups=mesh['gx_0'=4,'gx_1'=4,'gy_0'=4,'gy_1'=2] {'gx_0'}, use_global_device_ids=true, to_apply=%region_21.24 | all-reduce | flops 3072 | bytes 24576 | tf_op jit(solution)/shard_map/psum | solution.py:42
  305.9 14.7 %all-reduce.40 = (f32[32,32]{0,1:T(8,128)S(1)}, f32[32,32]{1,0:T(8,128)S(1)}, f32[32,32]{1,0:T(8,128)S(1)}) all-reduce(f32[32,32]{0,1:T(8,128)S(1)} %get-tuple-element.186, f32[32,32]{1,0:T(8,128)S(1)} %get-tuple-element.187, f32[32,32]{1,0:T(8,128)S(1)} %get-tuple-element.188), channel_id=1, replica_groups=mesh['gx_0'=4,'gx_1'=4,'gy_0'=4,'gy_1'=2] {'gx_1'}, use_global_device_ids=true, to_apply=%region_22.25 | all-reduce | flops 3072 | bytes 24576 | tf_op jit(solution)/shard_map/psum | solution.py:42
  320.6 15.3 %all-reduce.36 = (f32[32,32]{0,1:T(8,128)S(1)}, f32[32,32]{1,0:T(8,128)S(1)}, f32[32,32]{1,0:T(8,128)S(1)}) all-reduce(f32[32,32]{0,1:T(8,128)S(1)} %get-tuple-element.174, f32[32,32]{1,0:T(8,128)S(1)} %get-tuple-element.175, f32[32,32]{1,0:T(8,128)S(1)} %get-tuple-element.176), channel_id=1, replica_groups=mesh['gx_0'=4,'gx_1'=4,'gy_0'=4,'gy_1'=2] {'gy_0'}, use_global_device_ids=true, to_apply=%region_23.26 | all-reduce | flops 3072 | bytes 24576 | tf_op jit(solution)/shard_map/psum | solution.py:42
  362.6 20.0 %psum.440 = f32[32,32]{0,1:T(8,128)S(1)} all-reduce(f32[32,32]{0,1:T(8,128)S(1)} %convolution_bitcast_fusion.11), channel_id=1, replica_groups=mesh['gx_0'=4,'gx_1'=4,'gy_0'=4,'gy_1'=2] {'gx_0'}, use_global_device_ids=true, to_apply=%region_33.36 | all-reduce | flops 1024 | bytes 8192 | tf_op jit(solution)/shard_map/psum | solution.py:42
  382.6 14.3 %psum.441 = f32[32,32]{0,1:T(8,128)S(1)} all-reduce(f32[32,32]{0,1:T(8,128)S(1)} %psum.440), channel_id=1, replica_groups=mesh['gx_0'=4,'gx_1'=4,'gy_0'=4,'gy_1'=2] {'gx_1'}, use_global_device_ids=true, to_apply=%region_34.37 | all-reduce | flops 1024 | bytes 8192 | tf_op jit(solution)/shard_map/psum | solution.py:42
  396.9 15.2 %psum.442 = f32[32,32]{0,1:T(8,128)S(1)} all-reduce(f32[32,32]{0,1:T(8,128)S(1)} %psum.441), channel_id=1, replica_groups=mesh['gx_0'=4,'gx_1'=4,'gy_0'=4,'gy_1'=2] {'gy_0'}, use_global_device_ids=true, to_apply=%region_35.38 | all-reduce | flops 1024 | bytes 8192 | tf_op jit(solution)/shard_map/psum | solution.py:42
  429.2 5.0 collective-permute-start.19
  442.6 5.0 collective-permute-start.23
  451.7 22.1 %all-reduce.43 = (f32[32,32]{0,1:T(8,128)S(1)}, f32[32,32]{0,1:T(8,128)S(1)}, f32[32,32]{1,0:T(8,128)S(1)}) all-reduce(f32[32,32]{0,1:T(8,128)S(1)} %convolution_bitcast_fusion.8, f32[32,32]{0,1:T(8,128)S(1)} %convolution_bitcast_fusion.9, ...), channel_id=1, replica_groups=mesh['gx_0'=4,'gx_1'=4,'gy_0'=4,'gy_1'=2] {'gx_0'}, use_global_device_ids=true, to_apply=%region_41.44 | all-reduce | flops 3072 | bytes 24576 | tf_op jit(solution)/shard_map/psum | solution.py:42
  473.7 14.8 %all-reduce.39 = (f32[32,32]{0,1:T(8,128)S(1)}, f32[32,32]{0,1:T(8,128)S(1)}, f32[32,32]{1,0:T(8,128)S(1)}) all-reduce(f32[32,32]{0,1:T(8,128)S(1)} %get-tuple-element.183, f32[32,32]{0,1:T(8,128)S(1)} %get-tuple-element.184, f32[32,32]{1,0:T(8,128)S(1)} %get-tuple-element.185), channel_id=1, replica_groups=mesh['gx_0'=4,'gx_1'=4,'gy_0'=4,'gy_1'=2] {'gx_1'}, use_global_device_ids=true, to_apply=%region_42.45 | all-reduce | flops 3072 | bytes 24576 | tf_op jit(solution)/shard_map/psum | solution.py:42
  488.5 15.4 %all-reduce.35 = (f32[32,32]{0,1:T(8,128)S(1)}, f32[32,32]{0,1:T(8,128)S(1)}, f32[32,32]{1,0:T(8,128)S(1)}) all-reduce(f32[32,32]{0,1:T(8,128)S(1)} %get-tuple-element.171, f32[32,32]{0,1:T(8,128)S(1)} %get-tuple-element.172, f32[32,32]{1,0:T(8,128)S(1)} %get-tuple-element.173), channel_id=1, replica_groups=mesh['gx_0'=4,'gx_1'=4,'gy_0'=4,'gy_1'=2] {'gy_0'}, use_global_device_ids=true, to_apply=%region_43.46 | all-reduce | flops 3072 | bytes 24576 | tf_op jit(solution)/shard_map/psum | solution.py:42
  551.2 18.6 %all-reduce.42 = (f32[32,32]{0,1:T(8,128)S(1)}, f32[32,32]{1,0:T(8,128)S(1)}, f32[32,32]{1,0:T(8,128)S(1)}) all-reduce(f32[32,32]{0,1:T(8,128)S(1)} %convolution_bitcast_fusion.5, f32[32,32]{1,0:T(8,128)S(1)} %convolution_bitcast_fusion.3, ...), channel_id=1, replica_groups=mesh['gx_0'=4,'gx_1'=4,'gy_0'=4,'gy_1'=2] {'gx_0'}, use_global_device_ids=true, to_apply=%region_49.52 | all-reduce | flops 3072 | bytes 24576 | tf_op jit(solution)/shard_map/psum | solution.py:42
  569.7 15.1 %all-reduce.38 = (f32[32,32]{0,1:T(8,128)S(1)}, f32[32,32]{1,0:T(8,128)S(1)}, f32[32,32]{1,0:T(8,128)S(1)}) all-reduce(f32[32,32]{0,1:T(8,128)S(1)} %get-tuple-element.180, f32[32,32]{1,0:T(8,128)S(1)} %get-tuple-element.181, f32[32,32]{1,0:T(8,128)S(1)} %get-tuple-element.182), channel_id=1, replica_groups=mesh['gx_0'=4,'gx_1'=4,'gy_0'=4,'gy_1'=2] {'gx_1'}, use_global_device_ids=true, to_apply=%region_50.53 | all-reduce | flops 3072 | bytes 24576 | tf_op jit(solution)/shard_map/psum | solution.py:42
  584.8 15.4 %all-reduce.34 = (f32[32,32]{0,1:T(8,128)S(1)}, f32[32,32]{1,0:T(8,128)S(1)}, f32[32,32]{1,0:T(8,128)S(1)}) all-reduce(f32[32,32]{0,1:T(8,128)S(1)} %get-tuple-element.168, f32[32,32]{1,0:T(8,128)S(1)} %get-tuple-element.169, f32[32,32]{1,0:T(8,128)S(1)} %get-tuple-element.170), channel_id=1, replica_groups=mesh['gx_0'=4,'gx_1'=4,'gy_0'=4,'gy_1'=2] {'gy_0'}, use_global_device_ids=true, to_apply=%region_51.54 | all-reduce | flops 3072 | bytes 24576 | tf_op jit(solution)/shard_map/psum | solution.py:42
  619.1 4.5 collective-permute-start.31
  627.1 19.5 %psum.468 = f32[32,32]{0,1:T(8,128)S(1)} all-reduce(f32[32,32]{0,1:T(8,128)S(1)} %convolution_bitcast_fusion.1), channel_id=1, replica_groups=mesh['gx_0'=4,'gx_1'=4,'gy_0'=4,'gy_1'=2] {'gx_0'}, use_global_device_ids=true, to_apply=%region_61.64 | all-reduce | flops 1024 | bytes 8192 | tf_op jit(solution)/shard_map/psum | solution.py:42
  646.6 14.3 %psum.469 = f32[32,32]{0,1:T(8,128)S(1)} all-reduce(f32[32,32]{0,1:T(8,128)S(1)} %psum.468), channel_id=1, replica_groups=mesh['gx_0'=4,'gx_1'=4,'gy_0'=4,'gy_1'=2] {'gx_1'}, use_global_device_ids=true, to_apply=%region_62.65 | all-reduce | flops 1024 | bytes 8192 | tf_op jit(solution)/shard_map/psum | solution.py:42
  660.8 15.2 %psum.470 = f32[32,32]{0,1:T(8,128)S(1)} all-reduce(f32[32,32]{0,1:T(8,128)S(1)} %psum.469), channel_id=1, replica_groups=mesh['gx_0'=4,'gx_1'=4,'gy_0'=4,'gy_1'=2] {'gy_0'}, use_global_device_ids=true, to_apply=%region_63.66 | all-reduce | flops 1024 | bytes 8192 | tf_op jit(solution)/shard_map/psum | solution.py:42
  (354 shorter events, 264.3 us)
Async XLA Ops:
  40.8 66.7 %all-to-all-start = ((bf16[64,128,128]{2,0,1:T(8,128)(2,1)}), bf16[64,128,128]{2,0,1:T(8,128)(2,1)S(1)}, u32[]{:S(2)}, u32[]{:S(2)}) async-start(bf16[64,128,128]{2,0,1:T(8,128)(2,1)} %copy.199), calls=%async_computation | async-start | bytes 4194304 | tf_op jit(solution)/shard_map/all_to_all | solution.py:104
  53.0 52.0 %collective-permute-start.2 = (f32[32,4,1,128]{3,0,2,1:T(8,128)}, f32[32,4,1,128]{3,0,2,1:T(8,128)S(1)}, u32[]{:S(2)}, u32[]{:S(2)}) collective-permute-start(f32[32,4,1,128]{3,0,2,1:T(8,128)} %get-tuple-element.251), channel_id=1, source_target_pairs={{0,8},{8,16},{16,24},{24,32},{32,40},{40,48},{48,56},{56,64},{64,7... | collective-permute-start | bytes 196616 | tf_op jit(solution)/shard_map/ppermute | solution.py:23
  55.8 51.1 %collective-permute-start = (f32[32,4,1,128]{3,0,2,1:T(8,128)S(1)}, f32[32,4,1,128]{3,0,2,1:T(8,128)S(1)}, u32[]{:S(2)}, u32[]{:S(2)}) collective-permute-start(f32[32,4,1,128]{3,0,2,1:T(8,128)S(1)} %get-tuple-element.250), channel_id=1, source_target_pairs={{8,0},{16,8},{24,16},{32,24},{40,32},{48,40},{56,48},{64,56},{72,6... | collective-permute-start | bytes 196616 | tf_op jit(solution)/shard_map/ppermute | solution.py:24
  57.8 41.7 %collective-permute-start.4 = (f32[4,8,1]{2,1,0:T(8,128)}, f32[4,8,1]{2,1,0:T(8,128)}, u32[]{:S(2)}, u32[]{:S(2)}) collective-permute-start(f32[4,8,1]{2,1,0:T(8,128)} %slice.379), channel_id=1, source_target_pairs={{0,1},{1,2},{2,3},{3,4},{4,5},{5,6},{6,7},{8,9},{9,10},{10,11},{11... | collective-permute-start | bytes 392 | tf_op jit(solution)/shard_map/ppermute | solution.py:38
  60.2 44.8 %collective-permute-start.1 = (f32[4,1,128]{2,1,0:T(1,128)S(1)}, f32[4,1,128]{2,1,0:T(1,128)S(1)}, u32[]{:S(2)}, u32[]{:S(2)}) collective-permute-start(f32[4,1,128]{2,1,0:T(1,128)S(1)} %slice.373), channel_id=1, source_target_pairs={{0,8},{8,16},{16,24},{24,32},{32,40},{40,48},{48,56},{56,64},{64,7... | collective-permute-start | bytes 6152 | tf_op jit(solution)/shard_map/ppermute | solution.py:38
  65.5 108.0 %collective-permute-start.3 = (f32[32,4,8,1]{3,0,2,1:T(8,128)}, f32[32,4,8,1]{3,0,2,1:T(8,128)}, u32[]{:S(2)}, u32[]{:S(2)}) collective-permute-start(f32[32,4,8,1]{3,0,2,1:T(8,128)} %get-tuple-element.248), channel_id=1, source_target_pairs={{1,0},{2,1},{3,2},{4,3},{5,4},{6,5},{7,6},{9,8},{10,9},{11,10},{12... | collective-permute-start | bytes 12296 | tf_op jit(solution)/shard_map/ppermute | solution.py:24
  99.5 74.1 %collective-permute-start.5 = (f32[32,4,8,1]{3,0,2,1:T(8,128)}, f32[32,4,8,1]{3,0,2,1:T(8,128)}, u32[]{:S(2)}, u32[]{:S(2)}) collective-permute-start(f32[32,4,8,1]{3,0,2,1:T(8,128)} %get-tuple-element.249), channel_id=1, source_target_pairs={{0,1},{1,2},{2,3},{3,4},{4,5},{5,6},{6,7},{8,9},{9,10},{10,11},{11... | collective-permute-start | bytes 12296 | tf_op jit(solution)/shard_map/ppermute | solution.py:23
  107.6 21.8 %all-to-all-start.1 = ((s32[1,128,128]{2,0,1:T(1,128)}), s32[1,128,128]{2,0,1:T(1,128)S(1)}, u32[]{:S(2)}, u32[]{:S(2)}) async-start(s32[1,128,128]{2,0,1:T(1,128)} %bitcast.5), calls=%async_computation.1 | async-start | bytes 131072 | tf_op jit(solution)/shard_map/all_to_all | solution.py:105
  176.1 11.5 %collective-permute-start.8 = (f32[32,4,8,1]{3,0,2,1:T(8,128)S(1)}, f32[32,4,8,1]{3,0,2,1:T(8,128)S(1)}, u32[]{:S(2)}, u32[]{:S(2)}) collective-permute-start(f32[32,4,8,1]{3,0,2,1:T(8,128)S(1)} %get-tuple-element.242), channel_id=1, source_target_pairs={{1,0},{2,1},{3,2},{4,3},{5,4},{6,5},{7,6},{9,8},{10,9},{11,10},{12... | collective-permute-start | bytes 12296 | tf_op jit(solution)/shard_map/ppermute | solution.py:24
  177.4 10.2 %collective-permute-start.9 = (f32[32,4,8,1]{3,0,2,1:T(8,128)S(1)}, f32[32,4,8,1]{3,0,2,1:T(8,128)S(1)}, u32[]{:S(2)}, u32[]{:S(2)}) collective-permute-start(f32[32,4,8,1]{3,0,2,1:T(8,128)S(1)} %get-tuple-element.243), channel_id=1, source_target_pairs={{0,1},{1,2},{2,3},{3,4},{4,5},{5,6},{6,7},{8,9},{9,10},{10,11},{11... | collective-permute-start | bytes 12296 | tf_op jit(solution)/shard_map/ppermute | solution.py:23
  180.5 7.1 %collective-permute-start.6 = (f32[32,4,1,128]{3,0,2,1:T(8,128)S(1)}, f32[32,4,1,128]{3,0,2,1:T(8,128)S(1)}, u32[]{:S(2)}, u32[]{:S(2)}) collective-permute-start(f32[32,4,1,128]{3,0,2,1:T(8,128)S(1)} %get-tuple-element.245), channel_id=1, source_target_pairs={{8,0},{16,8},{24,16},{32,24},{40,32},{48,40},{56,48},{64,56},{72,6... | collective-permute-start | bytes 196616 | tf_op jit(solution)/shard_map/ppermute | solution.py:24
  268.6 14.2 %collective-permute-start.12 = (f32[32,4,8,1]{3,0,2,1:T(8,128)}, f32[32,4,8,1]{3,0,2,1:T(8,128)S(1)}, u32[]{:S(2)}, u32[]{:S(2)}) collective-permute-start(f32[32,4,8,1]{3,0,2,1:T(8,128)} %get-tuple-element.236), channel_id=1, source_target_pairs={{1,0},{2,1},{3,2},{4,3},{5,4},{6,5},{7,6},{9,8},{10,9},{11,10},{12... | collective-permute-start | bytes 12296 | tf_op jit(solution)/shard_map/ppermute | solution.py:24
  269.8 12.9 %collective-permute-start.13 = (f32[32,4,8,1]{3,0,2,1:T(8,128)}, f32[32,4,8,1]{3,0,2,1:T(8,128)}, u32[]{:S(2)}, u32[]{:S(2)}) collective-permute-start(f32[32,4,8,1]{3,0,2,1:T(8,128)} %get-tuple-element.237), channel_id=1, source_target_pairs={{0,1},{1,2},{2,3},{3,4},{4,5},{5,6},{6,7},{8,9},{9,10},{10,11},{11... | collective-permute-start | bytes 12296 | tf_op jit(solution)/shard_map/ppermute | solution.py:23
  273.7 9.1 %collective-permute-start.10 = (f32[32,4,1,128]{3,0,2,1:T(8,128)}, f32[32,4,1,128]{3,0,2,1:T(8,128)S(1)}, u32[]{:S(2)}, u32[]{:S(2)}) collective-permute-start(f32[32,4,1,128]{3,0,2,1:T(8,128)} %get-tuple-element.239), channel_id=1, source_target_pairs={{8,0},{16,8},{24,16},{32,24},{40,32},{48,40},{56,48},{64,56},{72,6... | collective-permute-start | bytes 196616 | tf_op jit(solution)/shard_map/ppermute | solution.py:24
  275.0 7.8 %collective-permute-start.11 = (f32[32,4,1,128]{3,0,2,1:T(8,128)}, f32[32,4,1,128]{3,0,2,1:T(8,128)S(1)}, u32[]{:S(2)}, u32[]{:S(2)}) collective-permute-start(f32[32,4,1,128]{3,0,2,1:T(8,128)} %get-tuple-element.238), channel_id=1, source_target_pairs={{0,8},{8,16},{16,24},{24,32},{32,40},{40,48},{48,56},{56,64},{64,7... | collective-permute-start | bytes 196616 | tf_op jit(solution)/shard_map/ppermute | solution.py:23
  349.1 10.9 %collective-permute-start.16 = (f32[32,4,8,1]{3,0,2,1:T(8,128)S(1)}, f32[32,4,8,1]{3,0,2,1:T(8,128)S(1)}, u32[]{:S(2)}, u32[]{:S(2)}) collective-permute-start(f32[32,4,8,1]{3,0,2,1:T(8,128)S(1)} %get-tuple-element.230), channel_id=1, source_target_pairs={{1,0},{2,1},{3,2},{4,3},{5,4},{6,5},{7,6},{9,8},{10,9},{11,10},{12... | collective-permute-start | bytes 12296 | tf_op jit(solution)/shard_map/ppermute | solution.py:24
  350.4 9.6 %collective-permute-start.17 = (f32[32,4,8,1]{3,0,2,1:T(8,128)S(1)}, f32[32,4,8,1]{3,0,2,1:T(8,128)S(1)}, u32[]{:S(2)}, u32[]{:S(2)}) collective-permute-start(f32[32,4,8,1]{3,0,2,1:T(8,128)S(1)} %get-tuple-element.231), channel_id=1, source_target_pairs={{0,1},{1,2},{2,3},{3,4},{4,5},{5,6},{6,7},{8,9},{9,10},{10,11},{11... | collective-permute-start | bytes 12296 | tf_op jit(solution)/shard_map/ppermute | solution.py:23
  354.8 6.7 collective-permute-start.15
  423.6 10.7 %collective-permute-start.20 = (f32[32,4,8,1]{3,0,2,1:T(8,128)S(1)}, f32[32,4,8,1]{3,0,2,1:T(8,128)S(1)}, u32[]{:S(2)}, u32[]{:S(2)}) collective-permute-start(f32[32,4,8,1]{3,0,2,1:T(8,128)S(1)} %get-tuple-element.224), channel_id=1, source_target_pairs={{1,0},{2,1},{3,2},{4,3},{5,4},{6,5},{7,6},{9,8},{10,9},{11,10},{12... | collective-permute-start | bytes 12296 | tf_op jit(solution)/shard_map/ppermute | solution.py:24
  424.9 9.4 %collective-permute-start.21 = (f32[32,4,8,1]{3,0,2,1:T(8,128)S(1)}, f32[32,4,8,1]{3,0,2,1:T(8,128)S(1)}, u32[]{:S(2)}, u32[]{:S(2)}) collective-permute-start(f32[32,4,8,1]{3,0,2,1:T(8,128)S(1)} %get-tuple-element.225), channel_id=1, source_target_pairs={{0,1},{1,2},{2,3},{3,4},{4,5},{5,6},{6,7},{8,9},{9,10},{10,11},{11... | collective-permute-start | bytes 12296 | tf_op jit(solution)/shard_map/ppermute | solution.py:23
  429.2 6.7 collective-permute-start.19
  436.9 11.3 %collective-permute-start.24 = (f32[32,4,8,1]{3,0,2,1:T(8,128)S(1)}, f32[32,4,8,1]{3,0,2,1:T(8,128)S(1)}, u32[]{:S(2)}, u32[]{:S(2)}) collective-permute-start(f32[32,4,8,1]{3,0,2,1:T(8,128)S(1)} %get-tuple-element.218), channel_id=1, source_target_pairs={{1,0},{2,1},{3,2},{4,3},{5,4},{6,5},{7,6},{9,8},{10,9},{11,10},{12... | collective-permute-start | bytes 12296 | tf_op jit(solution)/shard_map/ppermute | solution.py:24
  438.2 10.0 %collective-permute-start.25 = (f32[32,4,8,1]{3,0,2,1:T(8,128)S(1)}, f32[32,4,8,1]{3,0,2,1:T(8,128)S(1)}, u32[]{:S(2)}, u32[]{:S(2)}) collective-permute-start(f32[32,4,8,1]{3,0,2,1:T(8,128)S(1)} %get-tuple-element.219), channel_id=1, source_target_pairs={{0,1},{1,2},{2,3},{3,4},{4,5},{5,6},{6,7},{8,9},{9,10},{10,11},{11... | collective-permute-start | bytes 12296 | tf_op jit(solution)/shard_map/ppermute | solution.py:23
  441.3 6.9 %collective-permute-start.22 = (f32[32,4,1,128]{3,0,2,1:T(8,128)S(1)}, f32[32,4,1,128]{3,0,2,1:T(8,128)S(1)}, u32[]{:S(2)}, u32[]{:S(2)}) collective-permute-start(f32[32,4,1,128]{3,0,2,1:T(8,128)S(1)} %get-tuple-element.221), channel_id=1, source_target_pairs={{8,0},{16,8},{24,16},{32,24},{40,32},{48,40},{56,48},{64,56},{72,6... | collective-permute-start | bytes 196616 | tf_op jit(solution)/shard_map/ppermute | solution.py:24
  442.6 7.2 %collective-permute-start.23 = (f32[32,4,1,128]{3,0,2,1:T(8,128)S(1)}, f32[32,4,1,128]{3,0,2,1:T(8,128)S(1)}, u32[]{:S(2)}, u32[]{:S(2)}) collective-permute-start(f32[32,4,1,128]{3,0,2,1:T(8,128)S(1)} %get-tuple-element.220), channel_id=1, source_target_pairs={{0,8},{8,16},{16,24},{24,32},{32,40},{40,48},{48,56},{56,64},{64,7... | collective-permute-start | bytes 196616 | tf_op jit(solution)/shard_map/ppermute | solution.py:23
  532.2 14.7 %collective-permute-start.28 = (f32[32,4,8,1]{3,0,2,1:T(8,128)}, f32[32,4,8,1]{3,0,2,1:T(8,128)S(1)}, u32[]{:S(2)}, u32[]{:S(2)}) collective-permute-start(f32[32,4,8,1]{3,0,2,1:T(8,128)} %get-tuple-element.212), channel_id=1, source_target_pairs={{1,0},{2,1},{3,2},{4,3},{5,4},{6,5},{7,6},{9,8},{10,9},{11,10},{12... | collective-permute-start | bytes 12296 | tf_op jit(solution)/shard_map/ppermute | solution.py:24
  533.4 13.4 %collective-permute-start.29 = (f32[32,4,8,1]{3,0,2,1:T(8,128)}, f32[32,4,8,1]{3,0,2,1:T(8,128)}, u32[]{:S(2)}, u32[]{:S(2)}) collective-permute-start(f32[32,4,8,1]{3,0,2,1:T(8,128)} %get-tuple-element.213), channel_id=1, source_target_pairs={{0,1},{1,2},{2,3},{3,4},{4,5},{5,6},{6,7},{8,9},{9,10},{10,11},{11... | collective-permute-start | bytes 12296 | tf_op jit(solution)/shard_map/ppermute | solution.py:23
  537.3 9.6 %collective-permute-start.26 = (f32[32,4,1,128]{3,0,2,1:T(8,128)}, f32[32,4,1,128]{3,0,2,1:T(8,128)S(1)}, u32[]{:S(2)}, u32[]{:S(2)}) collective-permute-start(f32[32,4,1,128]{3,0,2,1:T(8,128)} %get-tuple-element.215), channel_id=1, source_target_pairs={{8,0},{16,8},{24,16},{32,24},{40,32},{48,40},{56,48},{64,56},{72,6... | collective-permute-start | bytes 196616 | tf_op jit(solution)/shard_map/ppermute | solution.py:24
  538.6 8.3 %collective-permute-start.27 = (f32[32,4,1,128]{3,0,2,1:T(8,128)}, f32[32,4,1,128]{3,0,2,1:T(8,128)S(1)}, u32[]{:S(2)}, u32[]{:S(2)}) collective-permute-start(f32[32,4,1,128]{3,0,2,1:T(8,128)} %get-tuple-element.214), channel_id=1, source_target_pairs={{0,8},{8,16},{16,24},{24,32},{32,40},{40,48},{48,56},{56,64},{64,7... | collective-permute-start | bytes 196616 | tf_op jit(solution)/shard_map/ppermute | solution.py:23
  613.4 10.9 %collective-permute-start.32 = (f32[32,4,8,1]{3,0,2,1:T(8,128)S(1)}, f32[32,4,8,1]{3,0,2,1:T(8,128)S(1)}, u32[]{:S(2)}, u32[]{:S(2)}) collective-permute-start(f32[32,4,8,1]{3,0,2,1:T(8,128)S(1)} %get-tuple-element.206), channel_id=1, source_target_pairs={{1,0},{2,1},{3,2},{4,3},{5,4},{6,5},{7,6},{9,8},{10,9},{11,10},{12... | collective-permute-start | bytes 12296 | tf_op jit(solution)/shard_map/ppermute | solution.py:24
  614.7 9.6 %collective-permute-start.33 = (f32[32,4,8,1]{3,0,2,1:T(8,128)S(1)}, f32[32,4,8,1]{3,0,2,1:T(8,128)S(1)}, u32[]{:S(2)}, u32[]{:S(2)}) collective-permute-start(f32[32,4,8,1]{3,0,2,1:T(8,128)S(1)} %get-tuple-element.207), channel_id=1, source_target_pairs={{0,1},{1,2},{2,3},{3,4},{4,5},{5,6},{6,7},{8,9},{9,10},{10,11},{11... | collective-permute-start | bytes 12296 | tf_op jit(solution)/shard_map/ppermute | solution.py:23
  619.1 6.7 collective-permute-start.31
  (33 other events, 880.5 us)
where the time goes:
time: 702 us; the launch traced here: 690 us
  blocking collectives  320 us (46%)
  starting transfers between devices  114 us (16%)
  other arithmetic  87.7 us (12%)
  local copies, waits for them, and re-layouts  82.2 us (12%)
  matrix products  69.4 us (10%)
  waiting for transfers between devices  14.9 us (2%)
    psum x24, blocking collectives, by_axis(): return functools.reduce(lax.psum, axes, x)  320 us
    ppermute x16, starting transfers between devices, with_halo(): lax.ppermute(last, axis, up)  63.4 us
    dot_general x16, matrix products, add_block(): jnp.dot(piece_values, one_hot, preferred_element_type=jnp.float32)  43 us
    unnamed x63, local copies, waits for them, and re-layouts  38.7 us
    another operation x30, other arithmetic, spd_solve(): factor = jnp.linalg.cholesky(matrix)  36 us
    another operation x20, other arithmetic, spd_solve(): return jax.scipy.linalg.cho_solve((factor, True), right)  31.4 us
    scatter x1, local copies, waits for them, and re-layouts, body(): jnp.zeros((currents.shape[0], slots_all), jnp.bfloat16).at[:, slot_index]  23.6 us
    ppermute x16, starting transfers between devices, with_halo(): lax.ppermute(initial, axis, [(b, a) for a, b in up])  20.6 us
  transfers between devices with their start and end apart: 36, of which 6 were waited for; matrix products, arithmetic and copies ran while one was open for 14% of the time, Pallas kernels for 0%

commit v1 on v0

v1 whole, which is shorter than its diff:
```python
import jax
import jax.numpy as jnp
from jax import lax
from jax.experimental import pallas as pl
from jax.experimental.pallas import tpu as pltpu
from jax.sharding import Mesh
from jax.sharding import PartitionSpec as P

GX = ("gx_0", "gx_1")
GY = ("gy_0", "gy_1")
GX_GY = GX + GY
F32 = jnp.float32
BF16 = jnp.bfloat16
HIGHEST = lax.Precision.HIGHEST
SHIFT = 7.0
SCALE = 7.0
XE = 22
YE = 144


def iota(shape, dim):
    return lax.broadcasted_iota(jnp.int32, shape, dim)


def dot(a, b, dims, precision=None):
    return lax.dot_general(
        a, b, (dims, ((), ())), precision=precision, preferred_element_type=F32
    )


def split3(x):
    hi = x.astype(BF16)
    rest = x - hi.astype(F32)
    mid = rest.astype(BF16)
    return hi, mid, (rest - mid.astype(F32)).astype(BF16)


def call(kernel, outs, args, scratch=(), limit=48):
    return pl.pallas_call(
        kernel,
        out_shape=tuple(jax.ShapeDtypeStruct(s, F32) for s in outs),
        scratch_shapes=list(scratch),
        compiler_params=pltpu.CompilerParams(vmem_limit_bytes=limit << 20),
        name=kernel.__name__,
    )(*args)


def to_lanes(volts, cap, cond_x, cond_y, via, v_out, c_out, low_out, high_out, stack):
    for c, ref in enumerate((cap, cond_x, cond_y, via)):
        stack[c * 32 : (c + 1) * 32, :] = ref[...]
    for x in range(8):
        rows = [volts[pl.ds(l * 8 + x, 32, stride=32), :] for l in range(4)]
        field = jnp.concatenate(rows, axis=0).T
        v_out[x] = field
        coef = stack[pl.ds(x, 16, stride=8), :]
        coef = jnp.concatenate([coef, jnp.zeros((112, 128), F32)], axis=0).T
        c_out[x] = coef
        low_out[x * 8 : x * 8 + 8, :] = field[:8]
        low_out[64 + x * 8 : 72 + x * 8, :] = coef[:8]
        high_out[x * 8 : x * 8 + 8, :] = field[120:]
        high_out[64 + x * 8 : 72 + x * 8, :] = coef[120:]


def widened(low, own, high, x, base=0):
    at = pl.ds(base + x * 8, 8)
    return jnp.concatenate([low[at, :], own[x], high[at, :]], axis=0)


def pack_rows(v, c, low, high, first_out, last_out):
    for x in range(8):
        field = widened(low, v, high, x)
        coef = widened(low, c, high, x, 64)
        packed = coef[:24]
        for g in range(1, 6):
            packed = packed + pltpu.roll(coef[g * 24 : (g + 1) * 24], 16 * g, 1)
        row = jnp.concatenate([field, packed], axis=0)
        if x < 7:
            first_out[x] = row
        if x > 0:
            last_out[x - 1] = row


def place_slots(tile, cell, wave, amp, out, acc):
    acc[...] = jnp.zeros_like(acc)
    lane = iota((128, 256), 1)
    before = ((iota((128, 256), 0) < lane) | (lane >= 128)).astype(F32).astype(BF16)
    tile_line = iota((128, 128), 0)

    def chunk(turn, seen):
        at = pl.ds(pl.multiple_of(turn * 8, 8), 8)
        tiles = tile[at, :]
        code = cell[at, :] * 64 + wave[at, :]
        parts = list(split3(amp[at, :]))
        parts.append((code >> 8).astype(F32).astype(BF16))
        parts.append((code & 255).astype(F32).astype(BF16))
        hits = [
            (tile_line == tiles[j : j + 1, :]).astype(F32) for j in range(8)
        ]
        hits_b = [h.astype(BF16) for h in hits]
        ranks = dot(jnp.concatenate(hits_b, axis=0), before, ((1,), (0,)))
        slots = []
        for j in range(8):
            rank = ranks[j * 128 : (j + 1) * 128]
            slot = jnp.sum(hits[j] * (rank[:, :128] + seen), axis=0, keepdims=True)
            slots.append((tile_line == slot.astype(jnp.int32)).astype(F32).astype(BF16))
            seen = seen + rank[:, 128:]
        hit = jnp.concatenate(hits_b, axis=1)
        slot = jnp.concatenate(slots, axis=1)
        left = []
        for part in parts:
            wide = part.astype(F32)
            wide = jnp.concatenate([wide[j : j + 1, :] for j in range(8)], axis=1)
            left.append(hit * wide.astype(BF16))
        acc[...] += dot(jnp.concatenate(left, axis=0), slot, ((1,), (1,)))
        return seen

    lax.fori_loop(0, 8, chunk, jnp.zeros((128, 128), F32))
    out[:, 0, :] = acc[0:128] + acc[128:256] + acc[256:384]
    out[:, 1, :] = acc[384:512] * 256.0 + acc[512:640]


def add_currents(slots, waves, out, low_out, high_out, acc):
    acc[...] = jnp.zeros_like(acc)
    table = jnp.concatenate([p.astype(F32) for p in split3(waves[...])], axis=0).astype(BF16)
    wave_line = iota((64, 512), 0)
    cell_line = iota((256, 512), 0)

    def chunk(turn, carry):
        rows = [slots[turn * 4 + j] for j in range(4)]
        amp = jnp.concatenate([r[0:1, :] for r in rows], axis=1)
        code = jnp.concatenate([r[1:2, :] for r in rows], axis=1).astype(jnp.int32)
        hit = (wave_line == (code & 63)).astype(F32).astype(BF16)
        picked = dot(table, hit, ((1,), (0,)))
        current = (picked[:64] + picked[64:128]) + picked[128:]
        current = (current * amp).astype(BF16).astype(F32)
        cell = code >> 6
        block = cell >> 8
        right = [jnp.where(block == r, current, 0.0).astype(BF16) for r in range(4)]
        left = (cell_line == (cell & 255)).astype(F32).astype(BF16)
        acc[...] += dot(left, jnp.concatenate(right, axis=0), ((1,), (1,)))
        return carry

    lax.fori_loop(0, 32, chunk, 0)
    low_lanes = iota((256, 128), 1) < 64
    for r in range(4):
        half = acc[:, (r // 2) * 128 : (r // 2 + 1) * 128]
        if r % 2:
            half = pltpu.roll(half, 64, 1)
        half = jnp.where(low_lanes, half, 0.0)
        for b in range(2):
            x = 2 * r + b
            rows = half[b * 128 : (b + 1) * 128]
            out[x] = rows
            low_out[x * 8 : x * 8 + 8, :] = rows[:8]
            high_out[x * 8 : x * 8 + 8, :] = rows[120:]


def pack_injected(own, low, high, first_out, last_out):
    rows = [widened(low, own, high, x) for x in range(8)]
    for j in range(3):
        first_out[j] = rows[j] + pltpu.roll(rows[j + 3], 64, 1)
        last_out[j] = rows[j + 2] + pltpu.roll(rows[j + 5], 64, 1)


def apply_row(src, i, diag, wx, wy, wv):
    v = src[i]
    wyi, wvi = wy[i], wv[i]
    out = diag[i] * v - wx[i] * src[i + 1] - wx[i - 1] * src[i - 1]
    out = out - wyi * pltpu.roll(v, YE - 1, 0) - pltpu.roll(wyi * v, 1, 0)
    return out - wvi * pltpu.roll(v, 96, 1) - pltpu.roll(wvi * v, 32, 1)


def power(src, dst, first, last, weights):
    def row(i, carry):
        dst[i] = apply_row(src, i, *weights)
        return carry

    lax.fori_loop(first, last + 1, row, 0)


def moments(fields, out, first):
    own = [f[first : first + 8, 8:136, :].reshape(1024, 128) for f in fields]
    lane = iota((32, 128), 1)
    blocks = [jnp.zeros((32, 128), F32), jnp.zeros((32, 128), F32)]
    for k in range(3):
        pair = jnp.concatenate([own[k], own[k + 1]], axis=1)
        product = dot(own[k], pair, ((0,), (0,)), HIGHEST)
        for b in range(2):
            n = 2 * k + b
            place = 32 * (n % 4)
            total = jnp.zeros((32, 128), F32)
            for l in range(4):
                piece = product[l * 32 : (l + 1) * 32, b * 128 : (b + 1) * 128]
                turn = (place - 32 * l) % 128
                total = total + (pltpu.roll(piece, turn, 1) if turn else piece)
            inside = (lane >= place) & (lane < place + 32)
            blocks[n // 4] = blocks[n // 4] + jnp.where(inside, total, 0.0)
    out[0:32, :] = blocks[0]
    out[32:64, :] = blocks[1]


def coefficients(gram):
    lane = iota((32, 128), 1)

    def moment(k, place):
        block = gram[(k // 4) * 32 : (k // 4) * 32 + 32, :]
        turn = (place - 32 * (k % 4)) % 128
        block = pltpu.roll(block, turn, 1) if turn else block
        return jnp.where((lane >= place) & (lane < place + 32), block, 0.0)

    tiles = []
    for i in range(3):
        block = moment(i, 96)
        for j in range(3):
            block = block + SCALE * moment(i + j + 1, 32 * j) + SHIFT * moment(i + j, 32 * j)
        tiles += [block[r * 8 : r * 8 + 8] for r in range(4)]
    sub = iota((8, 128), 0)
    for k in range(96):
        mine, at = tiles[k // 8], k % 8
        row = mine[at : at + 1, :]
        row = row * (1.0 / row[:, k : k + 1])
        new = []
        for t, block in enumerate(tiles):
            less = block - block[:, k : k + 1] * row
            new.append(jnp.where(sub == at, row, less) if t == k // 8 else less)
        tiles = new
    lane = iota((32, 128), 1)
    outs = []
    for i in range(3):
        y = jnp.concatenate(tiles[i * 4 : i * 4 + 4], axis=0)
        y = jnp.where(lane >= 96, y, 0.0)
        y = y + pltpu.roll(y, 32, 1) + pltpu.roll(y, 64, 1) + pltpu.roll(y, 96, 1)
        outs.append(
            jnp.concatenate([jnp.where(lane // 32 == l, y, 0.0) for l in range(4)], axis=0)
        )
    return outs


def combination(gram):
    y0, y1, y2 = coefficients(gram)
    step = jnp.concatenate([y0, y1, y2, jnp.zeros_like(y0)], axis=0)
    less = jnp.concatenate(
        [
            -SHIFT * y0,
            -SCALE * y0 - SHIFT * y1,
            -SCALE * y1 - SHIFT * y2,
            -SCALE * y2,
        ],
        axis=0,
    )
    return jnp.concatenate([step, less], axis=1)


def first_basis(
    v, c, low, high, x_low, x_high, inj, i_low, i_high, ix_low, ix_high,
    diag, wx, wy, wv, cap, change, v0, v1, v2, v3, gram, ext,
):
    lane = iota((YE, 128), 1)
    n = iota((128, 512), 1)
    q = iota((128, 512), 0)
    spread = ((q % 16 == (n // 128) * 4 + (n % 128) // 32) & (q < 48)).astype(F32).astype(BF16)

    def expand(i, coef):
        hi, mid, lo = [p.astype(F32) for p in split3(coef)]
        parts = hi + pltpu.roll(mid, 16, 1) + pltpu.roll(lo, 32, 1)
        wide = dot(parts.astype(BF16), spread, ((1,), (0,)))
        cap[i] = wide[:, :128]
        wx[i] = wide[:, 128:256]
        wy[i] = wide[:, 256:384]
        wv[i] = jnp.where(lane < 96, wide[:, 384:], 0.0)
        diag[i] = wide[:, :128] + wide[:, 384:]

    def halo_row(j, ref, base):
        ext[base + j] = ref[j, :YE, :]
        packed = ref[j, YE:, :]
        groups = [packed] + [pltpu.roll(packed, 128 - 16 * g, 1) for g in range(1, 6)]
        coef = jnp.concatenate(groups, axis=0)
        expand(base + j, jnp.where(lane < 16, coef, 0.0))

    def own_row(x, carry):
        at = pl.ds(pl.multiple_of(x * 8, 8), 8)
        at_c = pl.ds(pl.multiple_of(64 + x * 8, 8), 8)
        ext[7 + x] = jnp.concatenate([low[at, :], v[x], high[at, :]], axis=0)
        expand(7 + x, jnp.concatenate([low[at_c, :], c[x], high[at_c, :]], axis=0))
        return carry

    def halo_rows(j, carry):
        halo_row(j, x_low, 0)
        halo_row(j, x_high, 15)
        return carry

    lax.fori_loop(0, 8, own_row, 0)
    lax.fori_loop(0, 7, halo_rows, 0)

    def diagonal(i, carry):
        total = diag[i] + wx[i] + wx[i - 1] + wy[i] + pltpu.roll(wy[i], 1, 0)
        total = total + pltpu.roll(wv[i], 32, 1)
        diag[i] = (total - SHIFT) * (1.0 / SCALE)
        return carry

    lax.fori_loop(1, 21, diagonal, 0)

    def edges(i, carry):
        wx[i] = jnp.where(cap[i + 1] > 0, wx[i] * (1.0 / SCALE), 0.0)
        wy[i] = jnp.where(pltpu.roll(cap[i], YE - 1, 0) > 0, wy[i] * (1.0 / SCALE), 0.0)
        wv[i] = wv[i] * (1.0 / SCALE)
        return carry

    lax.fori_loop(0, 21, edges, 0)
    weights = (diag, wx, wy, wv)

    def start(i, both):
        now = jnp.where(lane < 32, both, 0.0)
        then = jnp.where(lane < 32, pltpu.roll(both, 96, 1), 0.0)
        change[i] = now - then
        e = ext[i]
        v0[i] = (cap[i] - SHIFT) * e - SCALE * apply_row(ext, i, *weights) - now

    def own_start(x, carry):
        at = pl.ds(pl.multiple_of(x * 8, 8), 8)
        start(7 + x, jnp.concatenate([i_low[at, :], inj[x], i_high[at, :]], axis=0))
        return carry

    def halo_start(j, carry):
        for ref, base in ((ix_low, 1), (ix_high, 15)):
            both = ref[j]
            start(base + j, both)
            start(base + 3 + j, pltpu.roll(both, 64, 1))
        return carry

    lax.fori_loop(0, 8, own_start, 0)
    lax.fori_loop(0, 3, halo_start, 0)
    power(v0, v1, 2, 19, weights)
    power(v1, v2, 3, 18, weights)
    power(v2, v3, 4, 17, weights)
    moments((v0, v1, v2, v3), gram, 7)


def second_basis(
    gram, diag, wx, wy, wv, cap, change, v0, v1, v2, v3, v,
    w0, w1, w2, w3, volts, gram_out, b0, b1, b2, b3, step,
):
    weights = (diag, wx, wy, wv)
    mix = combination(gram)

    def row(i, carry):
        fields = jnp.concatenate([v0[i], v1[i], v2[i], v3[i]], axis=1)
        both = dot(fields, mix, ((1,), (0,)), HIGHEST)
        moved = both[:, :128]
        step[i] = moved
        b0[i] = v0[i] + both[:, 128:] + cap[i] * moved + change[i]
        return carry

    lax.fori_loop(4, 18, row, 0)
    power(b0, b1, 5, 16, weights)
    power(b1, b2, 6, 15, weights)
    power(b2, b3, 7, 14, weights)
    moments((b0, b1, b2, b3), gram_out, 7)
    for x in range(8):
        volts[x] = v[x] + step[7 + x, 8:136, :]
        for src, dst in ((b0, w0), (b1, w1), (b2, w2), (b3, w3)):
            dst[x] = src[7 + x, 8:136, :]


def finish(gram, w0, w1, w2, w3, volts, volts_out, residual_out):
    mix = combination(gram)
    for x in range(8):
        fields = jnp.concatenate([w0[x], w1[x], w2[x], w3[x]], axis=1)
        both = dot(fields, mix, ((1,), (0,)), HIGHEST)
        for value, out in (
            (volts[x] + both[:, :128], volts_out),
            (w0[x] + both[:, 128:], residual_out),
        ):
            value = value.T
            for l in range(4):
                out[pl.ds(l * 8 + x, 32, stride=32), :] = value[l * 32 : (l + 1) * 32]


def neighbours(to_low, to_high, axis):
    size = lax.axis_size(axis)
    up = [(i, i + 1) for i in range(size - 1)]
    from_low = lax.ppermute(to_high, axis, up)
    return from_low, lax.ppermute(to_low, axis, [(b, a) for a, b in up])


def everywhere(x):
    x = x + lax.ppermute(x, "gy_1", [(0, 1), (1, 0)])
    for axis in ("gy_0", "gx_1", "gx_0"):
        x = x + lax.ppermute(x, axis, [(0, 1), (1, 0), (2, 3), (3, 2)])
        x = x + lax.ppermute(x, axis, [(0, 3), (3, 0), (1, 2), (2, 1)])
    return x


def body(volts, cap, cond_x, cond_y, via, waveforms, placement, cells, wave_ids, amps):
    vmem = pltpu.VMEM
    coefs = [a.reshape(32, 128) for a in (cap, cond_x, cond_y, via)]
    v, c, y_low, y_high = call(
        to_lanes,
        [(8, 128, 128), (8, 128, 128), (128, 128), (128, 128)],
        [volts.reshape(1024, 128)] + coefs,
        [vmem((128, 128), F32)],
    )
    y_low, y_high = neighbours(y_low, y_high, GY)
    lists = [a.reshape(64, 128) for a in (placement, cells, wave_ids, amps)]
    (slots,) = call(place_slots, [(128, 2, 128)], lists, [vmem((640, 128), F32)])
    x_low, x_high = call(pack_rows, [(7, 168, 128)] * 2, [v, c, y_low, y_high])
    x_low, x_high = neighbours(x_low, x_high, GX)
    slots = lax.all_to_all(slots, GX_GY, split_axis=0, concat_axis=0, tiled=True)
    inj, i_low, i_high = call(
        add_currents,
        [(8, 128, 128), (64, 128), (64, 128)],
        [slots, waveforms],
        [vmem((256, 256), F32)],
    )
    i_low, i_high = neighbours(i_low, i_high, GY)
    ix_low, ix_high = call(pack_injected, [(3, YE, 128)] * 2, [inj, i_low, i_high])
    ix_low, ix_high = neighbours(ix_low, ix_high, GX)
    wide = (XE, YE, 128)
    *kept, gram = call(
        first_basis,
        [wide] * 10 + [(64, 128)],
        [v, c, y_low, y_high, x_low, x_high, inj, i_low, i_high, ix_low, ix_high],
        [vmem(wide, F32)],
    )
    own = (8, 128, 128)
    *basis, gram = call(
        second_basis,
        [own] * 5 + [(64, 128)],
        [everywhere(gram)] + kept + [v],
        [vmem(wide, F32)] * 5,
    )
    outs = call(finish, [(1024, 128)] * 2, [everywhere(gram)] + basis)
    return tuple(o.reshape(volts.shape) for o in outs)


def solution(mesh):
    finer = Mesh(mesh.devices.reshape(4, 4, 4, 2), ("gx_0", "gx_1", "gy_0", "gy_1"))
    in_specs = (
        P(None, None, GX, GY),
        P(None, GX, GY),
        P(None, GX, GY),
        P(None, GX, GY),
        P(None, GX, GY),
        P(),
        P(GX_GY, None),
        P(GX_GY),
        P(GX_GY),
        P(GX_GY),
    )
    out_specs = (P(None, None, GX, GY), P(None, None, GX, GY))
    return jax.shard_map(body, mesh=finer, in_specs=in_specs, out_specs=out_specs, check_vma=False)
```

time: 702 us -> 197 us (0.28); the launches traced: 690 us -> 196 us
  blocking collectives: 320 us -> 23.3 us
  other arithmetic: 87.7 us -> 0.07 us
  starting transfers between devices: 114 us -> 33.1 us
  Pallas kernels: 0 us -> 80.5 us
  local copies, waits for them, and re-layouts: 82.2 us -> 3.92 us
  matrix products: 69.4 us -> 0 us
  waiting for transfers between devices: 14.9 us -> 54.1 us
    psum x24 -> x0, blocking collectives: 320 us -> none  [by_axis(): return functools.reduce(lax.psum, axes, x)]
    pallas_call x0 -> x8, Pallas kernels: none -> 80.5 us  [call(): pl.pallas_call(kernel, out_shape=tuple((jax.ShapeDtypeStruct(s, F32) for...]
    another operation x52 -> x0, other arithmetic: 68.6 us -> none  [the longest x30 36 us: spd_solve(): factor = jnp.linalg.cholesky(matrix)]
    dot_general x58 -> x0, matrix products: 65.3 us -> none  [the longest x16 43 us: add_block(): jnp.dot(piece_values, one_hot, preferred_element_type=jnp.float32)]
    ppermute x34 -> x22, starting transfers between devices: 90.7 us -> 33.1 us  [the longest x6 12.6 us: everywhere(): x = x + lax.ppermute(x, axis, [(0, 3), (3, 0), (1, 2), (2, 1)])]
    ppermute x34 -> x22, waiting for transfers between devices: 6.88 us -> 54.1 us  [the longest x6 19.6 us: everywhere(): x = x + lax.ppermute(x, axis, [(0, 3), (3, 0), (1, 2), (2, 1)])]
    unnamed x63 -> x20, local copies, waits for them, and re-layouts: 38.7 us -> 3.92 us
    scatter x1 -> x0, local copies, waits for them, and re-layouts: 23.6 us -> none  [body(): jnp.zeros((currents.shape[0], slots_all), jnp.bfloat16).at[:, slot_index]]
  transfers between devices with their start and end apart: 36 -> 22, of which waited for: 6 -> 18; matrix products, arithmetic and copies ran while one was open for 14% -> 0% of each run, Pallas kernels for 0% -> 11%
where the time goes in v1:
time: 197 us; the launch traced here: 196 us
  Pallas kernels  80.5 us (41%)
  waiting for transfers between devices  54.1 us (27%)
  starting transfers between devices  33.1 us (17%)
  blocking collectives  23.3 us (12%)
  local copies, waits for them, and re-layouts  3.92 us (2%)
    pallas_call x8, Pallas kernels, call(): pl.pallas_call(kernel, out_shape=tuple((jax.ShapeDtypeStruct(s, F32) for...  80.5 us
    all_to_all x1, blocking collectives, body(): lax.all_to_all(slots, GX_GY, split_axis=0, concat_axis=0, tiled=True)  23.3 us
    ppermute x6, waiting for transfers between devices, everywhere(): x = x + lax.ppermute(x, axis, [(0, 3), (3, 0), (1, 2), (2, 1)])  19.6 us
    ppermute x6, waiting for transfers between devices, everywhere(): x = x + lax.ppermute(x, axis, [(0, 1), (1, 0), (2, 3), (3, 2)])  18.7 us
    ppermute x6, starting transfers between devices, everywhere(): x = x + lax.ppermute(x, axis, [(0, 3), (3, 0), (1, 2), (2, 1)])  12.6 us
    ppermute x4, waiting for transfers between devices, neighbours(): return (from_low, lax.ppermute(to_low, axis, [(b, a) for a, b in up]))  11.1 us
    ppermute x4, starting transfers between devices, neighbours(): from_low = lax.ppermute(to_high, axis, up)  8.46 us
    ppermute x6, starting transfers between devices, everywhere(): x = x + lax.ppermute(x, axis, [(0, 1), (1, 0), (2, 3), (3, 2)])  5.48 us
  transfers between devices with their start and end apart: 22, of which 18 were waited for; matrix products, arithmetic and copies ran while one was open for 0% of the time, Pallas kernels for 11%

profile of v1, /device:TPU:0, one launch (start us, length us, event | category | flops | bytes accessed | tf_op | source)
XLA Modules:
  0.0 195.9 jit_solution(3169589948337526186)
XLA Ops:
  5.0 1.3 collective-permute-start
  7.6 4.1 %collective-permute-done.1.high = f32[128,128]{1,0:T(8,128)S(1)} collective-permute-done((f32[128,128]{1,0:T(8,128)S(1)}, f32[128,128]{1,0:T(8,128)S(1)}, u32[]{:S(2)}, u32[]{:S(2)}) %collective-permute-start.1) | collective-permute-done | bytes 65568 | tf_op jit(solution)/shard_map/ppermute | solution.py:383
  11.9 3.5 %collective-permute-start.2 = (f32[7,168,128]{2,1,0:T(8,128)S(1)}, f32[7,168,128]{2,1,0:T(8,128)S(1)}, u32[]{:S(2)}, u32[]{:S(2)}) collective-permute-start(f32[7,168,128]{2,1,0:T(8,128)S(1)} %get-tuple-element.36), channel_id=1, source_target_pairs={{0,8},{8,16},{16,24},{24,32},{32,40},{40,48},{48,56},{56,64},{64,7... | collective-permute-start | bytes 1806344 | tf_op jit(solution)/shard_map/ppermute | solution.py:382
  16.7 6.8 %place_slots.1 = f32[128,2,128]{2,1,0:T(2,128)S(1)} custom-call(s32[64,128]{1,0:T(8,128)S(1)} %bitcast.12, s32[64,128]{1,0:T(8,128)S(1)} %bitcast.13, s32[64,128]{1,0:T(8,128)S(1)} %bitcast.14, f32[64,128]{1,0:T(8,128)S(1)} %bitcast.15), custom_call_target="tpu_custom_call" | custom-call | tf_op jit(solution)/shard_map/place_slots/pallas_call | solution.py:39
  23.5 23.3 %all_to_all.5.slots = f32[128,2,128]{2,1,0:T(2,128)S(1)} all-to-all(f32[128,2,128]{2,1,0:T(2,128)S(1)} %place_slots.1), channel_id=1, replica_groups=mesh['gx_0'=4,'gx_1'=4,'gy_0'=4,'gy_1'=2] {'gx_0','gx_1','gy_0','gy_1'}, dimensions={0} | all-to-all | bytes 262144 | tf_op jit(solution)/shard_map/all_to_all | solution.py:408
  46.8 14.6 %add_currents.1 = (f32[8,128,128]{2,1,0:T(8,128)S(1)}, f32[64,128]{1,0:T(8,128)S(1)}, f32[64,128]{1,0:T(8,128)S(1)}) custom-call(f32[128,2,128]{2,1,0:T(2,128)S(1)} %all_to_all.5.slots, f32[64,64]{1,0:T(8,128)S(1)} %copy-done.1), custom_call_target="tpu_custom_call" | custom-call | tf_op jit(solution)/shard_map/add_currents/pallas_call | solution.py:39
  61.4 1.4 collective-permute-start.4
  62.8 1.3 collective-permute-start.5
  64.1 2.3 %collective-permute-done.5.high.i_high = f32[64,128]{1,0:T(8,128)S(1)} collective-permute-done((f32[64,128]{1,0:T(8,128)S(1)}, f32[64,128]{1,0:T(8,128)S(1)}, u32[]{:S(2)}, u32[]{:S(2)}) %collective-permute-start.5) | collective-permute-done | bytes 32800 | tf_op jit(solution)/shard_map/ppermute | solution.py:383
  66.6 2.2 %collective-permute-start.6 = (f32[3,144,128]{2,1,0:T(8,128)S(1)}, f32[3,144,128]{2,1,0:T(8,128)S(1)}, u32[]{:S(2)}, u32[]{:S(2)}) collective-permute-start(f32[3,144,128]{2,1,0:T(8,128)S(1)} %get-tuple-element.41), channel_id=1, source_target_pairs={{0,8},{8,16},{16,24},{24,32},{32,40},{40,48},{48,56},{56,64},{64,7... | collective-permute-start | bytes 663560 | tf_op jit(solution)/shard_map/ppermute | solution.py:382
  70.1 2.8 %collective-permute-done.6.ix_low = f32[3,144,128]{2,1,0:T(8,128)S(1)} collective-permute-done((f32[3,144,128]{2,1,0:T(8,128)S(1)}, f32[3,144,128]{2,1,0:T(8,128)S(1)}, u32[]{:S(2)}, u32[]{:S(2)}) %collective-permute-start.6) | collective-permute-done | bytes 221216 | tf_op jit(solution)/shard_map/ppermute | solution.py:382
  72.9 4.7 %collective-permute-done.7.ix_high = f32[3,144,128]{2,1,0:T(8,128)S(1)} collective-permute-done((f32[3,144,128]{2,1,0:T(8,128)S(1)}, f32[3,144,128]{2,1,0:T(8,128)S(1)}, u32[]{:S(2)}, u32[]{:S(2)}) %collective-permute-start.7) | collective-permute-done | bytes 221216 | tf_op jit(solution)/shard_map/ppermute | solution.py:383
  77.6 20.6 %first_basis.1 = (f32[22,144,128]{2,1,0:T(8,128)S(1)}, f32[22,144,128]{2,1,0:T(8,128)}, f32[22,144,128]{2,1,0:T(8,128)}, f32[22,144,128]{2,1,0:T(8,128)}, f32[22...) custom-call(f32[8,128,128]{2,1,0:T(8,128)S(1)} %get-tuple-element.32, ...), custom_call_target="tpu_custom_call" | custom-call | tf_op jit(solution)/shard_map/first_basis/pallas_call | solution.py:39
  100.3 2.7 %collective-permute-start.9 = (f32[64,128]{1,0:T(8,128)S(1)}, f32[64,128]{1,0:T(8,128)S(1)}, u32[]{:S(2)}, u32[]{:S(2)}) collective-permute-start(f32[64,128]{1,0:T(8,128)S(1)} %add.42), channel_id=1, source_target_pairs={{0,2},{2,0},{4,6},{6,4},{1,3},{3,1},{5,7},{7,5},{8,10},{10,8},{12,... | collective-permute-start | bytes 98312 | tf_op jit(solution)/shard_map/ppermute | solution.py:389
  103.0 1.9 collective-permute-done.9
  104.9 1.7 collective-permute-start.10
  106.6 3.4 %collective-permute-done.10 = f32[64,128]{1,0:T(8,128)S(1)} collective-permute-done((f32[64,128]{1,0:T(8,128)S(1)}, f32[64,128]{1,0:T(8,128)S(1)}, u32[]{:S(2)}, u32[]{:S(2)}) %collective-permute-start.10) | collective-permute-done | bytes 32800 | tf_op jit(solution)/shard_map/ppermute | solution.py:390
  111.1 2.9 %collective-permute-done.11 = f32[64,128]{1,0:T(8,128)S(1)} collective-permute-done((f32[64,128]{1,0:T(8,128)S(1)}, f32[64,128]{1,0:T(8,128)S(1)}, u32[]{:S(2)}, u32[]{:S(2)}) %collective-permute-start.11) | collective-permute-done | bytes 32800 | tf_op jit(solution)/shard_map/ppermute | solution.py:389
  113.9 4.7 %collective-permute-start.12 = (f32[64,128]{1,0:T(8,128)S(1)}, f32[64,128]{1,0:T(8,128)S(1)}, u32[]{:S(2)}, u32[]{:S(2)}) collective-permute-start(f32[64,128]{1,0:T(8,128)S(1)} %add.45), channel_id=1, source_target_pairs={{0,24},{24,0},{8,16},{16,8},{1,25},{25,1},{9,17},{17,9},{2,26},{26... | collective-permute-start | bytes 98312 | tf_op jit(solution)/shard_map/ppermute | solution.py:390
  118.6 1.9 collective-permute-done.12
  121.5 3.0 %collective-permute-done.13 = f32[64,128]{1,0:T(8,128)S(1)} collective-permute-done((f32[64,128]{1,0:T(8,128)S(1)}, f32[64,128]{1,0:T(8,128)S(1)}, u32[]{:S(2)}, u32[]{:S(2)}) %collective-permute-start.13) | collective-permute-done | bytes 32800 | tf_op jit(solution)/shard_map/ppermute | solution.py:389
  125.1 4.4 %collective-permute-done.14 = f32[64,128]{1,0:T(8,128)S(1)} collective-permute-done((f32[64,128]{1,0:T(8,128)S(1)}, f32[64,128]{1,0:T(8,128)S(1)}, u32[]{:S(2)}, u32[]{:S(2)}) %collective-permute-start.14) | collective-permute-done | bytes 32800 | tf_op jit(solution)/shard_map/ppermute | solution.py:390
  129.6 25.6 %second_basis.1 = (f32[8,128,128]{2,1,0:T(8,128)S(1)}, f32[8,128,128]{2,1,0:T(8,128)S(1)}, f32[8,128,128]{2,1,0:T(8,128)S(1)}, f32[8,128,128]{2,1,0:T(8,128)S(1)...) custom-call(f32[64,128]{1,0:T(8,128)S(1)} %add.48.gram, f32[22,144,128]{2,1,0:T(8,128)S(1)} %get-tuple-element.44.diag, ...), custom_call_target="tpu_custom_call" | custom-call | tf_op jit(solution)/shard_map/second_basis/pallas_call | solution.py:39
  157.2 3.1 %collective-permute-done.16 = f32[64,128]{1,0:T(8,128)S(1)} collective-permute-done((f32[64,128]{1,0:T(8,128)S(1)}, f32[64,128]{1,0:T(8,128)S(1)}, u32[]{:S(2)}, u32[]{:S(2)}) %collective-permute-start.16) | collective-permute-done | bytes 32800 | tf_op jit(solution)/shard_map/ppermute | solution.py:389
  160.4 1.7 collective-permute-start.17
  162.0 3.5 %collective-permute-done.17 = f32[64,128]{1,0:T(8,128)S(1)} collective-permute-done((f32[64,128]{1,0:T(8,128)S(1)}, f32[64,128]{1,0:T(8,128)S(1)}, u32[]{:S(2)}, u32[]{:S(2)}) %collective-permute-start.17) | collective-permute-done | bytes 32800 | tf_op jit(solution)/shard_map/ppermute | solution.py:390
  165.5 3.9 %collective-permute-done.18 = f32[64,128]{1,0:T(8,128)S(1)} collective-permute-done((f32[64,128]{1,0:T(8,128)S(1)}, f32[64,128]{1,0:T(8,128)S(1)}, u32[]{:S(2)}, u32[]{:S(2)}) %collective-permute-start.18) | collective-permute-done | bytes 32800 | tf_op jit(solution)/shard_map/ppermute | solution.py:389
  169.4 3.2 %collective-permute-start.19 = (f32[64,128]{1,0:T(8,128)S(1)}, f32[64,128]{1,0:T(8,128)S(1)}, u32[]{:S(2)}, u32[]{:S(2)}) collective-permute-start(f32[64,128]{1,0:T(8,128)S(1)} %add.52), channel_id=1, source_target_pairs={{0,24},{24,0},{8,16},{16,8},{1,25},{25,1},{9,17},{17,9},{2,26},{26... | collective-permute-start | bytes 98312 | tf_op jit(solution)/shard_map/ppermute | solution.py:390
  172.6 1.9 collective-permute-done.19
  174.6 3.9 %collective-permute-done.20 = f32[64,128]{1,0:T(8,128)S(1)} collective-permute-done((f32[64,128]{1,0:T(8,128)S(1)}, f32[64,128]{1,0:T(8,128)S(1)}, u32[]{:S(2)}, u32[]{:S(2)}) %collective-permute-start.20) | collective-permute-done | bytes 32800 | tf_op jit(solution)/shard_map/ppermute | solution.py:389
  179.1 4.4 %collective-permute-done.21 = f32[64,128]{1,0:T(8,128)S(1)} collective-permute-done((f32[64,128]{1,0:T(8,128)S(1)}, f32[64,128]{1,0:T(8,128)S(1)}, u32[]{:S(2)}, u32[]{:S(2)}) %collective-permute-start.21) | collective-permute-done | bytes 32800 | tf_op jit(solution)/shard_map/ppermute | solution.py:390
  183.6 12.3 %finish.1 = (f32[1024,128]{1,0:T(8,128)}, f32[1024,128]{1,0:T(8,128)}) custom-call(f32[64,128]{1,0:T(8,128)S(1)} %add.55.gram, f32[8,128,128]{2,1,0:T(8,128)S(1)} %get-tuple-element.55.w0, f32[8,128,128]{2,1,0:T(8,128)S(1)} %get-tuple-element.56.w1, f32[8,128,128]{2,1,0:T(8,128)S(1)} %get-tuple-element.57.w2, f32[8,128,128]{2,1,0:T(8,128)S(1)} %get-tuple-element.58.w3, ...), custom_call_target="tpu_custom_call" | custom-call | tf_op jit(solution)/shard_map/finish/pallas_call | solution.py:39
  (55 shorter events, 16.2 us)
Async XLA Ops:
  0.6 1.0 copy-start
  1.7 0.7 copy-start.6
  2.4 0.7 copy-start.7
  3.1 0.7 copy-start.8
  3.8 0.7 copy-start.9
  4.5 12.2 %copy-start.2 = (s32[8192,1]{0,1:T(1,128)S(1)}, s32[8192,1]{0,1:T(1,128)}, u32[]{:S(2)}) copy-start(s32[8192,1]{0,1:T(1,128)} %param.16) | copy-start | bytes 98308
  4.5 12.2 %copy-start.3 = (s32[8192]{0:T(1024)S(1)}, s32[8192]{0:T(1024)}, u32[]{:S(2)}) copy-start(s32[8192]{0:T(1024)} %param.17) | copy-start | bytes 98308
  4.6 12.2 %copy-start.4 = (s32[8192]{0:T(1024)S(1)}, s32[8192]{0:T(1024)}, u32[]{:S(2)}) copy-start(s32[8192]{0:T(1024)} %param.18) | copy-start | bytes 98308
  4.6 12.2 %copy-start.5 = (f32[8192]{0:T(1024)S(1)}, f32[8192]{0:T(1024)}, u32[]{:S(2)}) copy-start(f32[8192]{0:T(1024)} %param.19) | copy-start | bytes 98308
  4.6 42.3 %copy-start.1 = (f32[64,64]{1,0:T(8,128)S(1)}, f32[64,64]{1,0:T(8,128)}, u32[]{:S(2)}) copy-start(f32[64,64]{1,0:T(8,128)} %waves.1) | copy-start | bytes 49156
  5.0 2.6 %collective-permute-start = (f32[128,128]{1,0:T(8,128)S(1)}, f32[128,128]{1,0:T(8,128)S(1)}, u32[]{:S(2)}, u32[]{:S(2)}) collective-permute-start(f32[128,128]{1,0:T(8,128)S(1)} %get-tuple-element.34), channel_id=1, source_target_pairs={{0,1},{1,2},{2,3},{3,4},{4,5},{5,6},{6,7},{8,9},{9,10},{10,11},{11... | collective-permute-start | bytes 196616 | tf_op jit(solution)/shard_map/ppermute | solution.py:382
  6.3 5.4 %collective-permute-start.1 = (f32[128,128]{1,0:T(8,128)S(1)}, f32[128,128]{1,0:T(8,128)S(1)}, u32[]{:S(2)}, u32[]{:S(2)}) collective-permute-start(f32[128,128]{1,0:T(8,128)S(1)} %get-tuple-element.35), channel_id=1, source_target_pairs={{1,0},{2,1},{3,2},{4,3},{5,4},{6,5},{7,6},{9,8},{10,9},{11,10},{12... | collective-permute-start | bytes 196616 | tf_op jit(solution)/shard_map/ppermute | solution.py:383
  11.9 65.7 %collective-permute-start.2 = (f32[7,168,128]{2,1,0:T(8,128)S(1)}, f32[7,168,128]{2,1,0:T(8,128)S(1)}, u32[]{:S(2)}, u32[]{:S(2)}) collective-permute-start(f32[7,168,128]{2,1,0:T(8,128)S(1)} %get-tuple-element.36), channel_id=1, source_target_pairs={{0,8},{8,16},{16,24},{24,32},{32,40},{40,48},{48,56},{56,64},{64,7... | collective-permute-start | bytes 1806344 | tf_op jit(solution)/shard_map/ppermute | solution.py:382
  15.4 62.2 %collective-permute-start.3 = (f32[7,168,128]{2,1,0:T(8,128)S(1)}, f32[7,168,128]{2,1,0:T(8,128)S(1)}, u32[]{:S(2)}, u32[]{:S(2)}) collective-permute-start(f32[7,168,128]{2,1,0:T(8,128)S(1)} %get-tuple-element.37), channel_id=1, source_target_pairs={{8,0},{16,8},{24,16},{32,24},{40,32},{48,40},{56,48},{64,56},{72,6... | collective-permute-start | bytes 1806344 | tf_op jit(solution)/shard_map/ppermute | solution.py:383
  61.4 2.7 %collective-permute-start.4 = (f32[64,128]{1,0:T(8,128)S(1)}, f32[64,128]{1,0:T(8,128)S(1)}, u32[]{:S(2)}, u32[]{:S(2)}) collective-permute-start(f32[64,128]{1,0:T(8,128)S(1)} %get-tuple-element.39), channel_id=1, source_target_pairs={{0,1},{1,2},{2,3},{3,4},{4,5},{5,6},{6,7},{8,9},{9,10},{10,11},{11... | collective-permute-start | bytes 98312 | tf_op jit(solution)/shard_map/ppermute | solution.py:382
  62.8 3.6 %collective-permute-start.5 = (f32[64,128]{1,0:T(8,128)S(1)}, f32[64,128]{1,0:T(8,128)S(1)}, u32[]{:S(2)}, u32[]{:S(2)}) collective-permute-start(f32[64,128]{1,0:T(8,128)S(1)} %get-tuple-element.40), channel_id=1, source_target_pairs={{1,0},{2,1},{3,2},{4,3},{5,4},{6,5},{7,6},{9,8},{10,9},{11,10},{12... | collective-permute-start | bytes 98312 | tf_op jit(solution)/shard_map/ppermute | solution.py:383
  66.6 6.3 %collective-permute-start.6 = (f32[3,144,128]{2,1,0:T(8,128)S(1)}, f32[3,144,128]{2,1,0:T(8,128)S(1)}, u32[]{:S(2)}, u32[]{:S(2)}) collective-permute-start(f32[3,144,128]{2,1,0:T(8,128)S(1)} %get-tuple-element.41), channel_id=1, source_target_pairs={{0,8},{8,16},{16,24},{24,32},{32,40},{40,48},{48,56},{56,64},{64,7... | collective-permute-start | bytes 663560 | tf_op jit(solution)/shard_map/ppermute | solution.py:382
  68.8 8.8 %collective-permute-start.7 = (f32[3,144,128]{2,1,0:T(8,128)S(1)}, f32[3,144,128]{2,1,0:T(8,128)S(1)}, u32[]{:S(2)}, u32[]{:S(2)}) collective-permute-start(f32[3,144,128]{2,1,0:T(8,128)S(1)} %get-tuple-element.42), channel_id=1, source_target_pairs={{8,0},{16,8},{24,16},{32,24},{40,32},{48,40},{56,48},{64,56},{72,6... | collective-permute-start | bytes 663560 | tf_op jit(solution)/shard_map/ppermute | solution.py:383
  98.2 2.1 %collective-permute-start.8 = (f32[64,128]{1,0:T(8,128)S(1)}, f32[64,128]{1,0:T(8,128)S(1)}, u32[]{:S(2)}, u32[]{:S(2)}) collective-permute-start(f32[64,128]{1,0:T(8,128)S(1)} %get-tuple-element.43), channel_id=1, source_target_pairs={{0,1},{1,0},{2,3},{3,2},{4,5},{5,4},{6,7},{7,6},{8,9},{9,8},{10,11... | collective-permute-start | bytes 98312 | tf_op jit(solution)/shard_map/ppermute | solution.py:387
  100.3 4.6 %collective-permute-start.9 = (f32[64,128]{1,0:T(8,128)S(1)}, f32[64,128]{1,0:T(8,128)S(1)}, u32[]{:S(2)}, u32[]{:S(2)}) collective-permute-start(f32[64,128]{1,0:T(8,128)S(1)} %add.42), channel_id=1, source_target_pairs={{0,2},{2,0},{4,6},{6,4},{1,3},{3,1},{5,7},{7,5},{8,10},{10,8},{12,... | collective-permute-start | bytes 98312 | tf_op jit(solution)/shard_map/ppermute | solution.py:389
  104.9 5.1 %collective-permute-start.10 = (f32[64,128]{1,0:T(8,128)S(1)}, f32[64,128]{1,0:T(8,128)S(1)}, u32[]{:S(2)}, u32[]{:S(2)}) collective-permute-start(f32[64,128]{1,0:T(8,128)S(1)} %add.43), channel_id=1, source_target_pairs={{0,6},{6,0},{2,4},{4,2},{1,7},{7,1},{3,5},{5,3},{8,14},{14,8},{10,... | collective-permute-start | bytes 98312 | tf_op jit(solution)/shard_map/ppermute | solution.py:390
  110.0 3.9 %collective-permute-start.11 = (f32[64,128]{1,0:T(8,128)S(1)}, f32[64,128]{1,0:T(8,128)S(1)}, u32[]{:S(2)}, u32[]{:S(2)}) collective-permute-start(f32[64,128]{1,0:T(8,128)S(1)} %add.44), channel_id=1, source_target_pairs={{0,8},{8,0},{16,24},{24,16},{1,9},{9,1},{17,25},{25,17},{2,10},{10... | collective-permute-start | bytes 98312 | tf_op jit(solution)/shard_map/ppermute | solution.py:389
  113.9 6.6 %collective-permute-start.12 = (f32[64,128]{1,0:T(8,128)S(1)}, f32[64,128]{1,0:T(8,128)S(1)}, u32[]{:S(2)}, u32[]{:S(2)}) collective-permute-start(f32[64,128]{1,0:T(8,128)S(1)} %add.45), channel_id=1, source_target_pairs={{0,24},{24,0},{8,16},{16,8},{1,25},{25,1},{9,17},{17,9},{2,26},{26... | collective-permute-start | bytes 98312 | tf_op jit(solution)/shard_map/ppermute | solution.py:390
  120.5 3.9 %collective-permute-start.13 = (f32[64,128]{1,0:T(8,128)S(1)}, f32[64,128]{1,0:T(8,128)S(1)}, u32[]{:S(2)}, u32[]{:S(2)}) collective-permute-start(f32[64,128]{1,0:T(8,128)S(1)} %add.46), channel_id=1, source_target_pairs={{0,32},{32,0},{64,96},{96,64},{1,33},{33,1},{65,97},{97,65},{2,34}... | collective-permute-start | bytes 98312 | tf_op jit(solution)/shard_map/ppermute | solution.py:389
  124.4 5.1 %collective-permute-start.14 = (f32[64,128]{1,0:T(8,128)S(1)}, f32[64,128]{1,0:T(8,128)S(1)}, u32[]{:S(2)}, u32[]{:S(2)}) collective-permute-start(f32[64,128]{1,0:T(8,128)S(1)} %add.47), channel_id=1, source_target_pairs={{0,96},{96,0},{32,64},{64,32},{1,97},{97,1},{33,65},{65,33},{2,98}... | collective-permute-start | bytes 98312 | tf_op jit(solution)/shard_map/ppermute | solution.py:390
  155.1 1.3 collective-permute-start.15
  156.4 3.9 %collective-permute-start.16 = (f32[64,128]{1,0:T(8,128)S(1)}, f32[64,128]{1,0:T(8,128)S(1)}, u32[]{:S(2)}, u32[]{:S(2)}) collective-permute-start(f32[64,128]{1,0:T(8,128)S(1)} %add.49), channel_id=1, source_target_pairs={{0,2},{2,0},{4,6},{6,4},{1,3},{3,1},{5,7},{7,5},{8,10},{10,8},{12,... | collective-permute-start | bytes 98312 | tf_op jit(solution)/shard_map/ppermute | solution.py:389
  160.4 5.1 %collective-permute-start.17 = (f32[64,128]{1,0:T(8,128)S(1)}, f32[64,128]{1,0:T(8,128)S(1)}, u32[]{:S(2)}, u32[]{:S(2)}) collective-permute-start(f32[64,128]{1,0:T(8,128)S(1)} %add.50), channel_id=1, source_target_pairs={{0,6},{6,0},{2,4},{4,2},{1,7},{7,1},{3,5},{5,3},{8,14},{14,8},{10,... | collective-permute-start | bytes 98312 | tf_op jit(solution)/shard_map/ppermute | solution.py:390
  165.5 3.9 %collective-permute-start.18 = (f32[64,128]{1,0:T(8,128)S(1)}, f32[64,128]{1,0:T(8,128)S(1)}, u32[]{:S(2)}, u32[]{:S(2)}) collective-permute-start(f32[64,128]{1,0:T(8,128)S(1)} %add.51), channel_id=1, source_target_pairs={{0,8},{8,0},{16,24},{24,16},{1,9},{9,1},{17,25},{25,17},{2,10},{10... | collective-permute-start | bytes 98312 | tf_op jit(solution)/shard_map/ppermute | solution.py:389
  169.4 5.1 %collective-permute-start.19 = (f32[64,128]{1,0:T(8,128)S(1)}, f32[64,128]{1,0:T(8,128)S(1)}, u32[]{:S(2)}, u32[]{:S(2)}) collective-permute-start(f32[64,128]{1,0:T(8,128)S(1)} %add.52), channel_id=1, source_target_pairs={{0,24},{24,0},{8,16},{16,8},{1,25},{25,1},{9,17},{17,9},{2,26},{26... | collective-permute-start | bytes 98312 | tf_op jit(solution)/shard_map/ppermute | solution.py:390
  174.5 3.9 %collective-permute-start.20 = (f32[64,128]{1,0:T(8,128)S(1)}, f32[64,128]{1,0:T(8,128)S(1)}, u32[]{:S(2)}, u32[]{:S(2)}) collective-permute-start(f32[64,128]{1,0:T(8,128)S(1)} %add.53), channel_id=1, source_target_pairs={{0,32},{32,0},{64,96},{96,64},{1,33},{33,1},{65,97},{97,65},{2,34}... | collective-permute-start | bytes 98312 | tf_op jit(solution)/shard_map/ppermute | solution.py:389
  178.5 5.1 %collective-permute-start.21 = (f32[64,128]{1,0:T(8,128)S(1)}, f32[64,128]{1,0:T(8,128)S(1)}, u32[]{:S(2)}, u32[]{:S(2)}) collective-permute-start(f32[64,128]{1,0:T(8,128)S(1)} %add.54), channel_id=1, source_target_pairs={{0,96},{96,0},{32,64},{64,32},{1,97},{97,1},{33,65},{65,33},{2,98}... | collective-permute-start | bytes 98312 | tf_op jit(solution)/shard_map/ppermute | solution.py:390

commit v2 on v1

--- a/solution.py
+++ b/solution.py
@@ -28,6 +28,17 @@
     )
 
 
+def split2(x):
+    hi = x.astype(BF16)
+    return hi, (x - hi.astype(F32)).astype(BF16)
+
+
+def dot_split(a, b, dims):
+    a_hi, a_lo = split2(a)
+    b_hi, b_lo = split2(b)
+    return dot(a_hi, b_hi, dims) + dot(a_hi, b_lo, dims) + dot(a_lo, b_hi, dims)
+
+
 def split3(x):
     hi = x.astype(BF16)
     rest = x - hi.astype(F32)
@@ -35,7 +46,7 @@
     return hi, mid, (rest - mid.astype(F32)).astype(BF16)
 
 
-def call(kernel, outs, args, scratch=(), limit=48):
+def call(kernel, outs, args, scratch=(), limit=14):
     return pl.pallas_call(
         kernel,
         out_shape=tuple(jax.ShapeDtypeStruct(s, F32) for s in outs),
@@ -184,7 +195,7 @@
     blocks = [jnp.zeros((32, 128), F32), jnp.zeros((32, 128), F32)]
     for k in range(3):
         pair = jnp.concatenate([own[k], own[k + 1]], axis=1)
-        product = dot(own[k], pair, ((0,), (0,)), HIGHEST)
+        product = dot_split(own[k], pair, ((0,), (0,)))
         for b in range(2):
             n = 2 * k + b
             place = 32 * (n % 4)
@@ -215,15 +226,23 @@
             block = block + SCALE * moment(i + j + 1, 32 * j) + SHIFT * moment(i + j, 32 * j)
         tiles += [block[r * 8 : r * 8 + 8] for r in range(4)]
     sub = iota((8, 128), 0)
-    for k in range(96):
-        mine, at = tiles[k // 8], k % 8
-        row = mine[at : at + 1, :]
-        row = row * (1.0 / row[:, k : k + 1])
-        new = []
-        for t, block in enumerate(tiles):
-            less = block - block[:, k : k + 1] * row
-            new.append(jnp.where(sub == at, row, less) if t == k // 8 else less)
-        tiles = new
+    for t in range(12):
+        rows = tiles[t]
+        cols = [jnp.broadcast_to(rows[:, t * 8 + j : t * 8 + j + 1], (8, 128)) for j in range(8)]
+        for j in range(8):
+            inverse = 1.0 / cols[j][j : j + 1, :]
+            pivot = rows[j : j + 1, :] * inverse
+            rows = jnp.where(sub == j, pivot, rows - cols[j] * pivot)
+            for n in range(j + 1, 8):
+                top = cols[n][j : j + 1, :] * inverse
+                cols[n] = jnp.where(sub == j, top, cols[n] - cols[j] * top)
+        for i in range(12):
+            block = tiles[i]
+            for j in range(8):
+                if i != t:
+                    block = block - tiles[i][:, t * 8 + j : t * 8 + j + 1] * rows[j : j + 1, :]
+            tiles[i] = block
+        tiles[t] = rows
     lane = iota((32, 128), 1)
     outs = []
     for i in range(3):
@@ -251,9 +270,8 @@
     return jnp.concatenate([step, less], axis=1)
 
 
-def first_basis(
-    v, c, low, high, x_low, x_high, inj, i_low, i_high, ix_low, ix_high,
-    diag, wx, wy, wv, cap, change, v0, v1, v2, v3, gram, ext,
+def grid_weights(
+    v, c, low, high, x_low, x_high, diag, wx, wy, wv, cap, free, ext,
 ):
     lane = iota((YE, 128), 1)
     n = iota((128, 512), 1)
@@ -309,12 +327,27 @@
     lax.fori_loop(0, 21, edges, 0)
     weights = (diag, wx, wy, wv)
 
+
+    def start(i, carry):
+        e = ext[i]
+        free[i] = (cap[i] - SHIFT) * e - SCALE * apply_row(ext, i, *weights)
+        return carry
+
+    lax.fori_loop(1, 21, start, 0)
+
+
+def first_basis(
+    diag, wx, wy, wv, free, inj, i_low, i_high, ix_low, ix_high,
+    change, v0, v1, v2, v3, gram,
+):
+    lane = iota((YE, 128), 1)
+    weights = (diag, wx, wy, wv)
+
     def start(i, both):
         now = jnp.where(lane < 32, both, 0.0)
         then = jnp.where(lane < 32, pltpu.roll(both, 96, 1), 0.0)
         change[i] = now - then
-        e = ext[i]
-        v0[i] = (cap[i] - SHIFT) * e - SCALE * apply_row(ext, i, *weights) - now
+        v0[i] = free[i] - now
 
     def own_start(x, carry):
         at = pl.ds(pl.multiple_of(x * 8, 8), 8)
@@ -345,7 +378,7 @@
 
     def row(i, carry):
         fields = jnp.concatenate([v0[i], v1[i], v2[i], v3[i]], axis=1)
-        both = dot(fields, mix, ((1,), (0,)), HIGHEST)
+        both = dot_split(fields, mix, ((1,), (0,)))
         moved = both[:, :128]
         step[i] = moved
         b0[i] = v0[i] + both[:, 128:] + cap[i] * moved + change[i]
@@ -366,7 +399,7 @@
     mix = combination(gram)
     for x in range(8):
         fields = jnp.concatenate([w0[x], w1[x], w2[x], w3[x]], axis=1)
-        both = dot(fields, mix, ((1,), (0,)), HIGHEST)
+        both = dot_split(fields, mix, ((1,), (0,)))
         for value, out in (
             (volts[x] + both[:, :128], volts_out),
             (w0[x] + both[:, 128:], residual_out),
@@ -389,6 +422,10 @@
         x = x + lax.ppermute(x, axis, [(0, 1), (1, 0), (2, 3), (3, 2)])
         x = x + lax.ppermute(x, axis, [(0, 3), (3, 0), (1, 2), (2, 1)])
     return x
+
+
+def exchange(slots):
+    return lax.all_to_all(slots, GX_GY, split_axis=0, concat_axis=0, tiled=True)
 
 
 def body(volts, cap, cond_x, cond_y, via, waveforms, placement, cells, wave_ids, amps):
@@ -403,9 +440,10 @@
     y_low, y_high = neighbours(y_low, y_high, GY)
     lists = [a.reshape(64, 128) for a in (placement, cells, wave_ids, amps)]
     (slots,) = call(place_slots, [(128, 2, 128)], lists, [vmem((640, 128), F32)])
+    y_low, y_high, slots = lax.optimization_barrier((y_low, y_high, slots))
     x_low, x_high = call(pack_rows, [(7, 168, 128)] * 2, [v, c, y_low, y_high])
     x_low, x_high = neighbours(x_low, x_high, GX)
-    slots = lax.all_to_all(slots, GX_GY, split_axis=0, concat_axis=0, tiled=True)
+    slots = exchange(slots)
     inj, i_low, i_high = call(
         add_currents,
         [(8, 128, 128), (64, 128), (64, 128)],
@@ -416,17 +454,19 @@
     ix_low, ix_high = call(pack_injected, [(3, YE, 128)] * 2, [inj, i_low, i_high])
     ix_low, ix_high = neighbours(ix_low, ix_high, GX)
     wide = (XE, YE, 128)
+    diag, wx, wy, wv, cap, free = call(
+        grid_weights, [wide] * 6, [v, c, y_low, y_high, x_low, x_high], [vmem(wide, F32)]
+    )
     *kept, gram = call(
         first_basis,
-        [wide] * 10 + [(64, 128)],
-        [v, c, y_low, y_high, x_low, x_high, inj, i_low, i_high, ix_low, ix_high],
-        [vmem(wide, F32)],
+        [wide] * 5 + [(64, 128)],
+        [diag, wx, wy, wv, free, inj, i_low, i_high, ix_low, ix_high],
     )
     own = (8, 128, 128)
     *basis, gram = call(
         second_basis,
         [own] * 5 + [(64, 128)],
-        [everywhere(gram)] + kept + [v],
+        [everywhere(gram), diag, wx, wy, wv, cap] + kept + [v],
         [vmem(wide, F32)] * 5,
     )
     outs = call(finish, [(1024, 128)] * 2, [everywhere(gram)] + basis)

time: 197 us -> 169 us (0.86)
  Pallas kernels: 80.5 us -> 55.8 us
  waiting for transfers between devices: 54.1 us -> 40.7 us
  starting transfers between devices: 33.1 us -> 38.3 us
  local copies, waits for them, and re-layouts: 3.92 us -> 6.93 us
  blocking collectives: 23.3 us -> 25.8 us
    pallas_call x8 -> x9, Pallas kernels: 80.5 us -> 55.8 us  [call(): pl.pallas_call(kernel, out_shape=tuple((jax.ShapeDtypeStruct(s, F32) for...]
    ppermute x4, waiting for transfers between devices: 11.1 us -> 1.8 us  [neighbours(): return (from_low, lax.ppermute(to_low, axis, [(b, a) for a, b in up]))]
    unnamed x20, local copies, waits for them, and re-layouts: 3.92 us -> 6.93 us
    ppermute x6, starting transfers between devices: 5.48 us -> 8.25 us  [everywhere(): x = x + lax.ppermute(x, axis, [(0, 1), (1, 0), (2, 3), (3, 2)])]
    ppermute x4, waiting for transfers between devices: 2.77 us -> 0.01 us  [neighbours(): from_low = lax.ppermute(to_high, axis, up)]
    all_to_all x1, blocking collectives: 23.3 us -> 25.8 us  [exchange(): return lax.all_to_all(slots, GX_GY, split_axis=0, concat_axis=0, tiled=True)]
    ppermute x4, starting transfers between devices: 8.46 us -> 10.5 us  [neighbours(): from_low = lax.ppermute(to_high, axis, up)]
  transfers between devices with their start and end apart: 22 -> 22, of which waited for: 18 -> 15; matrix products, arithmetic and copies ran while one was open for 0% -> 0% of each run, Pallas kernels for 11% -> 18%
where the time goes in v2:
time: 169 us
  Pallas kernels  55.8 us (33%)
  waiting for transfers between devices  40.7 us (24%)
  starting transfers between devices  38.3 us (23%)
  blocking collectives  25.8 us (15%)
  local copies, waits for them, and re-layouts  6.93 us (4%)
    pallas_call x9, Pallas kernels, call(): pl.pallas_call(kernel, out_shape=tuple((jax.ShapeDtypeStruct(s, F32) for...  55.8 us
    all_to_all x1, blocking collectives, exchange(): return lax.all_to_all(slots, GX_GY, split_axis=0, concat_axis=0, tiled=True)  25.8 us
    ppermute x6, waiting for transfers between devices, everywhere(): x = x + lax.ppermute(x, axis, [(0, 3), (3, 0), (1, 2), (2, 1)])  18.9 us
    ppermute x6, waiting for transfers between devices, everywhere(): x = x + lax.ppermute(x, axis, [(0, 1), (1, 0), (2, 3), (3, 2)])  17.9 us
    ppermute x6, starting transfers between devices, everywhere(): x = x + lax.ppermute(x, axis, [(0, 3), (3, 0), (1, 2), (2, 1)])  12.3 us
    ppermute x4, starting transfers between devices, neighbours(): from_low = lax.ppermute(to_high, axis, up)  10.5 us
    ppermute x6, starting transfers between devices, everywhere(): x = x + lax.ppermute(x, axis, [(0, 1), (1, 0), (2, 3), (3, 2)])  8.25 us
    unnamed x20, local copies, waits for them, and re-layouts  6.93 us
  transfers between devices with their start and end apart: 22, of which 15 were waited for; matrix products, arithmetic and copies ran while one was open for 0% of the time, Pallas kernels for 18%

profile of v2, /device:TPU:0, one launch (start us, length us, event | category | flops | bytes accessed | tf_op | source)
XLA Modules:
  0.0 168.5 jit_solution(1371389144546503556)
XLA Ops:
  4.9 1.3 collective-permute-start
  10.6 6.8 %place_slots.1 = f32[128,2,128]{2,1,0:T(2,128)S(1)} custom-call(s32[64,128]{1,0:T(8,128)S(1)} %bitcast.12, s32[64,128]{1,0:T(8,128)S(1)} %bitcast.13, s32[64,128]{1,0:T(8,128)S(1)} %bitcast.14, f32[64,128]{1,0:T(8,128)S(1)} %bitcast.15), custom_call_target="tpu_custom_call" | custom-call | tf_op jit(solution)/shard_map/place_slots/pallas_call | solution.py:50
  17.6 4.0 %collective-permute-start.2 = (f32[7,168,128]{2,1,0:T(8,128)S(1)}, f32[7,168,128]{2,1,0:T(8,128)S(1)}, u32[]{:S(2)}, u32[]{:S(2)}) collective-permute-start(f32[7,168,128]{2,1,0:T(8,128)S(1)} %get-tuple-element.42), channel_id=1, source_target_pairs={{0,8},{8,16},{16,24},{24,32},{32,40},{40,48},{48,56},{56,64},{64,7... | collective-permute-start | bytes 1806344 | tf_op jit(solution)/shard_map/ppermute | solution.py:415
  23.0 25.8 %all_to_all.5.slots = f32[128,2,128]{2,1,0:T(2,128)S(1)} all-to-all(f32[128,2,128]{2,1,0:T(2,128)S(1)} %place_slots.1), channel_id=1, replica_groups=mesh['gx_0'=4,'gx_1'=4,'gy_0'=4,'gy_1'=2] {'gx_0','gx_1','gy_0','gy_1'}, dimensions={0} | all-to-all | bytes 262144 | tf_op jit(solution)/shard_map/all_to_all | solution.py:428
  48.8 14.6 %add_currents.1 = (f32[8,128,128]{2,1,0:T(8,128)S(1)}, f32[64,128]{1,0:T(8,128)S(1)}, f32[64,128]{1,0:T(8,128)S(1)}) custom-call(f32[128,2,128]{2,1,0:T(2,128)S(1)} %all_to_all.5.slots, f32[64,64]{1,0:T(8,128)S(1)} %copy-done.1), custom_call_target="tpu_custom_call" | custom-call | tf_op jit(solution)/shard_map/add_currents/pallas_call | solution.py:50
  66.0 1.8 %collective-permute-done.5.high.i_high = f32[64,128]{1,0:T(8,128)S(1)} collective-permute-done((f32[64,128]{1,0:T(8,128)S(1)}, f32[64,128]{1,0:T(8,128)S(1)}, u32[]{:S(2)}, u32[]{:S(2)}) %collective-permute-start.5) | collective-permute-done | bytes 32800 | tf_op jit(solution)/shard_map/ppermute | solution.py:416
  67.9 3.8 %collective-permute-start.6 = (f32[3,144,128]{2,1,0:T(8,128)S(1)}, f32[3,144,128]{2,1,0:T(8,128)S(1)}, u32[]{:S(2)}, u32[]{:S(2)}) collective-permute-start(f32[3,144,128]{2,1,0:T(8,128)S(1)} %get-tuple-element.53), channel_id=1, source_target_pairs={{0,8},{8,16},{16,24},{24,32},{32,40},{40,48},{48,56},{56,64},{64,7... | collective-permute-start | bytes 663560 | tf_op jit(solution)/shard_map/ppermute | solution.py:415
  71.8 1.3 collective-permute-start.7
  73.1 9.6 %grid_weights.1 = (f32[22,144,128]{2,1,0:T(8,128)S(1)}, f32[22,144,128]{2,1,0:T(8,128)S(1)}, f32[22,144,128]{2,1,0:T(8,128)S(1)}, f32[22,144,128]{2,1,0:T(8,128)...) custom-call(f32[8,128,128]{2,1,0:T(8,128)S(1)} %get-tuple-element.36.v, ...), custom_call_target="tpu_custom_call" | custom-call | tf_op jit(solution)/shard_map/grid_weights/pallas_call | solution.py:50
  82.7 7.9 %first_basis.1 = (f32[22,144,128]{2,1,0:T(8,128)S(1)}, f32[22,144,128]{2,1,0:T(8,128)S(1)}, f32[22,144,128]{2,1,0:T(8,128)S(1)}, f32[22,144,128]{2,1,0:T(8,128)S...) custom-call(f32[22,144,128]{2,1,0:T(8,128)S(1)} %get-tuple-element.44.diag, ...), custom_call_target="tpu_custom_call" | custom-call | tf_op jit(solution)/shard_map/first_basis/pallas_call | solution.py:50
  90.6 2.0 %collective-permute-start.8 = (f32[64,128]{1,0:T(8,128)S(1)}, f32[64,128]{1,0:T(8,128)S(1)}, u32[]{:S(2)}, u32[]{:S(2)}) collective-permute-start(f32[64,128]{1,0:T(8,128)S(1)} %get-tuple-element.55), channel_id=1, source_target_pairs={{0,1},{1,0},{2,3},{3,2},{4,5},{5,4},{6,7},{7,6},{8,9},{9,8},{10,11... | collective-permute-start | bytes 98312 | tf_op jit(solution)/shard_map/ppermute | solution.py:420
  94.2 3.2 %collective-permute-done.9 = f32[64,128]{1,0:T(8,128)S(1)} collective-permute-done((f32[64,128]{1,0:T(8,128)S(1)}, f32[64,128]{1,0:T(8,128)S(1)}, u32[]{:S(2)}, u32[]{:S(2)}) %collective-permute-start.9) | collective-permute-done | bytes 32800 | tf_op jit(solution)/shard_map/ppermute | solution.py:422
  97.4 1.3 collective-permute-start.10
  98.8 3.8 %collective-permute-done.10 = f32[64,128]{1,0:T(8,128)S(1)} collective-permute-done((f32[64,128]{1,0:T(8,128)S(1)}, f32[64,128]{1,0:T(8,128)S(1)}, u32[]{:S(2)}, u32[]{:S(2)}) %collective-permute-start.10) | collective-permute-done | bytes 32800 | tf_op jit(solution)/shard_map/ppermute | solution.py:423
  102.6 2.4 %collective-permute-start.11 = (f32[64,128]{1,0:T(8,128)S(1)}, f32[64,128]{1,0:T(8,128)S(1)}, u32[]{:S(2)}, u32[]{:S(2)}) collective-permute-start(f32[64,128]{1,0:T(8,128)S(1)} %add.44), channel_id=1, source_target_pairs={{0,8},{8,0},{16,24},{24,16},{1,9},{9,1},{17,25},{25,17},{2,10},{10... | collective-permute-start | bytes 98312 | tf_op jit(solution)/shard_map/ppermute | solution.py:422
  104.9 1.9 %collective-permute-done.11 = f32[64,128]{1,0:T(8,128)S(1)} collective-permute-done((f32[64,128]{1,0:T(8,128)S(1)}, f32[64,128]{1,0:T(8,128)S(1)}, u32[]{:S(2)}, u32[]{:S(2)}) %collective-permute-start.11) | collective-permute-done | bytes 32800 | tf_op jit(solution)/shard_map/ppermute | solution.py:422
  106.8 3.7 %collective-permute-start.12 = (f32[64,128]{1,0:T(8,128)S(1)}, f32[64,128]{1,0:T(8,128)S(1)}, u32[]{:S(2)}, u32[]{:S(2)}) collective-permute-start(f32[64,128]{1,0:T(8,128)S(1)} %add.45), channel_id=1, source_target_pairs={{0,24},{24,0},{8,16},{16,8},{1,25},{25,1},{9,17},{17,9},{2,26},{26... | collective-permute-start | bytes 98312 | tf_op jit(solution)/shard_map/ppermute | solution.py:423
  110.5 1.9 %collective-permute-done.12 = f32[64,128]{1,0:T(8,128)S(1)} collective-permute-done((f32[64,128]{1,0:T(8,128)S(1)}, f32[64,128]{1,0:T(8,128)S(1)}, u32[]{:S(2)}, u32[]{:S(2)}) %collective-permute-start.12) | collective-permute-done | bytes 32800 | tf_op jit(solution)/shard_map/ppermute | solution.py:423
  112.4 4.4 %collective-permute-start.13 = (f32[64,128]{1,0:T(8,128)S(1)}, f32[64,128]{1,0:T(8,128)S(1)}, u32[]{:S(2)}, u32[]{:S(2)}) collective-permute-start(f32[64,128]{1,0:T(8,128)S(1)} %add.46), channel_id=1, source_target_pairs={{0,32},{32,0},{64,96},{96,64},{1,33},{33,1},{65,97},{97,65},{2,34}... | collective-permute-start | bytes 98312 | tf_op jit(solution)/shard_map/ppermute | solution.py:422
  116.8 1.9 %collective-permute-done.13 = f32[64,128]{1,0:T(8,128)S(1)} collective-permute-done((f32[64,128]{1,0:T(8,128)S(1)}, f32[64,128]{1,0:T(8,128)S(1)}, u32[]{:S(2)}, u32[]{:S(2)}) %collective-permute-start.13) | collective-permute-done | bytes 32800 | tf_op jit(solution)/shard_map/ppermute | solution.py:422
  118.7 2.4 %collective-permute-start.14 = (f32[64,128]{1,0:T(8,128)S(1)}, f32[64,128]{1,0:T(8,128)S(1)}, u32[]{:S(2)}, u32[]{:S(2)}) collective-permute-start(f32[64,128]{1,0:T(8,128)S(1)} %add.47), channel_id=1, source_target_pairs={{0,96},{96,0},{32,64},{64,32},{1,97},{97,1},{33,65},{65,33},{2,98}... | collective-permute-start | bytes 98312 | tf_op jit(solution)/shard_map/ppermute | solution.py:423
  121.1 2.7 %collective-permute-done.14 = f32[64,128]{1,0:T(8,128)S(1)} collective-permute-done((f32[64,128]{1,0:T(8,128)S(1)}, f32[64,128]{1,0:T(8,128)S(1)}, u32[]{:S(2)}, u32[]{:S(2)}) %collective-permute-start.14) | collective-permute-done | bytes 32800 | tf_op jit(solution)/shard_map/ppermute | solution.py:423
  123.8 11.2 %second_basis.1 = (f32[8,128,128]{2,1,0:T(8,128)S(1)}, f32[8,128,128]{2,1,0:T(8,128)S(1)}, f32[8,128,128]{2,1,0:T(8,128)S(1)}, f32[8,128,128]{2,1,0:T(8,128)S(1)...) custom-call(f32[64,128]{1,0:T(8,128)S(1)} %add.48.gram, f32[22,144,128]{2,1,0:T(8,128)S(1)} %get-tuple-element.44.diag, ...), custom_call_target="tpu_custom_call" | custom-call | tf_op jit(solution)/shard_map/second_basis/pallas_call | solution.py:50
  136.4 3.9 %collective-permute-done.16 = f32[64,128]{1,0:T(8,128)S(1)} collective-permute-done((f32[64,128]{1,0:T(8,128)S(1)}, f32[64,128]{1,0:T(8,128)S(1)}, u32[]{:S(2)}, u32[]{:S(2)}) %collective-permute-start.16) | collective-permute-done | bytes 32800 | tf_op jit(solution)/shard_map/ppermute | solution.py:422
  140.3 1.6 collective-permute-start.17
  141.9 3.5 %collective-permute-done.17 = f32[64,128]{1,0:T(8,128)S(1)} collective-permute-done((f32[64,128]{1,0:T(8,128)S(1)}, f32[64,128]{1,0:T(8,128)S(1)}, u32[]{:S(2)}, u32[]{:S(2)}) %collective-permute-start.17) | collective-permute-done | bytes 32800 | tf_op jit(solution)/shard_map/ppermute | solution.py:423
  145.4 3.9 %collective-permute-done.18 = f32[64,128]{1,0:T(8,128)S(1)} collective-permute-done((f32[64,128]{1,0:T(8,128)S(1)}, f32[64,128]{1,0:T(8,128)S(1)}, u32[]{:S(2)}, u32[]{:S(2)}) %collective-permute-start.18) | collective-permute-done | bytes 32800 | tf_op jit(solution)/shard_map/ppermute | solution.py:422
  150.2 4.3 %collective-permute-done.19 = f32[64,128]{1,0:T(8,128)S(1)} collective-permute-done((f32[64,128]{1,0:T(8,128)S(1)}, f32[64,128]{1,0:T(8,128)S(1)}, u32[]{:S(2)}, u32[]{:S(2)}) %collective-permute-start.19) | collective-permute-done | bytes 32800 | tf_op jit(solution)/shard_map/ppermute | solution.py:423
  155.3 3.1 %collective-permute-done.20 = f32[64,128]{1,0:T(8,128)S(1)} collective-permute-done((f32[64,128]{1,0:T(8,128)S(1)}, f32[64,128]{1,0:T(8,128)S(1)}, u32[]{:S(2)}, u32[]{:S(2)}) %collective-permute-start.20) | collective-permute-done | bytes 32800 | tf_op jit(solution)/shard_map/ppermute | solution.py:422
  158.4 2.4 %collective-permute-start.21 = (f32[64,128]{1,0:T(8,128)S(1)}, f32[64,128]{1,0:T(8,128)S(1)}, u32[]{:S(2)}, u32[]{:S(2)}) collective-permute-start(f32[64,128]{1,0:T(8,128)S(1)} %add.54), channel_id=1, source_target_pairs={{0,96},{96,0},{32,64},{64,32},{1,97},{97,1},{33,65},{65,33},{2,98}... | collective-permute-start | bytes 98312 | tf_op jit(solution)/shard_map/ppermute | solution.py:423
  160.8 2.7 %collective-permute-done.21 = f32[64,128]{1,0:T(8,128)S(1)} collective-permute-done((f32[64,128]{1,0:T(8,128)S(1)}, f32[64,128]{1,0:T(8,128)S(1)}, u32[]{:S(2)}, u32[]{:S(2)}) %collective-permute-start.21) | collective-permute-done | bytes 32800 | tf_op jit(solution)/shard_map/ppermute | solution.py:423
  163.5 5.0 %finish.1 = (f32[1024,128]{1,0:T(8,128)}, f32[1024,128]{1,0:T(8,128)}) custom-call(f32[64,128]{1,0:T(8,128)S(1)} %add.55.gram, f32[8,128,128]{2,1,0:T(8,128)S(1)} %get-tuple-element.63.w0, f32[8,128,128]{2,1,0:T(8,128)S(1)} %get-tuple-element.64.w1, f32[8,128,128]{2,1,0:T(8,128)S(1)} %get-tuple-element.65.w2, f32[8,128,128]{2,1,0:T(8,128)S(1)} %get-tuple-element.66.w3, ...), custom_call_target="tpu_custom_call" | custom-call | tf_op jit(solution)/shard_map/finish/pallas_call | solution.py:50
  (56 shorter events, 17.4 us)
Async XLA Ops:
  0.6 1.0 copy-start
  1.7 0.7 copy-start.6
  2.4 0.7 copy-start.7
  3.1 0.7 copy-start.8
  3.8 0.7 copy-start.9
  4.5 44.3 %copy-start.1 = (f32[64,64]{1,0:T(8,128)S(1)}, f32[64,64]{1,0:T(8,128)}, u32[]{:S(2)}) copy-start(f32[64,64]{1,0:T(8,128)} %waves.1) | copy-start | bytes 49156
  4.9 12.4 %collective-permute-start = (f32[128,128]{1,0:T(8,128)S(1)}, f32[128,128]{1,0:T(8,128)S(1)}, u32[]{:S(2)}, u32[]{:S(2)}) collective-permute-start(f32[128,128]{1,0:T(8,128)S(1)} %get-tuple-element.38), channel_id=1, source_target_pairs={{0,1},{1,2},{2,3},{3,4},{4,5},{5,6},{6,7},{8,9},{9,10},{10,11},{11... | collective-permute-start | bytes 196616 | tf_op jit(solution)/shard_map/ppermute | solution.py:415
  6.2 11.1 %collective-permute-start.1 = (f32[128,128]{1,0:T(8,128)S(1)}, f32[128,128]{1,0:T(8,128)S(1)}, u32[]{:S(2)}, u32[]{:S(2)}) collective-permute-start(f32[128,128]{1,0:T(8,128)S(1)} %get-tuple-element.39), channel_id=1, source_target_pairs={{1,0},{2,1},{3,2},{4,3},{5,4},{6,5},{7,6},{9,8},{10,9},{11,10},{12... | collective-permute-start | bytes 196616 | tf_op jit(solution)/shard_map/ppermute | solution.py:416
  7.5 0.8 copy-start.2
  8.3 0.8 copy-start.3
  9.1 0.8 copy-start.4
  9.8 0.8 copy-start.5
  17.6 55.5 %collective-permute-start.2 = (f32[7,168,128]{2,1,0:T(8,128)S(1)}, f32[7,168,128]{2,1,0:T(8,128)S(1)}, u32[]{:S(2)}, u32[]{:S(2)}) collective-permute-start(f32[7,168,128]{2,1,0:T(8,128)S(1)} %get-tuple-element.42), channel_id=1, source_target_pairs={{0,8},{8,16},{16,24},{24,32},{32,40},{40,48},{48,56},{56,64},{64,7... | collective-permute-start | bytes 1806344 | tf_op jit(solution)/shard_map/ppermute | solution.py:415
  21.7 51.4 %collective-permute-start.3 = (f32[7,168,128]{2,1,0:T(8,128)S(1)}, f32[7,168,128]{2,1,0:T(8,128)S(1)}, u32[]{:S(2)}, u32[]{:S(2)}) collective-permute-start(f32[7,168,128]{2,1,0:T(8,128)S(1)} %get-tuple-element.43), channel_id=1, source_target_pairs={{8,0},{16,8},{24,16},{32,24},{40,32},{48,40},{56,48},{64,56},{72,6... | collective-permute-start | bytes 1806344 | tf_op jit(solution)/shard_map/ppermute | solution.py:416
  63.4 2.6 %collective-permute-start.4 = (f32[64,128]{1,0:T(8,128)S(1)}, f32[64,128]{1,0:T(8,128)S(1)}, u32[]{:S(2)}, u32[]{:S(2)}) collective-permute-start(f32[64,128]{1,0:T(8,128)S(1)} %get-tuple-element.51), channel_id=1, source_target_pairs={{0,1},{1,2},{2,3},{3,4},{4,5},{5,6},{6,7},{8,9},{9,10},{10,11},{11... | collective-permute-start | bytes 98312 | tf_op jit(solution)/shard_map/ppermute | solution.py:415
  64.7 3.1 %collective-permute-start.5 = (f32[64,128]{1,0:T(8,128)S(1)}, f32[64,128]{1,0:T(8,128)S(1)}, u32[]{:S(2)}, u32[]{:S(2)}) collective-permute-start(f32[64,128]{1,0:T(8,128)S(1)} %get-tuple-element.52), channel_id=1, source_target_pairs={{1,0},{2,1},{3,2},{4,3},{5,4},{6,5},{7,6},{9,8},{10,9},{11,10},{12... | collective-permute-start | bytes 98312 | tf_op jit(solution)/shard_map/ppermute | solution.py:416
  67.9 14.8 %collective-permute-start.6 = (f32[3,144,128]{2,1,0:T(8,128)S(1)}, f32[3,144,128]{2,1,0:T(8,128)S(1)}, u32[]{:S(2)}, u32[]{:S(2)}) collective-permute-start(f32[3,144,128]{2,1,0:T(8,128)S(1)} %get-tuple-element.53), channel_id=1, source_target_pairs={{0,8},{8,16},{16,24},{24,32},{32,40},{40,48},{48,56},{56,64},{64,7... | collective-permute-start | bytes 663560 | tf_op jit(solution)/shard_map/ppermute | solution.py:415
  71.8 10.9 %collective-permute-start.7 = (f32[3,144,128]{2,1,0:T(8,128)S(1)}, f32[3,144,128]{2,1,0:T(8,128)S(1)}, u32[]{:S(2)}, u32[]{:S(2)}) collective-permute-start(f32[3,144,128]{2,1,0:T(8,128)S(1)} %get-tuple-element.54), channel_id=1, source_target_pairs={{8,0},{16,8},{24,16},{32,24},{40,32},{48,40},{56,48},{64,56},{72,6... | collective-permute-start | bytes 663560 | tf_op jit(solution)/shard_map/ppermute | solution.py:416
  90.6 2.9 %collective-permute-start.8 = (f32[64,128]{1,0:T(8,128)S(1)}, f32[64,128]{1,0:T(8,128)S(1)}, u32[]{:S(2)}, u32[]{:S(2)}) collective-permute-start(f32[64,128]{1,0:T(8,128)S(1)} %get-tuple-element.55), channel_id=1, source_target_pairs={{0,1},{1,0},{2,3},{3,2},{4,5},{5,4},{6,7},{7,6},{8,9},{9,8},{10,11... | collective-permute-start | bytes 98312 | tf_op jit(solution)/shard_map/ppermute | solution.py:420
  93.5 3.9 %collective-permute-start.9 = (f32[64,128]{1,0:T(8,128)S(1)}, f32[64,128]{1,0:T(8,128)S(1)}, u32[]{:S(2)}, u32[]{:S(2)}) collective-permute-start(f32[64,128]{1,0:T(8,128)S(1)} %add.42), channel_id=1, source_target_pairs={{0,2},{2,0},{4,6},{6,4},{1,3},{3,1},{5,7},{7,5},{8,10},{10,8},{12,... | collective-permute-start | bytes 98312 | tf_op jit(solution)/shard_map/ppermute | solution.py:422
  97.4 5.1 %collective-permute-start.10 = (f32[64,128]{1,0:T(8,128)S(1)}, f32[64,128]{1,0:T(8,128)S(1)}, u32[]{:S(2)}, u32[]{:S(2)}) collective-permute-start(f32[64,128]{1,0:T(8,128)S(1)} %add.43), channel_id=1, source_target_pairs={{0,6},{6,0},{2,4},{4,2},{1,7},{7,1},{3,5},{5,3},{8,14},{14,8},{10,... | collective-permute-start | bytes 98312 | tf_op jit(solution)/shard_map/ppermute | solution.py:423
  102.6 4.3 %collective-permute-start.11 = (f32[64,128]{1,0:T(8,128)S(1)}, f32[64,128]{1,0:T(8,128)S(1)}, u32[]{:S(2)}, u32[]{:S(2)}) collective-permute-start(f32[64,128]{1,0:T(8,128)S(1)} %add.44), channel_id=1, source_target_pairs={{0,8},{8,0},{16,24},{24,16},{1,9},{9,1},{17,25},{25,17},{2,10},{10... | collective-permute-start | bytes 98312 | tf_op jit(solution)/shard_map/ppermute | solution.py:422
  106.8 5.6 %collective-permute-start.12 = (f32[64,128]{1,0:T(8,128)S(1)}, f32[64,128]{1,0:T(8,128)S(1)}, u32[]{:S(2)}, u32[]{:S(2)}) collective-permute-start(f32[64,128]{1,0:T(8,128)S(1)} %add.45), channel_id=1, source_target_pairs={{0,24},{24,0},{8,16},{16,8},{1,25},{25,1},{9,17},{17,9},{2,26},{26... | collective-permute-start | bytes 98312 | tf_op jit(solution)/shard_map/ppermute | solution.py:423
  112.4 6.3 %collective-permute-start.13 = (f32[64,128]{1,0:T(8,128)S(1)}, f32[64,128]{1,0:T(8,128)S(1)}, u32[]{:S(2)}, u32[]{:S(2)}) collective-permute-start(f32[64,128]{1,0:T(8,128)S(1)} %add.46), channel_id=1, source_target_pairs={{0,32},{32,0},{64,96},{96,64},{1,33},{33,1},{65,97},{97,65},{2,34}... | collective-permute-start | bytes 98312 | tf_op jit(solution)/shard_map/ppermute | solution.py:422
  118.7 5.1 %collective-permute-start.14 = (f32[64,128]{1,0:T(8,128)S(1)}, f32[64,128]{1,0:T(8,128)S(1)}, u32[]{:S(2)}, u32[]{:S(2)}) collective-permute-start(f32[64,128]{1,0:T(8,128)S(1)} %add.47), channel_id=1, source_target_pairs={{0,96},{96,0},{32,64},{64,32},{1,97},{97,1},{33,65},{65,33},{2,98}... | collective-permute-start | bytes 98312 | tf_op jit(solution)/shard_map/ppermute | solution.py:423
  135.1 1.3 collective-permute-start.15
  136.4 3.9 %collective-permute-start.16 = (f32[64,128]{1,0:T(8,128)S(1)}, f32[64,128]{1,0:T(8,128)S(1)}, u32[]{:S(2)}, u32[]{:S(2)}) collective-permute-start(f32[64,128]{1,0:T(8,128)S(1)} %add.49), channel_id=1, source_target_pairs={{0,2},{2,0},{4,6},{6,4},{1,3},{3,1},{5,7},{7,5},{8,10},{10,8},{12,... | collective-permute-start | bytes 98312 | tf_op jit(solution)/shard_map/ppermute | solution.py:422
  140.3 5.1 %collective-permute-start.17 = (f32[64,128]{1,0:T(8,128)S(1)}, f32[64,128]{1,0:T(8,128)S(1)}, u32[]{:S(2)}, u32[]{:S(2)}) collective-permute-start(f32[64,128]{1,0:T(8,128)S(1)} %add.50), channel_id=1, source_target_pairs={{0,6},{6,0},{2,4},{4,2},{1,7},{7,1},{3,5},{5,3},{8,14},{14,8},{10,... | collective-permute-start | bytes 98312 | tf_op jit(solution)/shard_map/ppermute | solution.py:423
  145.4 3.9 %collective-permute-start.18 = (f32[64,128]{1,0:T(8,128)S(1)}, f32[64,128]{1,0:T(8,128)S(1)}, u32[]{:S(2)}, u32[]{:S(2)}) collective-permute-start(f32[64,128]{1,0:T(8,128)S(1)} %add.51), channel_id=1, source_target_pairs={{0,8},{8,0},{16,24},{24,16},{1,9},{9,1},{17,25},{25,17},{2,10},{10... | collective-permute-start | bytes 98312 | tf_op jit(solution)/shard_map/ppermute | solution.py:422
  149.4 5.1 %collective-permute-start.19 = (f32[64,128]{1,0:T(8,128)S(1)}, f32[64,128]{1,0:T(8,128)S(1)}, u32[]{:S(2)}, u32[]{:S(2)}) collective-permute-start(f32[64,128]{1,0:T(8,128)S(1)} %add.52), channel_id=1, source_target_pairs={{0,24},{24,0},{8,16},{16,8},{1,25},{25,1},{9,17},{17,9},{2,26},{26... | collective-permute-start | bytes 98312 | tf_op jit(solution)/shard_map/ppermute | solution.py:423
  154.5 3.9 %collective-permute-start.20 = (f32[64,128]{1,0:T(8,128)S(1)}, f32[64,128]{1,0:T(8,128)S(1)}, u32[]{:S(2)}, u32[]{:S(2)}) collective-permute-start(f32[64,128]{1,0:T(8,128)S(1)} %add.53), channel_id=1, source_target_pairs={{0,32},{32,0},{64,96},{96,64},{1,33},{33,1},{65,97},{97,65},{2,34}... | collective-permute-start | bytes 98312 | tf_op jit(solution)/shard_map/ppermute | solution.py:422
  158.4 5.1 %collective-permute-start.21 = (f32[64,128]{1,0:T(8,128)S(1)}, f32[64,128]{1,0:T(8,128)S(1)}, u32[]{:S(2)}, u32[]{:S(2)}) collective-permute-start(f32[64,128]{1,0:T(8,128)S(1)} %add.54), channel_id=1, source_target_pairs={{0,96},{96,0},{32,64},{64,32},{1,97},{97,1},{33,65},{65,33},{2,98}... | collective-permute-start | bytes 98312 | tf_op jit(solution)/shard_map/ppermute | solution.py:423

commit v3 on v2

--- a/solution.py
+++ b/solution.py
@@ -46,19 +46,32 @@
     return hi, mid, (rest - mid.astype(F32)).astype(BF16)
 
 
-def call(kernel, outs, args, scratch=(), limit=14):
+def call(kernel, outs, args, scratch=(), limit=14, in_specs=None):
+    outs = [o if isinstance(o, jax.ShapeDtypeStruct) else jax.ShapeDtypeStruct(o, F32) for o in outs]
+    specs = {} if in_specs is None else {"in_specs": in_specs}
     return pl.pallas_call(
         kernel,
-        out_shape=tuple(jax.ShapeDtypeStruct(s, F32) for s in outs),
+        out_shape=tuple(outs),
         scratch_shapes=list(scratch),
+        **specs,
         compiler_params=pltpu.CompilerParams(vmem_limit_bytes=limit << 20),
         name=kernel.__name__,
     )(*args)
 
 
-def to_lanes(volts, cap, cond_x, cond_y, via, v_out, c_out, low_out, high_out, stack):
+def to_lanes(
+    volts_in, cap, cond_x, cond_y, via, tile_in, cell_in, wave_in, amp_in,
+    v_out, c_out, low_out, high_out, tile, cell, wave, amp, volts, stack, sems,
+):
+    pairs = [(volts_in, volts)]
     for c, ref in enumerate((cap, cond_x, cond_y, via)):
-        stack[c * 32 : (c + 1) * 32, :] = ref[...]
+        pairs.append((ref, stack.at[pl.ds(c * 32, 32), :]))
+    pairs += [(tile_in, tile), (cell_in, cell), (wave_in, wave), (amp_in, amp)]
+    copies = [pltpu.make_async_copy(src, dst, sems.at[n]) for n, (src, dst) in enumerate(pairs)]
+    for copy in copies:
+        copy.start()
+    for copy in copies:
+        copy.wait()
     for x in range(8):
         rows = [volts[pl.ds(l * 8 + x, 32, stride=32), :] for l in range(4)]
         field = jnp.concatenate(rows, axis=0).T
@@ -101,7 +114,7 @@
         at = pl.ds(pl.multiple_of(turn * 8, 8), 8)
         tiles = tile[at, :]
         code = cell[at, :] * 64 + wave[at, :]
-        parts = list(split3(amp[at, :]))
+        parts = list(split2(amp[at, :]))
         parts.append((code >> 8).astype(F32).astype(BF16))
         parts.append((code & 255).astype(F32).astype(BF16))
         hits = [
@@ -125,33 +138,34 @@
         acc[...] += dot(jnp.concatenate(left, axis=0), slot, ((1,), (1,)))
         return seen
 
-    lax.fori_loop(0, 8, chunk, jnp.zeros((128, 128), F32))
-    out[:, 0, :] = acc[0:128] + acc[128:256] + acc[256:384]
-    out[:, 1, :] = acc[384:512] * 256.0 + acc[512:640]
+    lax.fori_loop(0, 8, chunk, jnp.zeros((128, 128), F32), unroll=8)
+    out[:, 0, :] = acc[0:128] + acc[128:256]
+    out[:, 1, :] = acc[256:384] * 256.0 + acc[384:512]
 
 
 def add_currents(slots, waves, out, low_out, high_out, acc):
     acc[...] = jnp.zeros_like(acc)
     table = jnp.concatenate([p.astype(F32) for p in split3(waves[...])], axis=0).astype(BF16)
-    wave_line = iota((64, 512), 0)
-    cell_line = iota((256, 512), 0)
+    wave_line = iota((64, 2048), 0).astype(F32).astype(BF16)
+    cell_line = iota((256, 2048), 0).astype(F32).astype(BF16)
+    one, zero = jnp.ones((), BF16), jnp.zeros((), BF16)
 
     def chunk(turn, carry):
-        rows = [slots[turn * 4 + j] for j in range(4)]
+        rows = [slots[turn * 16 + j] for j in range(16)]
         amp = jnp.concatenate([r[0:1, :] for r in rows], axis=1)
         code = jnp.concatenate([r[1:2, :] for r in rows], axis=1).astype(jnp.int32)
-        hit = (wave_line == (code & 63)).astype(F32).astype(BF16)
+        hit = jnp.where(wave_line == (code & 63).astype(F32).astype(BF16), one, zero)
         picked = dot(table, hit, ((1,), (0,)))
         current = (picked[:64] + picked[64:128]) + picked[128:]
-        current = (current * amp).astype(BF16).astype(F32)
+        current = (current * amp).astype(BF16)
         cell = code >> 6
-        block = cell >> 8
-        right = [jnp.where(block == r, current, 0.0).astype(BF16) for r in range(4)]
-        left = (cell_line == (cell & 255)).astype(F32).astype(BF16)
+        block = (cell >> 8).astype(F32).astype(BF16)
+        right = [jnp.where(block == jnp.array(r, BF16), current, zero) for r in range(4)]
+        left = jnp.where(cell_line == (cell & 255).astype(F32).astype(BF16), one, zero)
         acc[...] += dot(left, jnp.concatenate(right, axis=0), ((1,), (1,)))
         return carry
 
-    lax.fori_loop(0, 32, chunk, 0)
+    lax.fori_loop(0, 8, chunk, 0, unroll=2)
     low_lanes = iota((256, 128), 1) < 64
     for r in range(4):
         half = acc[:, (r // 2) * 128 : (r // 2 + 1) * 128]
@@ -186,7 +200,7 @@
         dst[i] = apply_row(src, i, *weights)
         return carry
 
-    lax.fori_loop(first, last + 1, row, 0)
+    lax.fori_loop(first, last + 1, row, 0, unroll=2)
 
 
 def moments(fields, out, first):
@@ -307,7 +321,7 @@
         halo_row(j, x_high, 15)
         return carry
 
-    lax.fori_loop(0, 8, own_row, 0)
+    lax.fori_loop(0, 8, own_row, 0, unroll=2)
     lax.fori_loop(0, 7, halo_rows, 0)
 
     def diagonal(i, carry):
@@ -316,7 +330,7 @@
         diag[i] = (total - SHIFT) * (1.0 / SCALE)
         return carry
 
-    lax.fori_loop(1, 21, diagonal, 0)
+    lax.fori_loop(1, 21, diagonal, 0, unroll=2)
 
     def edges(i, carry):
         wx[i] = jnp.where(cap[i + 1] > 0, wx[i] * (1.0 / SCALE), 0.0)
@@ -324,7 +338,7 @@
         wv[i] = wv[i] * (1.0 / SCALE)
         return carry
 
-    lax.fori_loop(0, 21, edges, 0)
+    lax.fori_loop(0, 21, edges, 0, unroll=3)
     weights = (diag, wx, wy, wv)
 
 
@@ -333,7 +347,7 @@
         free[i] = (cap[i] - SHIFT) * e - SCALE * apply_row(ext, i, *weights)
         return carry
 
-    lax.fori_loop(1, 21, start, 0)
+    lax.fori_loop(1, 21, start, 0, unroll=2)
 
 
 def first_basis(
@@ -384,7 +398,7 @@
         b0[i] = v0[i] + both[:, 128:] + cap[i] * moved + change[i]
         return carry
 
-    lax.fori_loop(4, 18, row, 0)
+    lax.fori_loop(4, 18, row, 0, unroll=2)
     power(b0, b1, 5, 16, weights)
     power(b1, b2, 6, 15, weights)
     power(b2, b3, 7, 14, weights)
@@ -419,8 +433,10 @@
 def everywhere(x):
     x = x + lax.ppermute(x, "gy_1", [(0, 1), (1, 0)])
     for axis in ("gy_0", "gx_1", "gx_0"):
-        x = x + lax.ppermute(x, axis, [(0, 1), (1, 0), (2, 3), (3, 2)])
-        x = x + lax.ppermute(x, axis, [(0, 3), (3, 0), (1, 2), (2, 1)])
+        one, two, three = [
+            lax.ppermute(x, axis, [(i, i ^ k) for i in range(4)]) for k in (1, 2, 3)
+        ]
+        x = (x + one) + (two + three)
     return x
 
 
@@ -431,15 +447,17 @@
 def body(volts, cap, cond_x, cond_y, via, waveforms, placement, cells, wave_ids, amps):
     vmem = pltpu.VMEM
     coefs = [a.reshape(32, 128) for a in (cap, cond_x, cond_y, via)]
-    v, c, y_low, y_high = call(
+    lists = [a.reshape(64, 128) for a in (placement, cells, wave_ids, amps)]
+    v, c, y_low, y_high, *lists = call(
         to_lanes,
-        [(8, 128, 128), (8, 128, 128), (128, 128), (128, 128)],
-        [volts.reshape(1024, 128)] + coefs,
-        [vmem((128, 128), F32)],
+        [(8, 128, 128), (8, 128, 128), (128, 128), (128, 128)]
+        + [jax.ShapeDtypeStruct(a.shape, a.dtype) for a in lists],
+        [volts.reshape(1024, 128)] + coefs + lists,
+        [vmem((1024, 128), F32), vmem((128, 128), F32), pltpu.SemaphoreType.DMA((9,))],
+        in_specs=[pl.BlockSpec(memory_space=pl.ANY)] * 9,
     )
     y_low, y_high = neighbours(y_low, y_high, GY)
-    lists = [a.reshape(64, 128) for a in (placement, cells, wave_ids, amps)]
-    (slots,) = call(place_slots, [(128, 2, 128)], lists, [vmem((640, 128), F32)])
+    (slots,) = call(place_slots, [(128, 2, 128)], lists, [vmem((512, 128), F32)])
     y_low, y_high, slots = lax.optimization_barrier((y_low, y_high, slots))
     x_low, x_high = call(pack_rows, [(7, 168, 128)] * 2, [v, c, y_low, y_high])
     x_low, x_high = neighbours(x_low, x_high, GX)

time: 169 us -> 143 us (0.85)
  waiting for transfers between devices: 40.7 us -> 23.9 us
  Pallas kernels: 55.8 us -> 39.6 us
  starting transfers between devices: 38.3 us -> 44.5 us
    ppermute x12 -> x18, waiting for transfers between devices: 36.9 us -> 19.4 us  [everywhere(): lax.ppermute(x, axis, [(i, i ^ k) for i in range(4)])]
    pallas_call x9, Pallas kernels: 55.8 us -> 39.6 us  [call(): pl.pallas_call(kernel, out_shape=tuple(outs), scratch_shapes=list(scratch...]
    ppermute x12 -> x18, starting transfers between devices: 20.5 us -> 27.4 us  [everywhere(): lax.ppermute(x, axis, [(i, i ^ k) for i in range(4)])]
  transfers between devices with their start and end apart: 22 -> 28, of which waited for: 15 -> 17; matrix products, arithmetic and copies ran while one was open for 0% -> 0% of each run, Pallas kernels for 18% -> 13%
where the time goes in v3:
time: 143 us; the launch traced here: 142 us
  starting transfers between devices  44.5 us (31%)
  Pallas kernels  39.6 us (28%)
  blocking collectives  25.8 us (18%)
  waiting for transfers between devices  23.9 us (17%)
  local copies, waits for them, and re-layouts  6.94 us (5%)
    pallas_call x9, Pallas kernels, call(): pl.pallas_call(kernel, out_shape=tuple(outs), scratch_shapes=list(scratch...  39.6 us
    ppermute x18, starting transfers between devices, everywhere(): lax.ppermute(x, axis, [(i, i ^ k) for i in range(4)])  27.4 us
    all_to_all x1, blocking collectives, exchange(): return lax.all_to_all(slots, GX_GY, split_axis=0, concat_axis=0, tiled=True)  25.8 us
    ppermute x18, waiting for transfers between devices, everywhere(): lax.ppermute(x, axis, [(i, i ^ k) for i in range(4)])  19.4 us
    ppermute x4, starting transfers between devices, neighbours(): from_low = lax.ppermute(to_high, axis, up)  10.5 us
    unnamed x20, local copies, waits for them, and re-layouts  6.94 us
    ppermute x4, starting transfers between devices, neighbours(): return (from_low, lax.ppermute(to_low, axis, [(b, a) for a, b in up]))  5.17 us
  transfers between devices with their start and end apart: 28, of which 17 were waited for; matrix products, arithmetic and copies ran while one was open for 0% of the time, Pallas kernels for 13%

profile of v3, /device:TPU:0, one launch (start us, length us, event | category | flops | bytes accessed | tf_op | source)
XLA Modules:
  0.0 141.7 jit_solution(10094930326362068533)
XLA Ops:
  8.4 1.3 collective-permute-start
  9.7 1.3 collective-permute-start.1
  11.0 5.3 %place_slots.1 = f32[128,2,128]{2,1,0:T(2,128)S(1)} custom-call(s32[64,128]{1,0:T(8,128)S(1)} %get-tuple-element.44.tile, s32[64,128]{1,0:T(8,128)S(1)} %get-tuple-element.45.cell, s32[64,128]{1,0:T(8,128)S(1)} %get-tuple-element.46.wave, f32[64,128]{1,0:T(8,128)S(1)} %get-tuple-element.47.amp), custom_call_target="tpu_custom_call" | custom-call | tf_op jit(solution)/shard_map/place_slots/pallas_call | solution.py:52
  16.5 4.0 %collective-permute-start.2 = (f32[7,168,128]{2,1,0:T(8,128)S(1)}, f32[7,168,128]{2,1,0:T(8,128)S(1)}, u32[]{:S(2)}, u32[]{:S(2)}) collective-permute-start(f32[7,168,128]{2,1,0:T(8,128)S(1)} %get-tuple-element.50), channel_id=1, source_target_pairs={{0,8},{8,16},{16,24},{24,32},{32,40},{40,48},{48,56},{56,64},{64,7... | collective-permute-start | bytes 1806344 | tf_op jit(solution)/shard_map/ppermute | solution.py:429
  20.6 1.3 collective-permute-start.3
  21.9 25.8 %all_to_all.5.slots = f32[128,2,128]{2,1,0:T(2,128)S(1)} all-to-all(f32[128,2,128]{2,1,0:T(2,128)S(1)} %place_slots.1), channel_id=1, replica_groups=mesh['gx_0'=4,'gx_1'=4,'gy_0'=4,'gy_1'=2] {'gx_0','gx_1','gy_0','gy_1'}, dimensions={0} | all-to-all | bytes 262144 | tf_op jit(solution)/shard_map/all_to_all | solution.py:444
  47.7 6.1 %add_currents.1 = (f32[8,128,128]{2,1,0:T(8,128)S(1)}, f32[64,128]{1,0:T(8,128)S(1)}, f32[64,128]{1,0:T(8,128)S(1)}) custom-call(f32[128,2,128]{2,1,0:T(2,128)S(1)} %all_to_all.5.slots, f32[64,64]{1,0:T(8,128)S(1)} %copy-done.5), custom_call_target="tpu_custom_call" | custom-call | tf_op jit(solution)/shard_map/add_currents/pallas_call | solution.py:52
  55.1 1.3 collective-permute-start.5
  56.4 1.8 %collective-permute-done.5.high.i_high = f32[64,128]{1,0:T(8,128)S(1)} collective-permute-done((f32[64,128]{1,0:T(8,128)S(1)}, f32[64,128]{1,0:T(8,128)S(1)}, u32[]{:S(2)}, u32[]{:S(2)}) %collective-permute-start.5) | collective-permute-done | bytes 32800 | tf_op jit(solution)/shard_map/ppermute | solution.py:430
  58.4 3.8 %collective-permute-start.6 = (f32[3,144,128]{2,1,0:T(8,128)S(1)}, f32[3,144,128]{2,1,0:T(8,128)S(1)}, u32[]{:S(2)}, u32[]{:S(2)}) collective-permute-start(f32[3,144,128]{2,1,0:T(8,128)S(1)} %get-tuple-element.61), channel_id=1, source_target_pairs={{0,8},{8,16},{16,24},{24,32},{32,40},{40,48},{48,56},{56,64},{64,7... | collective-permute-start | bytes 663560 | tf_op jit(solution)/shard_map/ppermute | solution.py:429
  63.6 7.2 %grid_weights.1 = (f32[22,144,128]{2,1,0:T(8,128)S(1)}, f32[22,144,128]{2,1,0:T(8,128)S(1)}, f32[22,144,128]{2,1,0:T(8,128)S(1)}, f32[22,144,128]{2,1,0:T(8,128)...) custom-call(f32[8,128,128]{2,1,0:T(8,128)S(1)} %get-tuple-element.40.v, ...), custom_call_target="tpu_custom_call" | custom-call | tf_op jit(solution)/shard_map/grid_weights/pallas_call | solution.py:52
  71.5 6.1 %first_basis.1 = (f32[22,144,128]{2,1,0:T(8,128)S(1)}, f32[22,144,128]{2,1,0:T(8,128)S(1)}, f32[22,144,128]{2,1,0:T(8,128)S(1)}, f32[22,144,128]{2,1,0:T(8,128)S...) custom-call(f32[22,144,128]{2,1,0:T(8,128)S(1)} %get-tuple-element.52.diag, ...), custom_call_target="tpu_custom_call" | custom-call | tf_op jit(solution)/shard_map/first_basis/pallas_call | solution.py:52
  77.6 1.4 collective-permute-start.8
  79.8 1.3 collective-permute-start.11
  81.1 2.4 %collective-permute-start.10 = (f32[64,128]{1,0:T(8,128)S(1)}, f32[64,128]{1,0:T(8,128)S(1)}, u32[]{:S(2)}, u32[]{:S(2)}) collective-permute-start(f32[64,128]{1,0:T(8,128)S(1)} %add.60), channel_id=1, source_target_pairs={{0,4},{2,6},{4,0},{6,2},{1,5},{3,7},{5,1},{7,3},{8,12},{10,14},{12... | collective-permute-start | bytes 98312 | tf_op jit(solution)/shard_map/ppermute | solution.py:437
  84.9 1.6 %collective-permute-done.10 = f32[64,128]{1,0:T(8,128)S(1)} collective-permute-done((f32[64,128]{1,0:T(8,128)S(1)}, f32[64,128]{1,0:T(8,128)S(1)}, u32[]{:S(2)}, u32[]{:S(2)}) %collective-permute-start.10) | collective-permute-done | bytes 32800 | tf_op jit(solution)/shard_map/ppermute | solution.py:437
  87.5 5.6 %collective-permute-start.14 = (f32[64,128]{1,0:T(8,128)S(1)}, f32[64,128]{1,0:T(8,128)S(1)}, u32[]{:S(2)}, u32[]{:S(2)}) collective-permute-start(f32[64,128]{1,0:T(8,128)S(1)} %add_add_fusion.5), channel_id=1, source_target_pairs={{0,24},{8,16},{16,8},{24,0},{1,25},{9,17},{17,9},{25,1},{2,26},{10... | collective-permute-start | bytes 98312 | tf_op jit(solution)/shard_map/ppermute | solution.py:437
  95.0 3.5 %collective-permute-done.13 = f32[64,128]{1,0:T(8,128)S(1)} collective-permute-done((f32[64,128]{1,0:T(8,128)S(1)}, f32[64,128]{1,0:T(8,128)S(1)}, u32[]{:S(2)}, u32[]{:S(2)}) %collective-permute-start.13) | collective-permute-done | bytes 32800 | tf_op jit(solution)/shard_map/ppermute | solution.py:437
  99.7 1.5 %collective-permute-start.16 = (f32[64,128]{1,0:T(8,128)S(1)}, f32[64,128]{1,0:T(8,128)S(1)}, u32[]{:S(2)}, u32[]{:S(2)}) collective-permute-start(f32[64,128]{1,0:T(8,128)S(1)} %add_add_fusion.4), channel_id=1, source_target_pairs={{0,64},{32,96},{64,0},{96,32},{1,65},{33,97},{65,1},{97,33},{2,66}... | collective-permute-start | bytes 98312 | tf_op jit(solution)/shard_map/ppermute | solution.py:437
  101.2 1.6 %collective-permute-start.15 = (f32[64,128]{1,0:T(8,128)S(1)}, f32[64,128]{1,0:T(8,128)S(1)}, u32[]{:S(2)}, u32[]{:S(2)}) collective-permute-start(f32[64,128]{1,0:T(8,128)S(1)} %add_add_fusion.4), channel_id=1, source_target_pairs={{0,32},{32,0},{64,96},{96,64},{1,33},{33,1},{65,97},{97,65},{2,34}... | collective-permute-start | bytes 98312 | tf_op jit(solution)/shard_map/ppermute | solution.py:437
  105.2 8.7 %second_basis.1 = (f32[8,128,128]{2,1,0:T(8,128)S(1)}, f32[8,128,128]{2,1,0:T(8,128)S(1)}, f32[8,128,128]{2,1,0:T(8,128)S(1)}, f32[8,128,128]{2,1,0:T(8,128)S(1)...) custom-call(f32[64,128]{1,0:T(8,128)S(1)} %add_add_fusion.3.gram, f32[22,144,128]{2,1,0:T(8,128)S(1)} %get-tuple-element.52.diag, ...), custom_call_target="tpu_custom_call" | custom-call | tf_op jit(solution)/shard_map/second_basis/pallas_call | solution.py:52
  115.2 1.5 %collective-permute-start.21 = (f32[64,128]{1,0:T(8,128)S(1)}, f32[64,128]{1,0:T(8,128)S(1)}, u32[]{:S(2)}, u32[]{:S(2)}) collective-permute-start(f32[64,128]{1,0:T(8,128)S(1)} %add.70), channel_id=1, source_target_pairs={{0,6},{2,4},{4,2},{6,0},{1,7},{3,5},{5,3},{7,1},{8,14},{10,12},{12... | collective-permute-start | bytes 98312 | tf_op jit(solution)/shard_map/ppermute | solution.py:437
  117.8 1.5 %collective-permute-start.19 = (f32[64,128]{1,0:T(8,128)S(1)}, f32[64,128]{1,0:T(8,128)S(1)}, u32[]{:S(2)}, u32[]{:S(2)}) collective-permute-start(f32[64,128]{1,0:T(8,128)S(1)} %add.70), channel_id=1, source_target_pairs={{0,2},{2,0},{4,6},{6,4},{1,3},{3,1},{5,7},{7,5},{8,10},{10,8},{12,... | collective-permute-start | bytes 98312 | tf_op jit(solution)/shard_map/ppermute | solution.py:437
  120.3 1.8 %collective-permute-done.20 = f32[64,128]{1,0:T(8,128)S(1)} collective-permute-done((f32[64,128]{1,0:T(8,128)S(1)}, f32[64,128]{1,0:T(8,128)S(1)}, u32[]{:S(2)}, u32[]{:S(2)}) %collective-permute-start.20) | collective-permute-done | bytes 32800 | tf_op jit(solution)/shard_map/ppermute | solution.py:437
  122.1 2.3 %collective-permute-start.24 = (f32[64,128]{1,0:T(8,128)S(1)}, f32[64,128]{1,0:T(8,128)S(1)}, u32[]{:S(2)}, u32[]{:S(2)}) collective-permute-start(f32[64,128]{1,0:T(8,128)S(1)} %add_add_fusion.2), channel_id=1, source_target_pairs={{0,24},{8,16},{16,8},{24,0},{1,25},{9,17},{17,9},{25,1},{2,26},{10... | collective-permute-start | bytes 98312 | tf_op jit(solution)/shard_map/ppermute | solution.py:437
  124.4 1.4 %collective-permute-start.23 = (f32[64,128]{1,0:T(8,128)S(1)}, f32[64,128]{1,0:T(8,128)S(1)}, u32[]{:S(2)}, u32[]{:S(2)}) collective-permute-start(f32[64,128]{1,0:T(8,128)S(1)} %add_add_fusion.2), channel_id=1, source_target_pairs={{0,16},{8,24},{16,0},{24,8},{1,17},{9,25},{17,1},{25,9},{2,18},{10... | collective-permute-start | bytes 98312 | tf_op jit(solution)/shard_map/ppermute | solution.py:437
  126.3 1.4 collective-permute-done.24
  127.6 2.2 %collective-permute-done.23 = f32[64,128]{1,0:T(8,128)S(1)} collective-permute-done((f32[64,128]{1,0:T(8,128)S(1)}, f32[64,128]{1,0:T(8,128)S(1)}, u32[]{:S(2)}, u32[]{:S(2)}) %collective-permute-start.23) | collective-permute-done | bytes 32800 | tf_op jit(solution)/shard_map/ppermute | solution.py:437
  129.8 1.5 %collective-permute-start.27 = (f32[64,128]{1,0:T(8,128)S(1)}, f32[64,128]{1,0:T(8,128)S(1)}, u32[]{:S(2)}, u32[]{:S(2)}) collective-permute-start(f32[64,128]{1,0:T(8,128)S(1)} %add_add_fusion.1), channel_id=1, source_target_pairs={{0,96},{32,64},{64,32},{96,0},{1,97},{33,65},{65,33},{97,1},{2,98}... | collective-permute-start | bytes 98312 | tf_op jit(solution)/shard_map/ppermute | solution.py:437
  132.3 1.7 %collective-permute-start.25 = (f32[64,128]{1,0:T(8,128)S(1)}, f32[64,128]{1,0:T(8,128)S(1)}, u32[]{:S(2)}, u32[]{:S(2)}) collective-permute-start(f32[64,128]{1,0:T(8,128)S(1)} %add_add_fusion.1), channel_id=1, source_target_pairs={{0,32},{32,0},{64,96},{96,64},{1,33},{33,1},{65,97},{97,65},{2,34}... | collective-permute-start | bytes 98312 | tf_op jit(solution)/shard_map/ppermute | solution.py:437
  135.0 1.7 %collective-permute-done.26 = f32[64,128]{1,0:T(8,128)S(1)} collective-permute-done((f32[64,128]{1,0:T(8,128)S(1)}, f32[64,128]{1,0:T(8,128)S(1)}, u32[]{:S(2)}, u32[]{:S(2)}) %collective-permute-start.26) | collective-permute-done | bytes 32800 | tf_op jit(solution)/shard_map/ppermute | solution.py:437
  136.7 5.0 %finish.1 = (f32[1024,128]{1,0:T(8,128)}, f32[1024,128]{1,0:T(8,128)}) custom-call(f32[64,128]{1,0:T(8,128)S(1)} %add_add_fusion.gram, f32[8,128,128]{2,1,0:T(8,128)S(1)} %get-tuple-element.71.w0, f32[8,128,128]{2,1,0:T(8,128)S(1)} %get-tuple-element.72.w1, f32[8,128,128]{2,1,0:T(8,128)S(1)} %get-tuple-element.73.w2, ...), custom_call_target="tpu_custom_call" | custom-call | tf_op jit(solution)/shard_map/finish/pallas_call | solution.py:52
  (62 shorter events, 25.9 us)
Async XLA Ops:
  0.6 1.0 copy-start
  1.7 0.8 copy-start.1
  2.4 0.8 copy-start.2
  7.6 40.1 %copy-start.5 = (f32[64,64]{1,0:T(8,128)S(1)}, f32[64,64]{1,0:T(8,128)}, u32[]{:S(2)}) copy-start(f32[64,64]{1,0:T(8,128)} %waves.1) | copy-start | bytes 49156
  8.4 7.9 %collective-permute-start = (f32[128,128]{1,0:T(8,128)S(1)}, f32[128,128]{1,0:T(8,128)S(1)}, u32[]{:S(2)}, u32[]{:S(2)}) collective-permute-start(f32[128,128]{1,0:T(8,128)S(1)} %get-tuple-element.42), channel_id=1, source_target_pairs={{0,1},{1,2},{2,3},{3,4},{4,5},{5,6},{6,7},{8,9},{9,10},{10,11},{11... | collective-permute-start | bytes 196616 | tf_op jit(solution)/shard_map/ppermute | solution.py:429
  9.7 6.6 %collective-permute-start.1 = (f32[128,128]{1,0:T(8,128)S(1)}, f32[128,128]{1,0:T(8,128)S(1)}, u32[]{:S(2)}, u32[]{:S(2)}) collective-permute-start(f32[128,128]{1,0:T(8,128)S(1)} %get-tuple-element.43), channel_id=1, source_target_pairs={{1,0},{2,1},{3,2},{4,3},{5,4},{6,5},{7,6},{9,8},{10,9},{11,10},{12... | collective-permute-start | bytes 196616 | tf_op jit(solution)/shard_map/ppermute | solution.py:430
  16.5 47.1 %collective-permute-start.2 = (f32[7,168,128]{2,1,0:T(8,128)S(1)}, f32[7,168,128]{2,1,0:T(8,128)S(1)}, u32[]{:S(2)}, u32[]{:S(2)}) collective-permute-start(f32[7,168,128]{2,1,0:T(8,128)S(1)} %get-tuple-element.50), channel_id=1, source_target_pairs={{0,8},{8,16},{16,24},{24,32},{32,40},{40,48},{48,56},{56,64},{64,7... | collective-permute-start | bytes 1806344 | tf_op jit(solution)/shard_map/ppermute | solution.py:429
  20.6 43.0 %collective-permute-start.3 = (f32[7,168,128]{2,1,0:T(8,128)S(1)}, f32[7,168,128]{2,1,0:T(8,128)S(1)}, u32[]{:S(2)}, u32[]{:S(2)}) collective-permute-start(f32[7,168,128]{2,1,0:T(8,128)S(1)} %get-tuple-element.51), channel_id=1, source_target_pairs={{8,0},{16,8},{24,16},{32,24},{40,32},{48,40},{56,48},{64,56},{72,6... | collective-permute-start | bytes 1806344 | tf_op jit(solution)/shard_map/ppermute | solution.py:430
  53.8 2.6 %collective-permute-start.4 = (f32[64,128]{1,0:T(8,128)S(1)}, f32[64,128]{1,0:T(8,128)S(1)}, u32[]{:S(2)}, u32[]{:S(2)}) collective-permute-start(f32[64,128]{1,0:T(8,128)S(1)} %get-tuple-element.59), channel_id=1, source_target_pairs={{0,1},{1,2},{2,3},{3,4},{4,5},{5,6},{6,7},{8,9},{9,10},{10,11},{11... | collective-permute-start | bytes 98312 | tf_op jit(solution)/shard_map/ppermute | solution.py:429
  55.1 3.1 %collective-permute-start.5 = (f32[64,128]{1,0:T(8,128)S(1)}, f32[64,128]{1,0:T(8,128)S(1)}, u32[]{:S(2)}, u32[]{:S(2)}) collective-permute-start(f32[64,128]{1,0:T(8,128)S(1)} %get-tuple-element.60), channel_id=1, source_target_pairs={{1,0},{2,1},{3,2},{4,3},{5,4},{6,5},{7,6},{9,8},{10,9},{11,10},{12... | collective-permute-start | bytes 98312 | tf_op jit(solution)/shard_map/ppermute | solution.py:430
  58.4 12.4 %collective-permute-start.6 = (f32[3,144,128]{2,1,0:T(8,128)S(1)}, f32[3,144,128]{2,1,0:T(8,128)S(1)}, u32[]{:S(2)}, u32[]{:S(2)}) collective-permute-start(f32[3,144,128]{2,1,0:T(8,128)S(1)} %get-tuple-element.61), channel_id=1, source_target_pairs={{0,8},{8,16},{16,24},{24,32},{32,40},{40,48},{48,56},{56,64},{64,7... | collective-permute-start | bytes 663560 | tf_op jit(solution)/shard_map/ppermute | solution.py:429
  62.2 9.2 %collective-permute-start.7 = (f32[3,144,128]{2,1,0:T(8,128)S(1)}, f32[3,144,128]{2,1,0:T(8,128)S(1)}, u32[]{:S(2)}, u32[]{:S(2)}) collective-permute-start(f32[3,144,128]{2,1,0:T(8,128)S(1)} %get-tuple-element.62), channel_id=1, source_target_pairs={{8,0},{16,8},{24,16},{32,24},{40,32},{48,40},{56,48},{64,56},{72,6... | collective-permute-start | bytes 663560 | tf_op jit(solution)/shard_map/ppermute | solution.py:430
  77.6 2.2 %collective-permute-start.8 = (f32[64,128]{1,0:T(8,128)S(1)}, f32[64,128]{1,0:T(8,128)S(1)}, u32[]{:S(2)}, u32[]{:S(2)}) collective-permute-start(f32[64,128]{1,0:T(8,128)S(1)} %get-tuple-element.63), channel_id=1, source_target_pairs={{0,1},{1,0},{2,3},{3,2},{4,5},{5,4},{6,7},{7,6},{8,9},{9,8},{10,11... | collective-permute-start | bytes 98312 | tf_op jit(solution)/shard_map/ppermute | solution.py:434
  79.8 5.1 %collective-permute-start.11 = (f32[64,128]{1,0:T(8,128)S(1)}, f32[64,128]{1,0:T(8,128)S(1)}, u32[]{:S(2)}, u32[]{:S(2)}) collective-permute-start(f32[64,128]{1,0:T(8,128)S(1)} %add.60), channel_id=1, source_target_pairs={{0,6},{2,4},{4,2},{6,0},{1,7},{3,5},{5,3},{7,1},{8,14},{10,12},{12... | collective-permute-start | bytes 98312 | tf_op jit(solution)/shard_map/ppermute | solution.py:437
  81.1 5.4 %collective-permute-start.10 = (f32[64,128]{1,0:T(8,128)S(1)}, f32[64,128]{1,0:T(8,128)S(1)}, u32[]{:S(2)}, u32[]{:S(2)}) collective-permute-start(f32[64,128]{1,0:T(8,128)S(1)} %add.60), channel_id=1, source_target_pairs={{0,4},{2,6},{4,0},{6,2},{1,5},{3,7},{5,1},{7,3},{8,12},{10,14},{12... | collective-permute-start | bytes 98312 | tf_op jit(solution)/shard_map/ppermute | solution.py:437
  83.5 3.9 %collective-permute-start.9 = (f32[64,128]{1,0:T(8,128)S(1)}, f32[64,128]{1,0:T(8,128)S(1)}, u32[]{:S(2)}, u32[]{:S(2)}) collective-permute-start(f32[64,128]{1,0:T(8,128)S(1)} %add.60), channel_id=1, source_target_pairs={{0,2},{2,0},{4,6},{6,4},{1,3},{3,1},{5,7},{7,5},{8,10},{10,8},{12,... | collective-permute-start | bytes 98312 | tf_op jit(solution)/shard_map/ppermute | solution.py:437
  87.5 7.5 %collective-permute-start.14 = (f32[64,128]{1,0:T(8,128)S(1)}, f32[64,128]{1,0:T(8,128)S(1)}, u32[]{:S(2)}, u32[]{:S(2)}) collective-permute-start(f32[64,128]{1,0:T(8,128)S(1)} %add_add_fusion.5), channel_id=1, source_target_pairs={{0,24},{8,16},{16,8},{24,0},{1,25},{9,17},{17,9},{25,1},{2,26},{10... | collective-permute-start | bytes 98312 | tf_op jit(solution)/shard_map/ppermute | solution.py:437
  93.1 5.4 %collective-permute-start.13 = (f32[64,128]{1,0:T(8,128)S(1)}, f32[64,128]{1,0:T(8,128)S(1)}, u32[]{:S(2)}, u32[]{:S(2)}) collective-permute-start(f32[64,128]{1,0:T(8,128)S(1)} %add_add_fusion.5), channel_id=1, source_target_pairs={{0,16},{8,24},{16,0},{24,8},{1,17},{9,25},{17,1},{25,9},{2,18},{10... | collective-permute-start | bytes 98312 | tf_op jit(solution)/shard_map/ppermute | solution.py:437
  93.1 5.4 %collective-permute-start.12 = (f32[64,128]{1,0:T(8,128)S(1)}, f32[64,128]{1,0:T(8,128)S(1)}, u32[]{:S(2)}, u32[]{:S(2)}) collective-permute-start(f32[64,128]{1,0:T(8,128)S(1)} %add_add_fusion.5), channel_id=1, source_target_pairs={{0,8},{8,0},{16,24},{24,16},{1,9},{9,1},{17,25},{25,17},{2,10},{10... | collective-permute-start | bytes 98312 | tf_op jit(solution)/shard_map/ppermute | solution.py:437
  98.5 5.4 %collective-permute-start.17 = (f32[64,128]{1,0:T(8,128)S(1)}, f32[64,128]{1,0:T(8,128)S(1)}, u32[]{:S(2)}, u32[]{:S(2)}) collective-permute-start(f32[64,128]{1,0:T(8,128)S(1)} %add_add_fusion.4), channel_id=1, source_target_pairs={{0,96},{32,64},{64,32},{96,0},{1,97},{33,65},{65,33},{97,1},{2,98}... | collective-permute-start | bytes 98312 | tf_op jit(solution)/shard_map/ppermute | solution.py:437
  99.7 5.4 %collective-permute-start.16 = (f32[64,128]{1,0:T(8,128)S(1)}, f32[64,128]{1,0:T(8,128)S(1)}, u32[]{:S(2)}, u32[]{:S(2)}) collective-permute-start(f32[64,128]{1,0:T(8,128)S(1)} %add_add_fusion.4), channel_id=1, source_target_pairs={{0,64},{32,96},{64,0},{96,32},{1,65},{33,97},{65,1},{97,33},{2,66}... | collective-permute-start | bytes 98312 | tf_op jit(solution)/shard_map/ppermute | solution.py:437
  101.2 3.9 %collective-permute-start.15 = (f32[64,128]{1,0:T(8,128)S(1)}, f32[64,128]{1,0:T(8,128)S(1)}, u32[]{:S(2)}, u32[]{:S(2)}) collective-permute-start(f32[64,128]{1,0:T(8,128)S(1)} %add_add_fusion.4), channel_id=1, source_target_pairs={{0,32},{32,0},{64,96},{96,64},{1,33},{33,1},{65,97},{97,65},{2,34}... | collective-permute-start | bytes 98312 | tf_op jit(solution)/shard_map/ppermute | solution.py:437
  113.9 1.3 collective-permute-start.18
  115.2 5.1 %collective-permute-start.21 = (f32[64,128]{1,0:T(8,128)S(1)}, f32[64,128]{1,0:T(8,128)S(1)}, u32[]{:S(2)}, u32[]{:S(2)}) collective-permute-start(f32[64,128]{1,0:T(8,128)S(1)} %add.70), channel_id=1, source_target_pairs={{0,6},{2,4},{4,2},{6,0},{1,7},{3,5},{5,3},{7,1},{8,14},{10,12},{12... | collective-permute-start | bytes 98312 | tf_op jit(solution)/shard_map/ppermute | solution.py:437
  116.7 5.4 %collective-permute-start.20 = (f32[64,128]{1,0:T(8,128)S(1)}, f32[64,128]{1,0:T(8,128)S(1)}, u32[]{:S(2)}, u32[]{:S(2)}) collective-permute-start(f32[64,128]{1,0:T(8,128)S(1)} %add.70), channel_id=1, source_target_pairs={{0,4},{2,6},{4,0},{6,2},{1,5},{3,7},{5,1},{7,3},{8,12},{10,14},{12... | collective-permute-start | bytes 98312 | tf_op jit(solution)/shard_map/ppermute | solution.py:437
  117.8 4.3 %collective-permute-start.19 = (f32[64,128]{1,0:T(8,128)S(1)}, f32[64,128]{1,0:T(8,128)S(1)}, u32[]{:S(2)}, u32[]{:S(2)}) collective-permute-start(f32[64,128]{1,0:T(8,128)S(1)} %add.70), channel_id=1, source_target_pairs={{0,2},{2,0},{4,6},{6,4},{1,3},{3,1},{5,7},{7,5},{8,10},{10,8},{12,... | collective-permute-start | bytes 98312 | tf_op jit(solution)/shard_map/ppermute | solution.py:437
  122.1 5.5 %collective-permute-start.24 = (f32[64,128]{1,0:T(8,128)S(1)}, f32[64,128]{1,0:T(8,128)S(1)}, u32[]{:S(2)}, u32[]{:S(2)}) collective-permute-start(f32[64,128]{1,0:T(8,128)S(1)} %add_add_fusion.2), channel_id=1, source_target_pairs={{0,24},{8,16},{16,8},{24,0},{1,25},{9,17},{17,9},{25,1},{2,26},{10... | collective-permute-start | bytes 98312 | tf_op jit(solution)/shard_map/ppermute | solution.py:437
  124.4 5.4 %collective-permute-start.23 = (f32[64,128]{1,0:T(8,128)S(1)}, f32[64,128]{1,0:T(8,128)S(1)}, u32[]{:S(2)}, u32[]{:S(2)}) collective-permute-start(f32[64,128]{1,0:T(8,128)S(1)} %add_add_fusion.2), channel_id=1, source_target_pairs={{0,16},{8,24},{16,0},{24,8},{1,17},{9,25},{17,1},{25,9},{2,18},{10... | collective-permute-start | bytes 98312 | tf_op jit(solution)/shard_map/ppermute | solution.py:437
  125.8 4.0 %collective-permute-start.22 = (f32[64,128]{1,0:T(8,128)S(1)}, f32[64,128]{1,0:T(8,128)S(1)}, u32[]{:S(2)}, u32[]{:S(2)}) collective-permute-start(f32[64,128]{1,0:T(8,128)S(1)} %add_add_fusion.2), channel_id=1, source_target_pairs={{0,8},{8,0},{16,24},{24,16},{1,9},{9,1},{17,25},{25,17},{2,10},{10... | collective-permute-start | bytes 98312 | tf_op jit(solution)/shard_map/ppermute | solution.py:437
  129.8 5.2 %collective-permute-start.27 = (f32[64,128]{1,0:T(8,128)S(1)}, f32[64,128]{1,0:T(8,128)S(1)}, u32[]{:S(2)}, u32[]{:S(2)}) collective-permute-start(f32[64,128]{1,0:T(8,128)S(1)} %add_add_fusion.1), channel_id=1, source_target_pairs={{0,96},{32,64},{64,32},{96,0},{1,97},{33,65},{65,33},{97,1},{2,98}... | collective-permute-start | bytes 98312 | tf_op jit(solution)/shard_map/ppermute | solution.py:437
  131.3 5.4 %collective-permute-start.26 = (f32[64,128]{1,0:T(8,128)S(1)}, f32[64,128]{1,0:T(8,128)S(1)}, u32[]{:S(2)}, u32[]{:S(2)}) collective-permute-start(f32[64,128]{1,0:T(8,128)S(1)} %add_add_fusion.1), channel_id=1, source_target_pairs={{0,64},{32,96},{64,0},{96,32},{1,65},{33,97},{65,1},{97,33},{2,66}... | collective-permute-start | bytes 98312 | tf_op jit(solution)/shard_map/ppermute | solution.py:437
  132.3 4.4 %collective-permute-start.25 = (f32[64,128]{1,0:T(8,128)S(1)}, f32[64,128]{1,0:T(8,128)S(1)}, u32[]{:S(2)}, u32[]{:S(2)}) collective-permute-start(f32[64,128]{1,0:T(8,128)S(1)} %add_add_fusion.1), channel_id=1, source_target_pairs={{0,32},{32,0},{64,96},{96,64},{1,33},{33,1},{65,97},{97,65},{2,34}... | collective-permute-start | bytes 98312 | tf_op jit(solution)/shard_map/ppermute | solution.py:437
  (6 other events, 4.4 us)

commit v4 on v3

--- a/solution.py
+++ b/solution.py
@@ -59,19 +59,7 @@
     )(*args)
 
 
-def to_lanes(
-    volts_in, cap, cond_x, cond_y, via, tile_in, cell_in, wave_in, amp_in,
-    v_out, c_out, low_out, high_out, tile, cell, wave, amp, volts, stack, sems,
-):
-    pairs = [(volts_in, volts)]
-    for c, ref in enumerate((cap, cond_x, cond_y, via)):
-        pairs.append((ref, stack.at[pl.ds(c * 32, 32), :]))
-    pairs += [(tile_in, tile), (cell_in, cell), (wave_in, wave), (amp_in, amp)]
-    copies = [pltpu.make_async_copy(src, dst, sems.at[n]) for n, (src, dst) in enumerate(pairs)]
-    for copy in copies:
-        copy.start()
-    for copy in copies:
-        copy.wait()
+def to_lanes(volts, stack, v_out, c_out, low_out, high_out):
     for x in range(8):
         rows = [volts[pl.ds(l * 8 + x, 32, stride=32), :] for l in range(4)]
         field = jnp.concatenate(rows, axis=0).T
@@ -104,7 +92,7 @@
             last_out[x - 1] = row
 
 
-def place_slots(tile, cell, wave, amp, out, acc):
+def place_slots(codes, amps, out, acc):
     acc[...] = jnp.zeros_like(acc)
     lane = iota((128, 256), 1)
     before = ((iota((128, 256), 0) < lane) | (lane >= 128)).astype(F32).astype(BF16)
@@ -112,10 +100,10 @@
 
     def chunk(turn, seen):
         at = pl.ds(pl.multiple_of(turn * 8, 8), 8)
-        tiles = tile[at, :]
-        code = cell[at, :] * 64 + wave[at, :]
-        parts = list(split2(amp[at, :]))
-        parts.append((code >> 8).astype(F32).astype(BF16))
+        code = codes[at, :]
+        tiles = code >> 16
+        parts = list(split2(amps[at, :]))
+        parts.append(((code >> 8) & 255).astype(F32).astype(BF16))
         parts.append((code & 255).astype(F32).astype(BF16))
         hits = [
             (tile_line == tiles[j : j + 1, :]).astype(F32) for j in range(8)
@@ -200,38 +188,49 @@
         dst[i] = apply_row(src, i, *weights)
         return carry
 
-    lax.fori_loop(first, last + 1, row, 0, unroll=2)
+    lax.fori_loop(first, last + 1, row, 0, unroll=4)
 
 
 def moments(fields, out, first):
     own = [f[first : first + 8, 8:136, :].reshape(1024, 128) for f in fields]
-    lane = iota((32, 128), 1)
-    blocks = [jnp.zeros((32, 128), F32), jnp.zeros((32, 128), F32)]
+    lane, row = iota((32, 128), 1), iota((32, 128), 0)
+    packed = jnp.zeros((32, 128), F32)
     for k in range(3):
         pair = jnp.concatenate([own[k], own[k + 1]], axis=1)
         product = dot_split(own[k], pair, ((0,), (0,)))
+        column = lane - 32 * k
+        totals = []
         for b in range(2):
-            n = 2 * k + b
-            place = 32 * (n % 4)
             total = jnp.zeros((32, 128), F32)
             for l in range(4):
                 piece = product[l * 32 : (l + 1) * 32, b * 128 : (b + 1) * 128]
-                turn = (place - 32 * l) % 128
+                turn = (32 * (k - l)) % 128
                 total = total + (pltpu.roll(piece, turn, 1) if turn else piece)
-            inside = (lane >= place) & (lane < place + 32)
-            blocks[n // 4] = blocks[n // 4] + jnp.where(inside, total, 0.0)
-    out[0:32, :] = blocks[0]
-    out[32:64, :] = blocks[1]
+            totals.append(total)
+        even, odd = totals
+        inside = (column >= 0) & (column < 32)
+        packed = packed + jnp.where(inside, jnp.where(column > row, even, odd), 0.0)
+        diagonal = jnp.sum(jnp.where(column == row, even, 0.0), axis=1, keepdims=True)
+        packed = packed + jnp.where(lane == 96 + k, diagonal, 0.0)
+    out[...] = packed
 
 
 def coefficients(gram):
-    lane = iota((32, 128), 1)
+    lane, row = iota((32, 128), 1), iota((32, 128), 0)
+    packed = gram[...]
+    flipped = jnp.concatenate([packed, jnp.zeros((96, 128), F32)], axis=0).T
+    bases = []
+    for k in range(3):
+        direct = pltpu.roll(packed, 128 - 32 * k, 1) if k else packed
+        mirror = flipped[k * 32 : (k + 1) * 32, :]
+        even = jnp.where(lane > row, direct, mirror)
+        even = jnp.where(lane == row, packed[:, 96 + k : 97 + k], even)
+        bases.append(jnp.where(lane < 32, even, 0.0))
+        odd = jnp.where(lane > row, mirror, direct)
+        bases.append(jnp.where(lane < 32, odd, 0.0))
 
     def moment(k, place):
-        block = gram[(k // 4) * 32 : (k // 4) * 32 + 32, :]
-        turn = (place - 32 * (k % 4)) % 128
-        block = pltpu.roll(block, turn, 1) if turn else block
-        return jnp.where((lane >= place) & (lane < place + 32), block, 0.0)
+        return pltpu.roll(bases[k], place, 1) if place else bases[k]
 
     tiles = []
     for i in range(3):
@@ -446,18 +445,17 @@
 
 def body(volts, cap, cond_x, cond_y, via, waveforms, placement, cells, wave_ids, amps):
     vmem = pltpu.VMEM
-    coefs = [a.reshape(32, 128) for a in (cap, cond_x, cond_y, via)]
-    lists = [a.reshape(64, 128) for a in (placement, cells, wave_ids, amps)]
-    v, c, y_low, y_high, *lists = call(
+    coefs = jnp.concatenate([a.reshape(32, 128) for a in (cap, cond_x, cond_y, via)], axis=0)
+    v, c, y_low, y_high = call(
         to_lanes,
-        [(8, 128, 128), (8, 128, 128), (128, 128), (128, 128)]
-        + [jax.ShapeDtypeStruct(a.shape, a.dtype) for a in lists],
-        [volts.reshape(1024, 128)] + coefs + lists,
-        [vmem((1024, 128), F32), vmem((128, 128), F32), pltpu.SemaphoreType.DMA((9,))],
-        in_specs=[pl.BlockSpec(memory_space=pl.ANY)] * 9,
+        [(8, 128, 128), (8, 128, 128), (128, 128), (128, 128)],
+        [volts.reshape(1024, 128), coefs],
     )
     y_low, y_high = neighbours(y_low, y_high, GY)
-    (slots,) = call(place_slots, [(128, 2, 128)], lists, [vmem((512, 128), F32)])
+    codes = (placement.reshape(-1) * 65536 + cells * 64 + wave_ids).reshape(64, 128)
+    (slots,) = call(
+        place_slots, [(128, 2, 128)], [codes, amps.reshape(64, 128)], [vmem((512, 128), F32)]
+    )
     y_low, y_high, slots = lax.optimization_barrier((y_low, y_high, slots))
     x_low, x_high = call(pack_rows, [(7, 168, 128)] * 2, [v, c, y_low, y_high])
     x_low, x_high = neighbours(x_low, x_high, GX)
@@ -477,13 +475,13 @@
     )
     *kept, gram = call(
         first_basis,
-        [wide] * 5 + [(64, 128)],
+        [wide] * 5 + [(32, 128)],
         [diag, wx, wy, wv, free, inj, i_low, i_high, ix_low, ix_high],
     )
     own = (8, 128, 128)
     *basis, gram = call(
         second_basis,
-        [own] * 5 + [(64, 128)],
+        [own] * 5 + [(32, 128)],
         [everywhere(gram), diag, wx, wy, wv, cap] + kept + [v],
         [vmem(wide, F32)] * 5,
     )

time: 143 us -> 137 us (0.958)
  local copies, waits for them, and re-layouts: 6.94 us -> 1.8 us
  other arithmetic: 0.07 us -> 2.41 us
    unnamed x20 -> x6, local copies, waits for them, and re-layouts: 6.94 us -> 1.8 us
  transfers between devices with their start and end apart: 28 -> 28, of which waited for: 17 -> 18; matrix products, arithmetic and copies ran while one was open for 0% -> 1% of each run, Pallas kernels for 13% -> 14%
where the time goes in v4:
time: 137 us
  starting transfers between devices  44.3 us (32%)
  Pallas kernels  38.8 us (28%)
  blocking collectives  25.8 us (19%)
  waiting for transfers between devices  22.8 us (17%)
  other arithmetic  2.41 us (2%)
  local copies, waits for them, and re-layouts  1.8 us (1%)
    pallas_call x9, Pallas kernels, call(): pl.pallas_call(kernel, out_shape=tuple(outs), scratch_shapes=list(scratch...  38.8 us
    ppermute x18, starting transfers between devices, everywhere(): lax.ppermute(x, axis, [(i, i ^ k) for i in range(4)])  27.2 us
    all_to_all x1, blocking collectives, exchange(): return lax.all_to_all(slots, GX_GY, split_axis=0, concat_axis=0, tiled=True)  25.8 us
    ppermute x18, waiting for transfers between devices, everywhere(): lax.ppermute(x, axis, [(i, i ^ k) for i in range(4)])  18.3 us
    ppermute x4, starting transfers between devices, neighbours(): from_low = lax.ppermute(to_high, axis, up)  10.5 us
    ppermute x4, starting transfers between devices, neighbours(): return (from_low, lax.ppermute(to_low, axis, [(b, a) for a, b in up]))  5.17 us
  transfers between devices with their start and end apart: 28, of which 18 were waited for; matrix products, arithmetic and copies ran while one was open for 1% of the time, Pallas kernels for 14%

profile of v4, /device:TPU:0, one launch (start us, length us, event | category | flops | bytes accessed | tf_op | source)
XLA Modules:
  0.0 136.9 jit_solution(6248407194351771066)
XLA Ops:
  4.1 1.3 collective-permute-start.1
  7.8 5.3 %place_slots.1 = f32[128,2,128]{2,1,0:T(2,128)S(1)} custom-call(s32[64,128]{1,0:T(8,128)S(1)} %add_bitcast_fusion.codes, f32[64,128]{1,0:T(8,128)S(1)} %bitcast.12), custom_call_target="tpu_custom_call" | custom-call | tf_op jit(solution)/shard_map/place_slots/pallas_call | solution.py:52
  13.3 4.1 %collective-permute-start.2 = (f32[7,168,128]{2,1,0:T(8,128)S(1)}, f32[7,168,128]{2,1,0:T(8,128)S(1)}, u32[]{:S(2)}, u32[]{:S(2)}) collective-permute-start(f32[7,168,128]{2,1,0:T(8,128)S(1)} %get-tuple-element.42), channel_id=1, source_target_pairs={{0,8},{8,16},{16,24},{24,32},{32,40},{40,48},{48,56},{56,64},{64,7... | collective-permute-start | bytes 1806344 | tf_op jit(solution)/shard_map/ppermute | solution.py:428
  17.4 1.3 collective-permute-start.3
  18.7 25.8 %all_to_all.5.slots = f32[128,2,128]{2,1,0:T(2,128)S(1)} all-to-all(f32[128,2,128]{2,1,0:T(2,128)S(1)} %place_slots.1), channel_id=1, replica_groups=mesh['gx_0'=4,'gx_1'=4,'gy_0'=4,'gy_1'=2] {'gx_0','gx_1','gy_0','gy_1'}, dimensions={0} | all-to-all | bytes 262144 | tf_op jit(solution)/shard_map/all_to_all | solution.py:443
  44.5 6.1 %add_currents.1 = (f32[8,128,128]{2,1,0:T(8,128)S(1)}, f32[64,128]{1,0:T(8,128)S(1)}, f32[64,128]{1,0:T(8,128)S(1)}) custom-call(f32[128,2,128]{2,1,0:T(2,128)S(1)} %all_to_all.5.slots, f32[64,64]{1,0:T(8,128)S(1)} %copy-done.1), custom_call_target="tpu_custom_call" | custom-call | tf_op jit(solution)/shard_map/add_currents/pallas_call | solution.py:52
  50.7 1.3 collective-permute-start.4
  52.0 1.3 collective-permute-start.5
  53.3 1.8 %collective-permute-done.5.high.i_high = f32[64,128]{1,0:T(8,128)S(1)} collective-permute-done((f32[64,128]{1,0:T(8,128)S(1)}, f32[64,128]{1,0:T(8,128)S(1)}, u32[]{:S(2)}, u32[]{:S(2)}) %collective-permute-start.5) | collective-permute-done | bytes 32800 | tf_op jit(solution)/shard_map/ppermute | solution.py:429
  55.2 3.9 %collective-permute-start.6 = (f32[3,144,128]{2,1,0:T(8,128)S(1)}, f32[3,144,128]{2,1,0:T(8,128)S(1)}, u32[]{:S(2)}, u32[]{:S(2)}) collective-permute-start(f32[3,144,128]{2,1,0:T(8,128)S(1)} %get-tuple-element.53), channel_id=1, source_target_pairs={{0,8},{8,16},{16,24},{24,32},{32,40},{40,48},{48,56},{56,64},{64,7... | collective-permute-start | bytes 663560 | tf_op jit(solution)/shard_map/ppermute | solution.py:428
  59.1 1.3 collective-permute-start.7
  60.4 7.2 %grid_weights.1 = (f32[22,144,128]{2,1,0:T(8,128)S(1)}, f32[22,144,128]{2,1,0:T(8,128)S(1)}, f32[22,144,128]{2,1,0:T(8,128)S(1)}, f32[22,144,128]{2,1,0:T(8,128)...) custom-call(f32[8,128,128]{2,1,0:T(8,128)S(1)} %get-tuple-element.36.v, ...), custom_call_target="tpu_custom_call" | custom-call | tf_op jit(solution)/shard_map/grid_weights/pallas_call | solution.py:52
  68.3 5.7 %first_basis.1 = (f32[22,144,128]{2,1,0:T(8,128)S(1)}, f32[22,144,128]{2,1,0:T(8,128)S(1)}, f32[22,144,128]{2,1,0:T(8,128)S(1)}, f32[22,144,128]{2,1,0:T(8,128)S...) custom-call(f32[22,144,128]{2,1,0:T(8,128)S(1)} %get-tuple-element.44.diag, ...), custom_call_target="tpu_custom_call" | custom-call | tf_op jit(solution)/shard_map/first_basis/pallas_call | solution.py:52
  74.0 1.3 collective-permute-start.8
  76.2 1.3 collective-permute-start.11
  77.5 2.4 %collective-permute-start.10 = (f32[32,128]{1,0:T(8,128)S(1)}, f32[32,128]{1,0:T(8,128)S(1)}, u32[]{:S(2)}, u32[]{:S(2)}) collective-permute-start(f32[32,128]{1,0:T(8,128)S(1)} %add.68), channel_id=1, source_target_pairs={{0,4},{2,6},{4,0},{6,2},{1,5},{3,7},{5,1},{7,3},{8,12},{10,14},{12... | collective-permute-start | bytes 49160 | tf_op jit(solution)/shard_map/ppermute | solution.py:436
  81.1 1.6 %collective-permute-done.10 = f32[32,128]{1,0:T(8,128)S(1)} collective-permute-done((f32[32,128]{1,0:T(8,128)S(1)}, f32[32,128]{1,0:T(8,128)S(1)}, u32[]{:S(2)}, u32[]{:S(2)}) %collective-permute-start.10) | collective-permute-done | bytes 16416 | tf_op jit(solution)/shard_map/ppermute | solution.py:436
  83.7 5.6 %collective-permute-start.14 = (f32[32,128]{1,0:T(8,128)S(1)}, f32[32,128]{1,0:T(8,128)S(1)}, u32[]{:S(2)}, u32[]{:S(2)}) collective-permute-start(f32[32,128]{1,0:T(8,128)S(1)} %add_add_fusion.5), channel_id=1, source_target_pairs={{0,24},{8,16},{16,8},{24,0},{1,25},{9,17},{17,9},{25,1},{2,26},{10... | collective-permute-start | bytes 49160 | tf_op jit(solution)/shard_map/ppermute | solution.py:436
  91.0 3.5 %collective-permute-done.13 = f32[32,128]{1,0:T(8,128)S(1)} collective-permute-done((f32[32,128]{1,0:T(8,128)S(1)}, f32[32,128]{1,0:T(8,128)S(1)}, u32[]{:S(2)}, u32[]{:S(2)}) %collective-permute-start.13) | collective-permute-done | bytes 16416 | tf_op jit(solution)/shard_map/ppermute | solution.py:436
  95.4 1.6 %collective-permute-start.16 = (f32[32,128]{1,0:T(8,128)S(1)}, f32[32,128]{1,0:T(8,128)S(1)}, u32[]{:S(2)}, u32[]{:S(2)}) collective-permute-start(f32[32,128]{1,0:T(8,128)S(1)} %add_add_fusion.4), channel_id=1, source_target_pairs={{0,64},{32,96},{64,0},{96,32},{1,65},{33,97},{65,1},{97,33},{2,66}... | collective-permute-start | bytes 49160 | tf_op jit(solution)/shard_map/ppermute | solution.py:436
  96.9 1.8 %collective-permute-start.15 = (f32[32,128]{1,0:T(8,128)S(1)}, f32[32,128]{1,0:T(8,128)S(1)}, u32[]{:S(2)}, u32[]{:S(2)}) collective-permute-start(f32[32,128]{1,0:T(8,128)S(1)} %add_add_fusion.4), channel_id=1, source_target_pairs={{0,32},{32,0},{64,96},{96,64},{1,33},{33,1},{65,97},{97,65},{2,34}... | collective-permute-start | bytes 49160 | tf_op jit(solution)/shard_map/ppermute | solution.py:436
  100.7 8.6 %second_basis.1 = (f32[8,128,128]{2,1,0:T(8,128)S(1)}, f32[8,128,128]{2,1,0:T(8,128)S(1)}, f32[8,128,128]{2,1,0:T(8,128)S(1)}, f32[8,128,128]{2,1,0:T(8,128)S(1)...) custom-call(f32[32,128]{1,0:T(8,128)S(1)} %add_add_fusion.3.gram, f32[22,144,128]{2,1,0:T(8,128)S(1)} %get-tuple-element.44.diag, ...), custom_call_target="tpu_custom_call" | custom-call | tf_op jit(solution)/shard_map/second_basis/pallas_call | solution.py:52
  110.6 1.7 %collective-permute-start.21 = (f32[32,128]{1,0:T(8,128)S(1)}, f32[32,128]{1,0:T(8,128)S(1)}, u32[]{:S(2)}, u32[]{:S(2)}) collective-permute-start(f32[32,128]{1,0:T(8,128)S(1)} %add.78), channel_id=1, source_target_pairs={{0,6},{2,4},{4,2},{6,0},{1,7},{3,5},{5,3},{7,1},{8,14},{10,12},{12... | collective-permute-start | bytes 49160 | tf_op jit(solution)/shard_map/ppermute | solution.py:436
  113.2 1.5 %collective-permute-start.19 = (f32[32,128]{1,0:T(8,128)S(1)}, f32[32,128]{1,0:T(8,128)S(1)}, u32[]{:S(2)}, u32[]{:S(2)}) collective-permute-start(f32[32,128]{1,0:T(8,128)S(1)} %add.78), channel_id=1, source_target_pairs={{0,2},{2,0},{4,6},{6,4},{1,3},{3,1},{5,7},{7,5},{8,10},{10,8},{12,... | collective-permute-start | bytes 49160 | tf_op jit(solution)/shard_map/ppermute | solution.py:436
  115.5 1.9 %collective-permute-done.20 = f32[32,128]{1,0:T(8,128)S(1)} collective-permute-done((f32[32,128]{1,0:T(8,128)S(1)}, f32[32,128]{1,0:T(8,128)S(1)}, u32[]{:S(2)}, u32[]{:S(2)}) %collective-permute-start.20) | collective-permute-done | bytes 16416 | tf_op jit(solution)/shard_map/ppermute | solution.py:436
  117.5 2.3 %collective-permute-start.24 = (f32[32,128]{1,0:T(8,128)S(1)}, f32[32,128]{1,0:T(8,128)S(1)}, u32[]{:S(2)}, u32[]{:S(2)}) collective-permute-start(f32[32,128]{1,0:T(8,128)S(1)} %add_add_fusion.2), channel_id=1, source_target_pairs={{0,24},{8,16},{16,8},{24,0},{1,25},{9,17},{17,9},{25,1},{2,26},{10... | collective-permute-start | bytes 49160 | tf_op jit(solution)/shard_map/ppermute | solution.py:436
  119.8 1.4 %collective-permute-start.23 = (f32[32,128]{1,0:T(8,128)S(1)}, f32[32,128]{1,0:T(8,128)S(1)}, u32[]{:S(2)}, u32[]{:S(2)}) collective-permute-start(f32[32,128]{1,0:T(8,128)S(1)} %add_add_fusion.2), channel_id=1, source_target_pairs={{0,16},{8,24},{16,0},{24,8},{1,17},{9,25},{17,1},{25,9},{2,18},{10... | collective-permute-start | bytes 49160 | tf_op jit(solution)/shard_map/ppermute | solution.py:436
  122.7 2.3 %collective-permute-done.23 = f32[32,128]{1,0:T(8,128)S(1)} collective-permute-done((f32[32,128]{1,0:T(8,128)S(1)}, f32[32,128]{1,0:T(8,128)S(1)}, u32[]{:S(2)}, u32[]{:S(2)}) %collective-permute-start.23) | collective-permute-done | bytes 16416 | tf_op jit(solution)/shard_map/ppermute | solution.py:436
  125.0 1.4 %collective-permute-start.27 = (f32[32,128]{1,0:T(8,128)S(1)}, f32[32,128]{1,0:T(8,128)S(1)}, u32[]{:S(2)}, u32[]{:S(2)}) collective-permute-start(f32[32,128]{1,0:T(8,128)S(1)} %add_add_fusion.1), channel_id=1, source_target_pairs={{0,96},{32,64},{64,32},{96,0},{1,97},{33,65},{65,33},{97,1},{2,98}... | collective-permute-start | bytes 49160 | tf_op jit(solution)/shard_map/ppermute | solution.py:436
  127.4 1.8 %collective-permute-start.25 = (f32[32,128]{1,0:T(8,128)S(1)}, f32[32,128]{1,0:T(8,128)S(1)}, u32[]{:S(2)}, u32[]{:S(2)}) collective-permute-start(f32[32,128]{1,0:T(8,128)S(1)} %add_add_fusion.1), channel_id=1, source_target_pairs={{0,32},{32,0},{64,96},{96,64},{1,33},{33,1},{65,97},{97,65},{2,34}... | collective-permute-start | bytes 49160 | tf_op jit(solution)/shard_map/ppermute | solution.py:436
  130.1 1.7 %collective-permute-done.26 = f32[32,128]{1,0:T(8,128)S(1)} collective-permute-done((f32[32,128]{1,0:T(8,128)S(1)}, f32[32,128]{1,0:T(8,128)S(1)}, u32[]{:S(2)}, u32[]{:S(2)}) %collective-permute-start.26) | collective-permute-done | bytes 16416 | tf_op jit(solution)/shard_map/ppermute | solution.py:436
  131.7 5.1 %finish.1 = (f32[1024,128]{1,0:T(8,128)}, f32[1024,128]{1,0:T(8,128)}) custom-call(f32[32,128]{1,0:T(8,128)S(1)} %add_add_fusion.gram, f32[8,128,128]{2,1,0:T(8,128)S(1)} %get-tuple-element.63.w0, f32[8,128,128]{2,1,0:T(8,128)S(1)} %get-tuple-element.64.w1, f32[8,128,128]{2,1,0:T(8,128)S(1)} %get-tuple-element.65.w2, ...), custom_call_target="tpu_custom_call" | custom-call | tf_op jit(solution)/shard_map/finish/pallas_call | solution.py:52
  (51 shorter events, 20.8 us)
Async XLA Ops:
  0.6 43.9 %copy-start.1 = (f32[64,64]{1,0:T(8,128)S(1)}, f32[64,64]{1,0:T(8,128)}, u32[]{:S(2)}) copy-start(f32[64,64]{1,0:T(8,128)} %waves.1) | copy-start | bytes 49156
  1.4 1.0 copy-start
  2.9 10.2 %collective-permute-start = (f32[128,128]{1,0:T(8,128)S(1)}, f32[128,128]{1,0:T(8,128)S(1)}, u32[]{:S(2)}, u32[]{:S(2)}) collective-permute-start(f32[128,128]{1,0:T(8,128)S(1)} %get-tuple-element.38), channel_id=1, source_target_pairs={{0,1},{1,2},{2,3},{3,4},{4,5},{5,6},{6,7},{8,9},{9,10},{10,11},{11... | collective-permute-start | bytes 196616 | tf_op jit(solution)/shard_map/ppermute | solution.py:428
  4.1 8.9 %collective-permute-start.1 = (f32[128,128]{1,0:T(8,128)S(1)}, f32[128,128]{1,0:T(8,128)S(1)}, u32[]{:S(2)}, u32[]{:S(2)}) collective-permute-start(f32[128,128]{1,0:T(8,128)S(1)} %get-tuple-element.39), channel_id=1, source_target_pairs={{1,0},{2,1},{3,2},{4,3},{5,4},{6,5},{7,6},{9,8},{10,9},{11,10},{12... | collective-permute-start | bytes 196616 | tf_op jit(solution)/shard_map/ppermute | solution.py:429
  7.0 0.8 copy-start.2
  13.3 47.1 %collective-permute-start.2 = (f32[7,168,128]{2,1,0:T(8,128)S(1)}, f32[7,168,128]{2,1,0:T(8,128)S(1)}, u32[]{:S(2)}, u32[]{:S(2)}) collective-permute-start(f32[7,168,128]{2,1,0:T(8,128)S(1)} %get-tuple-element.42), channel_id=1, source_target_pairs={{0,8},{8,16},{16,24},{24,32},{32,40},{40,48},{48,56},{56,64},{64,7... | collective-permute-start | bytes 1806344 | tf_op jit(solution)/shard_map/ppermute | solution.py:428
  17.4 43.0 %collective-permute-start.3 = (f32[7,168,128]{2,1,0:T(8,128)S(1)}, f32[7,168,128]{2,1,0:T(8,128)S(1)}, u32[]{:S(2)}, u32[]{:S(2)}) collective-permute-start(f32[7,168,128]{2,1,0:T(8,128)S(1)} %get-tuple-element.43), channel_id=1, source_target_pairs={{8,0},{16,8},{24,16},{32,24},{40,32},{48,40},{56,48},{64,56},{72,6... | collective-permute-start | bytes 1806344 | tf_op jit(solution)/shard_map/ppermute | solution.py:429
  50.7 2.6 %collective-permute-start.4 = (f32[64,128]{1,0:T(8,128)S(1)}, f32[64,128]{1,0:T(8,128)S(1)}, u32[]{:S(2)}, u32[]{:S(2)}) collective-permute-start(f32[64,128]{1,0:T(8,128)S(1)} %get-tuple-element.51), channel_id=1, source_target_pairs={{0,1},{1,2},{2,3},{3,4},{4,5},{5,6},{6,7},{8,9},{9,10},{10,11},{11... | collective-permute-start | bytes 98312 | tf_op jit(solution)/shard_map/ppermute | solution.py:428
  52.0 3.1 %collective-permute-start.5 = (f32[64,128]{1,0:T(8,128)S(1)}, f32[64,128]{1,0:T(8,128)S(1)}, u32[]{:S(2)}, u32[]{:S(2)}) collective-permute-start(f32[64,128]{1,0:T(8,128)S(1)} %get-tuple-element.52), channel_id=1, source_target_pairs={{1,0},{2,1},{3,2},{4,3},{5,4},{6,5},{7,6},{9,8},{10,9},{11,10},{12... | collective-permute-start | bytes 98312 | tf_op jit(solution)/shard_map/ppermute | solution.py:429
  55.2 12.4 %collective-permute-start.6 = (f32[3,144,128]{2,1,0:T(8,128)S(1)}, f32[3,144,128]{2,1,0:T(8,128)S(1)}, u32[]{:S(2)}, u32[]{:S(2)}) collective-permute-start(f32[3,144,128]{2,1,0:T(8,128)S(1)} %get-tuple-element.53), channel_id=1, source_target_pairs={{0,8},{8,16},{16,24},{24,32},{32,40},{40,48},{48,56},{56,64},{64,7... | collective-permute-start | bytes 663560 | tf_op jit(solution)/shard_map/ppermute | solution.py:428
  59.1 9.3 %collective-permute-start.7 = (f32[3,144,128]{2,1,0:T(8,128)S(1)}, f32[3,144,128]{2,1,0:T(8,128)S(1)}, u32[]{:S(2)}, u32[]{:S(2)}) collective-permute-start(f32[3,144,128]{2,1,0:T(8,128)S(1)} %get-tuple-element.54), channel_id=1, source_target_pairs={{8,0},{16,8},{24,16},{32,24},{40,32},{48,40},{56,48},{64,56},{72,6... | collective-permute-start | bytes 663560 | tf_op jit(solution)/shard_map/ppermute | solution.py:429
  74.0 2.2 %collective-permute-start.8 = (f32[32,128]{1,0:T(8,128)S(1)}, f32[32,128]{1,0:T(8,128)S(1)}, u32[]{:S(2)}, u32[]{:S(2)}) collective-permute-start(f32[32,128]{1,0:T(8,128)S(1)} %get-tuple-element.55), channel_id=1, source_target_pairs={{0,1},{1,0},{2,3},{3,2},{4,5},{5,4},{6,7},{7,6},{8,9},{9,8},{10,11... | collective-permute-start | bytes 49160 | tf_op jit(solution)/shard_map/ppermute | solution.py:433
  76.2 4.9 %collective-permute-start.11 = (f32[32,128]{1,0:T(8,128)S(1)}, f32[32,128]{1,0:T(8,128)S(1)}, u32[]{:S(2)}, u32[]{:S(2)}) collective-permute-start(f32[32,128]{1,0:T(8,128)S(1)} %add.68), channel_id=1, source_target_pairs={{0,6},{2,4},{4,2},{6,0},{1,7},{3,5},{5,3},{7,1},{8,14},{10,12},{12... | collective-permute-start | bytes 49160 | tf_op jit(solution)/shard_map/ppermute | solution.py:436
  77.5 5.2 %collective-permute-start.10 = (f32[32,128]{1,0:T(8,128)S(1)}, f32[32,128]{1,0:T(8,128)S(1)}, u32[]{:S(2)}, u32[]{:S(2)}) collective-permute-start(f32[32,128]{1,0:T(8,128)S(1)} %add.68), channel_id=1, source_target_pairs={{0,4},{2,6},{4,0},{6,2},{1,5},{3,7},{5,1},{7,3},{8,12},{10,14},{12... | collective-permute-start | bytes 49160 | tf_op jit(solution)/shard_map/ppermute | solution.py:436
  79.9 3.7 %collective-permute-start.9 = (f32[32,128]{1,0:T(8,128)S(1)}, f32[32,128]{1,0:T(8,128)S(1)}, u32[]{:S(2)}, u32[]{:S(2)}) collective-permute-start(f32[32,128]{1,0:T(8,128)S(1)} %add.68), channel_id=1, source_target_pairs={{0,2},{2,0},{4,6},{6,4},{1,3},{3,1},{5,7},{7,5},{8,10},{10,8},{12,... | collective-permute-start | bytes 49160 | tf_op jit(solution)/shard_map/ppermute | solution.py:436
  83.7 7.3 %collective-permute-start.14 = (f32[32,128]{1,0:T(8,128)S(1)}, f32[32,128]{1,0:T(8,128)S(1)}, u32[]{:S(2)}, u32[]{:S(2)}) collective-permute-start(f32[32,128]{1,0:T(8,128)S(1)} %add_add_fusion.5), channel_id=1, source_target_pairs={{0,24},{8,16},{16,8},{24,0},{1,25},{9,17},{17,9},{25,1},{2,26},{10... | collective-permute-start | bytes 49160 | tf_op jit(solution)/shard_map/ppermute | solution.py:436
  89.3 5.2 %collective-permute-start.13 = (f32[32,128]{1,0:T(8,128)S(1)}, f32[32,128]{1,0:T(8,128)S(1)}, u32[]{:S(2)}, u32[]{:S(2)}) collective-permute-start(f32[32,128]{1,0:T(8,128)S(1)} %add_add_fusion.5), channel_id=1, source_target_pairs={{0,16},{8,24},{16,0},{24,8},{1,17},{9,25},{17,1},{25,9},{2,18},{10... | collective-permute-start | bytes 49160 | tf_op jit(solution)/shard_map/ppermute | solution.py:436
  89.3 5.2 %collective-permute-start.12 = (f32[32,128]{1,0:T(8,128)S(1)}, f32[32,128]{1,0:T(8,128)S(1)}, u32[]{:S(2)}, u32[]{:S(2)}) collective-permute-start(f32[32,128]{1,0:T(8,128)S(1)} %add_add_fusion.5), channel_id=1, source_target_pairs={{0,8},{8,0},{16,24},{24,16},{1,9},{9,1},{17,25},{25,17},{2,10},{10... | collective-permute-start | bytes 49160 | tf_op jit(solution)/shard_map/ppermute | solution.py:436
  94.5 5.0 %collective-permute-start.17 = (f32[32,128]{1,0:T(8,128)S(1)}, f32[32,128]{1,0:T(8,128)S(1)}, u32[]{:S(2)}, u32[]{:S(2)}) collective-permute-start(f32[32,128]{1,0:T(8,128)S(1)} %add_add_fusion.4), channel_id=1, source_target_pairs={{0,96},{32,64},{64,32},{96,0},{1,97},{33,65},{65,33},{97,1},{2,98}... | collective-permute-start | bytes 49160 | tf_op jit(solution)/shard_map/ppermute | solution.py:436
  95.4 5.2 %collective-permute-start.16 = (f32[32,128]{1,0:T(8,128)S(1)}, f32[32,128]{1,0:T(8,128)S(1)}, u32[]{:S(2)}, u32[]{:S(2)}) collective-permute-start(f32[32,128]{1,0:T(8,128)S(1)} %add_add_fusion.4), channel_id=1, source_target_pairs={{0,64},{32,96},{64,0},{96,32},{1,65},{33,97},{65,1},{97,33},{2,66}... | collective-permute-start | bytes 49160 | tf_op jit(solution)/shard_map/ppermute | solution.py:436
  96.9 3.7 %collective-permute-start.15 = (f32[32,128]{1,0:T(8,128)S(1)}, f32[32,128]{1,0:T(8,128)S(1)}, u32[]{:S(2)}, u32[]{:S(2)}) collective-permute-start(f32[32,128]{1,0:T(8,128)S(1)} %add_add_fusion.4), channel_id=1, source_target_pairs={{0,32},{32,0},{64,96},{96,64},{1,33},{33,1},{65,97},{97,65},{2,34}... | collective-permute-start | bytes 49160 | tf_op jit(solution)/shard_map/ppermute | solution.py:436
  109.3 1.3 collective-permute-start.18
  110.6 4.9 %collective-permute-start.21 = (f32[32,128]{1,0:T(8,128)S(1)}, f32[32,128]{1,0:T(8,128)S(1)}, u32[]{:S(2)}, u32[]{:S(2)}) collective-permute-start(f32[32,128]{1,0:T(8,128)S(1)} %add.78), channel_id=1, source_target_pairs={{0,6},{2,4},{4,2},{6,0},{1,7},{3,5},{5,3},{7,1},{8,14},{10,12},{12... | collective-permute-start | bytes 49160 | tf_op jit(solution)/shard_map/ppermute | solution.py:436
  112.2 5.2 %collective-permute-start.20 = (f32[32,128]{1,0:T(8,128)S(1)}, f32[32,128]{1,0:T(8,128)S(1)}, u32[]{:S(2)}, u32[]{:S(2)}) collective-permute-start(f32[32,128]{1,0:T(8,128)S(1)} %add.78), channel_id=1, source_target_pairs={{0,4},{2,6},{4,0},{6,2},{1,5},{3,7},{5,1},{7,3},{8,12},{10,14},{12... | collective-permute-start | bytes 49160 | tf_op jit(solution)/shard_map/ppermute | solution.py:436
  113.2 4.3 %collective-permute-start.19 = (f32[32,128]{1,0:T(8,128)S(1)}, f32[32,128]{1,0:T(8,128)S(1)}, u32[]{:S(2)}, u32[]{:S(2)}) collective-permute-start(f32[32,128]{1,0:T(8,128)S(1)} %add.78), channel_id=1, source_target_pairs={{0,2},{2,0},{4,6},{6,4},{1,3},{3,1},{5,7},{7,5},{8,10},{10,8},{12,... | collective-permute-start | bytes 49160 | tf_op jit(solution)/shard_map/ppermute | solution.py:436
  117.5 5.2 %collective-permute-start.24 = (f32[32,128]{1,0:T(8,128)S(1)}, f32[32,128]{1,0:T(8,128)S(1)}, u32[]{:S(2)}, u32[]{:S(2)}) collective-permute-start(f32[32,128]{1,0:T(8,128)S(1)} %add_add_fusion.2), channel_id=1, source_target_pairs={{0,24},{8,16},{16,8},{24,0},{1,25},{9,17},{17,9},{25,1},{2,26},{10... | collective-permute-start | bytes 49160 | tf_op jit(solution)/shard_map/ppermute | solution.py:436
  119.8 5.2 %collective-permute-start.23 = (f32[32,128]{1,0:T(8,128)S(1)}, f32[32,128]{1,0:T(8,128)S(1)}, u32[]{:S(2)}, u32[]{:S(2)}) collective-permute-start(f32[32,128]{1,0:T(8,128)S(1)} %add_add_fusion.2), channel_id=1, source_target_pairs={{0,16},{8,24},{16,0},{24,8},{1,17},{9,25},{17,1},{25,9},{2,18},{10... | collective-permute-start | bytes 49160 | tf_op jit(solution)/shard_map/ppermute | solution.py:436
  121.2 3.8 %collective-permute-start.22 = (f32[32,128]{1,0:T(8,128)S(1)}, f32[32,128]{1,0:T(8,128)S(1)}, u32[]{:S(2)}, u32[]{:S(2)}) collective-permute-start(f32[32,128]{1,0:T(8,128)S(1)} %add_add_fusion.2), channel_id=1, source_target_pairs={{0,8},{8,0},{16,24},{24,16},{1,9},{9,1},{17,25},{25,17},{2,10},{10... | collective-permute-start | bytes 49160 | tf_op jit(solution)/shard_map/ppermute | solution.py:436
  125.0 5.0 %collective-permute-start.27 = (f32[32,128]{1,0:T(8,128)S(1)}, f32[32,128]{1,0:T(8,128)S(1)}, u32[]{:S(2)}, u32[]{:S(2)}) collective-permute-start(f32[32,128]{1,0:T(8,128)S(1)} %add_add_fusion.1), channel_id=1, source_target_pairs={{0,96},{32,64},{64,32},{96,0},{1,97},{33,65},{65,33},{97,1},{2,98}... | collective-permute-start | bytes 49160 | tf_op jit(solution)/shard_map/ppermute | solution.py:436
  126.5 5.2 %collective-permute-start.26 = (f32[32,128]{1,0:T(8,128)S(1)}, f32[32,128]{1,0:T(8,128)S(1)}, u32[]{:S(2)}, u32[]{:S(2)}) collective-permute-start(f32[32,128]{1,0:T(8,128)S(1)} %add_add_fusion.1), channel_id=1, source_target_pairs={{0,64},{32,96},{64,0},{96,32},{1,65},{33,97},{65,1},{97,33},{2,66}... | collective-permute-start | bytes 49160 | tf_op jit(solution)/shard_map/ppermute | solution.py:436
  127.4 4.3 %collective-permute-start.25 = (f32[32,128]{1,0:T(8,128)S(1)}, f32[32,128]{1,0:T(8,128)S(1)}, u32[]{:S(2)}, u32[]{:S(2)}) collective-permute-start(f32[32,128]{1,0:T(8,128)S(1)} %add_add_fusion.1), channel_id=1, source_target_pairs={{0,32},{32,0},{64,96},{96,64},{1,33},{33,1},{65,97},{97,65},{2,34}... | collective-permute-start | bytes 49160 | tf_op jit(solution)/shard_map/ppermute | solution.py:436

commit v5 on v4

--- a/solution.py
+++ b/solution.py
@@ -61,8 +61,7 @@
 
 def to_lanes(volts, stack, v_out, c_out, low_out, high_out):
     for x in range(8):
-        rows = [volts[pl.ds(l * 8 + x, 32, stride=32), :] for l in range(4)]
-        field = jnp.concatenate(rows, axis=0).T
+        field = load_rows(volts, x).T
         v_out[x] = field
         coef = stack[pl.ds(x, 16, stride=8), :]
         coef = jnp.concatenate([coef, jnp.zeros((112, 128), F32)], axis=0).T
@@ -73,9 +72,15 @@
         high_out[64 + x * 8 : 72 + x * 8, :] = coef[120:]
 
 
+def inside(axis):
+    me = lax.axis_index(axis)
+    return (me > 0).astype(F32), (me < lax.axis_size(axis) - 1).astype(F32)
+
+
 def widened(low, own, high, x, base=0):
-    at = pl.ds(base + x * 8, 8)
-    return jnp.concatenate([low[at, :], own[x], high[at, :]], axis=0)
+    at = pl.ds(pl.multiple_of(base + x * 8, 8), 8)
+    low_in, high_in = inside(GY)
+    return jnp.concatenate([low[at, :] * low_in, own[x], high[at, :] * high_in], axis=0)
 
 
 def pack_rows(v, c, low, high, first_out, last_out):
@@ -133,7 +138,7 @@
 
 def add_currents(slots, waves, out, low_out, high_out, acc):
     acc[...] = jnp.zeros_like(acc)
-    table = jnp.concatenate([p.astype(F32) for p in split3(waves[...])], axis=0).astype(BF16)
+    table = jnp.concatenate([p.astype(F32) for p in split3(waves[...])], axis=1).astype(BF16)
     wave_line = iota((64, 2048), 0).astype(F32).astype(BF16)
     cell_line = iota((256, 2048), 0).astype(F32).astype(BF16)
     one, zero = jnp.ones((), BF16), jnp.zeros((), BF16)
@@ -143,9 +148,8 @@
         amp = jnp.concatenate([r[0:1, :] for r in rows], axis=1)
         code = jnp.concatenate([r[1:2, :] for r in rows], axis=1).astype(jnp.int32)
         hit = jnp.where(wave_line == (code & 63).astype(F32).astype(BF16), one, zero)
-        picked = dot(table, hit, ((1,), (0,)))
-        current = (picked[:64] + picked[64:128]) + picked[128:]
-        current = (current * amp).astype(BF16)
+        picked = dot(table, jnp.concatenate([hit, hit, hit], axis=0), ((1,), (0,)))
+        current = (picked * amp).astype(BF16)
         cell = code >> 6
         block = (cell >> 8).astype(F32).astype(BF16)
         right = [jnp.where(block == jnp.array(r, BF16), current, zero) for r in range(4)]
@@ -195,9 +199,13 @@
     own = [f[first : first + 8, 8:136, :].reshape(1024, 128) for f in fields]
     lane, row = iota((32, 128), 1), iota((32, 128), 0)
     packed = jnp.zeros((32, 128), F32)
+    parts = [split2(f) for f in own]
     for k in range(3):
-        pair = jnp.concatenate([own[k], own[k + 1]], axis=1)
-        product = dot_split(own[k], pair, ((0,), (0,)))
+        (hi, lo), (next_hi, next_lo) = parts[k], parts[k + 1]
+        left = jnp.concatenate([hi, lo], axis=1)
+        product = dot(left, jnp.concatenate([hi, next_hi], axis=1), ((0,), (0,)))
+        cross = dot(hi, jnp.concatenate([lo, next_lo], axis=1), ((0,), (0,)))
+        product = product[:128] + product[128:] + cross
         column = lane - 32 * k
         totals = []
         for b in range(2):
@@ -301,23 +309,22 @@
         wv[i] = jnp.where(lane < 96, wide[:, 384:], 0.0)
         diag[i] = wide[:, :128] + wide[:, 384:]
 
-    def halo_row(j, ref, base):
-        ext[base + j] = ref[j, :YE, :]
-        packed = ref[j, YE:, :]
+    def halo_row(j, ref, base, present):
+        ext[base + j] = ref[j, :YE, :] * present
+        packed = ref[j, YE:, :] * present
         groups = [packed] + [pltpu.roll(packed, 128 - 16 * g, 1) for g in range(1, 6)]
         coef = jnp.concatenate(groups, axis=0)
         expand(base + j, jnp.where(lane < 16, coef, 0.0))
 
     def own_row(x, carry):
-        at = pl.ds(pl.multiple_of(x * 8, 8), 8)
-        at_c = pl.ds(pl.multiple_of(64 + x * 8, 8), 8)
-        ext[7 + x] = jnp.concatenate([low[at, :], v[x], high[at, :]], axis=0)
-        expand(7 + x, jnp.concatenate([low[at_c, :], c[x], high[at_c, :]], axis=0))
+        ext[7 + x] = widened(low, v, high, x)
+        expand(7 + x, widened(low, c, high, x, 64))
         return carry
 
     def halo_rows(j, carry):
-        halo_row(j, x_low, 0)
-        halo_row(j, x_high, 15)
+        low_in, high_in = inside(GX)
+        halo_row(j, x_low, 0, low_in)
+        halo_row(j, x_high, 15, high_in)
         return carry
 
     lax.fori_loop(0, 8, own_row, 0, unroll=2)
@@ -363,13 +370,13 @@
         v0[i] = free[i] - now
 
     def own_start(x, carry):
-        at = pl.ds(pl.multiple_of(x * 8, 8), 8)
-        start(7 + x, jnp.concatenate([i_low[at, :], inj[x], i_high[at, :]], axis=0))
+        start(7 + x, widened(i_low, inj, i_high, x))
         return carry
 
     def halo_start(j, carry):
-        for ref, base in ((ix_low, 1), (ix_high, 15)):
-            both = ref[j]
+        low_in, high_in = inside(GX)
+        for ref, base, present in ((ix_low, 1, low_in), (ix_high, 15, high_in)):
+            both = ref[j] * present
             start(base + j, both)
             start(base + 3 + j, pltpu.roll(both, 64, 1))
         return carry
@@ -383,8 +390,7 @@
 
 
 def second_basis(
-    gram, diag, wx, wy, wv, cap, change, v0, v1, v2, v3, v,
-    w0, w1, w2, w3, volts, gram_out, b0, b1, b2, b3, step,
+    gram, diag, wx, wy, wv, cap, change, v0, v1, v2, v3, step, b0, b1, b2, b3, gram_out
 ):
     weights = (diag, wx, wy, wv)
     mix = combination(gram)
@@ -402,29 +408,43 @@
     power(b1, b2, 6, 15, weights)
     power(b2, b3, 7, 14, weights)
     moments((b0, b1, b2, b3), gram_out, 7)
+
+
+def store_rows(out, x, value):
+    for l in range(4):
+        out[pl.ds(l * 8 + x, 32, stride=32), :] = value[l * 32 : (l + 1) * 32]
+
+
+def load_rows(ref, x):
+    return jnp.concatenate([ref[pl.ds(l * 8 + x, 32, stride=32), :] for l in range(4)], axis=0)
+
+
+def from_lanes(step, b0, volts, volts_out, residual_out):
     for x in range(8):
-        volts[x] = v[x] + step[7 + x, 8:136, :]
-        for src, dst in ((b0, w0), (b1, w1), (b2, w2), (b3, w3)):
-            dst[x] = src[7 + x, 8:136, :]
-
-
-def finish(gram, w0, w1, w2, w3, volts, volts_out, residual_out):
+        store_rows(volts_out, x, load_rows(volts, x) + step[7 + x, 8:136, :].T)
+        store_rows(residual_out, x, b0[7 + x, 8:136, :].T)
+
+
+def finish(gram, b0, b1, b2, b3, volts, residual, volts_out, residual_out):
     mix = combination(gram)
-    for x in range(8):
-        fields = jnp.concatenate([w0[x], w1[x], w2[x], w3[x]], axis=1)
-        both = dot_split(fields, mix, ((1,), (0,)))
-        for value, out in (
-            (volts[x] + both[:, :128], volts_out),
-            (w0[x] + both[:, 128:], residual_out),
-        ):
-            value = value.T
-            for l in range(4):
-                out[pl.ds(l * 8 + x, 32, stride=32), :] = value[l * 32 : (l + 1) * 32]
+    for x in range(0, 8, 2):
+        fields = jnp.concatenate(
+            [
+                jnp.concatenate([b[7 + n, 8:136, :] for b in (b0, b1, b2, b3)], axis=1)
+                for n in (x, x + 1)
+            ],
+            axis=0,
+        )
+        both = dot_split(mix, fields, ((0,), (1,)))
+        for n in range(2):
+            own = both[:, n * 128 : (n + 1) * 128]
+            store_rows(volts_out, x + n, load_rows(volts, x + n) + own[:128])
+            store_rows(residual_out, x + n, load_rows(residual, x + n) + own[128:])
 
 
 def neighbours(to_low, to_high, axis):
     size = lax.axis_size(axis)
-    up = [(i, i + 1) for i in range(size - 1)]
+    up = [(i, (i + 1) % size) for i in range(size)]
     from_low = lax.ppermute(to_high, axis, up)
     return from_low, lax.ppermute(to_low, axis, [(b, a) for a, b in up])
 
@@ -478,14 +498,15 @@
         [wide] * 5 + [(32, 128)],
         [diag, wx, wy, wv, free, inj, i_low, i_high, ix_low, ix_high],
     )
-    own = (8, 128, 128)
-    *basis, gram = call(
+    step, *basis, gram = call(
         second_basis,
-        [own] * 5 + [(32, 128)],
-        [everywhere(gram), diag, wx, wy, wv, cap] + kept + [v],
-        [vmem(wide, F32)] * 5,
-    )
-    outs = call(finish, [(1024, 128)] * 2, [everywhere(gram)] + basis)
+        [wide] * 5 + [(32, 128)],
+        [everywhere(gram), diag, wx, wy, wv, cap] + kept,
+    )
+    so_far = call(
+        from_lanes, [(1024, 128)] * 2, [step, basis[0], volts.reshape(1024, 128)]
+    )
+    outs = call(finish, [(1024, 128)] * 2, [everywhere(gram)] + basis + list(so_far))
     return tuple(o.reshape(volts.shape) for o in outs)
 
 

time: 137 us -> 125 us (0.912)
  blocking collectives: 25.8 us -> 17.2 us
  waiting for transfers between devices: 22.8 us -> 19.4 us
  starting transfers between devices: 44.3 us -> 42.4 us
  Pallas kernels: 38.8 us -> 40.4 us
    ppermute x4, starting transfers between devices: 5.17 us -> 14.3 us  [neighbours(): return (from_low, lax.ppermute(to_low, axis, [(b, a) for a, b in up]))]
    all_to_all x1, blocking collectives: 25.8 us -> 17.2 us  [exchange(): return lax.all_to_all(slots, GX_GY, split_axis=0, concat_axis=0, tiled=True)]
    ppermute x4, starting transfers between devices: 10.5 us -> 3.04 us  [neighbours(): from_low = lax.ppermute(to_high, axis, up)]
    ppermute x18, waiting for transfers between devices: 18.3 us -> 15.4 us  [everywhere(): lax.ppermute(x, axis, [(i, i ^ k) for i in range(4)])]
    ppermute x4, waiting for transfers between devices: 2.49 us -> 0.01 us  [neighbours(): return (from_low, lax.ppermute(to_low, axis, [(b, a) for a, b in up]))]
    ppermute x18, starting transfers between devices: 27.2 us -> 24.9 us  [everywhere(): lax.ppermute(x, axis, [(i, i ^ k) for i in range(4)])]
    ppermute x4, waiting for transfers between devices: 0.01 us -> 1.6 us  [neighbours(): from_low = lax.ppermute(to_high, axis, up)]
    pallas_call x9 -> x10, Pallas kernels: 38.8 us -> 40.4 us  [call(): pl.pallas_call(kernel, out_shape=tuple(outs), scratch_shapes=list(scratch...]
  transfers between devices with their start and end apart: 28 -> 28, of which waited for: 18 -> 15; matrix products, arithmetic and copies ran while one was open for 1% -> 1% of each run, Pallas kernels for 14% -> 16%
where the time goes in v5:
time: 125 us; the launch traced here: 124 us
  starting transfers between devices  42.4 us (34%)
  Pallas kernels  40.4 us (32%)
  waiting for transfers between devices  19.4 us (16%)
  blocking collectives  17.2 us (14%)
  other arithmetic  2.4 us (2%)
  local copies, waits for them, and re-layouts  1.81 us (1%)
    pallas_call x10, Pallas kernels, call(): pl.pallas_call(kernel, out_shape=tuple(outs), scratch_shapes=list(scratch...  40.4 us
    ppermute x18, starting transfers between devices, everywhere(): lax.ppermute(x, axis, [(i, i ^ k) for i in range(4)])  24.9 us
    all_to_all x1, blocking collectives, exchange(): return lax.all_to_all(slots, GX_GY, split_axis=0, concat_axis=0, tiled=True)  17.2 us
    ppermute x18, waiting for transfers between devices, everywhere(): lax.ppermute(x, axis, [(i, i ^ k) for i in range(4)])  15.4 us
    ppermute x4, starting transfers between devices, neighbours(): return (from_low, lax.ppermute(to_low, axis, [(b, a) for a, b in up]))  14.3 us
    ppermute x4, starting transfers between devices, neighbours(): from_low = lax.ppermute(to_high, axis, up)  3.04 us
  transfers between devices with their start and end apart: 28, of which 15 were waited for; matrix products, arithmetic and copies ran while one was open for 1% of the time, Pallas kernels for 16%

profile of v5, /device:TPU:0, one launch (start us, length us, event | category | flops | bytes accessed | tf_op | source)
XLA Modules:
  0.0 124.5 jit_solution(9184227995289678881)
XLA Ops:
  2.9 3.6 %collective-permute-start.1 = (f32[128,128]{1,0:T(8,128)S(1)}, f32[128,128]{1,0:T(8,128)S(1)}, u32[]{:S(2)}, u32[]{:S(2)}) collective-permute-start(f32[128,128]{1,0:T(8,128)S(1)} %get-tuple-element.41), channel_id=1, source_target_pairs={{1,0},{2,1},{3,2},{4,3},{5,4},{6,5},{7,6},{0,7},{9,8},{10,9},{11,1... | collective-permute-start | bytes 196616 | tf_op jit(solution)/shard_map/ppermute | solution.py:449
  8.8 5.3 %place_slots.1 = f32[128,2,128]{2,1,0:T(2,128)S(1)} custom-call(s32[64,128]{1,0:T(8,128)S(1)} %add_bitcast_fusion.codes, f32[64,128]{1,0:T(8,128)S(1)} %bitcast.13), custom_call_target="tpu_custom_call" | custom-call | tf_op jit(solution)/shard_map/place_slots/pallas_call | solution.py:52
  14.3 1.6 %collective-permute-start.2 = (f32[7,168,128]{2,1,0:T(8,128)S(1)}, f32[7,168,128]{2,1,0:T(8,128)S(1)}, u32[]{:S(2)}, u32[]{:S(2)}) collective-permute-start(f32[7,168,128]{2,1,0:T(8,128)S(1)} %get-tuple-element.44), channel_id=1, source_target_pairs={{0,8},{8,16},{16,24},{24,32},{32,40},{40,48},{48,56},{56,64},{64,7... | collective-permute-start | bytes 1806344 | tf_op jit(solution)/shard_map/ppermute | solution.py:448
  16.0 3.8 %collective-permute-start.3 = (f32[7,168,128]{2,1,0:T(8,128)S(1)}, f32[7,168,128]{2,1,0:T(8,128)S(1)}, u32[]{:S(2)}, u32[]{:S(2)}) collective-permute-start(f32[7,168,128]{2,1,0:T(8,128)S(1)} %get-tuple-element.45), channel_id=1, source_target_pairs={{8,0},{16,8},{24,16},{32,24},{40,32},{48,40},{56,48},{64,56},{72,6... | collective-permute-start | bytes 1806344 | tf_op jit(solution)/shard_map/ppermute | solution.py:449
  19.7 17.2 %all_to_all.5.slots = f32[128,2,128]{2,1,0:T(2,128)S(1)} all-to-all(f32[128,2,128]{2,1,0:T(2,128)S(1)} %place_slots.1), channel_id=1, replica_groups=mesh['gx_0'=4,'gx_1'=4,'gy_0'=4,'gy_1'=2] {'gx_0','gx_1','gy_0','gy_1'}, dimensions={0} | all-to-all | bytes 262144 | tf_op jit(solution)/shard_map/all_to_all | solution.py:463
  37.0 6.3 %add_currents.1 = (f32[8,128,128]{2,1,0:T(8,128)S(1)}, f32[64,128]{1,0:T(8,128)S(1)}, f32[64,128]{1,0:T(8,128)S(1)}) custom-call(f32[128,2,128]{2,1,0:T(2,128)S(1)} %all_to_all.5.slots, f32[64,64]{1,0:T(8,128)S(1)} %copy-done.2), custom_call_target="tpu_custom_call" | custom-call | tf_op jit(solution)/shard_map/add_currents/pallas_call | solution.py:52
  43.4 2.9 %collective-permute-start.5 = (f32[64,128]{1,0:T(8,128)S(1)}, f32[64,128]{1,0:T(8,128)S(1)}, u32[]{:S(2)}, u32[]{:S(2)}) collective-permute-start(f32[64,128]{1,0:T(8,128)S(1)} %get-tuple-element.54), channel_id=1, source_target_pairs={{1,0},{2,1},{3,2},{4,3},{5,4},{6,5},{7,6},{0,7},{9,8},{10,9},{11,1... | collective-permute-start | bytes 98312 | tf_op jit(solution)/shard_map/ppermute | solution.py:449
  46.3 1.6 %collective-permute-done.4.low.i_low = f32[64,128]{1,0:T(8,128)S(1)} collective-permute-done((f32[64,128]{1,0:T(8,128)S(1)}, f32[64,128]{1,0:T(8,128)S(1)}, u32[]{:S(2)}, u32[]{:S(2)}) %collective-permute-start.4) | collective-permute-done | bytes 32800 | tf_op jit(solution)/shard_map/ppermute | solution.py:448
  48.0 1.3 %collective-permute-start.6 = (f32[3,144,128]{2,1,0:T(8,128)S(1)}, f32[3,144,128]{2,1,0:T(8,128)S(1)}, u32[]{:S(2)}, u32[]{:S(2)}) collective-permute-start(f32[3,144,128]{2,1,0:T(8,128)S(1)} %get-tuple-element.55), channel_id=1, source_target_pairs={{0,8},{8,16},{16,24},{24,32},{32,40},{40,48},{48,56},{56,64},{64,7... | collective-permute-start | bytes 663560 | tf_op jit(solution)/shard_map/ppermute | solution.py:448
  49.3 4.2 %collective-permute-start.7 = (f32[3,144,128]{2,1,0:T(8,128)S(1)}, f32[3,144,128]{2,1,0:T(8,128)S(1)}, u32[]{:S(2)}, u32[]{:S(2)}) collective-permute-start(f32[3,144,128]{2,1,0:T(8,128)S(1)} %get-tuple-element.56), channel_id=1, source_target_pairs={{8,0},{16,8},{24,16},{32,24},{40,32},{48,40},{56,48},{64,56},{72,6... | collective-permute-start | bytes 663560 | tf_op jit(solution)/shard_map/ppermute | solution.py:449
  53.4 7.3 %grid_weights.1 = (f32[22,144,128]{2,1,0:T(8,128)S(1)}, f32[22,144,128]{2,1,0:T(8,128)S(1)}, f32[22,144,128]{2,1,0:T(8,128)S(1)}, f32[22,144,128]{2,1,0:T(8,128)...) custom-call(f32[8,128,128]{2,1,0:T(8,128)S(1)} %get-tuple-element.38.v, ...), custom_call_target="tpu_custom_call" | custom-call | tf_op jit(solution)/shard_map/grid_weights/pallas_call | solution.py:52
  60.8 5.8 %first_basis.1 = (f32[22,144,128]{2,1,0:T(8,128)S(1)}, f32[22,144,128]{2,1,0:T(8,128)S(1)}, f32[22,144,128]{2,1,0:T(8,128)S(1)}, f32[22,144,128]{2,1,0:T(8,128)S...) custom-call(f32[22,144,128]{2,1,0:T(8,128)S(1)} %get-tuple-element.46.diag, ...), custom_call_target="tpu_custom_call" | custom-call | tf_op jit(solution)/shard_map/first_basis/pallas_call | solution.py:52
  66.7 1.2 collective-permute-done.8
  67.9 2.6 %collective-permute-start.11 = (f32[32,128]{1,0:T(8,128)S(1)}, f32[32,128]{1,0:T(8,128)S(1)}, u32[]{:S(2)}, u32[]{:S(2)}) collective-permute-start(f32[32,128]{1,0:T(8,128)S(1)} %add.68), channel_id=1, source_target_pairs={{0,6},{2,4},{4,2},{6,0},{1,7},{3,5},{5,3},{7,1},{8,14},{10,12},{12... | collective-permute-start | bytes 49160 | tf_op jit(solution)/shard_map/ppermute | solution.py:456
  70.4 1.5 %collective-permute-start.9 = (f32[32,128]{1,0:T(8,128)S(1)}, f32[32,128]{1,0:T(8,128)S(1)}, u32[]{:S(2)}, u32[]{:S(2)}) collective-permute-start(f32[32,128]{1,0:T(8,128)S(1)} %add.68), channel_id=1, source_target_pairs={{0,2},{2,0},{4,6},{6,4},{1,3},{3,1},{5,7},{7,5},{8,10},{10,8},{12,... | collective-permute-start | bytes 49160 | tf_op jit(solution)/shard_map/ppermute | solution.py:456
  72.8 2.8 %collective-permute-done.10 = f32[32,128]{1,0:T(8,128)S(1)} collective-permute-done((f32[32,128]{1,0:T(8,128)S(1)}, f32[32,128]{1,0:T(8,128)S(1)}, u32[]{:S(2)}, u32[]{:S(2)}) %collective-permute-start.10) | collective-permute-done | bytes 16416 | tf_op jit(solution)/shard_map/ppermute | solution.py:456
  75.9 4.0 %collective-permute-start.12 = (f32[32,128]{1,0:T(8,128)S(1)}, f32[32,128]{1,0:T(8,128)S(1)}, u32[]{:S(2)}, u32[]{:S(2)}) collective-permute-start(f32[32,128]{1,0:T(8,128)S(1)} %add_add_fusion.5), channel_id=1, source_target_pairs={{0,8},{8,0},{16,24},{24,16},{1,9},{9,1},{17,25},{25,17},{2,10},{10... | collective-permute-start | bytes 49160 | tf_op jit(solution)/shard_map/ppermute | solution.py:456
  81.7 1.8 %collective-permute-start.17 = (f32[32,128]{1,0:T(8,128)S(1)}, f32[32,128]{1,0:T(8,128)S(1)}, u32[]{:S(2)}, u32[]{:S(2)}) collective-permute-start(f32[32,128]{1,0:T(8,128)S(1)} %add_add_fusion.4), channel_id=1, source_target_pairs={{0,96},{32,64},{64,32},{96,0},{1,97},{33,65},{65,33},{97,1},{2,98}... | collective-permute-start | bytes 49160 | tf_op jit(solution)/shard_map/ppermute | solution.py:456
  84.5 1.4 %collective-permute-start.15 = (f32[32,128]{1,0:T(8,128)S(1)}, f32[32,128]{1,0:T(8,128)S(1)}, u32[]{:S(2)}, u32[]{:S(2)}) collective-permute-start(f32[32,128]{1,0:T(8,128)S(1)} %add_add_fusion.4), channel_id=1, source_target_pairs={{0,32},{32,0},{64,96},{96,64},{1,33},{33,1},{65,97},{97,65},{2,34}... | collective-permute-start | bytes 49160 | tf_op jit(solution)/shard_map/ppermute | solution.py:456
  86.8 2.0 %collective-permute-done.16 = f32[32,128]{1,0:T(8,128)S(1)} collective-permute-done((f32[32,128]{1,0:T(8,128)S(1)}, f32[32,128]{1,0:T(8,128)S(1)}, u32[]{:S(2)}, u32[]{:S(2)}) %collective-permute-start.16) | collective-permute-done | bytes 16416 | tf_op jit(solution)/shard_map/ppermute | solution.py:456
  88.8 8.6 %second_basis.1 = (f32[22,144,128]{2,1,0:T(8,128)S(1)}, f32[22,144,128]{2,1,0:T(8,128)S(1)}, f32[22,144,128]{2,1,0:T(8,128)S(1)}, f32[22,144,128]{2,1,0:T(8,128)...) custom-call(f32[32,128]{1,0:T(8,128)S(1)} %add_add_fusion.3.gram, f32[22,144,128]{2,1,0:T(8,128)S(1)} %get-tuple-element.46.diag, ...), custom_call_target="tpu_custom_call" | custom-call | tf_op jit(solution)/shard_map/second_basis/pallas_call | solution.py:52
  99.5 1.4 %collective-permute-start.20 = (f32[32,128]{1,0:T(8,128)S(1)}, f32[32,128]{1,0:T(8,128)S(1)}, u32[]{:S(2)}, u32[]{:S(2)}) collective-permute-start(f32[32,128]{1,0:T(8,128)S(1)} %add.78), channel_id=1, source_target_pairs={{0,4},{2,6},{4,0},{6,2},{1,5},{3,7},{5,1},{7,3},{8,12},{10,14},{12... | collective-permute-start | bytes 49160 | tf_op jit(solution)/shard_map/ppermute | solution.py:456
  100.9 1.8 %collective-permute-start.19 = (f32[32,128]{1,0:T(8,128)S(1)}, f32[32,128]{1,0:T(8,128)S(1)}, u32[]{:S(2)}, u32[]{:S(2)}) collective-permute-start(f32[32,128]{1,0:T(8,128)S(1)} %add.78), channel_id=1, source_target_pairs={{0,2},{2,0},{4,6},{6,4},{1,3},{3,1},{5,7},{7,5},{8,10},{10,8},{12,... | collective-permute-start | bytes 49160 | tf_op jit(solution)/shard_map/ppermute | solution.py:456
  104.8 2.5 %collective-permute-start.24 = (f32[32,128]{1,0:T(8,128)S(1)}, f32[32,128]{1,0:T(8,128)S(1)}, u32[]{:S(2)}, u32[]{:S(2)}) collective-permute-start(f32[32,128]{1,0:T(8,128)S(1)} %add_add_fusion.2), channel_id=1, source_target_pairs={{0,24},{8,16},{16,8},{24,0},{1,25},{9,17},{17,9},{25,1},{2,26},{10... | collective-permute-start | bytes 49160 | tf_op jit(solution)/shard_map/ppermute | solution.py:456
  107.3 1.4 %collective-permute-start.23 = (f32[32,128]{1,0:T(8,128)S(1)}, f32[32,128]{1,0:T(8,128)S(1)}, u32[]{:S(2)}, u32[]{:S(2)}) collective-permute-start(f32[32,128]{1,0:T(8,128)S(1)} %add_add_fusion.2), channel_id=1, source_target_pairs={{0,16},{8,24},{16,0},{24,8},{1,17},{9,25},{17,1},{25,9},{2,18},{10... | collective-permute-start | bytes 49160 | tf_op jit(solution)/shard_map/ppermute | solution.py:456
  109.8 2.7 %collective-permute-done.23 = f32[32,128]{1,0:T(8,128)S(1)} collective-permute-done((f32[32,128]{1,0:T(8,128)S(1)}, f32[32,128]{1,0:T(8,128)S(1)}, u32[]{:S(2)}, u32[]{:S(2)}) %collective-permute-start.23) | collective-permute-done | bytes 16416 | tf_op jit(solution)/shard_map/ppermute | solution.py:456
  112.5 1.6 %collective-permute-start.27 = (f32[32,128]{1,0:T(8,128)S(1)}, f32[32,128]{1,0:T(8,128)S(1)}, u32[]{:S(2)}, u32[]{:S(2)}) collective-permute-start(f32[32,128]{1,0:T(8,128)S(1)} %add_add_fusion.1), channel_id=1, source_target_pairs={{0,96},{32,64},{64,32},{96,0},{1,97},{33,65},{65,33},{97,1},{2,98}... | collective-permute-start | bytes 49160 | tf_op jit(solution)/shard_map/ppermute | solution.py:456
  114.1 1.4 %collective-permute-start.26 = (f32[32,128]{1,0:T(8,128)S(1)}, f32[32,128]{1,0:T(8,128)S(1)}, u32[]{:S(2)}, u32[]{:S(2)}) collective-permute-start(f32[32,128]{1,0:T(8,128)S(1)} %add_add_fusion.1), channel_id=1, source_target_pairs={{0,64},{32,96},{64,0},{96,32},{1,65},{33,97},{65,1},{97,33},{2,66}... | collective-permute-start | bytes 49160 | tf_op jit(solution)/shard_map/ppermute | solution.py:456
  115.5 1.2 collective-permute-start.25
  116.7 1.2 from_lanes.1
  118.0 1.4 %collective-permute-done.26 = f32[32,128]{1,0:T(8,128)S(1)} collective-permute-done((f32[32,128]{1,0:T(8,128)S(1)}, f32[32,128]{1,0:T(8,128)S(1)}, u32[]{:S(2)}, u32[]{:S(2)}) %collective-permute-start.26) | collective-permute-done | bytes 16416 | tf_op jit(solution)/shard_map/ppermute | solution.py:456
  119.4 5.1 %finish.1 = (f32[1024,128]{1,0:T(8,128)}, f32[1024,128]{1,0:T(8,128)}) custom-call(f32[32,128]{1,0:T(8,128)S(1)} %add_add_fusion.gram, f32[22,144,128]{2,1,0:T(8,128)S(1)} %get-tuple-element.65.b0, f32[22,144,128]{2,1,0:T(8,128)S(1)} %get-tuple-element.66.b1, f32[22,144,128]{2,1,0:T(8,128)S(1)} %get-tuple-element.67.b2, ...), custom_call_target="tpu_custom_call" | custom-call | tf_op jit(solution)/shard_map/finish/pallas_call | solution.py:52
  (54 shorter events, 15.2 us)
Async XLA Ops:
  0.6 36.3 %copy-start.2 = (f32[64,64]{1,0:T(8,128)S(1)}, f32[64,64]{1,0:T(8,128)}, u32[]{:S(2)}) copy-start(f32[64,64]{1,0:T(8,128)} %waves.1) | copy-start | bytes 49156
  1.4 1.0 copy-start
  2.9 11.2 %collective-permute-start = (f32[128,128]{1,0:T(8,128)S(1)}, f32[128,128]{1,0:T(8,128)S(1)}, u32[]{:S(2)}, u32[]{:S(2)}) collective-permute-start(f32[128,128]{1,0:T(8,128)S(1)} %get-tuple-element.40), channel_id=1, source_target_pairs={{0,1},{1,2},{2,3},{3,4},{4,5},{5,6},{6,7},{7,0},{8,9},{9,10},{10,1... | collective-permute-start | bytes 196616 | tf_op jit(solution)/shard_map/ppermute | solution.py:448
  2.9 11.2 %collective-permute-start.1 = (f32[128,128]{1,0:T(8,128)S(1)}, f32[128,128]{1,0:T(8,128)S(1)}, u32[]{:S(2)}, u32[]{:S(2)}) collective-permute-start(f32[128,128]{1,0:T(8,128)S(1)} %get-tuple-element.41), channel_id=1, source_target_pairs={{1,0},{2,1},{3,2},{4,3},{5,4},{6,5},{7,6},{0,7},{9,8},{10,9},{11,1... | collective-permute-start | bytes 196616 | tf_op jit(solution)/shard_map/ppermute | solution.py:449
  8.0 0.8 copy-start.3
  14.3 39.1 %collective-permute-start.2 = (f32[7,168,128]{2,1,0:T(8,128)S(1)}, f32[7,168,128]{2,1,0:T(8,128)S(1)}, u32[]{:S(2)}, u32[]{:S(2)}) collective-permute-start(f32[7,168,128]{2,1,0:T(8,128)S(1)} %get-tuple-element.44), channel_id=1, source_target_pairs={{0,8},{8,16},{16,24},{24,32},{32,40},{40,48},{48,56},{56,64},{64,7... | collective-permute-start | bytes 1806344 | tf_op jit(solution)/shard_map/ppermute | solution.py:448
  16.0 37.5 %collective-permute-start.3 = (f32[7,168,128]{2,1,0:T(8,128)S(1)}, f32[7,168,128]{2,1,0:T(8,128)S(1)}, u32[]{:S(2)}, u32[]{:S(2)}) collective-permute-start(f32[7,168,128]{2,1,0:T(8,128)S(1)} %get-tuple-element.45), channel_id=1, source_target_pairs={{8,0},{16,8},{24,16},{32,24},{40,32},{48,40},{56,48},{64,56},{72,6... | collective-permute-start | bytes 1806344 | tf_op jit(solution)/shard_map/ppermute | solution.py:449
  43.3 4.6 %collective-permute-start.4 = (f32[64,128]{1,0:T(8,128)S(1)}, f32[64,128]{1,0:T(8,128)S(1)}, u32[]{:S(2)}, u32[]{:S(2)}) collective-permute-start(f32[64,128]{1,0:T(8,128)S(1)} %get-tuple-element.53), channel_id=1, source_target_pairs={{0,1},{1,2},{2,3},{3,4},{4,5},{5,6},{6,7},{7,0},{8,9},{9,10},{10,1... | collective-permute-start | bytes 98312 | tf_op jit(solution)/shard_map/ppermute | solution.py:448
  43.4 4.4 %collective-permute-start.5 = (f32[64,128]{1,0:T(8,128)S(1)}, f32[64,128]{1,0:T(8,128)S(1)}, u32[]{:S(2)}, u32[]{:S(2)}) collective-permute-start(f32[64,128]{1,0:T(8,128)S(1)} %get-tuple-element.54), channel_id=1, source_target_pairs={{1,0},{2,1},{3,2},{4,3},{5,4},{6,5},{7,6},{0,7},{9,8},{10,9},{11,1... | collective-permute-start | bytes 98312 | tf_op jit(solution)/shard_map/ppermute | solution.py:449
  48.0 12.8 %collective-permute-start.6 = (f32[3,144,128]{2,1,0:T(8,128)S(1)}, f32[3,144,128]{2,1,0:T(8,128)S(1)}, u32[]{:S(2)}, u32[]{:S(2)}) collective-permute-start(f32[3,144,128]{2,1,0:T(8,128)S(1)} %get-tuple-element.55), channel_id=1, source_target_pairs={{0,8},{8,16},{16,24},{24,32},{32,40},{40,48},{48,56},{56,64},{64,7... | collective-permute-start | bytes 663560 | tf_op jit(solution)/shard_map/ppermute | solution.py:448
  49.3 11.5 %collective-permute-start.7 = (f32[3,144,128]{2,1,0:T(8,128)S(1)}, f32[3,144,128]{2,1,0:T(8,128)S(1)}, u32[]{:S(2)}, u32[]{:S(2)}) collective-permute-start(f32[3,144,128]{2,1,0:T(8,128)S(1)} %get-tuple-element.56), channel_id=1, source_target_pairs={{8,0},{16,8},{24,16},{32,24},{40,32},{48,40},{56,48},{64,56},{72,6... | collective-permute-start | bytes 663560 | tf_op jit(solution)/shard_map/ppermute | solution.py:449
  66.6 1.3 %collective-permute-start.8 = (f32[32,128]{1,0:T(8,128)S(1)}, f32[32,128]{1,0:T(8,128)S(1)}, u32[]{:S(2)}, u32[]{:S(2)}) collective-permute-start(f32[32,128]{1,0:T(8,128)S(1)} %get-tuple-element.57), channel_id=1, source_target_pairs={{0,1},{1,0},{2,3},{3,2},{4,5},{5,4},{6,7},{7,6},{8,9},{9,8},{10,11... | collective-permute-start | bytes 49160 | tf_op jit(solution)/shard_map/ppermute | solution.py:453
  67.9 4.9 %collective-permute-start.11 = (f32[32,128]{1,0:T(8,128)S(1)}, f32[32,128]{1,0:T(8,128)S(1)}, u32[]{:S(2)}, u32[]{:S(2)}) collective-permute-start(f32[32,128]{1,0:T(8,128)S(1)} %add.68), channel_id=1, source_target_pairs={{0,6},{2,4},{4,2},{6,0},{1,7},{3,5},{5,3},{7,1},{8,14},{10,12},{12... | collective-permute-start | bytes 49160 | tf_op jit(solution)/shard_map/ppermute | solution.py:456
  70.4 5.2 %collective-permute-start.10 = (f32[32,128]{1,0:T(8,128)S(1)}, f32[32,128]{1,0:T(8,128)S(1)}, u32[]{:S(2)}, u32[]{:S(2)}) collective-permute-start(f32[32,128]{1,0:T(8,128)S(1)} %add.68), channel_id=1, source_target_pairs={{0,4},{2,6},{4,0},{6,2},{1,5},{3,7},{5,1},{7,3},{8,12},{10,14},{12... | collective-permute-start | bytes 49160 | tf_op jit(solution)/shard_map/ppermute | solution.py:456
  70.4 5.2 %collective-permute-start.9 = (f32[32,128]{1,0:T(8,128)S(1)}, f32[32,128]{1,0:T(8,128)S(1)}, u32[]{:S(2)}, u32[]{:S(2)}) collective-permute-start(f32[32,128]{1,0:T(8,128)S(1)} %add.68), channel_id=1, source_target_pairs={{0,2},{2,0},{4,6},{6,4},{1,3},{3,1},{5,7},{7,5},{8,10},{10,8},{12,... | collective-permute-start | bytes 49160 | tf_op jit(solution)/shard_map/ppermute | solution.py:456
  75.7 5.0 %collective-permute-start.14 = (f32[32,128]{1,0:T(8,128)S(1)}, f32[32,128]{1,0:T(8,128)S(1)}, u32[]{:S(2)}, u32[]{:S(2)}) collective-permute-start(f32[32,128]{1,0:T(8,128)S(1)} %add_add_fusion.5), channel_id=1, source_target_pairs={{0,24},{8,16},{16,8},{24,0},{1,25},{9,17},{17,9},{25,1},{2,26},{10... | collective-permute-start | bytes 49160 | tf_op jit(solution)/shard_map/ppermute | solution.py:456
  75.8 5.3 %collective-permute-start.13 = (f32[32,128]{1,0:T(8,128)S(1)}, f32[32,128]{1,0:T(8,128)S(1)}, u32[]{:S(2)}, u32[]{:S(2)}) collective-permute-start(f32[32,128]{1,0:T(8,128)S(1)} %add_add_fusion.5), channel_id=1, source_target_pairs={{0,16},{8,24},{16,0},{24,8},{1,17},{9,25},{17,1},{25,9},{2,18},{10... | collective-permute-start | bytes 49160 | tf_op jit(solution)/shard_map/ppermute | solution.py:456
  75.9 5.9 %collective-permute-start.12 = (f32[32,128]{1,0:T(8,128)S(1)}, f32[32,128]{1,0:T(8,128)S(1)}, u32[]{:S(2)}, u32[]{:S(2)}) collective-permute-start(f32[32,128]{1,0:T(8,128)S(1)} %add_add_fusion.5), channel_id=1, source_target_pairs={{0,8},{8,0},{16,24},{24,16},{1,9},{9,1},{17,25},{25,17},{2,10},{10... | collective-permute-start | bytes 49160 | tf_op jit(solution)/shard_map/ppermute | solution.py:456
  81.7 5.0 %collective-permute-start.17 = (f32[32,128]{1,0:T(8,128)S(1)}, f32[32,128]{1,0:T(8,128)S(1)}, u32[]{:S(2)}, u32[]{:S(2)}) collective-permute-start(f32[32,128]{1,0:T(8,128)S(1)} %add_add_fusion.4), channel_id=1, source_target_pairs={{0,96},{32,64},{64,32},{96,0},{1,97},{33,65},{65,33},{97,1},{2,98}... | collective-permute-start | bytes 49160 | tf_op jit(solution)/shard_map/ppermute | solution.py:456
  83.5 5.2 %collective-permute-start.16 = (f32[32,128]{1,0:T(8,128)S(1)}, f32[32,128]{1,0:T(8,128)S(1)}, u32[]{:S(2)}, u32[]{:S(2)}) collective-permute-start(f32[32,128]{1,0:T(8,128)S(1)} %add_add_fusion.4), channel_id=1, source_target_pairs={{0,64},{32,96},{64,0},{96,32},{1,65},{33,97},{65,1},{97,33},{2,66}... | collective-permute-start | bytes 49160 | tf_op jit(solution)/shard_map/ppermute | solution.py:456
  84.5 4.3 %collective-permute-start.15 = (f32[32,128]{1,0:T(8,128)S(1)}, f32[32,128]{1,0:T(8,128)S(1)}, u32[]{:S(2)}, u32[]{:S(2)}) collective-permute-start(f32[32,128]{1,0:T(8,128)S(1)} %add_add_fusion.4), channel_id=1, source_target_pairs={{0,32},{32,0},{64,96},{96,64},{1,33},{33,1},{65,97},{97,65},{2,34}... | collective-permute-start | bytes 49160 | tf_op jit(solution)/shard_map/ppermute | solution.py:456
  88.8 27.9 %copy-start.1 = (f32[32,4,8,128]{3,2,1,0:T(8,128)S(1)}, f32[32,4,8,128]{3,2,1,0:T(8,128)}, u32[]{:S(2)}) copy-start(f32[32,4,8,128]{3,2,1,0:T(8,128)} %param.10) | copy-start | bytes 1572868
  97.4 1.3 %collective-permute-start.18 = (f32[32,128]{1,0:T(8,128)S(1)}, f32[32,128]{1,0:T(8,128)S(1)}, u32[]{:S(2)}, u32[]{:S(2)}) collective-permute-start(f32[32,128]{1,0:T(8,128)S(1)} %get-tuple-element.64), channel_id=1, source_target_pairs={{0,1},{1,0},{2,3},{3,2},{4,5},{5,4},{6,7},{7,6},{8,9},{9,8},{10,11... | collective-permute-start | bytes 49160 | tf_op jit(solution)/shard_map/ppermute | solution.py:453
  98.6 5.0 %collective-permute-start.21 = (f32[32,128]{1,0:T(8,128)S(1)}, f32[32,128]{1,0:T(8,128)S(1)}, u32[]{:S(2)}, u32[]{:S(2)}) collective-permute-start(f32[32,128]{1,0:T(8,128)S(1)} %add.78), channel_id=1, source_target_pairs={{0,6},{2,4},{4,2},{6,0},{1,7},{3,5},{5,3},{7,1},{8,14},{10,12},{12... | collective-permute-start | bytes 49160 | tf_op jit(solution)/shard_map/ppermute | solution.py:456
  99.5 5.2 %collective-permute-start.20 = (f32[32,128]{1,0:T(8,128)S(1)}, f32[32,128]{1,0:T(8,128)S(1)}, u32[]{:S(2)}, u32[]{:S(2)}) collective-permute-start(f32[32,128]{1,0:T(8,128)S(1)} %add.78), channel_id=1, source_target_pairs={{0,4},{2,6},{4,0},{6,2},{1,5},{3,7},{5,1},{7,3},{8,12},{10,14},{12... | collective-permute-start | bytes 49160 | tf_op jit(solution)/shard_map/ppermute | solution.py:456
  100.9 3.8 %collective-permute-start.19 = (f32[32,128]{1,0:T(8,128)S(1)}, f32[32,128]{1,0:T(8,128)S(1)}, u32[]{:S(2)}, u32[]{:S(2)}) collective-permute-start(f32[32,128]{1,0:T(8,128)S(1)} %add.78), channel_id=1, source_target_pairs={{0,2},{2,0},{4,6},{6,4},{1,3},{3,1},{5,7},{7,5},{8,10},{10,8},{12,... | collective-permute-start | bytes 49160 | tf_op jit(solution)/shard_map/ppermute | solution.py:456
  104.8 5.0 %collective-permute-start.24 = (f32[32,128]{1,0:T(8,128)S(1)}, f32[32,128]{1,0:T(8,128)S(1)}, u32[]{:S(2)}, u32[]{:S(2)}) collective-permute-start(f32[32,128]{1,0:T(8,128)S(1)} %add_add_fusion.2), channel_id=1, source_target_pairs={{0,24},{8,16},{16,8},{24,0},{1,25},{9,17},{17,9},{25,1},{2,26},{10... | collective-permute-start | bytes 49160 | tf_op jit(solution)/shard_map/ppermute | solution.py:456
  107.3 5.2 %collective-permute-start.23 = (f32[32,128]{1,0:T(8,128)S(1)}, f32[32,128]{1,0:T(8,128)S(1)}, u32[]{:S(2)}, u32[]{:S(2)}) collective-permute-start(f32[32,128]{1,0:T(8,128)S(1)} %add_add_fusion.2), channel_id=1, source_target_pairs={{0,16},{8,24},{16,0},{24,8},{1,17},{9,25},{17,1},{25,9},{2,18},{10... | collective-permute-start | bytes 49160 | tf_op jit(solution)/shard_map/ppermute | solution.py:456
  108.7 3.8 %collective-permute-start.22 = (f32[32,128]{1,0:T(8,128)S(1)}, f32[32,128]{1,0:T(8,128)S(1)}, u32[]{:S(2)}, u32[]{:S(2)}) collective-permute-start(f32[32,128]{1,0:T(8,128)S(1)} %add_add_fusion.2), channel_id=1, source_target_pairs={{0,8},{8,0},{16,24},{24,16},{1,9},{9,1},{17,25},{25,17},{2,10},{10... | collective-permute-start | bytes 49160 | tf_op jit(solution)/shard_map/ppermute | solution.py:456
  112.5 5.4 %collective-permute-start.27 = (f32[32,128]{1,0:T(8,128)S(1)}, f32[32,128]{1,0:T(8,128)S(1)}, u32[]{:S(2)}, u32[]{:S(2)}) collective-permute-start(f32[32,128]{1,0:T(8,128)S(1)} %add_add_fusion.1), channel_id=1, source_target_pairs={{0,96},{32,64},{64,32},{96,0},{1,97},{33,65},{65,33},{97,1},{2,98}... | collective-permute-start | bytes 49160 | tf_op jit(solution)/shard_map/ppermute | solution.py:456
  114.1 5.2 %collective-permute-start.26 = (f32[32,128]{1,0:T(8,128)S(1)}, f32[32,128]{1,0:T(8,128)S(1)}, u32[]{:S(2)}, u32[]{:S(2)}) collective-permute-start(f32[32,128]{1,0:T(8,128)S(1)} %add_add_fusion.1), channel_id=1, source_target_pairs={{0,64},{32,96},{64,0},{96,32},{1,65},{33,97},{65,1},{97,33},{2,66}... | collective-permute-start | bytes 49160 | tf_op jit(solution)/shard_map/ppermute | solution.py:456
  115.5 3.9 %collective-permute-start.25 = (f32[32,128]{1,0:T(8,128)S(1)}, f32[32,128]{1,0:T(8,128)S(1)}, u32[]{:S(2)}, u32[]{:S(2)}) collective-permute-start(f32[32,128]{1,0:T(8,128)S(1)} %add_add_fusion.1), channel_id=1, source_target_pairs={{0,32},{32,0},{64,96},{96,64},{1,33},{33,1},{65,97},{97,65},{2,34}... | collective-permute-start | bytes 49160 | tf_op jit(solution)/shard_map/ppermute | solution.py:456

commit v6 on v5

--- a/solution.py
+++ b/solution.py
@@ -97,7 +97,7 @@
             last_out[x - 1] = row
 
 
-def place_slots(codes, amps, out, acc):
+def place_slots(listed, amps, out, acc):
     acc[...] = jnp.zeros_like(acc)
     lane = iota((128, 256), 1)
     before = ((iota((128, 256), 0) < lane) | (lane >= 128)).astype(F32).astype(BF16)
@@ -105,10 +105,11 @@
 
     def chunk(turn, seen):
         at = pl.ds(pl.multiple_of(turn * 8, 8), 8)
-        code = codes[at, :]
-        tiles = code >> 16
+        tiles = listed[at, :]
+        cells = listed[pl.ds(pl.multiple_of(64 + turn * 8, 8), 8), :]
+        code = cells * 64 + listed[pl.ds(pl.multiple_of(128 + turn * 8, 8), 8), :]
         parts = list(split2(amps[at, :]))
-        parts.append(((code >> 8) & 255).astype(F32).astype(BF16))
+        parts.append((code >> 8).astype(F32).astype(BF16))
         parts.append((code & 255).astype(F32).astype(BF16))
         hits = [
             (tile_line == tiles[j : j + 1, :]).astype(F32) for j in range(8)
@@ -225,7 +226,10 @@
 
 def coefficients(gram):
     lane, row = iota((32, 128), 1), iota((32, 128), 0)
-    packed = gram[...]
+    sums = [gram[n] for n in range(gram.shape[0])]
+    while len(sums) > 1:
+        sums = [a + b for a, b in zip(sums[::2], sums[1::2])]
+    packed = sums[0]
     flipped = jnp.concatenate([packed, jnp.zeros((96, 128), F32)], axis=0).T
     bases = []
     for k in range(3):
@@ -449,14 +453,15 @@
     return from_low, lax.ppermute(to_low, axis, [(b, a) for a, b in up])
 
 
-def everywhere(x):
+def everywhere(x, beside=()):
     x = x + lax.ppermute(x, "gy_1", [(0, 1), (1, 0)])
-    for axis in ("gy_0", "gx_1", "gx_0"):
-        one, two, three = [
-            lax.ppermute(x, axis, [(i, i ^ k) for i in range(4)]) for k in (1, 2, 3)
-        ]
-        x = (x + one) + (two + three)
-    return x
+    one, two, three = [
+        lax.ppermute(x, "gy_0", [(i, i ^ k) for i in range(4)]) for k in (1, 2, 3)
+    ]
+    x = (x + one) + (two + three)
+    x, beside = lax.optimization_barrier((x, beside))
+    x = jnp.broadcast_to(x[None], (lax.axis_size(GX),) + x.shape)
+    return lax.all_to_all(x, GX, split_axis=0, concat_axis=0, tiled=True), beside
 
 
 def exchange(slots):
@@ -472,9 +477,12 @@
         [volts.reshape(1024, 128), coefs],
     )
     y_low, y_high = neighbours(y_low, y_high, GY)
-    codes = (placement.reshape(-1) * 65536 + cells * 64 + wave_ids).reshape(64, 128)
+    listed = [a.reshape(64, 128) for a in (placement, cells, wave_ids)]
     (slots,) = call(
-        place_slots, [(128, 2, 128)], [codes, amps.reshape(64, 128)], [vmem((512, 128), F32)]
+        place_slots,
+        [(128, 2, 128)],
+        [jnp.concatenate(listed, axis=0), amps.reshape(64, 128)],
+        [vmem((512, 128), F32)],
     )
     y_low, y_high, slots = lax.optimization_barrier((y_low, y_high, slots))
     x_low, x_high = call(pack_rows, [(7, 168, 128)] * 2, [v, c, y_low, y_high])
@@ -498,15 +506,17 @@
         [wide] * 5 + [(32, 128)],
         [diag, wx, wy, wv, free, inj, i_low, i_high, ix_low, ix_high],
     )
+    gram, _ = everywhere(gram)
     step, *basis, gram = call(
         second_basis,
         [wide] * 5 + [(32, 128)],
-        [everywhere(gram), diag, wx, wy, wv, cap] + kept,
+        [gram, diag, wx, wy, wv, cap] + kept,
     )
     so_far = call(
         from_lanes, [(1024, 128)] * 2, [step, basis[0], volts.reshape(1024, 128)]
     )
-    outs = call(finish, [(1024, 128)] * 2, [everywhere(gram)] + basis + list(so_far))
+    gram, so_far = everywhere(gram, so_far)
+    outs = call(finish, [(1024, 128)] * 2, [gram] + basis + list(so_far))
     return tuple(o.reshape(volts.shape) for o in outs)
 
 

time: 125 us -> 120 us (0.960)
  blocking collectives: 17.2 us -> 40.6 us
  starting transfers between devices: 42.4 us -> 25.7 us
  waiting for transfers between devices: 19.4 us -> 8.54 us
    all_to_all x0 -> x2, blocking collectives: none -> 23.3 us  [everywhere(): lax.all_to_all(x, GX, split_axis=0, concat_axis=0, tiled=True)]
    ppermute x18 -> x6, starting transfers between devices: 24.9 us -> 8.19 us  [everywhere(): lax.ppermute(x, 'gy_0', [(i, i ^ k) for i in range(4)])]
    ppermute x18 -> x6, waiting for transfers between devices: 15.4 us -> 4.58 us  [everywhere(): lax.ppermute(x, 'gy_0', [(i, i ^ k) for i in range(4)])]
  transfers between devices with their start and end apart: 28 -> 16, of which waited for: 15 -> 6; matrix products, arithmetic and copies ran while one was open for 1% -> 1% of each run, Pallas kernels for 16% -> 17%
where the time goes in v6:
time: 120 us; the launch traced here: 119 us
  blocking collectives  40.6 us (34%)
  Pallas kernels  40.2 us (34%)
  starting transfers between devices  25.7 us (21%)
  waiting for transfers between devices  8.54 us (7%)
  local copies, waits for them, and re-layouts  1.84 us (2%)
  other arithmetic  1.6 us (1%)
    pallas_call x10, Pallas kernels, call(): pl.pallas_call(kernel, out_shape=tuple(outs), scratch_shapes=list(scratch...  40.2 us
    all_to_all x2, blocking collectives, everywhere(): lax.all_to_all(x, GX, split_axis=0, concat_axis=0, tiled=True)  23.3 us
    all_to_all x1, blocking collectives, exchange(): return lax.all_to_all(slots, GX_GY, split_axis=0, concat_axis=0, tiled=True)  17.2 us
    ppermute x4, starting transfers between devices, neighbours(): return (from_low, lax.ppermute(to_low, axis, [(b, a) for a, b in up]))  14.3 us
    ppermute x6, starting transfers between devices, everywhere(): lax.ppermute(x, 'gy_0', [(i, i ^ k) for i in range(4)])  8.19 us
    ppermute x6, waiting for transfers between devices, everywhere(): lax.ppermute(x, 'gy_0', [(i, i ^ k) for i in range(4)])  4.58 us
    ppermute x4, starting transfers between devices, neighbours(): from_low = lax.ppermute(to_high, axis, up)  3.04 us
  transfers between devices with their start and end apart: 16, of which 6 were waited for; matrix products, arithmetic and copies ran while one was open for 1% of the time, Pallas kernels for 17%

profile of v6, /device:TPU:0, one launch (start us, length us, event | category | flops | bytes accessed | tf_op | source)
XLA Modules:
  0.0 119.3 jit_solution(305460268432668255)
XLA Ops:
  0.6 0.8 pad_maximum_fusion.stack
  1.4 1.0 copy-done
  2.5 0.4 to_lanes.1
  2.9 3.6 %collective-permute-start.1 = (f32[128,128]{1,0:T(8,128)S(1)}, f32[128,128]{1,0:T(8,128)S(1)}, u32[]{:S(2)}, u32[]{:S(2)}) collective-permute-start(f32[128,128]{1,0:T(8,128)S(1)} %get-tuple-element.44), channel_id=1, source_target_pairs={{1,0},{2,1},{3,2},{4,3},{5,4},{6,5},{7,6},{0,7},{9,8},{10,9},{11,1... | collective-permute-start | bytes 196616 | tf_op jit(solution)/shard_map/ppermute | solution.py:453
  6.4 0.8 pad_add_fusion.listed
  7.2 0.8 copy-done.3
  8.0 5.3 %place_slots.1 = f32[128,2,128]{2,1,0:T(2,128)S(1)} custom-call(s32[192,128]{1,0:T(8,128)S(1)} %pad_add_fusion.listed, f32[64,128]{1,0:T(8,128)S(1)} %bitcast.13), custom_call_target="tpu_custom_call" | custom-call | tf_op jit(solution)/shard_map/place_slots/pallas_call | solution.py:52
  13.5 1.6 %collective-permute-start.2 = (f32[7,168,128]{2,1,0:T(8,128)S(1)}, f32[7,168,128]{2,1,0:T(8,128)S(1)}, u32[]{:S(2)}, u32[]{:S(2)}) collective-permute-start(f32[7,168,128]{2,1,0:T(8,128)S(1)} %get-tuple-element.47), channel_id=1, source_target_pairs={{0,8},{8,16},{16,24},{24,32},{32,40},{40,48},{48,56},{56,64},{64,7... | collective-permute-start | bytes 1806344 | tf_op jit(solution)/shard_map/ppermute | solution.py:452
  15.2 3.8 %collective-permute-start.3 = (f32[7,168,128]{2,1,0:T(8,128)S(1)}, f32[7,168,128]{2,1,0:T(8,128)S(1)}, u32[]{:S(2)}, u32[]{:S(2)}) collective-permute-start(f32[7,168,128]{2,1,0:T(8,128)S(1)} %get-tuple-element.48), channel_id=1, source_target_pairs={{8,0},{16,8},{24,16},{32,24},{40,32},{48,40},{56,48},{64,56},{72,6... | collective-permute-start | bytes 1806344 | tf_op jit(solution)/shard_map/ppermute | solution.py:453
  19.0 17.2 %all_to_all.15.slots = f32[128,2,128]{2,1,0:T(2,128)S(1)} all-to-all(f32[128,2,128]{2,1,0:T(2,128)S(1)} %place_slots.1), channel_id=1, replica_groups=mesh['gx_0'=4,'gx_1'=4,'gy_0'=4,'gy_1'=2] {'gx_0','gx_1','gy_0','gy_1'}, dimensions={0} | all-to-all | bytes 262144 | tf_op jit(solution)/shard_map/all_to_all | solution.py:468
  36.2 6.3 %add_currents.1 = (f32[8,128,128]{2,1,0:T(8,128)S(1)}, f32[64,128]{1,0:T(8,128)S(1)}, f32[64,128]{1,0:T(8,128)S(1)}) custom-call(f32[128,2,128]{2,1,0:T(2,128)S(1)} %all_to_all.15.slots, f32[64,64]{1,0:T(8,128)S(1)} %copy-done.2), custom_call_target="tpu_custom_call" | custom-call | tf_op jit(solution)/shard_map/add_currents/pallas_call | solution.py:52
  42.6 2.9 %collective-permute-start.5 = (f32[64,128]{1,0:T(8,128)S(1)}, f32[64,128]{1,0:T(8,128)S(1)}, u32[]{:S(2)}, u32[]{:S(2)}) collective-permute-start(f32[64,128]{1,0:T(8,128)S(1)} %get-tuple-element.57), channel_id=1, source_target_pairs={{1,0},{2,1},{3,2},{4,3},{5,4},{6,5},{7,6},{0,7},{9,8},{10,9},{11,1... | collective-permute-start | bytes 98312 | tf_op jit(solution)/shard_map/ppermute | solution.py:453
  45.5 1.6 %collective-permute-done.4.low.i_low = f32[64,128]{1,0:T(8,128)S(1)} collective-permute-done((f32[64,128]{1,0:T(8,128)S(1)}, f32[64,128]{1,0:T(8,128)S(1)}, u32[]{:S(2)}, u32[]{:S(2)}) %collective-permute-start.4) | collective-permute-done | bytes 32800 | tf_op jit(solution)/shard_map/ppermute | solution.py:452
  47.2 1.3 %collective-permute-start.6 = (f32[3,144,128]{2,1,0:T(8,128)S(1)}, f32[3,144,128]{2,1,0:T(8,128)S(1)}, u32[]{:S(2)}, u32[]{:S(2)}) collective-permute-start(f32[3,144,128]{2,1,0:T(8,128)S(1)} %get-tuple-element.58), channel_id=1, source_target_pairs={{0,8},{8,16},{16,24},{24,32},{32,40},{40,48},{48,56},{56,64},{64,7... | collective-permute-start | bytes 663560 | tf_op jit(solution)/shard_map/ppermute | solution.py:452
  48.5 4.1 %collective-permute-start.7 = (f32[3,144,128]{2,1,0:T(8,128)S(1)}, f32[3,144,128]{2,1,0:T(8,128)S(1)}, u32[]{:S(2)}, u32[]{:S(2)}) collective-permute-start(f32[3,144,128]{2,1,0:T(8,128)S(1)} %get-tuple-element.59), channel_id=1, source_target_pairs={{8,0},{16,8},{24,16},{32,24},{40,32},{48,40},{56,48},{64,56},{72,6... | collective-permute-start | bytes 663560 | tf_op jit(solution)/shard_map/ppermute | solution.py:453
  52.7 7.3 %grid_weights.1 = (f32[22,144,128]{2,1,0:T(8,128)S(1)}, f32[22,144,128]{2,1,0:T(8,128)S(1)}, f32[22,144,128]{2,1,0:T(8,128)S(1)}, f32[22,144,128]{2,1,0:T(8,128)...) custom-call(f32[8,128,128]{2,1,0:T(8,128)S(1)} %get-tuple-element.41.v, ...), custom_call_target="tpu_custom_call" | custom-call | tf_op jit(solution)/shard_map/grid_weights/pallas_call | solution.py:52
  60.0 5.7 %first_basis.1 = (f32[22,144,128]{2,1,0:T(8,128)S(1)}, f32[22,144,128]{2,1,0:T(8,128)S(1)}, f32[22,144,128]{2,1,0:T(8,128)S(1)}, f32[22,144,128]{2,1,0:T(8,128)S...) custom-call(f32[22,144,128]{2,1,0:T(8,128)S(1)} %get-tuple-element.49.diag, ...), custom_call_target="tpu_custom_call" | custom-call | tf_op jit(solution)/shard_map/first_basis/pallas_call | solution.py:52
  65.8 1.2 collective-permute-done.8
  66.9 2.6 %collective-permute-start.11 = (f32[32,128]{1,0:T(8,128)S(1)}, f32[32,128]{1,0:T(8,128)S(1)}, u32[]{:S(2)}, u32[]{:S(2)}) collective-permute-start(f32[32,128]{1,0:T(8,128)S(1)} %add.24), channel_id=1, source_target_pairs={{0,6},{2,4},{4,2},{6,0},{1,7},{3,5},{5,3},{7,1},{8,14},{10,12},{12... | collective-permute-start | bytes 49160 | tf_op jit(solution)/shard_map/ppermute | solution.py:459
  69.5 1.5 %collective-permute-start.9 = (f32[32,128]{1,0:T(8,128)S(1)}, f32[32,128]{1,0:T(8,128)S(1)}, u32[]{:S(2)}, u32[]{:S(2)}) collective-permute-start(f32[32,128]{1,0:T(8,128)S(1)} %add.24), channel_id=1, source_target_pairs={{0,2},{2,0},{4,6},{6,4},{1,3},{3,1},{5,7},{7,5},{8,10},{10,8},{12,... | collective-permute-start | bytes 49160 | tf_op jit(solution)/shard_map/ppermute | solution.py:459
  71.0 0.9 collective-permute-done.11
  71.9 2.9 %collective-permute-done.10 = f32[32,128]{1,0:T(8,128)S(1)} collective-permute-done((f32[32,128]{1,0:T(8,128)S(1)}, f32[32,128]{1,0:T(8,128)S(1)}, u32[]{:S(2)}, u32[]{:S(2)}) %collective-permute-start.10) | collective-permute-done | bytes 16416 | tf_op jit(solution)/shard_map/ppermute | solution.py:459
  74.8 11.4 %all_to_all.16.gram = f32[16,32,128]{2,1,0:T(8,128)S(1)} all-to-all(f32[16,32,128]{2,1,0:T(8,128)S(1)} %broadcast_in_dim.4), channel_id=1, replica_groups=mesh['gx_0'=4,'gx_1'=4,'gy_0'=4,'gy_1'=2] {'gx_0','gx_1'}, dimensions={0} | all-to-all | bytes 524288 | tf_op jit(solution)/shard_map/all_to_all | solution.py:464
  86.2 8.5 %second_basis.1 = (f32[22,144,128]{2,1,0:T(8,128)S(1)}, f32[22,144,128]{2,1,0:T(8,128)S(1)}, f32[22,144,128]{2,1,0:T(8,128)S(1)}, f32[22,144,128]{2,1,0:T(8,128)...) custom-call(f32[16,32,128]{2,1,0:T(8,128)S(1)} %all_to_all.16.gram, ...), custom_call_target="tpu_custom_call" | custom-call | tf_op jit(solution)/shard_map/second_basis/pallas_call | solution.py:52
  94.8 1.2 collective-permute-done.12
  96.0 1.0 collective-permute-start.15
  97.0 1.4 %collective-permute-start.14 = (f32[32,128]{1,0:T(8,128)S(1)}, f32[32,128]{1,0:T(8,128)S(1)}, u32[]{:S(2)}, u32[]{:S(2)}) collective-permute-start(f32[32,128]{1,0:T(8,128)S(1)} %add.28), channel_id=1, source_target_pairs={{0,4},{2,6},{4,0},{6,2},{1,5},{3,7},{5,1},{7,3},{8,12},{10,14},{12... | collective-permute-start | bytes 49160 | tf_op jit(solution)/shard_map/ppermute | solution.py:459
  98.4 1.7 %collective-permute-start.13 = (f32[32,128]{1,0:T(8,128)S(1)}, f32[32,128]{1,0:T(8,128)S(1)}, u32[]{:S(2)}, u32[]{:S(2)}) collective-permute-start(f32[32,128]{1,0:T(8,128)S(1)} %add.28), channel_id=1, source_target_pairs={{0,2},{2,0},{4,6},{6,4},{1,3},{3,1},{5,7},{7,5},{8,10},{10,8},{12,... | collective-permute-start | bytes 49160 | tf_op jit(solution)/shard_map/ppermute | solution.py:459
  100.1 1.2 %from_lanes.1 = (f32[1024,128]{1,0:T(8,128)S(1)}, f32[1024,128]{1,0:T(8,128)S(1)}) custom-call(f32[22,144,128]{2,1,0:T(8,128)S(1)} %get-tuple-element.68.step, f32[22,144,128]{2,1,0:T(8,128)S(1)} %get-tuple-element.69.b0, f32[1024,128]{1,0:T(8,128)S(1)} %bitcast.12), custom_call_target="tpu_custom_call" | custom-call | tf_op jit(solution)/shard_map/from_lanes/pallas_call | solution.py:52
  101.3 0.9 collective-permute-done.14
  102.3 11.9 %all_to_all.17.gram = f32[16,32,128]{2,1,0:T(8,128)S(1)} all-to-all(f32[16,32,128]{2,1,0:T(8,128)S(1)} %broadcast_in_dim.5), channel_id=1, replica_groups=mesh['gx_0'=4,'gx_1'=4,'gy_0'=4,'gy_1'=2] {'gx_0','gx_1'}, dimensions={0} | all-to-all | bytes 524288 | tf_op jit(solution)/shard_map/all_to_all | solution.py:464
  114.2 5.1 %finish.1 = (f32[1024,128]{1,0:T(8,128)}, f32[1024,128]{1,0:T(8,128)}) custom-call(f32[16,32,128]{2,1,0:T(8,128)S(1)} %all_to_all.17.gram, f32[22,144,128]{2,1,0:T(8,128)S(1)} %get-tuple-element.69.b0, f32[22,144,128]{2,1,0:T(8,128)S(1)} %get-tuple-element.73.b1, f32[22,144,128]{2,1,0:T(8,128)S(1)} %get-tuple-element.74.b2, ...), custom_call_target="tpu_custom_call" | custom-call | tf_op jit(solution)/shard_map/finish/pallas_call | solution.py:52
  (29 shorter events, 0.8 us)
Async XLA Ops:
  0.6 35.5 %copy-start.2 = (f32[64,64]{1,0:T(8,128)S(1)}, f32[64,64]{1,0:T(8,128)}, u32[]{:S(2)}) copy-start(f32[64,64]{1,0:T(8,128)} %waves.1) | copy-start | bytes 49156
  1.4 1.0 copy-start
  2.9 10.4 %collective-permute-start = (f32[128,128]{1,0:T(8,128)S(1)}, f32[128,128]{1,0:T(8,128)S(1)}, u32[]{:S(2)}, u32[]{:S(2)}) collective-permute-start(f32[128,128]{1,0:T(8,128)S(1)} %get-tuple-element.43), channel_id=1, source_target_pairs={{0,1},{1,2},{2,3},{3,4},{4,5},{5,6},{6,7},{7,0},{8,9},{9,10},{10,1... | collective-permute-start | bytes 196616 | tf_op jit(solution)/shard_map/ppermute | solution.py:452
  2.9 10.4 %collective-permute-start.1 = (f32[128,128]{1,0:T(8,128)S(1)}, f32[128,128]{1,0:T(8,128)S(1)}, u32[]{:S(2)}, u32[]{:S(2)}) collective-permute-start(f32[128,128]{1,0:T(8,128)S(1)} %get-tuple-element.44), channel_id=1, source_target_pairs={{1,0},{2,1},{3,2},{4,3},{5,4},{6,5},{7,6},{0,7},{9,8},{10,9},{11,1... | collective-permute-start | bytes 196616 | tf_op jit(solution)/shard_map/ppermute | solution.py:453
  7.2 0.8 copy-start.3
  13.5 39.1 %collective-permute-start.2 = (f32[7,168,128]{2,1,0:T(8,128)S(1)}, f32[7,168,128]{2,1,0:T(8,128)S(1)}, u32[]{:S(2)}, u32[]{:S(2)}) collective-permute-start(f32[7,168,128]{2,1,0:T(8,128)S(1)} %get-tuple-element.47), channel_id=1, source_target_pairs={{0,8},{8,16},{16,24},{24,32},{32,40},{40,48},{48,56},{56,64},{64,7... | collective-permute-start | bytes 1806344 | tf_op jit(solution)/shard_map/ppermute | solution.py:452
  15.2 37.5 %collective-permute-start.3 = (f32[7,168,128]{2,1,0:T(8,128)S(1)}, f32[7,168,128]{2,1,0:T(8,128)S(1)}, u32[]{:S(2)}, u32[]{:S(2)}) collective-permute-start(f32[7,168,128]{2,1,0:T(8,128)S(1)} %get-tuple-element.48), channel_id=1, source_target_pairs={{8,0},{16,8},{24,16},{32,24},{40,32},{48,40},{56,48},{64,56},{72,6... | collective-permute-start | bytes 1806344 | tf_op jit(solution)/shard_map/ppermute | solution.py:453
  42.5 4.6 %collective-permute-start.4 = (f32[64,128]{1,0:T(8,128)S(1)}, f32[64,128]{1,0:T(8,128)S(1)}, u32[]{:S(2)}, u32[]{:S(2)}) collective-permute-start(f32[64,128]{1,0:T(8,128)S(1)} %get-tuple-element.56), channel_id=1, source_target_pairs={{0,1},{1,2},{2,3},{3,4},{4,5},{5,6},{6,7},{7,0},{8,9},{9,10},{10,1... | collective-permute-start | bytes 98312 | tf_op jit(solution)/shard_map/ppermute | solution.py:452
  42.6 4.5 %collective-permute-start.5 = (f32[64,128]{1,0:T(8,128)S(1)}, f32[64,128]{1,0:T(8,128)S(1)}, u32[]{:S(2)}, u32[]{:S(2)}) collective-permute-start(f32[64,128]{1,0:T(8,128)S(1)} %get-tuple-element.57), channel_id=1, source_target_pairs={{1,0},{2,1},{3,2},{4,3},{5,4},{6,5},{7,6},{0,7},{9,8},{10,9},{11,1... | collective-permute-start | bytes 98312 | tf_op jit(solution)/shard_map/ppermute | solution.py:453
  47.2 12.8 %collective-permute-start.6 = (f32[3,144,128]{2,1,0:T(8,128)S(1)}, f32[3,144,128]{2,1,0:T(8,128)S(1)}, u32[]{:S(2)}, u32[]{:S(2)}) collective-permute-start(f32[3,144,128]{2,1,0:T(8,128)S(1)} %get-tuple-element.58), channel_id=1, source_target_pairs={{0,8},{8,16},{16,24},{24,32},{32,40},{40,48},{48,56},{56,64},{64,7... | collective-permute-start | bytes 663560 | tf_op jit(solution)/shard_map/ppermute | solution.py:452
  48.5 11.5 %collective-permute-start.7 = (f32[3,144,128]{2,1,0:T(8,128)S(1)}, f32[3,144,128]{2,1,0:T(8,128)S(1)}, u32[]{:S(2)}, u32[]{:S(2)}) collective-permute-start(f32[3,144,128]{2,1,0:T(8,128)S(1)} %get-tuple-element.59), channel_id=1, source_target_pairs={{8,0},{16,8},{24,16},{32,24},{40,32},{48,40},{56,48},{64,56},{72,6... | collective-permute-start | bytes 663560 | tf_op jit(solution)/shard_map/ppermute | solution.py:453
  65.7 1.3 %collective-permute-start.8 = (f32[32,128]{1,0:T(8,128)S(1)}, f32[32,128]{1,0:T(8,128)S(1)}, u32[]{:S(2)}, u32[]{:S(2)}) collective-permute-start(f32[32,128]{1,0:T(8,128)S(1)} %get-tuple-element.60), channel_id=1, source_target_pairs={{0,1},{1,0},{2,3},{3,2},{4,5},{5,4},{6,7},{7,6},{8,9},{9,8},{10,11... | collective-permute-start | bytes 49160 | tf_op jit(solution)/shard_map/ppermute | solution.py:457
  66.9 4.9 %collective-permute-start.11 = (f32[32,128]{1,0:T(8,128)S(1)}, f32[32,128]{1,0:T(8,128)S(1)}, u32[]{:S(2)}, u32[]{:S(2)}) collective-permute-start(f32[32,128]{1,0:T(8,128)S(1)} %add.24), channel_id=1, source_target_pairs={{0,6},{2,4},{4,2},{6,0},{1,7},{3,5},{5,3},{7,1},{8,14},{10,12},{12... | collective-permute-start | bytes 49160 | tf_op jit(solution)/shard_map/ppermute | solution.py:459
  69.5 5.2 %collective-permute-start.10 = (f32[32,128]{1,0:T(8,128)S(1)}, f32[32,128]{1,0:T(8,128)S(1)}, u32[]{:S(2)}, u32[]{:S(2)}) collective-permute-start(f32[32,128]{1,0:T(8,128)S(1)} %add.24), channel_id=1, source_target_pairs={{0,4},{2,6},{4,0},{6,2},{1,5},{3,7},{5,1},{7,3},{8,12},{10,14},{12... | collective-permute-start | bytes 49160 | tf_op jit(solution)/shard_map/ppermute | solution.py:459
  69.5 5.2 %collective-permute-start.9 = (f32[32,128]{1,0:T(8,128)S(1)}, f32[32,128]{1,0:T(8,128)S(1)}, u32[]{:S(2)}, u32[]{:S(2)}) collective-permute-start(f32[32,128]{1,0:T(8,128)S(1)} %add.24), channel_id=1, source_target_pairs={{0,2},{2,0},{4,6},{6,4},{1,3},{3,1},{5,7},{7,5},{8,10},{10,8},{12,... | collective-permute-start | bytes 49160 | tf_op jit(solution)/shard_map/ppermute | solution.py:459
  86.2 13.9 %copy-start.1 = (f32[32,4,8,128]{3,2,1,0:T(8,128)S(1)}, f32[32,4,8,128]{3,2,1,0:T(8,128)}, u32[]{:S(2)}) copy-start(f32[32,4,8,128]{3,2,1,0:T(8,128)} %param.10) | copy-start | bytes 1572868
  94.7 1.3 %collective-permute-start.12 = (f32[32,128]{1,0:T(8,128)S(1)}, f32[32,128]{1,0:T(8,128)S(1)}, u32[]{:S(2)}, u32[]{:S(2)}) collective-permute-start(f32[32,128]{1,0:T(8,128)S(1)} %get-tuple-element.67), channel_id=1, source_target_pairs={{0,1},{1,0},{2,3},{3,2},{4,5},{5,4},{6,7},{7,6},{8,9},{9,8},{10,11... | collective-permute-start | bytes 49160 | tf_op jit(solution)/shard_map/ppermute | solution.py:457
  96.0 5.4 %collective-permute-start.15 = (f32[32,128]{1,0:T(8,128)S(1)}, f32[32,128]{1,0:T(8,128)S(1)}, u32[]{:S(2)}, u32[]{:S(2)}) collective-permute-start(f32[32,128]{1,0:T(8,128)S(1)} %add.28), channel_id=1, source_target_pairs={{0,6},{2,4},{4,2},{6,0},{1,7},{3,5},{5,3},{7,1},{8,14},{10,12},{12... | collective-permute-start | bytes 49160 | tf_op jit(solution)/shard_map/ppermute | solution.py:459
  97.0 5.2 %collective-permute-start.14 = (f32[32,128]{1,0:T(8,128)S(1)}, f32[32,128]{1,0:T(8,128)S(1)}, u32[]{:S(2)}, u32[]{:S(2)}) collective-permute-start(f32[32,128]{1,0:T(8,128)S(1)} %add.28), channel_id=1, source_target_pairs={{0,4},{2,6},{4,0},{6,2},{1,5},{3,7},{5,1},{7,3},{8,12},{10,14},{12... | collective-permute-start | bytes 49160 | tf_op jit(solution)/shard_map/ppermute | solution.py:459
  98.4 3.8 %collective-permute-start.13 = (f32[32,128]{1,0:T(8,128)S(1)}, f32[32,128]{1,0:T(8,128)S(1)}, u32[]{:S(2)}, u32[]{:S(2)}) collective-permute-start(f32[32,128]{1,0:T(8,128)S(1)} %add.28), channel_id=1, source_target_pairs={{0,2},{2,0},{4,6},{6,4},{1,3},{3,1},{5,7},{7,5},{8,10},{10,8},{12,... | collective-permute-start | bytes 49160 | tf_op jit(solution)/shard_map/ppermute | solution.py:459

commit v7 on v6

--- a/solution.py
+++ b/solution.py
@@ -11,7 +11,6 @@
 GX_GY = GX + GY
 F32 = jnp.float32
 BF16 = jnp.bfloat16
-HIGHEST = lax.Precision.HIGHEST
 SHIFT = 7.0
 SCALE = 7.0
 XE = 22
@@ -22,21 +21,13 @@
     return lax.broadcasted_iota(jnp.int32, shape, dim)
 
 
-def dot(a, b, dims, precision=None):
-    return lax.dot_general(
-        a, b, (dims, ((), ())), precision=precision, preferred_element_type=F32
-    )
+def dot(a, b, dims):
+    return lax.dot_general(a, b, (dims, ((), ())), preferred_element_type=F32)
 
 
 def split2(x):
     hi = x.astype(BF16)
     return hi, (x - hi.astype(F32)).astype(BF16)
-
-
-def dot_split(a, b, dims):
-    a_hi, a_lo = split2(a)
-    b_hi, b_lo = split2(b)
-    return dot(a_hi, b_hi, dims) + dot(a_hi, b_lo, dims) + dot(a_lo, b_hi, dims)
 
 
 def split3(x):
@@ -140,12 +131,12 @@
 def add_currents(slots, waves, out, low_out, high_out, acc):
     acc[...] = jnp.zeros_like(acc)
     table = jnp.concatenate([p.astype(F32) for p in split3(waves[...])], axis=1).astype(BF16)
-    wave_line = iota((64, 2048), 0).astype(F32).astype(BF16)
-    cell_line = iota((256, 2048), 0).astype(F32).astype(BF16)
+    wave_line = iota((64, 4096), 0).astype(F32).astype(BF16)
+    cell_line = iota((256, 4096), 0).astype(F32).astype(BF16)
     one, zero = jnp.ones((), BF16), jnp.zeros((), BF16)
 
     def chunk(turn, carry):
-        rows = [slots[turn * 16 + j] for j in range(16)]
+        rows = [slots[turn * 32 + j] for j in range(32)]
         amp = jnp.concatenate([r[0:1, :] for r in rows], axis=1)
         code = jnp.concatenate([r[1:2, :] for r in rows], axis=1).astype(jnp.int32)
         hit = jnp.where(wave_line == (code & 63).astype(F32).astype(BF16), one, zero)
@@ -158,7 +149,7 @@
         acc[...] += dot(left, jnp.concatenate(right, axis=0), ((1,), (1,)))
         return carry
 
-    lax.fori_loop(0, 8, chunk, 0, unroll=2)
+    lax.fori_loop(0, 4, chunk, 0, unroll=4)
     low_lanes = iota((256, 128), 1) < 64
     for r in range(4):
         half = acc[:, (r // 2) * 128 : (r // 2 + 1) * 128]
@@ -310,8 +301,7 @@
         cap[i] = wide[:, :128]
         wx[i] = wide[:, 128:256]
         wy[i] = wide[:, 256:384]
-        wv[i] = jnp.where(lane < 96, wide[:, 384:], 0.0)
-        diag[i] = wide[:, :128] + wide[:, 384:]
+        wv[i] = wide[:, 384:]
 
     def halo_row(j, ref, base, present):
         ext[base + j] = ref[j, :YE, :] * present
@@ -334,30 +324,24 @@
     lax.fori_loop(0, 8, own_row, 0, unroll=2)
     lax.fori_loop(0, 7, halo_rows, 0)
 
-    def diagonal(i, carry):
-        total = diag[i] + wx[i] + wx[i - 1] + wy[i] + pltpu.roll(wy[i], 1, 0)
-        total = total + pltpu.roll(wv[i], 32, 1)
-        diag[i] = (total - SHIFT) * (1.0 / SCALE)
-        return carry
-
-    lax.fori_loop(1, 21, diagonal, 0, unroll=2)
-
-    def edges(i, carry):
-        wx[i] = jnp.where(cap[i + 1] > 0, wx[i] * (1.0 / SCALE), 0.0)
-        wy[i] = jnp.where(pltpu.roll(cap[i], YE - 1, 0) > 0, wy[i] * (1.0 / SCALE), 0.0)
-        wv[i] = wv[i] * (1.0 / SCALE)
-        return carry
-
-    lax.fori_loop(0, 21, edges, 0, unroll=3)
-    weights = (diag, wx, wy, wv)
-
-
-    def start(i, carry):
-        e = ext[i]
-        free[i] = (cap[i] - SHIFT) * e - SCALE * apply_row(ext, i, *weights)
-        return carry
-
-    lax.fori_loop(1, 21, start, 0, unroll=2)
+    scale = 1.0 / SCALE
+
+    def edge_x(i):
+        wx[i] = jnp.where(cap[i + 1] > 0, wx[i] * scale, 0.0)
+
+    def weigh(i, carry):
+        own, raw_x, raw_y, raw_v = cap[i], wx[i], wy[i], wv[i]
+        edge_x(i)
+        wyi = jnp.where(pltpu.roll(own, YE - 1, 0) > 0, raw_y * scale, 0.0)
+        wvi = jnp.where(lane < 96, raw_v * scale, 0.0)
+        wy[i], wv[i] = wyi, wvi
+        total = (own + raw_x + raw_y + raw_v - SHIFT) * scale + wx[i - 1]
+        diag[i] = total + pltpu.roll(wyi, 1, 0) + pltpu.roll(wvi, 32, 1)
+        free[i] = (own - SHIFT) * ext[i] - SCALE * apply_row(ext, i, diag, wx, wy, wv)
+        return carry
+
+    edge_x(0)
+    lax.fori_loop(1, 21, weigh, 0, unroll=2)
 
 
 def first_basis(
@@ -393,15 +377,26 @@
     moments((v0, v1, v2, v3), gram, 7)
 
 
+def split_rows(v0, v1, v2, v3, hi_out, lo_out):
+    def row(i, carry):
+        for n, field in enumerate((v0, v1, v2, v3)):
+            at = slice(n * 128, (n + 1) * 128)
+            hi_out[i, :, at], lo_out[i, :, at] = split2(field[4 + i])
+        return carry
+
+    lax.fori_loop(0, 14, row, 0, unroll=2)
+
+
 def second_basis(
-    gram, diag, wx, wy, wv, cap, change, v0, v1, v2, v3, step, b0, b1, b2, b3, gram_out
+    gram, diag, wx, wy, wv, cap, change, v0, hi, lo, step, b0, b1, b2, b3, gram_out
 ):
     weights = (diag, wx, wy, wv)
-    mix = combination(gram)
+    mix_hi, mix_lo = split2(combination(gram))
+    across = ((1,), (0,))
 
     def row(i, carry):
-        fields = jnp.concatenate([v0[i], v1[i], v2[i], v3[i]], axis=1)
-        both = dot_split(fields, mix, ((1,), (0,)))
+        both = dot(hi[i - 4], mix_hi, across) + dot(hi[i - 4], mix_lo, across)
+        both = both + dot(lo[i - 4], mix_hi, across)
         moved = both[:, :128]
         step[i] = moved
         b0[i] = v0[i] + both[:, 128:] + cap[i] * moved + change[i]
@@ -423,27 +418,29 @@
     return jnp.concatenate([ref[pl.ds(l * 8 + x, 32, stride=32), :] for l in range(4)], axis=0)
 
 
-def from_lanes(step, b0, volts, volts_out, residual_out):
+def from_lanes(step, b0, b1, b2, b3, volts, volts_out, residual_out, hi_out, lo_out):
     for x in range(8):
-        store_rows(volts_out, x, load_rows(volts, x) + step[7 + x, 8:136, :].T)
-        store_rows(residual_out, x, b0[7 + x, 8:136, :].T)
-
-
-def finish(gram, b0, b1, b2, b3, volts, residual, volts_out, residual_out):
-    mix = combination(gram)
+        volts_out[x] = load_rows(volts, x) + step[7 + x, 8:136, :].T
+        for n, field in enumerate((b0, b1, b2, b3)):
+            rows = field[7 + x, 8:136, :].T
+            if n == 0:
+                residual_out[x] = rows
+            at = slice(n * 128, (n + 1) * 128)
+            hi_out[x, at, :], lo_out[x, at, :] = split2(rows)
+
+
+def finish(gram, hi, lo, volts, residual, volts_out, residual_out):
+    mix_hi, mix_lo = split2(combination(gram).T)
     for x in range(0, 8, 2):
-        fields = jnp.concatenate(
-            [
-                jnp.concatenate([b[7 + n, 8:136, :] for b in (b0, b1, b2, b3)], axis=1)
-                for n in (x, x + 1)
-            ],
-            axis=0,
-        )
-        both = dot_split(mix, fields, ((0,), (1,)))
+        field_hi = jnp.concatenate([hi[x], hi[x + 1]], axis=1)
+        field_lo = jnp.concatenate([lo[x], lo[x + 1]], axis=1)
+        across = ((1,), (0,))
+        both = dot(mix_hi, field_hi, across) + dot(mix_hi, field_lo, across)
+        both = both + dot(mix_lo, field_hi, across)
         for n in range(2):
             own = both[:, n * 128 : (n + 1) * 128]
-            store_rows(volts_out, x + n, load_rows(volts, x + n) + own[:128])
-            store_rows(residual_out, x + n, load_rows(residual, x + n) + own[128:])
+            store_rows(volts_out, x + n, volts[x + n] + own[:128])
+            store_rows(residual_out, x + n, residual[x + n] + own[128:])
 
 
 def neighbours(to_low, to_high, axis):
@@ -506,17 +503,23 @@
         [wide] * 5 + [(32, 128)],
         [diag, wx, wy, wv, free, inj, i_low, i_high, ix_low, ix_high],
     )
-    gram, _ = everywhere(gram)
+    change, *fields = kept
+    halves = [jax.ShapeDtypeStruct((14, YE, 512), BF16)] * 2
+    gram, (hi, lo) = everywhere(gram, call(split_rows, halves, fields))
     step, *basis, gram = call(
         second_basis,
         [wide] * 5 + [(32, 128)],
-        [gram, diag, wx, wy, wv, cap] + kept,
-    )
+        [gram, diag, wx, wy, wv, cap, change, fields[0], hi, lo],
+    )
+    halves = [jax.ShapeDtypeStruct((8, 512, 128), BF16)] * 2
     so_far = call(
-        from_lanes, [(1024, 128)] * 2, [step, basis[0], volts.reshape(1024, 128)]
+        from_lanes,
+        [(8, 128, 128)] * 2 + halves,
+        [step] + basis + [volts.reshape(1024, 128)],
     )
     gram, so_far = everywhere(gram, so_far)
-    outs = call(finish, [(1024, 128)] * 2, [gram] + basis + list(so_far))
+    volts_so_far, residual, hi, lo = so_far
+    outs = call(finish, [(1024, 128)] * 2, [gram, hi, lo, volts_so_far, residual])
     return tuple(o.reshape(volts.shape) for o in outs)
 
 

time: 120 us -> 118 us (0.983)
  Pallas kernels: 40.2 us -> 38 us
    pallas_call x10 -> x11, Pallas kernels: 40.2 us -> 38 us  [call(): pl.pallas_call(kernel, out_shape=tuple(outs), scratch_shapes=list(scratch...]
  transfers between devices with their start and end apart: 16 -> 16, of which waited for: 6 -> 7; matrix products, arithmetic and copies ran while one was open for 1% -> 1% of each run, Pallas kernels for 17% -> 16%
where the time goes in v7:
time: 118 us
  blocking collectives  40.6 us (34%)
  Pallas kernels  38 us (32%)
  starting transfers between devices  25.8 us (22%)
  waiting for transfers between devices  9.25 us (8%)
  local copies, waits for them, and re-layouts  1.84 us (2%)
  other arithmetic  1.6 us (1%)
    pallas_call x11, Pallas kernels, call(): pl.pallas_call(kernel, out_shape=tuple(outs), scratch_shapes=list(scratch...  38 us
    all_to_all x2, blocking collectives, everywhere(): lax.all_to_all(x, GX, split_axis=0, concat_axis=0, tiled=True)  23.4 us
    all_to_all x1, blocking collectives, exchange(): return lax.all_to_all(slots, GX_GY, split_axis=0, concat_axis=0, tiled=True)  17.2 us
    ppermute x4, starting transfers between devices, neighbours(): return (from_low, lax.ppermute(to_low, axis, [(b, a) for a, b in up]))  14.3 us
    ppermute x6, starting transfers between devices, everywhere(): lax.ppermute(x, 'gy_0', [(i, i ^ k) for i in range(4)])  8.19 us
    ppermute x6, waiting for transfers between devices, everywhere(): lax.ppermute(x, 'gy_0', [(i, i ^ k) for i in range(4)])  5.29 us
    ppermute x4, starting transfers between devices, neighbours(): from_low = lax.ppermute(to_high, axis, up)  3.05 us
  transfers between devices with their start and end apart: 16, of which 7 were waited for; matrix products, arithmetic and copies ran while one was open for 1% of the time, Pallas kernels for 16%

profile of v7, /device:TPU:0, one launch (start us, length us, event | category | flops | bytes accessed | tf_op | source)
XLA Modules:
  0.0 117.9 jit_solution(7042250692565018907)
XLA Ops:
  0.6 0.8 pad_maximum_fusion.stack
  1.4 1.0 copy-done
  2.5 0.4 to_lanes.1
  2.9 3.6 %collective-permute-start.1 = (f32[128,128]{1,0:T(8,128)S(1)}, f32[128,128]{1,0:T(8,128)S(1)}, u32[]{:S(2)}, u32[]{:S(2)}) collective-permute-start(f32[128,128]{1,0:T(8,128)S(1)} %get-tuple-element.53), channel_id=1, source_target_pairs={{1,0},{2,1},{3,2},{4,3},{5,4},{6,5},{7,6},{0,7},{9,8},{10,9},{11,1... | collective-permute-start | bytes 196616 | tf_op jit(solution)/shard_map/ppermute | solution.py:450
  6.4 0.8 pad_add_fusion.listed
  7.2 0.8 copy-done.3
  8.0 5.3 %place_slots.1 = f32[128,2,128]{2,1,0:T(2,128)S(1)} custom-call(s32[192,128]{1,0:T(8,128)S(1)} %pad_add_fusion.listed, f32[64,128]{1,0:T(8,128)S(1)} %bitcast.13), custom_call_target="tpu_custom_call" | custom-call | tf_op jit(solution)/shard_map/place_slots/pallas_call | solution.py:43
  13.5 1.6 %collective-permute-start.2 = (f32[7,168,128]{2,1,0:T(8,128)S(1)}, f32[7,168,128]{2,1,0:T(8,128)S(1)}, u32[]{:S(2)}, u32[]{:S(2)}) collective-permute-start(f32[7,168,128]{2,1,0:T(8,128)S(1)} %get-tuple-element.56), channel_id=1, source_target_pairs={{0,8},{8,16},{16,24},{24,32},{32,40},{40,48},{48,56},{56,64},{64,7... | collective-permute-start | bytes 1806344 | tf_op jit(solution)/shard_map/ppermute | solution.py:449
  15.2 3.8 %collective-permute-start.3 = (f32[7,168,128]{2,1,0:T(8,128)S(1)}, f32[7,168,128]{2,1,0:T(8,128)S(1)}, u32[]{:S(2)}, u32[]{:S(2)}) collective-permute-start(f32[7,168,128]{2,1,0:T(8,128)S(1)} %get-tuple-element.57), channel_id=1, source_target_pairs={{8,0},{16,8},{24,16},{32,24},{40,32},{48,40},{56,48},{64,56},{72,6... | collective-permute-start | bytes 1806344 | tf_op jit(solution)/shard_map/ppermute | solution.py:450
  19.0 17.2 %all_to_all.15.slots = f32[128,2,128]{2,1,0:T(2,128)S(1)} all-to-all(f32[128,2,128]{2,1,0:T(2,128)S(1)} %place_slots.1), channel_id=1, replica_groups=mesh['gx_0'=4,'gx_1'=4,'gy_0'=4,'gy_1'=2] {'gx_0','gx_1','gy_0','gy_1'}, dimensions={0} | all-to-all | bytes 262144 | tf_op jit(solution)/shard_map/all_to_all | solution.py:465
  36.2 5.2 %add_currents.1 = (f32[8,128,128]{2,1,0:T(8,128)S(1)}, f32[64,128]{1,0:T(8,128)S(1)}, f32[64,128]{1,0:T(8,128)S(1)}) custom-call(f32[128,2,128]{2,1,0:T(2,128)S(1)} %all_to_all.15.slots, f32[64,64]{1,0:T(8,128)S(1)} %copy-done.2), custom_call_target="tpu_custom_call" | custom-call | tf_op jit(solution)/shard_map/add_currents/pallas_call | solution.py:43
  41.5 2.9 %collective-permute-start.5 = (f32[64,128]{1,0:T(8,128)S(1)}, f32[64,128]{1,0:T(8,128)S(1)}, u32[]{:S(2)}, u32[]{:S(2)}) collective-permute-start(f32[64,128]{1,0:T(8,128)S(1)} %get-tuple-element.66), channel_id=1, source_target_pairs={{1,0},{2,1},{3,2},{4,3},{5,4},{6,5},{7,6},{0,7},{9,8},{10,9},{11,1... | collective-permute-start | bytes 98312 | tf_op jit(solution)/shard_map/ppermute | solution.py:450
  44.3 1.6 %collective-permute-done.4.low.i_low = f32[64,128]{1,0:T(8,128)S(1)} collective-permute-done((f32[64,128]{1,0:T(8,128)S(1)}, f32[64,128]{1,0:T(8,128)S(1)}, u32[]{:S(2)}, u32[]{:S(2)}) %collective-permute-start.4) | collective-permute-done | bytes 32800 | tf_op jit(solution)/shard_map/ppermute | solution.py:449
  46.1 1.3 %collective-permute-start.6 = (f32[3,144,128]{2,1,0:T(8,128)S(1)}, f32[3,144,128]{2,1,0:T(8,128)S(1)}, u32[]{:S(2)}, u32[]{:S(2)}) collective-permute-start(f32[3,144,128]{2,1,0:T(8,128)S(1)} %get-tuple-element.67), channel_id=1, source_target_pairs={{0,8},{8,16},{16,24},{24,32},{32,40},{40,48},{48,56},{56,64},{64,7... | collective-permute-start | bytes 663560 | tf_op jit(solution)/shard_map/ppermute | solution.py:449
  47.4 4.2 %collective-permute-start.7 = (f32[3,144,128]{2,1,0:T(8,128)S(1)}, f32[3,144,128]{2,1,0:T(8,128)S(1)}, u32[]{:S(2)}, u32[]{:S(2)}) collective-permute-start(f32[3,144,128]{2,1,0:T(8,128)S(1)} %get-tuple-element.68), channel_id=1, source_target_pairs={{8,0},{16,8},{24,16},{32,24},{40,32},{48,40},{56,48},{64,56},{72,6... | collective-permute-start | bytes 663560 | tf_op jit(solution)/shard_map/ppermute | solution.py:450
  51.5 6.5 %grid_weights.1 = (f32[22,144,128]{2,1,0:T(8,128)S(1)}, f32[22,144,128]{2,1,0:T(8,128)S(1)}, f32[22,144,128]{2,1,0:T(8,128)S(1)}, f32[22,144,128]{2,1,0:T(8,128)...) custom-call(f32[8,128,128]{2,1,0:T(8,128)S(1)} %get-tuple-element.50.v, ...), custom_call_target="tpu_custom_call" | custom-call | tf_op jit(solution)/shard_map/grid_weights/pallas_call | solution.py:43
  58.1 5.7 %first_basis.1 = (f32[22,144,128]{2,1,0:T(8,128)S(1)}, f32[22,144,128]{2,1,0:T(8,128)S(1)}, f32[22,144,128]{2,1,0:T(8,128)S(1)}, f32[22,144,128]{2,1,0:T(8,128)S...) custom-call(f32[22,144,128]{2,1,0:T(8,128)S(1)} %get-tuple-element.58.diag, ...), custom_call_target="tpu_custom_call" | custom-call | tf_op jit(solution)/shard_map/first_basis/pallas_call | solution.py:43
  63.8 1.2 collective-permute-done.8
  65.0 2.7 %collective-permute-start.11 = (f32[32,128]{1,0:T(8,128)S(1)}, f32[32,128]{1,0:T(8,128)S(1)}, u32[]{:S(2)}, u32[]{:S(2)}) collective-permute-start(f32[32,128]{1,0:T(8,128)S(1)} %add.24), channel_id=1, source_target_pairs={{0,6},{2,4},{4,2},{6,0},{1,7},{3,5},{5,3},{7,1},{8,14},{10,12},{12... | collective-permute-start | bytes 49160 | tf_op jit(solution)/shard_map/ppermute | solution.py:456
  67.7 1.4 %collective-permute-start.9 = (f32[32,128]{1,0:T(8,128)S(1)}, f32[32,128]{1,0:T(8,128)S(1)}, u32[]{:S(2)}, u32[]{:S(2)}) collective-permute-start(f32[32,128]{1,0:T(8,128)S(1)} %add.24), channel_id=1, source_target_pairs={{0,2},{2,0},{4,6},{6,4},{1,3},{3,1},{5,7},{7,5},{8,10},{10,8},{12,... | collective-permute-start | bytes 49160 | tf_op jit(solution)/shard_map/ppermute | solution.py:456
  69.1 0.7 split_rows.1
  70.0 3.0 %collective-permute-done.10 = f32[32,128]{1,0:T(8,128)S(1)} collective-permute-done((f32[32,128]{1,0:T(8,128)S(1)}, f32[32,128]{1,0:T(8,128)S(1)}, u32[]{:S(2)}, u32[]{:S(2)}) %collective-permute-start.10) | collective-permute-done | bytes 16416 | tf_op jit(solution)/shard_map/ppermute | solution.py:456
  73.0 11.5 %all_to_all.16.gram = f32[16,32,128]{2,1,0:T(8,128)S(1)} all-to-all(f32[16,32,128]{2,1,0:T(8,128)S(1)} %broadcast_in_dim.4), channel_id=1, replica_groups=mesh['gx_0'=4,'gx_1'=4,'gy_0'=4,'gy_1'=2] {'gx_0','gx_1'}, dimensions={0} | all-to-all | bytes 524288 | tf_op jit(solution)/shard_map/all_to_all | solution.py:461
  84.5 8.4 %second_basis.1 = (f32[22,144,128]{2,1,0:T(8,128)S(1)}, f32[22,144,128]{2,1,0:T(8,128)S(1)}, f32[22,144,128]{2,1,0:T(8,128)S(1)}, f32[22,144,128]{2,1,0:T(8,128)...) custom-call(f32[16,32,128]{2,1,0:T(8,128)S(1)} %all_to_all.16.gram, ...), custom_call_target="tpu_custom_call" | custom-call | tf_op jit(solution)/shard_map/second_basis/pallas_call | solution.py:43
  93.0 1.2 collective-permute-done.12
  94.2 1.7 %collective-permute-start.15 = (f32[32,128]{1,0:T(8,128)S(1)}, f32[32,128]{1,0:T(8,128)S(1)}, u32[]{:S(2)}, u32[]{:S(2)}) collective-permute-start(f32[32,128]{1,0:T(8,128)S(1)} %add.28), channel_id=1, source_target_pairs={{0,6},{2,4},{4,2},{6,0},{1,7},{3,5},{5,3},{7,1},{8,14},{10,12},{12... | collective-permute-start | bytes 49160 | tf_op jit(solution)/shard_map/ppermute | solution.py:456
  95.9 1.4 %collective-permute-start.14 = (f32[32,128]{1,0:T(8,128)S(1)}, f32[32,128]{1,0:T(8,128)S(1)}, u32[]{:S(2)}, u32[]{:S(2)}) collective-permute-start(f32[32,128]{1,0:T(8,128)S(1)} %add.28), channel_id=1, source_target_pairs={{0,4},{2,6},{4,0},{6,2},{1,5},{3,7},{5,1},{7,3},{8,12},{10,14},{12... | collective-permute-start | bytes 49160 | tf_op jit(solution)/shard_map/ppermute | solution.py:456
  97.3 1.0 collective-permute-start.13
  98.3 0.7 from_lanes.1
  99.2 2.0 %collective-permute-done.14 = f32[32,128]{1,0:T(8,128)S(1)} collective-permute-done((f32[32,128]{1,0:T(8,128)S(1)}, f32[32,128]{1,0:T(8,128)S(1)}, u32[]{:S(2)}, u32[]{:S(2)}) %collective-permute-start.14) | collective-permute-done | bytes 16416 | tf_op jit(solution)/shard_map/ppermute | solution.py:456
  101.2 11.9 %all_to_all.17.gram = f32[16,32,128]{2,1,0:T(8,128)S(1)} all-to-all(f32[16,32,128]{2,1,0:T(8,128)S(1)} %broadcast_in_dim.5), channel_id=1, replica_groups=mesh['gx_0'=4,'gx_1'=4,'gy_0'=4,'gy_1'=2] {'gx_0','gx_1'}, dimensions={0} | all-to-all | bytes 524288 | tf_op jit(solution)/shard_map/all_to_all | solution.py:461
  113.2 4.7 %finish.1 = (f32[1024,128]{1,0:T(8,128)}, f32[1024,128]{1,0:T(8,128)}) custom-call(f32[16,32,128]{2,1,0:T(8,128)S(1)} %all_to_all.17.gram, bf16[8,512,128]{2,1,0:T(8,128)(2,1)S(1)} %get-tuple-element.92.hi, bf16[8,512,128]{2,1,0:T(8,128)(2,1)S(1)} %get-tuple-element.93.lo, f32[8,128,128]{2,1,0:T(8,128)S(1)} %get-tuple-element.94.volts, ...), custom_call_target="tpu_custom_call" | custom-call | tf_op jit(solution)/shard_map/finish/pallas_call | solution.py:43
  (30 shorter events, 1.0 us)
Async XLA Ops:
  0.6 35.5 %copy-start.2 = (f32[64,64]{1,0:T(8,128)S(1)}, f32[64,64]{1,0:T(8,128)}, u32[]{:S(2)}) copy-start(f32[64,64]{1,0:T(8,128)} %waves.1) | copy-start | bytes 49156
  1.4 1.0 copy-start
  2.9 10.4 %collective-permute-start = (f32[128,128]{1,0:T(8,128)S(1)}, f32[128,128]{1,0:T(8,128)S(1)}, u32[]{:S(2)}, u32[]{:S(2)}) collective-permute-start(f32[128,128]{1,0:T(8,128)S(1)} %get-tuple-element.52), channel_id=1, source_target_pairs={{0,1},{1,2},{2,3},{3,4},{4,5},{5,6},{6,7},{7,0},{8,9},{9,10},{10,1... | collective-permute-start | bytes 196616 | tf_op jit(solution)/shard_map/ppermute | solution.py:449
  2.9 10.4 %collective-permute-start.1 = (f32[128,128]{1,0:T(8,128)S(1)}, f32[128,128]{1,0:T(8,128)S(1)}, u32[]{:S(2)}, u32[]{:S(2)}) collective-permute-start(f32[128,128]{1,0:T(8,128)S(1)} %get-tuple-element.53), channel_id=1, source_target_pairs={{1,0},{2,1},{3,2},{4,3},{5,4},{6,5},{7,6},{0,7},{9,8},{10,9},{11,1... | collective-permute-start | bytes 196616 | tf_op jit(solution)/shard_map/ppermute | solution.py:450
  7.2 0.8 copy-start.3
  13.5 38.0 %collective-permute-start.2 = (f32[7,168,128]{2,1,0:T(8,128)S(1)}, f32[7,168,128]{2,1,0:T(8,128)S(1)}, u32[]{:S(2)}, u32[]{:S(2)}) collective-permute-start(f32[7,168,128]{2,1,0:T(8,128)S(1)} %get-tuple-element.56), channel_id=1, source_target_pairs={{0,8},{8,16},{16,24},{24,32},{32,40},{40,48},{48,56},{56,64},{64,7... | collective-permute-start | bytes 1806344 | tf_op jit(solution)/shard_map/ppermute | solution.py:449
  15.2 36.3 %collective-permute-start.3 = (f32[7,168,128]{2,1,0:T(8,128)S(1)}, f32[7,168,128]{2,1,0:T(8,128)S(1)}, u32[]{:S(2)}, u32[]{:S(2)}) collective-permute-start(f32[7,168,128]{2,1,0:T(8,128)S(1)} %get-tuple-element.57), channel_id=1, source_target_pairs={{8,0},{16,8},{24,16},{32,24},{40,32},{48,40},{56,48},{64,56},{72,6... | collective-permute-start | bytes 1806344 | tf_op jit(solution)/shard_map/ppermute | solution.py:450
  41.4 4.6 %collective-permute-start.4 = (f32[64,128]{1,0:T(8,128)S(1)}, f32[64,128]{1,0:T(8,128)S(1)}, u32[]{:S(2)}, u32[]{:S(2)}) collective-permute-start(f32[64,128]{1,0:T(8,128)S(1)} %get-tuple-element.65), channel_id=1, source_target_pairs={{0,1},{1,2},{2,3},{3,4},{4,5},{5,6},{6,7},{7,0},{8,9},{9,10},{10,1... | collective-permute-start | bytes 98312 | tf_op jit(solution)/shard_map/ppermute | solution.py:449
  41.5 4.4 %collective-permute-start.5 = (f32[64,128]{1,0:T(8,128)S(1)}, f32[64,128]{1,0:T(8,128)S(1)}, u32[]{:S(2)}, u32[]{:S(2)}) collective-permute-start(f32[64,128]{1,0:T(8,128)S(1)} %get-tuple-element.66), channel_id=1, source_target_pairs={{1,0},{2,1},{3,2},{4,3},{5,4},{6,5},{7,6},{0,7},{9,8},{10,9},{11,1... | collective-permute-start | bytes 98312 | tf_op jit(solution)/shard_map/ppermute | solution.py:450
  46.1 12.0 %collective-permute-start.6 = (f32[3,144,128]{2,1,0:T(8,128)S(1)}, f32[3,144,128]{2,1,0:T(8,128)S(1)}, u32[]{:S(2)}, u32[]{:S(2)}) collective-permute-start(f32[3,144,128]{2,1,0:T(8,128)S(1)} %get-tuple-element.67), channel_id=1, source_target_pairs={{0,8},{8,16},{16,24},{24,32},{32,40},{40,48},{48,56},{56,64},{64,7... | collective-permute-start | bytes 663560 | tf_op jit(solution)/shard_map/ppermute | solution.py:449
  47.4 10.7 %collective-permute-start.7 = (f32[3,144,128]{2,1,0:T(8,128)S(1)}, f32[3,144,128]{2,1,0:T(8,128)S(1)}, u32[]{:S(2)}, u32[]{:S(2)}) collective-permute-start(f32[3,144,128]{2,1,0:T(8,128)S(1)} %get-tuple-element.68), channel_id=1, source_target_pairs={{8,0},{16,8},{24,16},{32,24},{40,32},{48,40},{56,48},{64,56},{72,6... | collective-permute-start | bytes 663560 | tf_op jit(solution)/shard_map/ppermute | solution.py:450
  63.7 1.3 %collective-permute-start.8 = (f32[32,128]{1,0:T(8,128)S(1)}, f32[32,128]{1,0:T(8,128)S(1)}, u32[]{:S(2)}, u32[]{:S(2)}) collective-permute-start(f32[32,128]{1,0:T(8,128)S(1)} %get-tuple-element.69), channel_id=1, source_target_pairs={{0,1},{1,0},{2,3},{3,2},{4,5},{5,4},{6,7},{7,6},{8,9},{9,8},{10,11... | collective-permute-start | bytes 49160 | tf_op jit(solution)/shard_map/ppermute | solution.py:454
  65.0 4.9 %collective-permute-start.11 = (f32[32,128]{1,0:T(8,128)S(1)}, f32[32,128]{1,0:T(8,128)S(1)}, u32[]{:S(2)}, u32[]{:S(2)}) collective-permute-start(f32[32,128]{1,0:T(8,128)S(1)} %add.24), channel_id=1, source_target_pairs={{0,6},{2,4},{4,2},{6,0},{1,7},{3,5},{5,3},{7,1},{8,14},{10,12},{12... | collective-permute-start | bytes 49160 | tf_op jit(solution)/shard_map/ppermute | solution.py:456
  67.7 5.2 %collective-permute-start.10 = (f32[32,128]{1,0:T(8,128)S(1)}, f32[32,128]{1,0:T(8,128)S(1)}, u32[]{:S(2)}, u32[]{:S(2)}) collective-permute-start(f32[32,128]{1,0:T(8,128)S(1)} %add.24), channel_id=1, source_target_pairs={{0,4},{2,6},{4,0},{6,2},{1,5},{3,7},{5,1},{7,3},{8,12},{10,14},{12... | collective-permute-start | bytes 49160 | tf_op jit(solution)/shard_map/ppermute | solution.py:456
  67.7 5.2 %collective-permute-start.9 = (f32[32,128]{1,0:T(8,128)S(1)}, f32[32,128]{1,0:T(8,128)S(1)}, u32[]{:S(2)}, u32[]{:S(2)}) collective-permute-start(f32[32,128]{1,0:T(8,128)S(1)} %add.24), channel_id=1, source_target_pairs={{0,2},{2,0},{4,6},{6,4},{1,3},{3,1},{5,7},{7,5},{8,10},{10,8},{12,... | collective-permute-start | bytes 49160 | tf_op jit(solution)/shard_map/ppermute | solution.py:456
  84.5 13.8 %copy-start.1 = (f32[32,4,8,128]{3,2,1,0:T(8,128)S(1)}, f32[32,4,8,128]{3,2,1,0:T(8,128)}, u32[]{:S(2)}) copy-start(f32[32,4,8,128]{3,2,1,0:T(8,128)} %param.10) | copy-start | bytes 1572868
  92.9 1.3 %collective-permute-start.12 = (f32[32,128]{1,0:T(8,128)S(1)}, f32[32,128]{1,0:T(8,128)S(1)}, u32[]{:S(2)}, u32[]{:S(2)}) collective-permute-start(f32[32,128]{1,0:T(8,128)S(1)} %get-tuple-element.81), channel_id=1, source_target_pairs={{0,1},{1,0},{2,3},{3,2},{4,5},{5,4},{6,7},{7,6},{8,9},{9,8},{10,11... | collective-permute-start | bytes 49160 | tf_op jit(solution)/shard_map/ppermute | solution.py:454
  94.2 4.9 %collective-permute-start.15 = (f32[32,128]{1,0:T(8,128)S(1)}, f32[32,128]{1,0:T(8,128)S(1)}, u32[]{:S(2)}, u32[]{:S(2)}) collective-permute-start(f32[32,128]{1,0:T(8,128)S(1)} %add.28), channel_id=1, source_target_pairs={{0,6},{2,4},{4,2},{6,0},{1,7},{3,5},{5,3},{7,1},{8,14},{10,12},{12... | collective-permute-start | bytes 49160 | tf_op jit(solution)/shard_map/ppermute | solution.py:456
  95.9 5.2 %collective-permute-start.14 = (f32[32,128]{1,0:T(8,128)S(1)}, f32[32,128]{1,0:T(8,128)S(1)}, u32[]{:S(2)}, u32[]{:S(2)}) collective-permute-start(f32[32,128]{1,0:T(8,128)S(1)} %add.28), channel_id=1, source_target_pairs={{0,4},{2,6},{4,0},{6,2},{1,5},{3,7},{5,1},{7,3},{8,12},{10,14},{12... | collective-permute-start | bytes 49160 | tf_op jit(solution)/shard_map/ppermute | solution.py:456
  97.3 3.8 %collective-permute-start.13 = (f32[32,128]{1,0:T(8,128)S(1)}, f32[32,128]{1,0:T(8,128)S(1)}, u32[]{:S(2)}, u32[]{:S(2)}) collective-permute-start(f32[32,128]{1,0:T(8,128)S(1)} %add.28), channel_id=1, source_target_pairs={{0,2},{2,0},{4,6},{6,4},{1,3},{3,1},{5,7},{7,5},{8,10},{10,8},{12,... | collective-permute-start | bytes 49160 | tf_op jit(solution)/shard_map/ppermute | solution.py:456

commit v8 on v7

--- a/solution.py
+++ b/solution.py
@@ -184,7 +184,7 @@
         dst[i] = apply_row(src, i, *weights)
         return carry
 
-    lax.fori_loop(first, last + 1, row, 0, unroll=4)
+    lax.fori_loop(first, last + 1, row, 0, unroll=True)
 
 
 def moments(fields, out, first):
@@ -286,34 +286,67 @@
     return jnp.concatenate([step, less], axis=1)
 
 
+def spreading():
+    n, q = iota((128, 512), 1), iota((128, 512), 0)
+    hit = (q % 16 == (n // 128) * 4 + (n % 128) // 32) & (q < 48)
+    return hit.astype(F32).astype(BF16)
+
+
+def expand(coef, spread, cap, wx, wy, wv, i):
+    hi, mid, lo = [p.astype(F32) for p in split3(coef)]
+    parts = hi + pltpu.roll(mid, 16, 1) + pltpu.roll(lo, 32, 1)
+    wide = dot(parts.astype(BF16), spread, ((1,), (0,)))
+    for n, out in enumerate((cap, wx, wy, wv)):
+        out[i] = wide[:, n * 128 : (n + 1) * 128]
+
+
+def weigh(i, ext, raw_x, diag, wx, wy, wv, cap, free):
+    scale = 1.0 / SCALE
+    own, raw_y, raw_v = cap[i], wy[i], wv[i]
+    wyi = jnp.where(pltpu.roll(own, YE - 1, 0) > 0, raw_y * scale, 0.0)
+    wvi = jnp.where(iota((YE, 128), 1) < 96, raw_v * scale, 0.0)
+    wy[i], wv[i] = wyi, wvi
+    total = (own + raw_x + raw_y + raw_v - SHIFT) * scale + wx[i - 1]
+    diag[i] = total + pltpu.roll(wyi, 1, 0) + pltpu.roll(wvi, 32, 1)
+    free[i] = (own - SHIFT) * ext[i] - SCALE * apply_row(ext, i, diag, wx, wy, wv)
+
+
+def own_weights(v, c, low, high, diag, wx, wy, wv, cap, free, ext, scaled):
+    spread = spreading()
+    for x in range(8):
+        ext[x] = widened(low, v, high, x)
+        expand(widened(low, c, high, x, 64), spread, cap, wx, wy, wv, x)
+        scaled[x] = wx[x] * (1.0 / SCALE)
+    for x in (0, 7):
+        diag[x] = jnp.zeros((YE, 128), F32)
+        free[x] = jnp.zeros((YE, 128), F32)
+    for x in range(1, 7):
+        weigh(x, ext, wx[x], diag, scaled, wy, wv, cap, free)
+        wx[x] = scaled[x]
+
+
 def grid_weights(
-    v, c, low, high, x_low, x_high, diag, wx, wy, wv, cap, free, ext,
+    v, low, high, x_low, x_high, diag_in, wx_in, wy_in, wv_in, cap_in, free_in,
+    diag, wx, wy, wv, cap, free, ext,
 ):
     lane = iota((YE, 128), 1)
-    n = iota((128, 512), 1)
-    q = iota((128, 512), 0)
-    spread = ((q % 16 == (n // 128) * 4 + (n % 128) // 32) & (q < 48)).astype(F32).astype(BF16)
-
-    def expand(i, coef):
-        hi, mid, lo = [p.astype(F32) for p in split3(coef)]
-        parts = hi + pltpu.roll(mid, 16, 1) + pltpu.roll(lo, 32, 1)
-        wide = dot(parts.astype(BF16), spread, ((1,), (0,)))
-        cap[i] = wide[:, :128]
-        wx[i] = wide[:, 128:256]
-        wy[i] = wide[:, 256:384]
-        wv[i] = wide[:, 384:]
+    spread = spreading()
+    for x in (0, 1, 6, 7):
+        ext[7 + x] = widened(low, v, high, x)
+
+    def own_row(x, carry):
+        for src, dst in (
+            (diag_in, diag), (wx_in, wx), (wy_in, wy), (wv_in, wv), (cap_in, cap), (free_in, free)
+        ):
+            dst[7 + x] = src[x]
+        return carry
 
     def halo_row(j, ref, base, present):
         ext[base + j] = ref[j, :YE, :] * present
         packed = ref[j, YE:, :] * present
         groups = [packed] + [pltpu.roll(packed, 128 - 16 * g, 1) for g in range(1, 6)]
-        coef = jnp.concatenate(groups, axis=0)
-        expand(base + j, jnp.where(lane < 16, coef, 0.0))
-
-    def own_row(x, carry):
-        ext[7 + x] = widened(low, v, high, x)
-        expand(7 + x, widened(low, c, high, x, 64))
-        return carry
+        coef = jnp.where(lane < 16, jnp.concatenate(groups, axis=0), 0.0)
+        expand(coef, spread, cap, wx, wy, wv, base + j)
 
     def halo_rows(j, carry):
         low_in, high_in = inside(GX)
@@ -321,27 +354,21 @@
         halo_row(j, x_high, 15, high_in)
         return carry
 
-    lax.fori_loop(0, 8, own_row, 0, unroll=2)
-    lax.fori_loop(0, 7, halo_rows, 0)
-
-    scale = 1.0 / SCALE
+    lax.fori_loop(0, 8, own_row, 0, unroll=True)
+    lax.fori_loop(0, 7, halo_rows, 0, unroll=True)
 
     def edge_x(i):
-        wx[i] = jnp.where(cap[i + 1] > 0, wx[i] * scale, 0.0)
-
-    def weigh(i, carry):
-        own, raw_x, raw_y, raw_v = cap[i], wx[i], wy[i], wv[i]
+        wx[i] = jnp.where(cap[i + 1] > 0, wx[i] * (1.0 / SCALE), 0.0)
+
+    def row(i, carry):
+        raw = wx[i]
         edge_x(i)
-        wyi = jnp.where(pltpu.roll(own, YE - 1, 0) > 0, raw_y * scale, 0.0)
-        wvi = jnp.where(lane < 96, raw_v * scale, 0.0)
-        wy[i], wv[i] = wyi, wvi
-        total = (own + raw_x + raw_y + raw_v - SHIFT) * scale + wx[i - 1]
-        diag[i] = total + pltpu.roll(wyi, 1, 0) + pltpu.roll(wvi, 32, 1)
-        free[i] = (own - SHIFT) * ext[i] - SCALE * apply_row(ext, i, diag, wx, wy, wv)
+        weigh(i, ext, raw, diag, wx, wy, wv, cap, free)
         return carry
 
     edge_x(0)
-    lax.fori_loop(1, 21, weigh, 0, unroll=2)
+    lax.fori_loop(1, 8, row, 0, unroll=True)
+    lax.fori_loop(14, 21, row, 0, unroll=True)
 
 
 def first_basis(
@@ -369,8 +396,8 @@
             start(base + 3 + j, pltpu.roll(both, 64, 1))
         return carry
 
-    lax.fori_loop(0, 8, own_start, 0)
-    lax.fori_loop(0, 3, halo_start, 0)
+    lax.fori_loop(0, 8, own_start, 0, unroll=True)
+    lax.fori_loop(0, 3, halo_start, 0, unroll=True)
     power(v0, v1, 2, 19, weights)
     power(v1, v2, 3, 18, weights)
     power(v2, v3, 4, 17, weights)
@@ -402,7 +429,7 @@
         b0[i] = v0[i] + both[:, 128:] + cap[i] * moved + change[i]
         return carry
 
-    lax.fori_loop(4, 18, row, 0, unroll=2)
+    lax.fori_loop(4, 18, row, 0, unroll=True)
     power(b0, b1, 5, 16, weights)
     power(b1, b2, 6, 15, weights)
     power(b2, b3, 7, 14, weights)
@@ -492,11 +519,20 @@
         [vmem((256, 256), F32)],
     )
     i_low, i_high = neighbours(i_low, i_high, GY)
+    tile = (8, YE, 128)
+    v, c, y_low, y_high, inj = lax.optimization_barrier((v, c, y_low, y_high, inj))
+    partial = call(
+        own_weights, [tile] * 6, [v, c, y_low, y_high], [vmem(tile, F32), vmem(tile, F32)]
+    )
+    i_low, i_high, partial = lax.optimization_barrier((i_low, i_high, partial))
     ix_low, ix_high = call(pack_injected, [(3, YE, 128)] * 2, [inj, i_low, i_high])
     ix_low, ix_high = neighbours(ix_low, ix_high, GX)
     wide = (XE, YE, 128)
     diag, wx, wy, wv, cap, free = call(
-        grid_weights, [wide] * 6, [v, c, y_low, y_high, x_low, x_high], [vmem(wide, F32)]
+        grid_weights,
+        [wide] * 6,
+        [v, y_low, y_high, x_low, x_high, *partial],
+        [vmem(wide, F32)],
     )
     *kept, gram = call(
         first_basis,

time: 118 us -> 114 us (0.966)
  Pallas kernels: 38 us -> 31.5 us
  blocking collectives: 40.6 us -> 44.1 us
    pallas_call x11 -> x12, Pallas kernels: 38 us -> 31.5 us  [call(): pl.pallas_call(kernel, out_shape=tuple(outs), scratch_shapes=list(scratch...]
    all_to_all x2, blocking collectives: 23.4 us -> 26.9 us  [everywhere(): lax.all_to_all(x, GX, split_axis=0, concat_axis=0, tiled=True)]
    ppermute x6, waiting for transfers between devices: 5.29 us -> 4.11 us  [everywhere(): lax.ppermute(x, 'gy_0', [(i, i ^ k) for i in range(4)])]
  transfers between devices with their start and end apart: 16 -> 16, of which waited for: 7 -> 8; matrix products, arithmetic and copies ran while one was open for 1% -> 1% of each run, Pallas kernels for 16% -> 14%
where the time goes in v8:
time: 114 us
  blocking collectives  44.1 us (39%)
  Pallas kernels  31.5 us (28%)
  starting transfers between devices  25.8 us (23%)
  waiting for transfers between devices  8.23 us (7%)
  local copies, waits for them, and re-layouts  1.84 us (2%)
  other arithmetic  1.6 us (1%)
    pallas_call x12, Pallas kernels, call(): pl.pallas_call(kernel, out_shape=tuple(outs), scratch_shapes=list(scratch...  31.5 us
    all_to_all x2, blocking collectives, everywhere(): lax.all_to_all(x, GX, split_axis=0, concat_axis=0, tiled=True)  26.9 us
    all_to_all x1, blocking collectives, exchange(): return lax.all_to_all(slots, GX_GY, split_axis=0, concat_axis=0, tiled=True)  17.2 us
    ppermute x4, starting transfers between devices, neighbours(): return (from_low, lax.ppermute(to_low, axis, [(b, a) for a, b in up]))  14.4 us
    ppermute x6, starting transfers between devices, everywhere(): lax.ppermute(x, 'gy_0', [(i, i ^ k) for i in range(4)])  8.19 us
    ppermute x6, waiting for transfers between devices, everywhere(): lax.ppermute(x, 'gy_0', [(i, i ^ k) for i in range(4)])  4.11 us
    ppermute x4, starting transfers between devices, neighbours(): from_low = lax.ppermute(to_high, axis, up)  3.05 us
    ppermute x2, waiting for transfers between devices, everywhere(): x = x + lax.ppermute(x, 'gy_1', [(0, 1), (1, 0)])  2.34 us
  transfers between devices with their start and end apart: 16, of which 8 were waited for; matrix products, arithmetic and copies ran while one was open for 1% of the time, Pallas kernels for 14%

profile of v8, /device:TPU:0, one launch (start us, length us, event | category | flops | bytes accessed | tf_op | source)
XLA Modules:
  0.0 113.8 jit_solution(7401238494237563354)
XLA Ops:
  0.6 0.8 pad_maximum_fusion.stack
  1.4 1.0 copy-done
  2.9 3.6 %collective-permute-start.1 = (f32[128,128]{1,0:T(8,128)S(1)}, f32[128,128]{1,0:T(8,128)S(1)}, u32[]{:S(2)}, u32[]{:S(2)}) collective-permute-start(f32[128,128]{1,0:T(8,128)S(1)} %get-tuple-element.72), channel_id=1, source_target_pairs={{1,0},{2,1},{3,2},{4,3},{5,4},{6,5},{7,6},{0,7},{9,8},{10,9},{11,1... | collective-permute-start | bytes 196616 | tf_op jit(solution)/shard_map/ppermute | solution.py:477
  6.4 0.8 pad_add_fusion.listed
  7.2 0.8 copy-done.3
  8.0 5.3 %place_slots.1 = f32[128,2,128]{2,1,0:T(2,128)S(1)} custom-call(s32[192,128]{1,0:T(8,128)S(1)} %pad_add_fusion.listed, f32[64,128]{1,0:T(8,128)S(1)} %bitcast.13), custom_call_target="tpu_custom_call" | custom-call | tf_op jit(solution)/shard_map/place_slots/pallas_call | solution.py:43
  13.5 1.6 %collective-permute-start.2 = (f32[7,168,128]{2,1,0:T(8,128)S(1)}, f32[7,168,128]{2,1,0:T(8,128)S(1)}, u32[]{:S(2)}, u32[]{:S(2)}) collective-permute-start(f32[7,168,128]{2,1,0:T(8,128)S(1)} %get-tuple-element.80), channel_id=1, source_target_pairs={{0,8},{8,16},{16,24},{24,32},{32,40},{40,48},{48,56},{56,64},{64,7... | collective-permute-start | bytes 1806344 | tf_op jit(solution)/shard_map/ppermute | solution.py:476
  15.2 3.8 %collective-permute-start.3 = (f32[7,168,128]{2,1,0:T(8,128)S(1)}, f32[7,168,128]{2,1,0:T(8,128)S(1)}, u32[]{:S(2)}, u32[]{:S(2)}) collective-permute-start(f32[7,168,128]{2,1,0:T(8,128)S(1)} %get-tuple-element.81), channel_id=1, source_target_pairs={{8,0},{16,8},{24,16},{32,24},{40,32},{48,40},{56,48},{64,56},{72,6... | collective-permute-start | bytes 1806344 | tf_op jit(solution)/shard_map/ppermute | solution.py:477
  19.0 17.2 %all_to_all.15.slots = f32[128,2,128]{2,1,0:T(2,128)S(1)} all-to-all(f32[128,2,128]{2,1,0:T(2,128)S(1)} %place_slots.1), channel_id=1, replica_groups=mesh['gx_0'=4,'gx_1'=4,'gy_0'=4,'gy_1'=2] {'gx_0','gx_1','gy_0','gy_1'}, dimensions={0} | all-to-all | bytes 262144 | tf_op jit(solution)/shard_map/all_to_all | solution.py:492
  36.2 5.2 %add_currents.1 = (f32[8,128,128]{2,1,0:T(8,128)S(1)}, f32[64,128]{1,0:T(8,128)S(1)}, f32[64,128]{1,0:T(8,128)S(1)}) custom-call(f32[128,2,128]{2,1,0:T(2,128)S(1)} %all_to_all.15.slots, f32[64,64]{1,0:T(8,128)S(1)} %copy-done.2), custom_call_target="tpu_custom_call" | custom-call | tf_op jit(solution)/shard_map/add_currents/pallas_call | solution.py:43
  41.5 2.9 %collective-permute-start.5 = (f32[64,128]{1,0:T(8,128)S(1)}, f32[64,128]{1,0:T(8,128)S(1)}, u32[]{:S(2)}, u32[]{:S(2)}) collective-permute-start(f32[64,128]{1,0:T(8,128)S(1)} %get-tuple-element.83), channel_id=1, source_target_pairs={{1,0},{2,1},{3,2},{4,3},{5,4},{6,5},{7,6},{0,7},{9,8},{10,9},{11,1... | collective-permute-start | bytes 98312 | tf_op jit(solution)/shard_map/ppermute | solution.py:477
  44.3 1.1 own_weights.1
  46.1 1.3 %collective-permute-start.6 = (f32[3,144,128]{2,1,0:T(8,128)S(1)}, f32[3,144,128]{2,1,0:T(8,128)S(1)}, u32[]{:S(2)}, u32[]{:S(2)}) collective-permute-start(f32[3,144,128]{2,1,0:T(8,128)S(1)} %get-tuple-element.105), channel_id=1, source_target_pairs={{0,8},{8,16},{16,24},{24,32},{32,40},{40,48},{48,56},{56,64},{64,7... | collective-permute-start | bytes 663560 | tf_op jit(solution)/shard_map/ppermute | solution.py:476
  47.4 4.2 %collective-permute-start.7 = (f32[3,144,128]{2,1,0:T(8,128)S(1)}, f32[3,144,128]{2,1,0:T(8,128)S(1)}, u32[]{:S(2)}, u32[]{:S(2)}) collective-permute-start(f32[3,144,128]{2,1,0:T(8,128)S(1)} %get-tuple-element.106), channel_id=1, source_target_pairs={{8,0},{16,8},{24,16},{32,24},{40,32},{48,40},{56,48},{64,56},{72,6... | collective-permute-start | bytes 663560 | tf_op jit(solution)/shard_map/ppermute | solution.py:477
  51.5 3.0 %grid_weights.1 = (f32[22,144,128]{2,1,0:T(8,128)S(1)}, f32[22,144,128]{2,1,0:T(8,128)S(1)}, f32[22,144,128]{2,1,0:T(8,128)S(1)}, f32[22,144,128]{2,1,0:T(8,128)...) custom-call(f32[8,128,128]{2,1,0:T(8,128)S(1)} %get-tuple-element.77.v, ...), custom_call_target="tpu_custom_call" | custom-call | tf_op jit(solution)/shard_map/grid_weights/pallas_call | solution.py:43
  54.5 1.2 %collective-permute-done.6.ix_low = f32[3,144,128]{2,1,0:T(8,128)S(1)} collective-permute-done((f32[3,144,128]{2,1,0:T(8,128)S(1)}, f32[3,144,128]{2,1,0:T(8,128)S(1)}, u32[]{:S(2)}, u32[]{:S(2)}) %collective-permute-start.6) | collective-permute-done | bytes 221216 | tf_op jit(solution)/shard_map/ppermute | solution.py:476
  55.8 4.2 %first_basis.1 = (f32[22,144,128]{2,1,0:T(8,128)S(1)}, f32[22,144,128]{2,1,0:T(8,128)S(1)}, f32[22,144,128]{2,1,0:T(8,128)S(1)}, f32[22,144,128]{2,1,0:T(8,128)S...) custom-call(f32[22,144,128]{2,1,0:T(8,128)S(1)} %get-tuple-element.97.diag, ...), custom_call_target="tpu_custom_call" | custom-call | tf_op jit(solution)/shard_map/first_basis/pallas_call | solution.py:43
  60.1 1.2 %collective-permute-done.8 = f32[32,128]{1,0:T(8,128)S(1)} collective-permute-done((f32[32,128]{1,0:T(8,128)S(1)}, f32[32,128]{1,0:T(8,128)S(1)}, u32[]{:S(2)}, u32[]{:S(2)}) %collective-permute-start.8) | collective-permute-done | bytes 16416 | tf_op jit(solution)/shard_map/ppermute | solution.py:481
  61.2 1.5 %collective-permute-start.11 = (f32[32,128]{1,0:T(8,128)S(1)}, f32[32,128]{1,0:T(8,128)S(1)}, u32[]{:S(2)}, u32[]{:S(2)}) collective-permute-start(f32[32,128]{1,0:T(8,128)S(1)} %add.24), channel_id=1, source_target_pairs={{0,6},{2,4},{4,2},{6,0},{1,7},{3,5},{5,3},{7,1},{8,14},{10,12},{12... | collective-permute-start | bytes 49160 | tf_op jit(solution)/shard_map/ppermute | solution.py:483
  62.8 1.4 %collective-permute-start.10 = (f32[32,128]{1,0:T(8,128)S(1)}, f32[32,128]{1,0:T(8,128)S(1)}, u32[]{:S(2)}, u32[]{:S(2)}) collective-permute-start(f32[32,128]{1,0:T(8,128)S(1)} %add.24), channel_id=1, source_target_pairs={{0,4},{2,6},{4,0},{6,2},{1,5},{3,7},{5,1},{7,3},{8,12},{10,14},{12... | collective-permute-start | bytes 49160 | tf_op jit(solution)/shard_map/ppermute | solution.py:483
  64.2 1.2 %collective-permute-start.9 = (f32[32,128]{1,0:T(8,128)S(1)}, f32[32,128]{1,0:T(8,128)S(1)}, u32[]{:S(2)}, u32[]{:S(2)}) collective-permute-start(f32[32,128]{1,0:T(8,128)S(1)} %add.24), channel_id=1, source_target_pairs={{0,2},{2,0},{4,6},{6,4},{1,3},{3,1},{5,7},{7,5},{8,10},{10,8},{12,... | collective-permute-start | bytes 49160 | tf_op jit(solution)/shard_map/ppermute | solution.py:483
  66.2 1.8 %collective-permute-done.10 = f32[32,128]{1,0:T(8,128)S(1)} collective-permute-done((f32[32,128]{1,0:T(8,128)S(1)}, f32[32,128]{1,0:T(8,128)S(1)}, u32[]{:S(2)}, u32[]{:S(2)}) %collective-permute-start.10) | collective-permute-done | bytes 16416 | tf_op jit(solution)/shard_map/ppermute | solution.py:483
  68.1 15.0 %all_to_all.16.gram = f32[16,32,128]{2,1,0:T(8,128)S(1)} all-to-all(f32[16,32,128]{2,1,0:T(8,128)S(1)} %broadcast_in_dim.4), channel_id=1, replica_groups=mesh['gx_0'=4,'gx_1'=4,'gy_0'=4,'gy_1'=2] {'gx_0','gx_1'}, dimensions={0} | all-to-all | bytes 524288 | tf_op jit(solution)/shard_map/all_to_all | solution.py:488
  83.0 5.9 %second_basis.1 = (f32[22,144,128]{2,1,0:T(8,128)S(1)}, f32[22,144,128]{2,1,0:T(8,128)S(1)}, f32[22,144,128]{2,1,0:T(8,128)S(1)}, f32[22,144,128]{2,1,0:T(8,128)...) custom-call(f32[16,32,128]{2,1,0:T(8,128)S(1)} %all_to_all.16.gram, ...), custom_call_target="tpu_custom_call" | custom-call | tf_op jit(solution)/shard_map/second_basis/pallas_call | solution.py:43
  89.0 1.2 %collective-permute-done.12 = f32[32,128]{1,0:T(8,128)S(1)} collective-permute-done((f32[32,128]{1,0:T(8,128)S(1)}, f32[32,128]{1,0:T(8,128)S(1)}, u32[]{:S(2)}, u32[]{:S(2)}) %collective-permute-start.12) | collective-permute-done | bytes 16416 | tf_op jit(solution)/shard_map/ppermute | solution.py:481
  90.2 1.7 %collective-permute-start.15 = (f32[32,128]{1,0:T(8,128)S(1)}, f32[32,128]{1,0:T(8,128)S(1)}, u32[]{:S(2)}, u32[]{:S(2)}) collective-permute-start(f32[32,128]{1,0:T(8,128)S(1)} %add.28), channel_id=1, source_target_pairs={{0,6},{2,4},{4,2},{6,0},{1,7},{3,5},{5,3},{7,1},{8,14},{10,12},{12... | collective-permute-start | bytes 49160 | tf_op jit(solution)/shard_map/ppermute | solution.py:483
  91.9 1.4 %collective-permute-start.14 = (f32[32,128]{1,0:T(8,128)S(1)}, f32[32,128]{1,0:T(8,128)S(1)}, u32[]{:S(2)}, u32[]{:S(2)}) collective-permute-start(f32[32,128]{1,0:T(8,128)S(1)} %add.28), channel_id=1, source_target_pairs={{0,4},{2,6},{4,0},{6,2},{1,5},{3,7},{5,1},{7,3},{8,12},{10,14},{12... | collective-permute-start | bytes 49160 | tf_op jit(solution)/shard_map/ppermute | solution.py:483
  93.3 1.0 collective-permute-start.13
  94.3 0.7 from_lanes.1
  95.1 2.0 %collective-permute-done.14 = f32[32,128]{1,0:T(8,128)S(1)} collective-permute-done((f32[32,128]{1,0:T(8,128)S(1)}, f32[32,128]{1,0:T(8,128)S(1)}, u32[]{:S(2)}, u32[]{:S(2)}) %collective-permute-start.14) | collective-permute-done | bytes 16416 | tf_op jit(solution)/shard_map/ppermute | solution.py:483
  97.2 11.9 %all_to_all.17.gram = f32[16,32,128]{2,1,0:T(8,128)S(1)} all-to-all(f32[16,32,128]{2,1,0:T(8,128)S(1)} %broadcast_in_dim.5), channel_id=1, replica_groups=mesh['gx_0'=4,'gx_1'=4,'gy_0'=4,'gy_1'=2] {'gx_0','gx_1'}, dimensions={0} | all-to-all | bytes 524288 | tf_op jit(solution)/shard_map/all_to_all | solution.py:488
  109.1 4.7 %finish.1 = (f32[1024,128]{1,0:T(8,128)}, f32[1024,128]{1,0:T(8,128)}) custom-call(f32[16,32,128]{2,1,0:T(8,128)S(1)} %all_to_all.17.gram, bf16[8,512,128]{2,1,0:T(8,128)(2,1)S(1)} %get-tuple-element.130.hi, bf16[8,512,128]{2,1,0:T(8,128)(2,1)S(1)} %get-tuple-element.131.lo, f32[8,128,128]{2,1,0:T(8,128)S(1)} %get-tuple-element.132.volts, ...), custom_call_target="tpu_custom_call" | custom-call | tf_op jit(solution)/shard_map/finish/pallas_call | solution.py:43
  (31 shorter events, 2.6 us)
Async XLA Ops:
  0.6 35.5 %copy-start.2 = (f32[64,64]{1,0:T(8,128)S(1)}, f32[64,64]{1,0:T(8,128)}, u32[]{:S(2)}) copy-start(f32[64,64]{1,0:T(8,128)} %waves.1) | copy-start | bytes 49156
  1.4 1.0 copy-start
  2.9 10.4 %collective-permute-start = (f32[128,128]{1,0:T(8,128)S(1)}, f32[128,128]{1,0:T(8,128)S(1)}, u32[]{:S(2)}, u32[]{:S(2)}) collective-permute-start(f32[128,128]{1,0:T(8,128)S(1)} %get-tuple-element.71), channel_id=1, source_target_pairs={{0,1},{1,2},{2,3},{3,4},{4,5},{5,6},{6,7},{7,0},{8,9},{9,10},{10,1... | collective-permute-start | bytes 196616 | tf_op jit(solution)/shard_map/ppermute | solution.py:476
  2.9 10.4 %collective-permute-start.1 = (f32[128,128]{1,0:T(8,128)S(1)}, f32[128,128]{1,0:T(8,128)S(1)}, u32[]{:S(2)}, u32[]{:S(2)}) collective-permute-start(f32[128,128]{1,0:T(8,128)S(1)} %get-tuple-element.72), channel_id=1, source_target_pairs={{1,0},{2,1},{3,2},{4,3},{5,4},{6,5},{7,6},{0,7},{9,8},{10,9},{11,1... | collective-permute-start | bytes 196616 | tf_op jit(solution)/shard_map/ppermute | solution.py:477
  7.2 0.8 copy-start.3
  13.5 38.0 %collective-permute-start.2 = (f32[7,168,128]{2,1,0:T(8,128)S(1)}, f32[7,168,128]{2,1,0:T(8,128)S(1)}, u32[]{:S(2)}, u32[]{:S(2)}) collective-permute-start(f32[7,168,128]{2,1,0:T(8,128)S(1)} %get-tuple-element.80), channel_id=1, source_target_pairs={{0,8},{8,16},{16,24},{24,32},{32,40},{40,48},{48,56},{56,64},{64,7... | collective-permute-start | bytes 1806344 | tf_op jit(solution)/shard_map/ppermute | solution.py:476
  15.2 36.4 %collective-permute-start.3 = (f32[7,168,128]{2,1,0:T(8,128)S(1)}, f32[7,168,128]{2,1,0:T(8,128)S(1)}, u32[]{:S(2)}, u32[]{:S(2)}) collective-permute-start(f32[7,168,128]{2,1,0:T(8,128)S(1)} %get-tuple-element.81), channel_id=1, source_target_pairs={{8,0},{16,8},{24,16},{32,24},{40,32},{48,40},{56,48},{64,56},{72,6... | collective-permute-start | bytes 1806344 | tf_op jit(solution)/shard_map/ppermute | solution.py:477
  41.4 4.6 %collective-permute-start.4 = (f32[64,128]{1,0:T(8,128)S(1)}, f32[64,128]{1,0:T(8,128)S(1)}, u32[]{:S(2)}, u32[]{:S(2)}) collective-permute-start(f32[64,128]{1,0:T(8,128)S(1)} %get-tuple-element.82), channel_id=1, source_target_pairs={{0,1},{1,2},{2,3},{3,4},{4,5},{5,6},{6,7},{7,0},{8,9},{9,10},{10,1... | collective-permute-start | bytes 98312 | tf_op jit(solution)/shard_map/ppermute | solution.py:476
  41.5 4.4 %collective-permute-start.5 = (f32[64,128]{1,0:T(8,128)S(1)}, f32[64,128]{1,0:T(8,128)S(1)}, u32[]{:S(2)}, u32[]{:S(2)}) collective-permute-start(f32[64,128]{1,0:T(8,128)S(1)} %get-tuple-element.83), channel_id=1, source_target_pairs={{1,0},{2,1},{3,2},{4,3},{5,4},{6,5},{7,6},{0,7},{9,8},{10,9},{11,1... | collective-permute-start | bytes 98312 | tf_op jit(solution)/shard_map/ppermute | solution.py:477
  46.1 9.7 %collective-permute-start.6 = (f32[3,144,128]{2,1,0:T(8,128)S(1)}, f32[3,144,128]{2,1,0:T(8,128)S(1)}, u32[]{:S(2)}, u32[]{:S(2)}) collective-permute-start(f32[3,144,128]{2,1,0:T(8,128)S(1)} %get-tuple-element.105), channel_id=1, source_target_pairs={{0,8},{8,16},{16,24},{24,32},{32,40},{40,48},{48,56},{56,64},{64,7... | collective-permute-start | bytes 663560 | tf_op jit(solution)/shard_map/ppermute | solution.py:476
  47.4 8.4 %collective-permute-start.7 = (f32[3,144,128]{2,1,0:T(8,128)S(1)}, f32[3,144,128]{2,1,0:T(8,128)S(1)}, u32[]{:S(2)}, u32[]{:S(2)}) collective-permute-start(f32[3,144,128]{2,1,0:T(8,128)S(1)} %get-tuple-element.106), channel_id=1, source_target_pairs={{8,0},{16,8},{24,16},{32,24},{40,32},{48,40},{56,48},{64,56},{72,6... | collective-permute-start | bytes 663560 | tf_op jit(solution)/shard_map/ppermute | solution.py:477
  60.0 1.3 %collective-permute-start.8 = (f32[32,128]{1,0:T(8,128)S(1)}, f32[32,128]{1,0:T(8,128)S(1)}, u32[]{:S(2)}, u32[]{:S(2)}) collective-permute-start(f32[32,128]{1,0:T(8,128)S(1)} %get-tuple-element.107), channel_id=1, source_target_pairs={{0,1},{1,0},{2,3},{3,2},{4,5},{5,4},{6,7},{7,6},{8,9},{9,8},{10,11... | collective-permute-start | bytes 49160 | tf_op jit(solution)/shard_map/ppermute | solution.py:481
  61.2 4.9 %collective-permute-start.11 = (f32[32,128]{1,0:T(8,128)S(1)}, f32[32,128]{1,0:T(8,128)S(1)}, u32[]{:S(2)}, u32[]{:S(2)}) collective-permute-start(f32[32,128]{1,0:T(8,128)S(1)} %add.24), channel_id=1, source_target_pairs={{0,6},{2,4},{4,2},{6,0},{1,7},{3,5},{5,3},{7,1},{8,14},{10,12},{12... | collective-permute-start | bytes 49160 | tf_op jit(solution)/shard_map/ppermute | solution.py:483
  62.8 5.2 %collective-permute-start.10 = (f32[32,128]{1,0:T(8,128)S(1)}, f32[32,128]{1,0:T(8,128)S(1)}, u32[]{:S(2)}, u32[]{:S(2)}) collective-permute-start(f32[32,128]{1,0:T(8,128)S(1)} %add.24), channel_id=1, source_target_pairs={{0,4},{2,6},{4,0},{6,2},{1,5},{3,7},{5,1},{7,3},{8,12},{10,14},{12... | collective-permute-start | bytes 49160 | tf_op jit(solution)/shard_map/ppermute | solution.py:483
  64.2 3.9 %collective-permute-start.9 = (f32[32,128]{1,0:T(8,128)S(1)}, f32[32,128]{1,0:T(8,128)S(1)}, u32[]{:S(2)}, u32[]{:S(2)}) collective-permute-start(f32[32,128]{1,0:T(8,128)S(1)} %add.24), channel_id=1, source_target_pairs={{0,2},{2,0},{4,6},{6,4},{1,3},{3,1},{5,7},{7,5},{8,10},{10,8},{12,... | collective-permute-start | bytes 49160 | tf_op jit(solution)/shard_map/ppermute | solution.py:483
  83.0 11.2 %copy-start.1 = (f32[32,4,8,128]{3,2,1,0:T(8,128)S(1)}, f32[32,4,8,128]{3,2,1,0:T(8,128)}, u32[]{:S(2)}) copy-start(f32[32,4,8,128]{3,2,1,0:T(8,128)} %param.10) | copy-start | bytes 1572868
  88.9 1.3 %collective-permute-start.12 = (f32[32,128]{1,0:T(8,128)S(1)}, f32[32,128]{1,0:T(8,128)S(1)}, u32[]{:S(2)}, u32[]{:S(2)}) collective-permute-start(f32[32,128]{1,0:T(8,128)S(1)} %get-tuple-element.119), channel_id=1, source_target_pairs={{0,1},{1,0},{2,3},{3,2},{4,5},{5,4},{6,7},{7,6},{8,9},{9,8},{10,11... | collective-permute-start | bytes 49160 | tf_op jit(solution)/shard_map/ppermute | solution.py:481
  90.2 4.9 %collective-permute-start.15 = (f32[32,128]{1,0:T(8,128)S(1)}, f32[32,128]{1,0:T(8,128)S(1)}, u32[]{:S(2)}, u32[]{:S(2)}) collective-permute-start(f32[32,128]{1,0:T(8,128)S(1)} %add.28), channel_id=1, source_target_pairs={{0,6},{2,4},{4,2},{6,0},{1,7},{3,5},{5,3},{7,1},{8,14},{10,12},{12... | collective-permute-start | bytes 49160 | tf_op jit(solution)/shard_map/ppermute | solution.py:483
  91.9 5.2 %collective-permute-start.14 = (f32[32,128]{1,0:T(8,128)S(1)}, f32[32,128]{1,0:T(8,128)S(1)}, u32[]{:S(2)}, u32[]{:S(2)}) collective-permute-start(f32[32,128]{1,0:T(8,128)S(1)} %add.28), channel_id=1, source_target_pairs={{0,4},{2,6},{4,0},{6,2},{1,5},{3,7},{5,1},{7,3},{8,12},{10,14},{12... | collective-permute-start | bytes 49160 | tf_op jit(solution)/shard_map/ppermute | solution.py:483
  93.3 3.8 %collective-permute-start.13 = (f32[32,128]{1,0:T(8,128)S(1)}, f32[32,128]{1,0:T(8,128)S(1)}, u32[]{:S(2)}, u32[]{:S(2)}) collective-permute-start(f32[32,128]{1,0:T(8,128)S(1)} %add.28), channel_id=1, source_target_pairs={{0,2},{2,0},{4,6},{6,4},{1,3},{3,1},{5,7},{7,5},{8,10},{10,8},{12,... | collective-permute-start | bytes 49160 | tf_op jit(solution)/shard_map/ppermute | solution.py:483

commit v9 on v8

--- a/solution.py
+++ b/solution.py
@@ -88,17 +88,18 @@
             last_out[x - 1] = row
 
 
-def place_slots(listed, amps, out, acc):
-    acc[...] = jnp.zeros_like(acc)
+def place_slots(listed, amps, out):
     lane = iota((128, 256), 1)
     before = ((iota((128, 256), 0) < lane) | (lane >= 128)).astype(F32).astype(BF16)
     tile_line = iota((128, 128), 0)
 
-    def chunk(turn, seen):
-        at = pl.ds(pl.multiple_of(turn * 8, 8), 8)
+    lefts, rights = [], []
+    seen = jnp.zeros((128, 128), F32)
+    for turn in range(8):
+        at = slice(turn * 8, turn * 8 + 8)
         tiles = listed[at, :]
-        cells = listed[pl.ds(pl.multiple_of(64 + turn * 8, 8), 8), :]
-        code = cells * 64 + listed[pl.ds(pl.multiple_of(128 + turn * 8, 8), 8), :]
+        cells = listed[64 + turn * 8 : 72 + turn * 8, :]
+        code = cells * 64 + listed[128 + turn * 8 : 136 + turn * 8, :]
         parts = list(split2(amps[at, :]))
         parts.append((code >> 8).astype(F32).astype(BF16))
         parts.append((code & 255).astype(F32).astype(BF16))
@@ -120,10 +121,10 @@
             wide = part.astype(F32)
             wide = jnp.concatenate([wide[j : j + 1, :] for j in range(8)], axis=1)
             left.append(hit * wide.astype(BF16))
-        acc[...] += dot(jnp.concatenate(left, axis=0), slot, ((1,), (1,)))
-        return seen
-
-    lax.fori_loop(0, 8, chunk, jnp.zeros((128, 128), F32), unroll=8)
+        lefts.append(jnp.concatenate(left, axis=0))
+        rights.append(slot)
+
+    acc = dot(jnp.concatenate(lefts, axis=1), jnp.concatenate(rights, axis=1), ((1,), (1,)))
     out[:, 0, :] = acc[0:128] + acc[128:256]
     out[:, 1, :] = acc[256:384] * 256.0 + acc[384:512]
 
@@ -131,12 +132,12 @@
 def add_currents(slots, waves, out, low_out, high_out, acc):
     acc[...] = jnp.zeros_like(acc)
     table = jnp.concatenate([p.astype(F32) for p in split3(waves[...])], axis=1).astype(BF16)
-    wave_line = iota((64, 4096), 0).astype(F32).astype(BF16)
-    cell_line = iota((256, 4096), 0).astype(F32).astype(BF16)
+    wave_line = iota((64, 16384), 0).astype(F32).astype(BF16)
+    cell_line = iota((256, 16384), 0).astype(F32).astype(BF16)
     one, zero = jnp.ones((), BF16), jnp.zeros((), BF16)
 
     def chunk(turn, carry):
-        rows = [slots[turn * 32 + j] for j in range(32)]
+        rows = [slots[turn * 128 + j] for j in range(128)]
         amp = jnp.concatenate([r[0:1, :] for r in rows], axis=1)
         code = jnp.concatenate([r[1:2, :] for r in rows], axis=1).astype(jnp.int32)
         hit = jnp.where(wave_line == (code & 63).astype(F32).astype(BF16), one, zero)
@@ -149,7 +150,7 @@
         acc[...] += dot(left, jnp.concatenate(right, axis=0), ((1,), (1,)))
         return carry
 
-    lax.fori_loop(0, 4, chunk, 0, unroll=4)
+    lax.fori_loop(0, 1, chunk, 0, unroll=1)
     low_lanes = iota((256, 128), 1) < 64
     for r in range(4):
         half = acc[:, (r // 2) * 128 : (r // 2 + 1) * 128]
@@ -506,7 +507,6 @@
         place_slots,
         [(128, 2, 128)],
         [jnp.concatenate(listed, axis=0), amps.reshape(64, 128)],
-        [vmem((512, 128), F32)],
     )
     y_low, y_high, slots = lax.optimization_barrier((y_low, y_high, slots))
     x_low, x_high = call(pack_rows, [(7, 168, 128)] * 2, [v, c, y_low, y_high])

time: 114 us -> 112 us (0.982)
  Pallas kernels: 31.5 us -> 28.9 us
    pallas_call x12, Pallas kernels: 31.5 us -> 28.9 us  [call(): pl.pallas_call(kernel, out_shape=tuple(outs), scratch_shapes=list(scratch...]
  transfers between devices with their start and end apart: 16 -> 16, of which waited for: 8 -> 8; matrix products, arithmetic and copies ran while one was open for 1% -> 1% of each run, Pallas kernels for 14% -> 12%
where the time goes in v9:
time: 112 us; the launch traced here: 111 us
  blocking collectives  44.1 us (39%)
  Pallas kernels  28.9 us (26%)
  starting transfers between devices  25.8 us (23%)
  waiting for transfers between devices  8.23 us (7%)
  local copies, waits for them, and re-layouts  1.84 us (2%)
  other arithmetic  1.6 us (1%)
    pallas_call x12, Pallas kernels, call(): pl.pallas_call(kernel, out_shape=tuple(outs), scratch_shapes=list(scratch...  28.9 us
    all_to_all x2, blocking collectives, everywhere(): lax.all_to_all(x, GX, split_axis=0, concat_axis=0, tiled=True)  26.9 us
    all_to_all x1, blocking collectives, exchange(): return lax.all_to_all(slots, GX_GY, split_axis=0, concat_axis=0, tiled=True)  17.2 us
    ppermute x4, starting transfers between devices, neighbours(): return (from_low, lax.ppermute(to_low, axis, [(b, a) for a, b in up]))  14.4 us
    ppermute x6, starting transfers between devices, everywhere(): lax.ppermute(x, 'gy_0', [(i, i ^ k) for i in range(4)])  8.19 us
    ppermute x6, waiting for transfers between devices, everywhere(): lax.ppermute(x, 'gy_0', [(i, i ^ k) for i in range(4)])  4.11 us
    ppermute x4, starting transfers between devices, neighbours(): from_low = lax.ppermute(to_high, axis, up)  3.04 us
    ppermute x2, waiting for transfers between devices, everywhere(): x = x + lax.ppermute(x, 'gy_1', [(0, 1), (1, 0)])  2.34 us
  transfers between devices with their start and end apart: 16, of which 8 were waited for; matrix products, arithmetic and copies ran while one was open for 1% of the time, Pallas kernels for 12%

profile of v9, /device:TPU:0, one launch (start us, length us, event | category | flops | bytes accessed | tf_op | source)
XLA Modules:
  0.0 111.2 jit_solution(18114247457109548688)
XLA Ops:
  0.6 0.8 pad_maximum_fusion.stack
  1.4 1.0 copy-done
  2.9 3.6 %collective-permute-start.1 = (f32[128,128]{1,0:T(8,128)S(1)}, f32[128,128]{1,0:T(8,128)S(1)}, u32[]{:S(2)}, u32[]{:S(2)}) collective-permute-start(f32[128,128]{1,0:T(8,128)S(1)} %get-tuple-element.72), channel_id=1, source_target_pairs={{1,0},{2,1},{3,2},{4,3},{5,4},{6,5},{7,6},{0,7},{9,8},{10,9},{11,1... | collective-permute-start | bytes 196616 | tf_op jit(solution)/shard_map/ppermute | solution.py:478
  6.4 0.8 pad_add_fusion.listed
  7.2 0.8 copy-done.3
  8.0 4.2 %place_slots.1 = f32[128,2,128]{2,1,0:T(2,128)S(1)} custom-call(s32[192,128]{1,0:T(8,128)S(1)} %pad_add_fusion.listed, f32[64,128]{1,0:T(8,128)S(1)} %bitcast.13), custom_call_target="tpu_custom_call" | custom-call | tf_op jit(solution)/shard_map/place_slots/pallas_call | solution.py:43
  12.4 1.6 %collective-permute-start.2 = (f32[7,168,128]{2,1,0:T(8,128)S(1)}, f32[7,168,128]{2,1,0:T(8,128)S(1)}, u32[]{:S(2)}, u32[]{:S(2)}) collective-permute-start(f32[7,168,128]{2,1,0:T(8,128)S(1)} %get-tuple-element.80), channel_id=1, source_target_pairs={{0,8},{8,16},{16,24},{24,32},{32,40},{40,48},{48,56},{56,64},{64,7... | collective-permute-start | bytes 1806344 | tf_op jit(solution)/shard_map/ppermute | solution.py:477
  14.1 3.8 %collective-permute-start.3 = (f32[7,168,128]{2,1,0:T(8,128)S(1)}, f32[7,168,128]{2,1,0:T(8,128)S(1)}, u32[]{:S(2)}, u32[]{:S(2)}) collective-permute-start(f32[7,168,128]{2,1,0:T(8,128)S(1)} %get-tuple-element.81), channel_id=1, source_target_pairs={{8,0},{16,8},{24,16},{32,24},{40,32},{48,40},{56,48},{64,56},{72,6... | collective-permute-start | bytes 1806344 | tf_op jit(solution)/shard_map/ppermute | solution.py:478
  17.9 17.2 %all_to_all.15.slots = f32[128,2,128]{2,1,0:T(2,128)S(1)} all-to-all(f32[128,2,128]{2,1,0:T(2,128)S(1)} %place_slots.1), channel_id=1, replica_groups=mesh['gx_0'=4,'gx_1'=4,'gy_0'=4,'gy_1'=2] {'gx_0','gx_1','gy_0','gy_1'}, dimensions={0} | all-to-all | bytes 262144 | tf_op jit(solution)/shard_map/all_to_all | solution.py:493
  35.1 3.7 %add_currents.1 = (f32[8,128,128]{2,1,0:T(8,128)S(1)}, f32[64,128]{1,0:T(8,128)S(1)}, f32[64,128]{1,0:T(8,128)S(1)}) custom-call(f32[128,2,128]{2,1,0:T(2,128)S(1)} %all_to_all.15.slots, f32[64,64]{1,0:T(8,128)S(1)} %copy-done.2), custom_call_target="tpu_custom_call" | custom-call | tf_op jit(solution)/shard_map/add_currents/pallas_call | solution.py:43
  38.9 2.9 %collective-permute-start.5 = (f32[64,128]{1,0:T(8,128)S(1)}, f32[64,128]{1,0:T(8,128)S(1)}, u32[]{:S(2)}, u32[]{:S(2)}) collective-permute-start(f32[64,128]{1,0:T(8,128)S(1)} %get-tuple-element.83), channel_id=1, source_target_pairs={{1,0},{2,1},{3,2},{4,3},{5,4},{6,5},{7,6},{0,7},{9,8},{10,9},{11,1... | collective-permute-start | bytes 98312 | tf_op jit(solution)/shard_map/ppermute | solution.py:478
  41.8 1.1 own_weights.1
  43.5 1.3 %collective-permute-start.6 = (f32[3,144,128]{2,1,0:T(8,128)S(1)}, f32[3,144,128]{2,1,0:T(8,128)S(1)}, u32[]{:S(2)}, u32[]{:S(2)}) collective-permute-start(f32[3,144,128]{2,1,0:T(8,128)S(1)} %get-tuple-element.105), channel_id=1, source_target_pairs={{0,8},{8,16},{16,24},{24,32},{32,40},{40,48},{48,56},{56,64},{64,7... | collective-permute-start | bytes 663560 | tf_op jit(solution)/shard_map/ppermute | solution.py:477
  44.8 4.2 %collective-permute-start.7 = (f32[3,144,128]{2,1,0:T(8,128)S(1)}, f32[3,144,128]{2,1,0:T(8,128)S(1)}, u32[]{:S(2)}, u32[]{:S(2)}) collective-permute-start(f32[3,144,128]{2,1,0:T(8,128)S(1)} %get-tuple-element.106), channel_id=1, source_target_pairs={{8,0},{16,8},{24,16},{32,24},{40,32},{48,40},{56,48},{64,56},{72,6... | collective-permute-start | bytes 663560 | tf_op jit(solution)/shard_map/ppermute | solution.py:478
  49.0 3.0 %grid_weights.1 = (f32[22,144,128]{2,1,0:T(8,128)S(1)}, f32[22,144,128]{2,1,0:T(8,128)S(1)}, f32[22,144,128]{2,1,0:T(8,128)S(1)}, f32[22,144,128]{2,1,0:T(8,128)...) custom-call(f32[8,128,128]{2,1,0:T(8,128)S(1)} %get-tuple-element.77.v, ...), custom_call_target="tpu_custom_call" | custom-call | tf_op jit(solution)/shard_map/grid_weights/pallas_call | solution.py:43
  52.0 1.2 %collective-permute-done.6.ix_low = f32[3,144,128]{2,1,0:T(8,128)S(1)} collective-permute-done((f32[3,144,128]{2,1,0:T(8,128)S(1)}, f32[3,144,128]{2,1,0:T(8,128)S(1)}, u32[]{:S(2)}, u32[]{:S(2)}) %collective-permute-start.6) | collective-permute-done | bytes 221216 | tf_op jit(solution)/shard_map/ppermute | solution.py:477
  53.2 4.2 %first_basis.1 = (f32[22,144,128]{2,1,0:T(8,128)S(1)}, f32[22,144,128]{2,1,0:T(8,128)S(1)}, f32[22,144,128]{2,1,0:T(8,128)S(1)}, f32[22,144,128]{2,1,0:T(8,128)S...) custom-call(f32[22,144,128]{2,1,0:T(8,128)S(1)} %get-tuple-element.97.diag, ...), custom_call_target="tpu_custom_call" | custom-call | tf_op jit(solution)/shard_map/first_basis/pallas_call | solution.py:43
  57.5 1.2 %collective-permute-done.8 = f32[32,128]{1,0:T(8,128)S(1)} collective-permute-done((f32[32,128]{1,0:T(8,128)S(1)}, f32[32,128]{1,0:T(8,128)S(1)}, u32[]{:S(2)}, u32[]{:S(2)}) %collective-permute-start.8) | collective-permute-done | bytes 16416 | tf_op jit(solution)/shard_map/ppermute | solution.py:482
  58.7 1.5 %collective-permute-start.11 = (f32[32,128]{1,0:T(8,128)S(1)}, f32[32,128]{1,0:T(8,128)S(1)}, u32[]{:S(2)}, u32[]{:S(2)}) collective-permute-start(f32[32,128]{1,0:T(8,128)S(1)} %add.24), channel_id=1, source_target_pairs={{0,6},{2,4},{4,2},{6,0},{1,7},{3,5},{5,3},{7,1},{8,14},{10,12},{12... | collective-permute-start | bytes 49160 | tf_op jit(solution)/shard_map/ppermute | solution.py:484
  60.2 1.4 %collective-permute-start.10 = (f32[32,128]{1,0:T(8,128)S(1)}, f32[32,128]{1,0:T(8,128)S(1)}, u32[]{:S(2)}, u32[]{:S(2)}) collective-permute-start(f32[32,128]{1,0:T(8,128)S(1)} %add.24), channel_id=1, source_target_pairs={{0,4},{2,6},{4,0},{6,2},{1,5},{3,7},{5,1},{7,3},{8,12},{10,14},{12... | collective-permute-start | bytes 49160 | tf_op jit(solution)/shard_map/ppermute | solution.py:484
  61.6 1.2 %collective-permute-start.9 = (f32[32,128]{1,0:T(8,128)S(1)}, f32[32,128]{1,0:T(8,128)S(1)}, u32[]{:S(2)}, u32[]{:S(2)}) collective-permute-start(f32[32,128]{1,0:T(8,128)S(1)} %add.24), channel_id=1, source_target_pairs={{0,2},{2,0},{4,6},{6,4},{1,3},{3,1},{5,7},{7,5},{8,10},{10,8},{12,... | collective-permute-start | bytes 49160 | tf_op jit(solution)/shard_map/ppermute | solution.py:484
  63.6 1.8 %collective-permute-done.10 = f32[32,128]{1,0:T(8,128)S(1)} collective-permute-done((f32[32,128]{1,0:T(8,128)S(1)}, f32[32,128]{1,0:T(8,128)S(1)}, u32[]{:S(2)}, u32[]{:S(2)}) %collective-permute-start.10) | collective-permute-done | bytes 16416 | tf_op jit(solution)/shard_map/ppermute | solution.py:484
  65.5 15.0 %all_to_all.16.gram = f32[16,32,128]{2,1,0:T(8,128)S(1)} all-to-all(f32[16,32,128]{2,1,0:T(8,128)S(1)} %broadcast_in_dim.4), channel_id=1, replica_groups=mesh['gx_0'=4,'gx_1'=4,'gy_0'=4,'gy_1'=2] {'gx_0','gx_1'}, dimensions={0} | all-to-all | bytes 524288 | tf_op jit(solution)/shard_map/all_to_all | solution.py:489
  80.5 5.9 %second_basis.1 = (f32[22,144,128]{2,1,0:T(8,128)S(1)}, f32[22,144,128]{2,1,0:T(8,128)S(1)}, f32[22,144,128]{2,1,0:T(8,128)S(1)}, f32[22,144,128]{2,1,0:T(8,128)...) custom-call(f32[16,32,128]{2,1,0:T(8,128)S(1)} %all_to_all.16.gram, ...), custom_call_target="tpu_custom_call" | custom-call | tf_op jit(solution)/shard_map/second_basis/pallas_call | solution.py:43
  86.4 1.2 %collective-permute-done.12 = f32[32,128]{1,0:T(8,128)S(1)} collective-permute-done((f32[32,128]{1,0:T(8,128)S(1)}, f32[32,128]{1,0:T(8,128)S(1)}, u32[]{:S(2)}, u32[]{:S(2)}) %collective-permute-start.12) | collective-permute-done | bytes 16416 | tf_op jit(solution)/shard_map/ppermute | solution.py:482
  87.6 1.7 %collective-permute-start.15 = (f32[32,128]{1,0:T(8,128)S(1)}, f32[32,128]{1,0:T(8,128)S(1)}, u32[]{:S(2)}, u32[]{:S(2)}) collective-permute-start(f32[32,128]{1,0:T(8,128)S(1)} %add.28), channel_id=1, source_target_pairs={{0,6},{2,4},{4,2},{6,0},{1,7},{3,5},{5,3},{7,1},{8,14},{10,12},{12... | collective-permute-start | bytes 49160 | tf_op jit(solution)/shard_map/ppermute | solution.py:484
  89.3 1.4 %collective-permute-start.14 = (f32[32,128]{1,0:T(8,128)S(1)}, f32[32,128]{1,0:T(8,128)S(1)}, u32[]{:S(2)}, u32[]{:S(2)}) collective-permute-start(f32[32,128]{1,0:T(8,128)S(1)} %add.28), channel_id=1, source_target_pairs={{0,4},{2,6},{4,0},{6,2},{1,5},{3,7},{5,1},{7,3},{8,12},{10,14},{12... | collective-permute-start | bytes 49160 | tf_op jit(solution)/shard_map/ppermute | solution.py:484
  90.7 1.0 collective-permute-start.13
  91.7 0.7 from_lanes.1
  92.5 2.0 %collective-permute-done.14 = f32[32,128]{1,0:T(8,128)S(1)} collective-permute-done((f32[32,128]{1,0:T(8,128)S(1)}, f32[32,128]{1,0:T(8,128)S(1)}, u32[]{:S(2)}, u32[]{:S(2)}) %collective-permute-start.14) | collective-permute-done | bytes 16416 | tf_op jit(solution)/shard_map/ppermute | solution.py:484
  94.6 11.9 %all_to_all.17.gram = f32[16,32,128]{2,1,0:T(8,128)S(1)} all-to-all(f32[16,32,128]{2,1,0:T(8,128)S(1)} %broadcast_in_dim.5), channel_id=1, replica_groups=mesh['gx_0'=4,'gx_1'=4,'gy_0'=4,'gy_1'=2] {'gx_0','gx_1'}, dimensions={0} | all-to-all | bytes 524288 | tf_op jit(solution)/shard_map/all_to_all | solution.py:489
  106.5 4.7 %finish.1 = (f32[1024,128]{1,0:T(8,128)}, f32[1024,128]{1,0:T(8,128)}) custom-call(f32[16,32,128]{2,1,0:T(8,128)S(1)} %all_to_all.17.gram, bf16[8,512,128]{2,1,0:T(8,128)(2,1)S(1)} %get-tuple-element.130.hi, bf16[8,512,128]{2,1,0:T(8,128)(2,1)S(1)} %get-tuple-element.131.lo, f32[8,128,128]{2,1,0:T(8,128)S(1)} %get-tuple-element.132.volts, ...), custom_call_target="tpu_custom_call" | custom-call | tf_op jit(solution)/shard_map/finish/pallas_call | solution.py:43
  (31 shorter events, 2.6 us)
Async XLA Ops:
  0.6 34.5 %copy-start.2 = (f32[64,64]{1,0:T(8,128)S(1)}, f32[64,64]{1,0:T(8,128)}, u32[]{:S(2)}) copy-start(f32[64,64]{1,0:T(8,128)} %waves.1) | copy-start | bytes 49156
  1.4 1.0 copy-start
  2.9 9.4 %collective-permute-start = (f32[128,128]{1,0:T(8,128)S(1)}, f32[128,128]{1,0:T(8,128)S(1)}, u32[]{:S(2)}, u32[]{:S(2)}) collective-permute-start(f32[128,128]{1,0:T(8,128)S(1)} %get-tuple-element.71), channel_id=1, source_target_pairs={{0,1},{1,2},{2,3},{3,4},{4,5},{5,6},{6,7},{7,0},{8,9},{9,10},{10,1... | collective-permute-start | bytes 196616 | tf_op jit(solution)/shard_map/ppermute | solution.py:477
  2.9 9.3 %collective-permute-start.1 = (f32[128,128]{1,0:T(8,128)S(1)}, f32[128,128]{1,0:T(8,128)S(1)}, u32[]{:S(2)}, u32[]{:S(2)}) collective-permute-start(f32[128,128]{1,0:T(8,128)S(1)} %get-tuple-element.72), channel_id=1, source_target_pairs={{1,0},{2,1},{3,2},{4,3},{5,4},{6,5},{7,6},{0,7},{9,8},{10,9},{11,1... | collective-permute-start | bytes 196616 | tf_op jit(solution)/shard_map/ppermute | solution.py:478
  7.2 0.8 copy-start.3
  12.4 36.5 %collective-permute-start.2 = (f32[7,168,128]{2,1,0:T(8,128)S(1)}, f32[7,168,128]{2,1,0:T(8,128)S(1)}, u32[]{:S(2)}, u32[]{:S(2)}) collective-permute-start(f32[7,168,128]{2,1,0:T(8,128)S(1)} %get-tuple-element.80), channel_id=1, source_target_pairs={{0,8},{8,16},{16,24},{24,32},{32,40},{40,48},{48,56},{56,64},{64,7... | collective-permute-start | bytes 1806344 | tf_op jit(solution)/shard_map/ppermute | solution.py:477
  14.1 34.9 %collective-permute-start.3 = (f32[7,168,128]{2,1,0:T(8,128)S(1)}, f32[7,168,128]{2,1,0:T(8,128)S(1)}, u32[]{:S(2)}, u32[]{:S(2)}) collective-permute-start(f32[7,168,128]{2,1,0:T(8,128)S(1)} %get-tuple-element.81), channel_id=1, source_target_pairs={{8,0},{16,8},{24,16},{32,24},{40,32},{48,40},{56,48},{64,56},{72,6... | collective-permute-start | bytes 1806344 | tf_op jit(solution)/shard_map/ppermute | solution.py:478
  38.8 4.6 %collective-permute-start.4 = (f32[64,128]{1,0:T(8,128)S(1)}, f32[64,128]{1,0:T(8,128)S(1)}, u32[]{:S(2)}, u32[]{:S(2)}) collective-permute-start(f32[64,128]{1,0:T(8,128)S(1)} %get-tuple-element.82), channel_id=1, source_target_pairs={{0,1},{1,2},{2,3},{3,4},{4,5},{5,6},{6,7},{7,0},{8,9},{9,10},{10,1... | collective-permute-start | bytes 98312 | tf_op jit(solution)/shard_map/ppermute | solution.py:477
  38.9 4.5 %collective-permute-start.5 = (f32[64,128]{1,0:T(8,128)S(1)}, f32[64,128]{1,0:T(8,128)S(1)}, u32[]{:S(2)}, u32[]{:S(2)}) collective-permute-start(f32[64,128]{1,0:T(8,128)S(1)} %get-tuple-element.83), channel_id=1, source_target_pairs={{1,0},{2,1},{3,2},{4,3},{5,4},{6,5},{7,6},{0,7},{9,8},{10,9},{11,1... | collective-permute-start | bytes 98312 | tf_op jit(solution)/shard_map/ppermute | solution.py:478
  43.5 9.7 %collective-permute-start.6 = (f32[3,144,128]{2,1,0:T(8,128)S(1)}, f32[3,144,128]{2,1,0:T(8,128)S(1)}, u32[]{:S(2)}, u32[]{:S(2)}) collective-permute-start(f32[3,144,128]{2,1,0:T(8,128)S(1)} %get-tuple-element.105), channel_id=1, source_target_pairs={{0,8},{8,16},{16,24},{24,32},{32,40},{40,48},{48,56},{56,64},{64,7... | collective-permute-start | bytes 663560 | tf_op jit(solution)/shard_map/ppermute | solution.py:477
  44.8 8.4 %collective-permute-start.7 = (f32[3,144,128]{2,1,0:T(8,128)S(1)}, f32[3,144,128]{2,1,0:T(8,128)S(1)}, u32[]{:S(2)}, u32[]{:S(2)}) collective-permute-start(f32[3,144,128]{2,1,0:T(8,128)S(1)} %get-tuple-element.106), channel_id=1, source_target_pairs={{8,0},{16,8},{24,16},{32,24},{40,32},{48,40},{56,48},{64,56},{72,6... | collective-permute-start | bytes 663560 | tf_op jit(solution)/shard_map/ppermute | solution.py:478
  57.4 1.3 %collective-permute-start.8 = (f32[32,128]{1,0:T(8,128)S(1)}, f32[32,128]{1,0:T(8,128)S(1)}, u32[]{:S(2)}, u32[]{:S(2)}) collective-permute-start(f32[32,128]{1,0:T(8,128)S(1)} %get-tuple-element.107), channel_id=1, source_target_pairs={{0,1},{1,0},{2,3},{3,2},{4,5},{5,4},{6,7},{7,6},{8,9},{9,8},{10,11... | collective-permute-start | bytes 49160 | tf_op jit(solution)/shard_map/ppermute | solution.py:482
  58.7 4.9 %collective-permute-start.11 = (f32[32,128]{1,0:T(8,128)S(1)}, f32[32,128]{1,0:T(8,128)S(1)}, u32[]{:S(2)}, u32[]{:S(2)}) collective-permute-start(f32[32,128]{1,0:T(8,128)S(1)} %add.24), channel_id=1, source_target_pairs={{0,6},{2,4},{4,2},{6,0},{1,7},{3,5},{5,3},{7,1},{8,14},{10,12},{12... | collective-permute-start | bytes 49160 | tf_op jit(solution)/shard_map/ppermute | solution.py:484
  60.2 5.2 %collective-permute-start.10 = (f32[32,128]{1,0:T(8,128)S(1)}, f32[32,128]{1,0:T(8,128)S(1)}, u32[]{:S(2)}, u32[]{:S(2)}) collective-permute-start(f32[32,128]{1,0:T(8,128)S(1)} %add.24), channel_id=1, source_target_pairs={{0,4},{2,6},{4,0},{6,2},{1,5},{3,7},{5,1},{7,3},{8,12},{10,14},{12... | collective-permute-start | bytes 49160 | tf_op jit(solution)/shard_map/ppermute | solution.py:484
  61.6 3.9 %collective-permute-start.9 = (f32[32,128]{1,0:T(8,128)S(1)}, f32[32,128]{1,0:T(8,128)S(1)}, u32[]{:S(2)}, u32[]{:S(2)}) collective-permute-start(f32[32,128]{1,0:T(8,128)S(1)} %add.24), channel_id=1, source_target_pairs={{0,2},{2,0},{4,6},{6,4},{1,3},{3,1},{5,7},{7,5},{8,10},{10,8},{12,... | collective-permute-start | bytes 49160 | tf_op jit(solution)/shard_map/ppermute | solution.py:484
  80.5 11.2 %copy-start.1 = (f32[32,4,8,128]{3,2,1,0:T(8,128)S(1)}, f32[32,4,8,128]{3,2,1,0:T(8,128)}, u32[]{:S(2)}) copy-start(f32[32,4,8,128]{3,2,1,0:T(8,128)} %param.10) | copy-start | bytes 1572868
  86.3 1.3 %collective-permute-start.12 = (f32[32,128]{1,0:T(8,128)S(1)}, f32[32,128]{1,0:T(8,128)S(1)}, u32[]{:S(2)}, u32[]{:S(2)}) collective-permute-start(f32[32,128]{1,0:T(8,128)S(1)} %get-tuple-element.119), channel_id=1, source_target_pairs={{0,1},{1,0},{2,3},{3,2},{4,5},{5,4},{6,7},{7,6},{8,9},{9,8},{10,11... | collective-permute-start | bytes 49160 | tf_op jit(solution)/shard_map/ppermute | solution.py:482
  87.6 4.9 %collective-permute-start.15 = (f32[32,128]{1,0:T(8,128)S(1)}, f32[32,128]{1,0:T(8,128)S(1)}, u32[]{:S(2)}, u32[]{:S(2)}) collective-permute-start(f32[32,128]{1,0:T(8,128)S(1)} %add.28), channel_id=1, source_target_pairs={{0,6},{2,4},{4,2},{6,0},{1,7},{3,5},{5,3},{7,1},{8,14},{10,12},{12... | collective-permute-start | bytes 49160 | tf_op jit(solution)/shard_map/ppermute | solution.py:484
  89.3 5.2 %collective-permute-start.14 = (f32[32,128]{1,0:T(8,128)S(1)}, f32[32,128]{1,0:T(8,128)S(1)}, u32[]{:S(2)}, u32[]{:S(2)}) collective-permute-start(f32[32,128]{1,0:T(8,128)S(1)} %add.28), channel_id=1, source_target_pairs={{0,4},{2,6},{4,0},{6,2},{1,5},{3,7},{5,1},{7,3},{8,12},{10,14},{12... | collective-permute-start | bytes 49160 | tf_op jit(solution)/shard_map/ppermute | solution.py:484
  90.7 3.8 %collective-permute-start.13 = (f32[32,128]{1,0:T(8,128)S(1)}, f32[32,128]{1,0:T(8,128)S(1)}, u32[]{:S(2)}, u32[]{:S(2)}) collective-permute-start(f32[32,128]{1,0:T(8,128)S(1)} %add.28), channel_id=1, source_target_pairs={{0,2},{2,0},{4,6},{6,4},{1,3},{3,1},{5,7},{7,5},{8,10},{10,8},{12,... | collective-permute-start | bytes 49160 | tf_op jit(solution)/shard_map/ppermute | solution.py:484

commit v10 on v9

--- a/solution.py
+++ b/solution.py
@@ -412,7 +412,7 @@
             hi_out[i, :, at], lo_out[i, :, at] = split2(field[4 + i])
         return carry
 
-    lax.fori_loop(0, 14, row, 0, unroll=2)
+    lax.fori_loop(0, 14, row, 0, unroll=True)
 
 
 def second_basis(
@@ -478,14 +478,19 @@
     return from_low, lax.ppermute(to_low, axis, [(b, a) for a, b in up])
 
 
+def sum_copies(a, b, c, d, out):
+    total = (a[...] + b[...]) + (c[...] + d[...])
+    for n in range(out.shape[0]):
+        out[n] = total
+
+
 def everywhere(x, beside=()):
     x = x + lax.ppermute(x, "gy_1", [(0, 1), (1, 0)])
     one, two, three = [
         lax.ppermute(x, "gy_0", [(i, i ^ k) for i in range(4)]) for k in (1, 2, 3)
     ]
-    x = (x + one) + (two + three)
-    x, beside = lax.optimization_barrier((x, beside))
-    x = jnp.broadcast_to(x[None], (lax.axis_size(GX),) + x.shape)
+    x, one, two, three, beside = lax.optimization_barrier((x, one, two, three, beside))
+    (x,) = call(sum_copies, [(lax.axis_size(GX),) + x.shape], [x, one, two, three])
     return lax.all_to_all(x, GX, split_axis=0, concat_axis=0, tiled=True), beside
 
 

time: 112 us -> 112 us (level)
    pallas_call x12 -> x14, Pallas kernels: 28.9 us -> 28.9 us  [call(): pl.pallas_call(kernel, out_shape=tuple(outs), scratch_shapes=list(scratch...]
where the time goes in v10:
time: 112 us; the launch traced here: 111 us
  blocking collectives  44.1 us (39%)
  Pallas kernels  28.9 us (26%)
  starting transfers between devices  25.8 us (23%)
  waiting for transfers between devices  8.25 us (7%)
  local copies, waits for them, and re-layouts  1.8 us (2%)
  other arithmetic  1.59 us (1%)
    pallas_call x14, Pallas kernels, call(): pl.pallas_call(kernel, out_shape=tuple(outs), scratch_shapes=list(scratch...  28.9 us
    all_to_all x2, blocking collectives, everywhere(): lax.all_to_all(x, GX, split_axis=0, concat_axis=0, tiled=True)  26.9 us
    all_to_all x1, blocking collectives, exchange(): return lax.all_to_all(slots, GX_GY, split_axis=0, concat_axis=0, tiled=True)  17.2 us
    ppermute x4, starting transfers between devices, neighbours(): return (from_low, lax.ppermute(to_low, axis, [(b, a) for a, b in up]))  14.4 us
    ppermute x6, starting transfers between devices, everywhere(): lax.ppermute(x, 'gy_0', [(i, i ^ k) for i in range(4)])  8.19 us
    ppermute x6, waiting for transfers between devices, everywhere(): lax.ppermute(x, 'gy_0', [(i, i ^ k) for i in range(4)])  4.13 us
    ppermute x4, starting transfers between devices, neighbours(): from_low = lax.ppermute(to_high, axis, up)  3.04 us
    ppermute x2, waiting for transfers between devices, everywhere(): x = x + lax.ppermute(x, 'gy_1', [(0, 1), (1, 0)])  2.34 us
  transfers between devices with their start and end apart: 16, of which 8 were waited for; matrix products, arithmetic and copies ran while one was open for 1% of the time, Pallas kernels for 12%

profile of v10, /device:TPU:0, one launch (start us, length us, event | category | flops | bytes accessed | tf_op | source)
XLA Modules:
  0.0 111.2 jit_solution(11630929341818785793)
XLA Ops:
  0.6 0.8 pad_maximum_fusion.stack
  1.4 1.0 copy-done
  2.9 3.6 %collective-permute-start.1 = (f32[128,128]{1,0:T(8,128)S(1)}, f32[128,128]{1,0:T(8,128)S(1)}, u32[]{:S(2)}, u32[]{:S(2)}) collective-permute-start(f32[128,128]{1,0:T(8,128)S(1)} %get-tuple-element.78), channel_id=1, source_target_pairs={{1,0},{2,1},{3,2},{4,3},{5,4},{6,5},{7,6},{0,7},{9,8},{10,9},{11,1... | collective-permute-start | bytes 196616 | tf_op jit(solution)/shard_map/ppermute | solution.py:478
  6.4 0.8 pad_add_fusion.listed
  7.2 0.8 copy-done.3
  8.0 4.2 %place_slots.1 = f32[128,2,128]{2,1,0:T(2,128)S(1)} custom-call(s32[192,128]{1,0:T(8,128)S(1)} %pad_add_fusion.listed, f32[64,128]{1,0:T(8,128)S(1)} %bitcast.13), custom_call_target="tpu_custom_call" | custom-call | tf_op jit(solution)/shard_map/place_slots/pallas_call | solution.py:43
  12.4 1.6 %collective-permute-start.2 = (f32[7,168,128]{2,1,0:T(8,128)S(1)}, f32[7,168,128]{2,1,0:T(8,128)S(1)}, u32[]{:S(2)}, u32[]{:S(2)}) collective-permute-start(f32[7,168,128]{2,1,0:T(8,128)S(1)} %get-tuple-element.86), channel_id=1, source_target_pairs={{0,8},{8,16},{16,24},{24,32},{32,40},{40,48},{48,56},{56,64},{64,7... | collective-permute-start | bytes 1806344 | tf_op jit(solution)/shard_map/ppermute | solution.py:477
  14.1 3.8 %collective-permute-start.3 = (f32[7,168,128]{2,1,0:T(8,128)S(1)}, f32[7,168,128]{2,1,0:T(8,128)S(1)}, u32[]{:S(2)}, u32[]{:S(2)}) collective-permute-start(f32[7,168,128]{2,1,0:T(8,128)S(1)} %get-tuple-element.87), channel_id=1, source_target_pairs={{8,0},{16,8},{24,16},{32,24},{40,32},{48,40},{56,48},{64,56},{72,6... | collective-permute-start | bytes 1806344 | tf_op jit(solution)/shard_map/ppermute | solution.py:478
  17.9 17.2 %all_to_all.15.slots = f32[128,2,128]{2,1,0:T(2,128)S(1)} all-to-all(f32[128,2,128]{2,1,0:T(2,128)S(1)} %place_slots.1), channel_id=1, replica_groups=mesh['gx_0'=4,'gx_1'=4,'gy_0'=4,'gy_1'=2] {'gx_0','gx_1','gy_0','gy_1'}, dimensions={0} | all-to-all | bytes 262144 | tf_op jit(solution)/shard_map/all_to_all | solution.py:498
  35.1 3.7 %add_currents.1 = (f32[8,128,128]{2,1,0:T(8,128)S(1)}, f32[64,128]{1,0:T(8,128)S(1)}, f32[64,128]{1,0:T(8,128)S(1)}) custom-call(f32[128,2,128]{2,1,0:T(2,128)S(1)} %all_to_all.15.slots, f32[64,64]{1,0:T(8,128)S(1)} %copy-done.2), custom_call_target="tpu_custom_call" | custom-call | tf_op jit(solution)/shard_map/add_currents/pallas_call | solution.py:43
  38.9 2.9 %collective-permute-start.5 = (f32[64,128]{1,0:T(8,128)S(1)}, f32[64,128]{1,0:T(8,128)S(1)}, u32[]{:S(2)}, u32[]{:S(2)}) collective-permute-start(f32[64,128]{1,0:T(8,128)S(1)} %get-tuple-element.89), channel_id=1, source_target_pairs={{1,0},{2,1},{3,2},{4,3},{5,4},{6,5},{7,6},{0,7},{9,8},{10,9},{11,1... | collective-permute-start | bytes 98312 | tf_op jit(solution)/shard_map/ppermute | solution.py:478
  41.8 1.1 own_weights.1
  43.5 1.3 %collective-permute-start.6 = (f32[3,144,128]{2,1,0:T(8,128)S(1)}, f32[3,144,128]{2,1,0:T(8,128)S(1)}, u32[]{:S(2)}, u32[]{:S(2)}) collective-permute-start(f32[3,144,128]{2,1,0:T(8,128)S(1)} %get-tuple-element.111), channel_id=1, source_target_pairs={{0,8},{8,16},{16,24},{24,32},{32,40},{40,48},{48,56},{56,64},{64,7... | collective-permute-start | bytes 663560 | tf_op jit(solution)/shard_map/ppermute | solution.py:477
  44.8 4.2 %collective-permute-start.7 = (f32[3,144,128]{2,1,0:T(8,128)S(1)}, f32[3,144,128]{2,1,0:T(8,128)S(1)}, u32[]{:S(2)}, u32[]{:S(2)}) collective-permute-start(f32[3,144,128]{2,1,0:T(8,128)S(1)} %get-tuple-element.112), channel_id=1, source_target_pairs={{8,0},{16,8},{24,16},{32,24},{40,32},{48,40},{56,48},{64,56},{72,6... | collective-permute-start | bytes 663560 | tf_op jit(solution)/shard_map/ppermute | solution.py:478
  49.0 3.0 %grid_weights.1 = (f32[22,144,128]{2,1,0:T(8,128)S(1)}, f32[22,144,128]{2,1,0:T(8,128)S(1)}, f32[22,144,128]{2,1,0:T(8,128)S(1)}, f32[22,144,128]{2,1,0:T(8,128)...) custom-call(f32[8,128,128]{2,1,0:T(8,128)S(1)} %get-tuple-element.83.v, ...), custom_call_target="tpu_custom_call" | custom-call | tf_op jit(solution)/shard_map/grid_weights/pallas_call | solution.py:43
  52.0 1.2 %collective-permute-done.6.ix_low = f32[3,144,128]{2,1,0:T(8,128)S(1)} collective-permute-done((f32[3,144,128]{2,1,0:T(8,128)S(1)}, f32[3,144,128]{2,1,0:T(8,128)S(1)}, u32[]{:S(2)}, u32[]{:S(2)}) %collective-permute-start.6) | collective-permute-done | bytes 221216 | tf_op jit(solution)/shard_map/ppermute | solution.py:477
  53.2 4.2 %first_basis.1 = (f32[22,144,128]{2,1,0:T(8,128)S(1)}, f32[22,144,128]{2,1,0:T(8,128)S(1)}, f32[22,144,128]{2,1,0:T(8,128)S(1)}, f32[22,144,128]{2,1,0:T(8,128)S...) custom-call(f32[22,144,128]{2,1,0:T(8,128)S(1)} %get-tuple-element.103.diag, ...), custom_call_target="tpu_custom_call" | custom-call | tf_op jit(solution)/shard_map/first_basis/pallas_call | solution.py:43
  57.5 1.2 %collective-permute-done.8 = f32[32,128]{1,0:T(8,128)S(1)} collective-permute-done((f32[32,128]{1,0:T(8,128)S(1)}, f32[32,128]{1,0:T(8,128)S(1)}, u32[]{:S(2)}, u32[]{:S(2)}) %collective-permute-start.8) | collective-permute-done | bytes 16416 | tf_op jit(solution)/shard_map/ppermute | solution.py:488
  58.7 1.5 %collective-permute-start.11 = (f32[32,128]{1,0:T(8,128)S(1)}, f32[32,128]{1,0:T(8,128)S(1)}, u32[]{:S(2)}, u32[]{:S(2)}) collective-permute-start(f32[32,128]{1,0:T(8,128)S(1)} %add.6.a), channel_id=1, source_target_pairs={{0,6},{2,4},{4,2},{6,0},{1,7},{3,5},{5,3},{7,1},{8,14},{10,12},{12... | collective-permute-start | bytes 49160 | tf_op jit(solution)/shard_map/ppermute | solution.py:490
  60.2 1.4 %collective-permute-start.10 = (f32[32,128]{1,0:T(8,128)S(1)}, f32[32,128]{1,0:T(8,128)S(1)}, u32[]{:S(2)}, u32[]{:S(2)}) collective-permute-start(f32[32,128]{1,0:T(8,128)S(1)} %add.6.a), channel_id=1, source_target_pairs={{0,4},{2,6},{4,0},{6,2},{1,5},{3,7},{5,1},{7,3},{8,12},{10,14},{12... | collective-permute-start | bytes 49160 | tf_op jit(solution)/shard_map/ppermute | solution.py:490
  61.6 1.2 %collective-permute-start.9 = (f32[32,128]{1,0:T(8,128)S(1)}, f32[32,128]{1,0:T(8,128)S(1)}, u32[]{:S(2)}, u32[]{:S(2)}) collective-permute-start(f32[32,128]{1,0:T(8,128)S(1)} %add.6.a), channel_id=1, source_target_pairs={{0,2},{2,0},{4,6},{6,4},{1,3},{3,1},{5,7},{7,5},{8,10},{10,8},{12,... | collective-permute-start | bytes 49160 | tf_op jit(solution)/shard_map/ppermute | solution.py:490
  63.6 1.8 %collective-permute-done.10.c = f32[32,128]{1,0:T(8,128)S(1)} collective-permute-done((f32[32,128]{1,0:T(8,128)S(1)}, f32[32,128]{1,0:T(8,128)S(1)}, u32[]{:S(2)}, u32[]{:S(2)}) %collective-permute-start.10) | collective-permute-done | bytes 16416 | tf_op jit(solution)/shard_map/ppermute | solution.py:490
  65.5 15.0 %all_to_all.16.gram = f32[16,32,128]{2,1,0:T(8,128)S(1)} all-to-all(f32[16,32,128]{2,1,0:T(8,128)S(1)} %sum_copies.2), channel_id=1, replica_groups=mesh['gx_0'=4,'gx_1'=4,'gy_0'=4,'gy_1'=2] {'gx_0','gx_1'}, dimensions={0} | all-to-all | bytes 524288 | tf_op jit(solution)/shard_map/all_to_all | solution.py:494
  80.5 5.9 %second_basis.1 = (f32[22,144,128]{2,1,0:T(8,128)S(1)}, f32[22,144,128]{2,1,0:T(8,128)S(1)}, f32[22,144,128]{2,1,0:T(8,128)S(1)}, f32[22,144,128]{2,1,0:T(8,128)...) custom-call(f32[16,32,128]{2,1,0:T(8,128)S(1)} %all_to_all.16.gram, ...), custom_call_target="tpu_custom_call" | custom-call | tf_op jit(solution)/shard_map/second_basis/pallas_call | solution.py:43
  86.4 1.2 %collective-permute-done.12 = f32[32,128]{1,0:T(8,128)S(1)} collective-permute-done((f32[32,128]{1,0:T(8,128)S(1)}, f32[32,128]{1,0:T(8,128)S(1)}, u32[]{:S(2)}, u32[]{:S(2)}) %collective-permute-start.12) | collective-permute-done | bytes 16416 | tf_op jit(solution)/shard_map/ppermute | solution.py:488
  87.6 1.7 %collective-permute-start.15 = (f32[32,128]{1,0:T(8,128)S(1)}, f32[32,128]{1,0:T(8,128)S(1)}, u32[]{:S(2)}, u32[]{:S(2)}) collective-permute-start(f32[32,128]{1,0:T(8,128)S(1)} %add.7.a), channel_id=1, source_target_pairs={{0,6},{2,4},{4,2},{6,0},{1,7},{3,5},{5,3},{7,1},{8,14},{10,12},{12... | collective-permute-start | bytes 49160 | tf_op jit(solution)/shard_map/ppermute | solution.py:490
  89.3 1.4 %collective-permute-start.14 = (f32[32,128]{1,0:T(8,128)S(1)}, f32[32,128]{1,0:T(8,128)S(1)}, u32[]{:S(2)}, u32[]{:S(2)}) collective-permute-start(f32[32,128]{1,0:T(8,128)S(1)} %add.7.a), channel_id=1, source_target_pairs={{0,4},{2,6},{4,0},{6,2},{1,5},{3,7},{5,1},{7,3},{8,12},{10,14},{12... | collective-permute-start | bytes 49160 | tf_op jit(solution)/shard_map/ppermute | solution.py:490
  90.7 1.0 collective-permute-start.13
  91.7 0.7 from_lanes.1
  92.5 2.0 %collective-permute-done.14.c = f32[32,128]{1,0:T(8,128)S(1)} collective-permute-done((f32[32,128]{1,0:T(8,128)S(1)}, f32[32,128]{1,0:T(8,128)S(1)}, u32[]{:S(2)}, u32[]{:S(2)}) %collective-permute-start.14) | collective-permute-done | bytes 16416 | tf_op jit(solution)/shard_map/ppermute | solution.py:490
  94.6 11.9 %all_to_all.17.gram = f32[16,32,128]{2,1,0:T(8,128)S(1)} all-to-all(f32[16,32,128]{2,1,0:T(8,128)S(1)} %sum_copies.3), channel_id=1, replica_groups=mesh['gx_0'=4,'gx_1'=4,'gy_0'=4,'gy_1'=2] {'gx_0','gx_1'}, dimensions={0} | all-to-all | bytes 524288 | tf_op jit(solution)/shard_map/all_to_all | solution.py:494
  106.5 4.7 %finish.1 = (f32[1024,128]{1,0:T(8,128)}, f32[1024,128]{1,0:T(8,128)}) custom-call(f32[16,32,128]{2,1,0:T(8,128)S(1)} %all_to_all.17.gram, bf16[8,512,128]{2,1,0:T(8,128)(2,1)S(1)} %get-tuple-element.142.hi, bf16[8,512,128]{2,1,0:T(8,128)(2,1)S(1)} %get-tuple-element.143.lo, f32[8,128,128]{2,1,0:T(8,128)S(1)} %get-tuple-element.144.volts, ...), custom_call_target="tpu_custom_call" | custom-call | tf_op jit(solution)/shard_map/finish/pallas_call | solution.py:43
  (29 shorter events, 2.6 us)
Async XLA Ops:
  0.6 34.5 %copy-start.2 = (f32[64,64]{1,0:T(8,128)S(1)}, f32[64,64]{1,0:T(8,128)}, u32[]{:S(2)}) copy-start(f32[64,64]{1,0:T(8,128)} %waves.1) | copy-start | bytes 49156
  1.4 1.0 copy-start
  2.9 9.4 %collective-permute-start = (f32[128,128]{1,0:T(8,128)S(1)}, f32[128,128]{1,0:T(8,128)S(1)}, u32[]{:S(2)}, u32[]{:S(2)}) collective-permute-start(f32[128,128]{1,0:T(8,128)S(1)} %get-tuple-element.77), channel_id=1, source_target_pairs={{0,1},{1,2},{2,3},{3,4},{4,5},{5,6},{6,7},{7,0},{8,9},{9,10},{10,1... | collective-permute-start | bytes 196616 | tf_op jit(solution)/shard_map/ppermute | solution.py:477
  2.9 9.3 %collective-permute-start.1 = (f32[128,128]{1,0:T(8,128)S(1)}, f32[128,128]{1,0:T(8,128)S(1)}, u32[]{:S(2)}, u32[]{:S(2)}) collective-permute-start(f32[128,128]{1,0:T(8,128)S(1)} %get-tuple-element.78), channel_id=1, source_target_pairs={{1,0},{2,1},{3,2},{4,3},{5,4},{6,5},{7,6},{0,7},{9,8},{10,9},{11,1... | collective-permute-start | bytes 196616 | tf_op jit(solution)/shard_map/ppermute | solution.py:478
  7.2 0.8 copy-start.3
  12.4 36.5 %collective-permute-start.2 = (f32[7,168,128]{2,1,0:T(8,128)S(1)}, f32[7,168,128]{2,1,0:T(8,128)S(1)}, u32[]{:S(2)}, u32[]{:S(2)}) collective-permute-start(f32[7,168,128]{2,1,0:T(8,128)S(1)} %get-tuple-element.86), channel_id=1, source_target_pairs={{0,8},{8,16},{16,24},{24,32},{32,40},{40,48},{48,56},{56,64},{64,7... | collective-permute-start | bytes 1806344 | tf_op jit(solution)/shard_map/ppermute | solution.py:477
  14.1 34.9 %collective-permute-start.3 = (f32[7,168,128]{2,1,0:T(8,128)S(1)}, f32[7,168,128]{2,1,0:T(8,128)S(1)}, u32[]{:S(2)}, u32[]{:S(2)}) collective-permute-start(f32[7,168,128]{2,1,0:T(8,128)S(1)} %get-tuple-element.87), channel_id=1, source_target_pairs={{8,0},{16,8},{24,16},{32,24},{40,32},{48,40},{56,48},{64,56},{72,6... | collective-permute-start | bytes 1806344 | tf_op jit(solution)/shard_map/ppermute | solution.py:478
  38.8 4.6 %collective-permute-start.4 = (f32[64,128]{1,0:T(8,128)S(1)}, f32[64,128]{1,0:T(8,128)S(1)}, u32[]{:S(2)}, u32[]{:S(2)}) collective-permute-start(f32[64,128]{1,0:T(8,128)S(1)} %get-tuple-element.88), channel_id=1, source_target_pairs={{0,1},{1,2},{2,3},{3,4},{4,5},{5,6},{6,7},{7,0},{8,9},{9,10},{10,1... | collective-permute-start | bytes 98312 | tf_op jit(solution)/shard_map/ppermute | solution.py:477
  38.9 4.5 %collective-permute-start.5 = (f32[64,128]{1,0:T(8,128)S(1)}, f32[64,128]{1,0:T(8,128)S(1)}, u32[]{:S(2)}, u32[]{:S(2)}) collective-permute-start(f32[64,128]{1,0:T(8,128)S(1)} %get-tuple-element.89), channel_id=1, source_target_pairs={{1,0},{2,1},{3,2},{4,3},{5,4},{6,5},{7,6},{0,7},{9,8},{10,9},{11,1... | collective-permute-start | bytes 98312 | tf_op jit(solution)/shard_map/ppermute | solution.py:478
  43.5 9.7 %collective-permute-start.6 = (f32[3,144,128]{2,1,0:T(8,128)S(1)}, f32[3,144,128]{2,1,0:T(8,128)S(1)}, u32[]{:S(2)}, u32[]{:S(2)}) collective-permute-start(f32[3,144,128]{2,1,0:T(8,128)S(1)} %get-tuple-element.111), channel_id=1, source_target_pairs={{0,8},{8,16},{16,24},{24,32},{32,40},{40,48},{48,56},{56,64},{64,7... | collective-permute-start | bytes 663560 | tf_op jit(solution)/shard_map/ppermute | solution.py:477
  44.8 8.4 %collective-permute-start.7 = (f32[3,144,128]{2,1,0:T(8,128)S(1)}, f32[3,144,128]{2,1,0:T(8,128)S(1)}, u32[]{:S(2)}, u32[]{:S(2)}) collective-permute-start(f32[3,144,128]{2,1,0:T(8,128)S(1)} %get-tuple-element.112), channel_id=1, source_target_pairs={{8,0},{16,8},{24,16},{32,24},{40,32},{48,40},{56,48},{64,56},{72,6... | collective-permute-start | bytes 663560 | tf_op jit(solution)/shard_map/ppermute | solution.py:478
  57.4 1.3 %collective-permute-start.8 = (f32[32,128]{1,0:T(8,128)S(1)}, f32[32,128]{1,0:T(8,128)S(1)}, u32[]{:S(2)}, u32[]{:S(2)}) collective-permute-start(f32[32,128]{1,0:T(8,128)S(1)} %get-tuple-element.113), channel_id=1, source_target_pairs={{0,1},{1,0},{2,3},{3,2},{4,5},{5,4},{6,7},{7,6},{8,9},{9,8},{10,11... | collective-permute-start | bytes 49160 | tf_op jit(solution)/shard_map/ppermute | solution.py:488
  58.7 4.9 %collective-permute-start.11 = (f32[32,128]{1,0:T(8,128)S(1)}, f32[32,128]{1,0:T(8,128)S(1)}, u32[]{:S(2)}, u32[]{:S(2)}) collective-permute-start(f32[32,128]{1,0:T(8,128)S(1)} %add.6.a), channel_id=1, source_target_pairs={{0,6},{2,4},{4,2},{6,0},{1,7},{3,5},{5,3},{7,1},{8,14},{10,12},{12... | collective-permute-start | bytes 49160 | tf_op jit(solution)/shard_map/ppermute | solution.py:490
  60.2 5.2 %collective-permute-start.10 = (f32[32,128]{1,0:T(8,128)S(1)}, f32[32,128]{1,0:T(8,128)S(1)}, u32[]{:S(2)}, u32[]{:S(2)}) collective-permute-start(f32[32,128]{1,0:T(8,128)S(1)} %add.6.a), channel_id=1, source_target_pairs={{0,4},{2,6},{4,0},{6,2},{1,5},{3,7},{5,1},{7,3},{8,12},{10,14},{12... | collective-permute-start | bytes 49160 | tf_op jit(solution)/shard_map/ppermute | solution.py:490
  61.6 3.9 %collective-permute-start.9 = (f32[32,128]{1,0:T(8,128)S(1)}, f32[32,128]{1,0:T(8,128)S(1)}, u32[]{:S(2)}, u32[]{:S(2)}) collective-permute-start(f32[32,128]{1,0:T(8,128)S(1)} %add.6.a), channel_id=1, source_target_pairs={{0,2},{2,0},{4,6},{6,4},{1,3},{3,1},{5,7},{7,5},{8,10},{10,8},{12,... | collective-permute-start | bytes 49160 | tf_op jit(solution)/shard_map/ppermute | solution.py:490
  80.4 11.2 %copy-start.1 = (f32[32,4,8,128]{3,2,1,0:T(8,128)S(1)}, f32[32,4,8,128]{3,2,1,0:T(8,128)}, u32[]{:S(2)}) copy-start(f32[32,4,8,128]{3,2,1,0:T(8,128)} %param.10) | copy-start | bytes 1572868
  86.3 1.3 %collective-permute-start.12 = (f32[32,128]{1,0:T(8,128)S(1)}, f32[32,128]{1,0:T(8,128)S(1)}, u32[]{:S(2)}, u32[]{:S(2)}) collective-permute-start(f32[32,128]{1,0:T(8,128)S(1)} %get-tuple-element.128), channel_id=1, source_target_pairs={{0,1},{1,0},{2,3},{3,2},{4,5},{5,4},{6,7},{7,6},{8,9},{9,8},{10,11... | collective-permute-start | bytes 49160 | tf_op jit(solution)/shard_map/ppermute | solution.py:488
  87.6 4.9 %collective-permute-start.15 = (f32[32,128]{1,0:T(8,128)S(1)}, f32[32,128]{1,0:T(8,128)S(1)}, u32[]{:S(2)}, u32[]{:S(2)}) collective-permute-start(f32[32,128]{1,0:T(8,128)S(1)} %add.7.a), channel_id=1, source_target_pairs={{0,6},{2,4},{4,2},{6,0},{1,7},{3,5},{5,3},{7,1},{8,14},{10,12},{12... | collective-permute-start | bytes 49160 | tf_op jit(solution)/shard_map/ppermute | solution.py:490
  89.3 5.2 %collective-permute-start.14 = (f32[32,128]{1,0:T(8,128)S(1)}, f32[32,128]{1,0:T(8,128)S(1)}, u32[]{:S(2)}, u32[]{:S(2)}) collective-permute-start(f32[32,128]{1,0:T(8,128)S(1)} %add.7.a), channel_id=1, source_target_pairs={{0,4},{2,6},{4,0},{6,2},{1,5},{3,7},{5,1},{7,3},{8,12},{10,14},{12... | collective-permute-start | bytes 49160 | tf_op jit(solution)/shard_map/ppermute | solution.py:490
  90.7 3.8 %collective-permute-start.13 = (f32[32,128]{1,0:T(8,128)S(1)}, f32[32,128]{1,0:T(8,128)S(1)}, u32[]{:S(2)}, u32[]{:S(2)}) collective-permute-start(f32[32,128]{1,0:T(8,128)S(1)} %add.7.a), channel_id=1, source_target_pairs={{0,2},{2,0},{4,6},{6,4},{1,3},{3,1},{5,7},{7,5},{8,10},{10,8},{12,... | collective-permute-start | bytes 49160 | tf_op jit(solution)/shard_map/ppermute | solution.py:490
